TPU v7x, 32 devices: a whole 2x2x4 slice. The times are simulated.
32 devices in a mesh: batch: 8 (over z, y), tensor: 4 (over x, core).
Axes of the slice: x: 2, y: 2, z: 4, core: 2. Of those that a mesh axis runs over, the one named last changes fastest.
Arguments:
- maps_five: bfloat16 [2, 48, 5, 5, 2048], P(None, 'batch', None, None, 'tensor'), may hold values from -6 to 6
- maps_seven: bfloat16 [2, 48, 7, 7, 2048], P(None, 'batch', None, None, 'tensor'), may hold values from -6 to 6
- maps_nine: bfloat16 [2, 24, 9, 9, 2048], P(None, 'batch', None, None, 'tensor'), may hold values from -6 to 6
- upstream_five: bfloat16 [2, 48, 5, 5, 2048], P(None, 'batch', None, None, 'tensor'), may hold values from -6 to 6
- upstream_seven: bfloat16 [2, 48, 7, 7, 2048], P(None, 'batch', None, None, 'tensor'), may hold values from -6 to 6
- upstream_nine: bfloat16 [2, 24, 9, 9, 2048], P(None, 'batch', None, None, 'tensor'), may hold values from -6 to 6
- reduce_weight: bfloat16 [2048, 1024], P(None, 'tensor'), may hold values from -0.125 to 0.125
- group_weight: bfloat16 [3, 3, 32, 32, 32], P(None, None, 'tensor'), may hold values from -0.375 to 0.375
- expand_weight: bfloat16 [1024, 2048], P('tensor'), may hold values from -0.1875 to 0.1875
- first_gain: float32 [1024], P('tensor'), may hold values from 0.25 to 1.75
- first_bias: float32 [1024], P('tensor'), may hold values from -3 to 3
- second_gain: float32 [1024], P('tensor'), may hold values from 0.25 to 1.75
- second_bias: float32 [1024], P('tensor'), may hold values from -3 to 3
- third_gain: float32 [2048], P('tensor'), may hold values from 0.25 to 1.75
- third_bias: float32 [2048], P('tensor'), may hold values from -3 to 3
- image_counts: int32 [2, 8, 3], P(None, 'batch'), may hold values from 0 to 6, as said below
Outputs:
- result_five: bfloat16 [2, 48, 5, 5, 2048], P(None, 'batch', None, None, 'tensor')
- result_seven: bfloat16 [2, 48, 7, 7, 2048], P(None, 'batch', None, None, 'tensor')
- result_nine: bfloat16 [2, 24, 9, 9, 2048], P(None, 'batch', None, None, 'tensor')
- backprop_five: float32 [2, 48, 5, 5, 2048], P(None, 'batch', None, None, 'tensor')
- backprop_seven: float32 [2, 48, 7, 7, 2048], P(None, 'batch', None, None, 'tensor')
- backprop_nine: float32 [2, 24, 9, 9, 2048], P(None, 'batch', None, None, 'tensor')
- reduce_grad: float32 [2048, 1024], P(None, 'tensor')
- group_grad: float32 [3, 3, 32, 32, 32], P(None, None, 'tensor')
- expand_grad: float32 [1024, 2048], P('tensor')
- first_gain_grad: float32 [1024], P('tensor')
- first_bias_grad: float32 [1024], P('tensor')
- second_gain_grad: float32 [1024], P('tensor')
- second_bias_grad: float32 [1024], P('tensor')
- third_gain_grad: float32 [2048], P('tensor')
- third_bias_grad: float32 [2048], P('tensor')
Inputs may be any that keep to these rules, and one draw needn't show every extreme that they name: image_counts[m, b, r] is the number of live images of resolution r (5x5, 7x7, 9x9) on rank b in micro-batch m, at most 6, 6, 3 for r = 0, 1, 2; a rank's live images fill its first slots; for every micro-batch and resolution some rank holds the most.
All inputs are finite; a program needn't handle non-finite values.
Results may differ from a plain program's by a relative error of at most 0.0095.
Values may be sent and summed in bfloat16 or wider, within the bound.
No kernel may reach another device: no remote copies, remote signals or barrier semaphores. Data moves between devices by JAX's collectives and lax.ppermute only.
A program may use at most 192 MiB of HBM per device.

v0:
```python
import jax
import jax.numpy as jnp
from jax import lax
from jax.sharding import PartitionSpec as P

EPSILON = 1e-05


def slope(values):
    sigmoid_value = jax.nn.sigmoid(values)
    return sigmoid_value * (1.0 + values * (1.0 - sigmoid_value))


def normed_parts(values, sums, squares, pixel_total):
    mean_value = sums / pixel_total
    variance = squares / pixel_total - mean_value * mean_value
    inverse = lax.rsqrt(variance + EPSILON)
    return ((values - mean_value) * inverse, inverse)


def norm_back(grad_pre, normed, inverse, gain, live_mask, pixel_total, grad_sum, grad_cross):
    return inverse * gain * (grad_pre - live_mask * (grad_sum + normed * grad_cross) / pixel_total)


def padded_blocks(flat, edges, slot_list):
    channel_count = flat.shape[1]
    offset = 0
    found = []
    for edge_size, slot_count in zip(edges, slot_list):
        pixel_count = slot_count * edge_size * edge_size
        blocks = flat[offset : offset + pixel_count].reshape(
            slot_count, edge_size, edge_size, channel_count
        )
        found.append(jnp.pad(blocks, ((0, 0), (1, 1), (1, 1), (0, 0))))
        offset = offset + pixel_count
    return found


def tap_conv(flat, matrices, edges, slot_list):
    channel_count = flat.shape[1]
    pieces = []
    for padded, edge_size, slot_count in zip(
        padded_blocks(flat, edges, slot_list), edges, slot_list
    ):
        pixel_count = slot_count * edge_size * edge_size
        summed = jnp.zeros((pixel_count, matrices.shape[2]), jnp.float32)
        for tap_index in range(9):
            row_start = tap_index // 3
            col_start = tap_index % 3
            window = padded[
                :, row_start : row_start + edge_size, col_start : col_start + edge_size, :
            ].reshape(pixel_count, channel_count)
            summed = summed + jnp.dot(
                window, matrices[tap_index], preferred_element_type=jnp.float32
            )
        pieces.append(summed)
    return jnp.concatenate(pieces, 0)


def kernel_grad(flat, grad_flat, edges, slot_list, group_count, group_width):
    collected = jnp.zeros((9, group_count, group_width, group_width), jnp.float32)
    offset = 0
    for padded, edge_size, slot_count in zip(
        padded_blocks(flat, edges, slot_list), edges, slot_list
    ):
        pixel_count = slot_count * edge_size * edge_size
        grad_part = grad_flat[offset : offset + pixel_count].reshape(
            pixel_count, group_count, group_width
        )
        taps_list = []
        for tap_index in range(9):
            row_start = tap_index // 3
            col_start = tap_index % 3
            window = padded[
                :, row_start : row_start + edge_size, col_start : col_start + edge_size, :
            ].reshape(pixel_count, group_count, group_width)
            taps_list.append(
                jnp.einsum("pgi,pgo->gio", window, grad_part, preferred_element_type=jnp.float32)
            )
        collected = collected + jnp.stack(taps_list, 0)
        offset = offset + pixel_count
    return collected.reshape(3, 3, group_count, group_width, group_width)


def split_back(flat, edges, slot_list, channel_count):
    found = []
    offset = 0
    for edge_size, slot_count in zip(edges, slot_list):
        pixel_count = slot_count * edge_size * edge_size
        found.append(
            flat[offset : offset + pixel_count].reshape(
                slot_count, edge_size, edge_size, channel_count
            )
        )
        offset = offset + pixel_count
    return found


def per_device(
    maps_five,
    maps_seven,
    maps_nine,
    upstream_five,
    upstream_seven,
    upstream_nine,
    reduce_weight,
    group_weight,
    expand_weight,
    first_gain,
    first_bias,
    second_gain,
    second_bias,
    third_gain,
    third_bias,
    image_counts,
):
    all_maps = (maps_five, maps_seven, maps_nine)
    all_upstream = (upstream_five, upstream_seven, upstream_nine)
    edges = tuple((piece.shape[2] for piece in all_maps))
    slot_list = tuple((piece.shape[1] for piece in all_maps))
    micro_count = maps_five.shape[0]
    chan_local = maps_five.shape[-1]
    group_count = group_weight.shape[2]
    group_width = group_weight.shape[3]
    inner_local = group_count * group_width
    identity = jnp.eye(group_count, dtype=jnp.bfloat16)
    matrices = jnp.einsum("abgio,gh->abgiho", group_weight, identity).reshape(
        9, inner_local, inner_local
    )
    matrices_back = jnp.transpose(jnp.flip(matrices, 0), (0, 2, 1))
    expand_cols = lax.all_to_all(expand_weight, "tensor", split_axis=1, concat_axis=0, tiled=True)
    reduce_rows = lax.all_to_all(reduce_weight, "tensor", split_axis=0, concat_axis=1, tiled=True)
    reduce_acc = jnp.zeros(reduce_weight.shape, jnp.float32)
    group_acc = jnp.zeros(group_weight.shape, jnp.float32)
    expand_acc = jnp.zeros(expand_weight.shape, jnp.float32)
    gain_one_acc = jnp.zeros_like(first_gain)
    bias_one_acc = jnp.zeros_like(first_bias)
    gain_two_acc = jnp.zeros_like(second_gain)
    bias_two_acc = jnp.zeros_like(second_bias)
    gain_three_acc = jnp.zeros_like(third_gain)
    bias_three_acc = jnp.zeros_like(third_bias)
    results = [[], [], []]
    backs = [[], [], []]
    for step_index in range(micro_count):
        local_maps = jnp.concatenate(
            [piece[step_index].reshape(-1, chan_local) for piece in all_maps], 0
        )
        counts_now = image_counts[step_index, 0]
        mask_pieces = []
        local_pixels = jnp.float32(0.0)
        for column in range(3):
            live = (jnp.arange(slot_list[column], dtype=jnp.int32) < counts_now[column]).astype(
                jnp.float32
            )
            mask_pieces.append(jnp.repeat(live, edges[column] * edges[column]))
            local_pixels = local_pixels + (
                counts_now[column] * edges[column] * edges[column]
            ).astype(jnp.float32)
        live_mask = jnp.concatenate(mask_pieces, 0)[:, None]
        full_maps = lax.all_gather(local_maps, "tensor", axis=1, tiled=True)
        first = jnp.dot(full_maps, reduce_weight, preferred_element_type=jnp.float32)
        sum_one, square_one, pixel_total = lax.psum(
            (jnp.sum(live_mask * first, 0), jnp.sum(live_mask * first * first, 0), local_pixels),
            "batch",
        )
        normed_one, inverse_one = normed_parts(first, sum_one, square_one, pixel_total)
        pre_one = first_gain * normed_one + first_bias
        act_one = (live_mask * jax.nn.silu(pre_one)).astype(jnp.bfloat16)
        second = tap_conv(act_one, matrices, edges, slot_list)
        sum_two, square_two = lax.psum(
            (jnp.sum(live_mask * second, 0), jnp.sum(live_mask * second * second, 0)), "batch"
        )
        normed_two, inverse_two = normed_parts(second, sum_two, square_two, pixel_total)
        pre_two = second_gain * normed_two + second_bias
        act_two = (live_mask * jax.nn.silu(pre_two)).astype(jnp.bfloat16)
        third = jnp.dot(
            lax.all_gather(act_two, "tensor", axis=1, tiled=True),
            expand_cols,
            preferred_element_type=jnp.float32,
        )
        sum_three, square_three = lax.psum(
            (jnp.sum(live_mask * third, 0), jnp.sum(live_mask * third * third, 0)), "batch"
        )
        normed_three, inverse_three = normed_parts(third, sum_three, square_three, pixel_total)
        pre_three = third_gain * normed_three + third_bias + local_maps.astype(jnp.float32)
        output = (live_mask * jax.nn.silu(pre_three)).astype(jnp.bfloat16)
        upstream = jnp.concatenate(
            [piece[step_index].reshape(-1, chan_local) for piece in all_upstream], 0
        ).astype(jnp.float32)
        grad_pre_three = live_mask * upstream * slope(pre_three)
        sum_g_three, cross_three = lax.psum(
            (jnp.sum(grad_pre_three, 0), jnp.sum(grad_pre_three * normed_three, 0)), "batch"
        )
        bias_three_acc = bias_three_acc + sum_g_three
        gain_three_acc = gain_three_acc + cross_three
        grad_third = norm_back(
            grad_pre_three,
            normed_three,
            inverse_three,
            third_gain,
            live_mask,
            pixel_total,
            sum_g_three,
            cross_three,
        ).astype(jnp.bfloat16)
        full_grad = lax.all_gather(grad_third, "tensor", axis=1, tiled=True)
        expand_step = lax.dot_general(
            act_two, full_grad, (((0,), (0,)), ((), ())), preferred_element_type=jnp.float32
        )
        grad_act_two = lax.dot_general(
            full_grad, expand_weight, (((1,), (1,)), ((), ())), preferred_element_type=jnp.float32
        )
        grad_pre_two = live_mask * grad_act_two * slope(pre_two)
        sum_g_two, cross_two = lax.psum(
            (jnp.sum(grad_pre_two, 0), jnp.sum(grad_pre_two * normed_two, 0)), "batch"
        )
        bias_two_acc = bias_two_acc + sum_g_two
        gain_two_acc = gain_two_acc + cross_two
        grad_second = norm_back(
            grad_pre_two,
            normed_two,
            inverse_two,
            second_gain,
            live_mask,
            pixel_total,
            sum_g_two,
            cross_two,
        ).astype(jnp.bfloat16)
        group_step = kernel_grad(act_one, grad_second, edges, slot_list, group_count, group_width)
        grad_act_one = tap_conv(grad_second, matrices_back, edges, slot_list)
        grad_pre_one = live_mask * grad_act_one * slope(pre_one)
        sum_g_one, cross_one = lax.psum(
            (jnp.sum(grad_pre_one, 0), jnp.sum(grad_pre_one * normed_one, 0)), "batch"
        )
        bias_one_acc = bias_one_acc + sum_g_one
        gain_one_acc = gain_one_acc + cross_one
        grad_first = norm_back(
            grad_pre_one,
            normed_one,
            inverse_one,
            first_gain,
            live_mask,
            pixel_total,
            sum_g_one,
            cross_one,
        ).astype(jnp.bfloat16)
        reduce_step = lax.dot_general(
            full_maps, grad_first, (((0,), (0,)), ((), ())), preferred_element_type=jnp.float32
        )
        back_local = lax.dot_general(
            lax.all_gather(grad_first, "tensor", axis=1, tiled=True),
            reduce_rows,
            (((1,), (1,)), ((), ())),
            preferred_element_type=jnp.float32,
        )
        backprop = grad_pre_three + back_local
        reduce_acc = reduce_acc + reduce_step
        group_acc = group_acc + group_step
        expand_acc = expand_acc + expand_step
        for column, piece in enumerate(split_back(output, edges, slot_list, chan_local)):
            results[column].append(piece)
        for column, piece in enumerate(split_back(backprop, edges, slot_list, chan_local)):
            backs[column].append(piece)
    reduce_acc, group_acc, expand_acc = lax.psum((reduce_acc, group_acc, expand_acc), "batch")
    stacked = [jnp.stack(results[column], 0) for column in range(3)]
    grads_in = [jnp.stack(backs[column], 0) for column in range(3)]
    return (
        stacked[0],
        stacked[1],
        stacked[2],
        grads_in[0],
        grads_in[1],
        grads_in[2],
        reduce_acc,
        group_acc,
        expand_acc,
        gain_one_acc,
        bias_one_acc,
        gain_two_acc,
        bias_two_acc,
        gain_three_acc,
        bias_three_acc,
    )


def solution(mesh):
    in_specs = (
        P(None, "batch", None, None, "tensor"),
        P(None, "batch", None, None, "tensor"),
        P(None, "batch", None, None, "tensor"),
        P(None, "batch", None, None, "tensor"),
        P(None, "batch", None, None, "tensor"),
        P(None, "batch", None, None, "tensor"),
        P(None, "tensor"),
        P(None, None, "tensor", None, None),
        P("tensor", None),
        P("tensor"),
        P("tensor"),
        P("tensor"),
        P("tensor"),
        P("tensor"),
        P("tensor"),
        P(None, "batch", None),
    )
    out_specs = (
        P(None, "batch", None, None, "tensor"),
        P(None, "batch", None, None, "tensor"),
        P(None, "batch", None, None, "tensor"),
        P(None, "batch", None, None, "tensor"),
        P(None, "batch", None, None, "tensor"),
        P(None, "batch", None, None, "tensor"),
        P(None, "tensor"),
        P(None, None, "tensor", None, None),
        P("tensor", None),
        P("tensor"),
        P("tensor"),
        P("tensor"),
        P("tensor"),
        P("tensor"),
        P("tensor"),
    )
    return jax.shard_map(
        per_device, mesh=mesh, in_specs=in_specs, out_specs=out_specs, check_vma=False
    )
```

profile of v0, /device:TPU:0, one launch (start us, length us, event | category | flops | bytes accessed | tf_op | source)
XLA Modules:
  0.0 804.1 jit_solution(13690166309197781689)
XLA Ops:
  7.2 3.5 slice_reduce_fusion.7
  10.9 2.6 slice_reduce_fusion.3
  27.0 2.8 multiply_bitcast_fusion
  29.8 5.8 reshape.665
  35.7 9.9 %all-gather.9.cloned.1.call-done = bf16[687,2048]{1,0:T(8,128)(2,1)} async-done(((bf16[687,512]{1,0:T(8,128)(2,1)}), bf16[687,2048]{1,0:T(8,128)(2,1)}) %all-gather.9.cloned.1.call-update) | async-done | bytes 2813968 | tf_op jit(solution)/shard_map/all_gather | solution.py:160
  45.6 3.0 fusion.58
  48.6 25.9 %all-gather.13.cloned.1.call-done = bf16[687,2048]{1,0:T(8,128)(2,1)} async-done(((bf16[687,512]{1,0:T(8,128)(2,1)}), bf16[687,2048]{1,0:T(8,128)(2,1)}) %all-gather.13.cloned.1.call-update) | async-done | bytes 2813968 | tf_op jit(solution)/shard_map/all_gather | solution.py:160
  74.5 3.0 fusion.60
  77.5 22.4 %all-reduce.17 = (f32[256]{0:T(256)S(1)}, f32[]{:T(128)}, f32[256]{0:T(256)S(1)}, f32[256]{0:T(256)S(1)}, f32[]{:T(128)}, /*index=5*/f32[256]{0:T(256)S(1)}) all-reduce(f32[256]{0:T(256)S(1)} %get-tuple-element.60, f32[]{:T(128)S(6)} %add.636, f32[256]{0:T(256)S(1)} %get-tuple-element.59, ...), channel_id=1, replica_groups=mesh['batch'=8,'tensor'=4] {'batch'}, use_global_device_ids=true, to_apply=%region_14.15 | all-reduce | flops 1026 | bytes 8208 | tf_op jit(solution)/shard_map/psum | solution.py:162
  99.9 2.0 fusion.143
  105.9 2.4 pad_slice_fusion.88
  108.4 1.7 reshape.664
  120.7 2.9 pad_slice_fusion.24
  123.7 1.8 reshape.674
  125.5 1.8 fusion.116
  138.5 3.3 pad_slice_fusion.56
  141.8 1.9 reshape.683
  143.7 1.8 fusion.115
  165.3 2.8 pad_slice_fusion.16
  168.2 1.8 reshape.704
  170.0 1.8 fusion.113
  181.2 3.3 pad_slice_fusion.48
  203.9 17.5 %all-reduce.16 = (f32[256]{0:T(256)S(1)}, f32[256]{0:T(256)S(1)}, f32[256]{0:T(256)S(1)}, f32[256]{0:T(256)S(1)}) all-reduce(f32[256]{0:T(256)S(1)} %get-tuple-element.56, f32[256]{0:T(256)S(1)} %get-tuple-element.55, f32[256]{0:T(256)S(1)} %get-tuple-element.54, ...), channel_id=1, replica_groups=mesh['batch'=8,'tensor'=4] {'batch'}, use_global_device_ids=true, to_apply=%region_19.20 | all-reduce | flops 1024 | bytes 8192 | tf_op jit(solution)/shard_map/psum | solution.py:170
  221.4 2.0 fusion.146
  225.5 2.3 copy.219
  227.8 3.5 all-to-all-start
  231.4 4.3 slice_reduce_fusion.5
  235.7 1.9 reshape_squeeze.44
  237.5 1.8 reshape_squeeze.47
  239.4 4.7 slice_reduce_fusion.1
  244.1 1.8 reshape_squeeze.43
  246.7 3.1 slice_reduce_fusion.9
  253.5 3.7 multiply_reduce_fusion.1
  257.3 12.4 %all-gather.15.cloned.1.call-done = bf16[687,1024]{1,0:T(8,128)(2,1)} async-done(((bf16[687,256]{1,0:T(8,128)(2,1)}), bf16[687,1024]{1,0:T(8,128)(2,1)}) %all-gather.15.cloned.1.call-update) | async-done | bytes 1406992 | tf_op jit(solution)/shard_map/all_gather | solution.py:177
  269.6 3.3 multiply_reduce_fusion
  273.0 21.6 %all-reduce.15 = (f32[512]{0:T(512)S(1)}, f32[512]{0:T(512)S(1)}, f32[512]{0:T(512)S(1)}, f32[512]{0:T(512)S(1)}) all-reduce(f32[512]{0:T(512)S(1)} %get-tuple-element.48, f32[512]{0:T(512)S(1)} %get-tuple-element.47, f32[512]{0:T(512)S(1)} %get-tuple-element.46, ...), channel_id=1, replica_groups=mesh['batch'=8,'tensor'=4] {'batch'}, use_global_device_ids=true, to_apply=%region_25.26 | all-reduce | flops 2048 | bytes 16384 | tf_op jit(solution)/shard_map/psum | solution.py:181
  294.6 2.0 fusion.149
  296.6 9.4 %fusion.137 = (f32[512]{0:T(512)}, f32[512]{0:T(512)}, f32[687,512]{1,0:T(8,128)}, bf16[687,512]{1,0:T(8,128)(2,1)}, bf16[687,512]{1,0:T(8,128)(2,1)}, /*index=5...) fusion(f32[512]{0:T(512)S(1)} %get-tuple-element.125, f32[687,512]{1,0:T(8,128)} %get-tuple-element.258, ...), kind=kLoop, calls=%fused_computation.511 | loop fusion | flops 22509568 | bytes 9874808 | tf_op jit(solution)/shard_map/reduce_sum | solution.py:192
  306.0 18.1 %all-reduce.14 = (f32[512]{0:T(512)}, f32[512]{0:T(512)}, f32[512]{0:T(512)}, f32[512]{0:T(512)}) all-reduce(f32[512]{0:T(512)} %get-tuple-element.229, f32[512]{0:T(512)} %get-tuple-element.230, f32[512]{0:T(512)} %get-tuple-element.50, f32[512]{0:T(512)} %get-tuple-element.49), channel_id=1, replica_groups=mesh['batch'=8,'tensor'=4] {'batch'}, use_global_device_ids=true, to_apply=%region_41.42 | all-reduce | flops 2048 | bytes 16384 | tf_op jit(solution)/shard_map/psum | solution.py:191
  324.1 3.3 multiply_convert_fusion
  327.5 3.7 multiply_convert_fusion.1
  331.6 2.2 reshape.785
  333.8 2.2 reshape.787
  385.0 2.1 reshape.832
  389.5 4.2 fusion.142
  393.7 4.1 fusion.140
  397.8 19.7 %all-reduce.13 = (f32[256]{0:T(256)}, f32[256]{0:T(256)}, f32[256]{0:T(256)S(1)}, f32[256]{0:T(256)S(1)}) all-reduce(f32[256]{0:T(256)S(1)} %get-tuple-element.68, f32[256]{0:T(256)S(1)} %get-tuple-element.67, f32[256]{0:T(256)S(1)} %get-tuple-element.64, f32[256]{0:T(256)S(1)} %get-tuple-element.63), channel_id=1, replica_groups=mesh['batch'=8,'tensor'=4] {'batch'}, use_global_device_ids=true, to_apply=%region_45.46 | all-reduce | flops 1024 | bytes 8192 | tf_op jit(solution)/shard_map/psum | solution.py:214
  417.5 2.1 multiply_convert_fusion.7
  500.2 3.2 pad_slice_fusion.40
  513.2 1.7 reshape.744
  530.7 17.3 %all-reduce.12 = (f32[256]{0:T(256)S(1)}, f32[256]{0:T(256)S(1)}, f32[256]{0:T(256)S(1)}, f32[256]{0:T(256)S(1)}) all-reduce(f32[256]{0:T(256)S(1)} %get-tuple-element.232, f32[256]{0:T(256)S(1)} %get-tuple-element.233, f32[256]{0:T(256)S(1)} %get-tuple-element.62, ...), channel_id=1, replica_groups=mesh['batch'=8,'tensor'=4] {'batch'}, use_global_device_ids=true, to_apply=%region_49.50 | all-reduce | flops 1024 | bytes 8192 | tf_op jit(solution)/shard_map/psum | solution.py:232
  578.7 1.7 multiply_convert_fusion.4
  581.6 2.9 fusion.153
  586.7 2.3 convolution_add_fusion
  589.1 2.4 convolution_add_fusion.1
  592.5 3.2 add_add_fusion
  596.9 16.9 %all_to_all.38 = bf16[4,512,256]{2,1,0:T(8,128)(2,1)S(1)} all-to-all(bf16[4,512,256]{2,1,0:T(8,128)(2,1)S(1)} %bitcast.594), channel_id=1, replica_groups=mesh['batch'=8,'tensor'=4] {'tensor'}, dimensions={0} | all-to-all | bytes 2097152 | tf_op jit(solution)/shard_map/all_to_all | solution.py:132
  620.1 2.2 pad_maximum_fusion.8
  624.5 2.5 convolution_add_fusion.3
  628.9 2.5 convolution_add_fusion.2
  634.7 1.7 copy.288
  637.8 2.0 copy.287
  641.4 149.5 %all-reduce.21.cloned.1.call-done = (f32[2048,256]{1,0:T(8,128)}, f32[3,3,8,32,32]{4,3,2,1,0:T(8,128)}, f32[256,2048]{1,0:T(8,128)}) async-done(((f32[2048,256]{1,0:T(8,128)}, f32[3,3,8,32,32]{4,3,2,1,0:T(8,128)}, f32[256,2048]{1,0:T(8,128)}), (f32[2048,256]{1,0:T(8,128)}, f32[3,3,8,32,32]{4,3,2,1,0:T(8,128)}, f32[256,2048]{1,0:T(8,128)})) %all-reduce.21.cloned.1.call-update) | async-done | bytes 4489232 | tf_op jit(solution)/shard_map/psum | solution.py:264
  790.9 3.1 copy.448
  (1073 shorter events, 302.2 us)
Async XLA Ops:
  7.2 38.4 %all-gather.9.cloned.1.call-start = ((), (), s32[]{:S(2)}) async-start(), calls=%async_computation.2 | async-start | bytes 3522560 | tf_op jit(solution)/shard_map/all_gather | solution.py:160
  16.1 58.4 %all-gather.13.cloned.1.call-start = ((), (), s32[]{:S(2)}) async-start(), calls=%async_computation.4 | async-start | bytes 3522560 | tf_op jit(solution)/shard_map/all_gather | solution.py:160
  16.5 10.5 %copy-start.85 = (bf16[150,512]{1,0:T(8,128)(2,1)}, bf16[150,512]{1,0:T(8,128)(2,1)S(1)}, u32[]{:S(2)}) copy-start(bf16[150,512]{1,0:T(8,128)(2,1)S(1)} %reshape_squeeze.39) | copy-start | bytes 460804
  16.5 10.5 %copy-start.209 = (bf16[3,3,8,32,32]{4,3,2,1,0:T(8,128)(2,1)S(1)}, bf16[3,3,8,32,32]{4,3,2,1,0:T(8,128)(2,1)}, u32[]{:S(2)}) copy-start(bf16[3,3,8,32,32]{4,3,2,1,0:T(8,128)(2,1)} %param.23) | copy-start | bytes 442372
  17.5 236.0 %all-gather.11.cloned.1.call-start = ((), (), s32[]{:S(2)}) async-start(), calls=%async_computation.3 | async-start | bytes 1761280 | tf_op jit(solution)/shard_map/all_gather | solution.py:177
  48.6 53.2 %copy-start.1 = (f32[687,256]{1,0:T(8,128)}, f32[687,256]{1,0:T(8,128)S(1)}, u32[]{:S(2)}) copy-start(f32[687,256]{1,0:T(8,128)S(1)} %get-tuple-element.256) | copy-start | bytes 2110468
  74.5 25.4 %copy-start.287 = (f32[256]{0:T(256)S(1)}, f32[256]{0:T(256)}, u32[]{:S(2)}) copy-start(f32[256]{0:T(256)} %param.25) | copy-start | bytes 3076
  74.5 27.4 %copy-start.308 = (f32[256]{0:T(256)S(1)}, f32[256]{0:T(256)}, u32[]{:S(2)}) copy-start(f32[256]{0:T(256)} %param.26) | copy-start | bytes 3076
  102.5 17.5 %copy-start.88 = (bf16[294,256]{1,0:T(8,128)(2,1)}, bf16[294,256]{1,0:T(8,128)(2,1)S(1)}, u32[]{:S(2)}) copy-start(bf16[294,256]{1,0:T(8,128)(2,1)S(1)} %slice.822) | copy-start | bytes 451588
  108.3 8.1 %copy-start.130 = (bf16[6,5,5,256]{3,2,1,0:T(8,128)(2,1)}, bf16[6,5,5,256]{3,2,1,0:T(8,128)(2,1)S(1)}, u32[]{:S(2)}) copy-start(bf16[6,5,5,256]{3,2,1,0:T(8,128)(2,1)S(1)} %get-tuple-element.215) | copy-start | bytes 230404
  108.3 8.1 %copy-start.132 = (bf16[6,5,5,256]{3,2,1,0:T(8,128)(2,1)}, bf16[6,5,5,256]{3,2,1,0:T(8,128)(2,1)S(1)}, u32[]{:S(2)}) copy-start(bf16[6,5,5,256]{3,2,1,0:T(8,128)(2,1)S(1)} %get-tuple-element.214) | copy-start | bytes 230404
  108.3 9.0 %copy-start.128 = (bf16[6,5,5,256]{3,2,1,0:T(8,128)(2,1)}, bf16[6,5,5,256]{3,2,1,0:T(8,128)(2,1)S(1)}, u32[]{:S(2)}) copy-start(bf16[6,5,5,256]{3,2,1,0:T(8,128)(2,1)S(1)} %get-tuple-element.216) | copy-start | bytes 230404
  108.3 9.6 %copy-start.126 = (bf16[6,5,5,256]{3,2,1,0:T(8,128)(2,1)}, bf16[6,5,5,256]{3,2,1,0:T(8,128)(2,1)S(1)}, u32[]{:S(2)}) copy-start(bf16[6,5,5,256]{3,2,1,0:T(8,128)(2,1)S(1)} %get-tuple-element.217) | copy-start | bytes 230404
  108.4 10.3 %copy-start.124 = (bf16[6,5,5,256]{3,2,1,0:T(8,128)(2,1)}, bf16[6,5,5,256]{3,2,1,0:T(8,128)(2,1)S(1)}, u32[]{:S(2)}) copy-start(bf16[6,5,5,256]{3,2,1,0:T(8,128)(2,1)S(1)} %get-tuple-element.218) | copy-start | bytes 230404
  108.4 11.0 %copy-start.122 = (bf16[6,5,5,256]{3,2,1,0:T(8,128)(2,1)}, bf16[6,5,5,256]{3,2,1,0:T(8,128)(2,1)S(1)}, u32[]{:S(2)}) copy-start(bf16[6,5,5,256]{3,2,1,0:T(8,128)(2,1)S(1)} %get-tuple-element.212) | copy-start | bytes 230404
  123.6 9.0 %copy-start.63 = (bf16[6,7,7,256]{3,2,1,0:T(8,128)(2,1)}, bf16[6,7,7,256]{3,2,1,0:T(8,128)(2,1)S(1)}, u32[]{:S(2)}) copy-start(bf16[6,7,7,256]{3,2,1,0:T(8,128)(2,1)S(1)} %get-tuple-element.183) | copy-start | bytes 451588
  123.6 11.3 %copy-start.61 = (bf16[6,7,7,256]{3,2,1,0:T(8,128)(2,1)}, bf16[6,7,7,256]{3,2,1,0:T(8,128)(2,1)S(1)}, u32[]{:S(2)}) copy-start(bf16[6,7,7,256]{3,2,1,0:T(8,128)(2,1)S(1)} %get-tuple-element.184) | copy-start | bytes 451588
  123.6 12.0 %copy-start.59 = (bf16[6,7,7,256]{3,2,1,0:T(8,128)(2,1)}, bf16[6,7,7,256]{3,2,1,0:T(8,128)(2,1)S(1)}, u32[]{:S(2)}) copy-start(bf16[6,7,7,256]{3,2,1,0:T(8,128)(2,1)S(1)} %get-tuple-element.185) | copy-start | bytes 451588
  123.6 12.7 %copy-start.57 = (bf16[6,7,7,256]{3,2,1,0:T(8,128)(2,1)}, bf16[6,7,7,256]{3,2,1,0:T(8,128)(2,1)S(1)}, u32[]{:S(2)}) copy-start(bf16[6,7,7,256]{3,2,1,0:T(8,128)(2,1)S(1)} %get-tuple-element.186) | copy-start | bytes 451588
  123.7 13.4 %copy-start.55 = (bf16[6,7,7,256]{3,2,1,0:T(8,128)(2,1)}, bf16[6,7,7,256]{3,2,1,0:T(8,128)(2,1)S(1)}, u32[]{:S(2)}) copy-start(bf16[6,7,7,256]{3,2,1,0:T(8,128)(2,1)S(1)} %get-tuple-element.180) | copy-start | bytes 451588
  141.8 12.1 %copy-start.37 = (bf16[3,9,9,256]{3,2,1,0:T(8,128)(2,1)}, bf16[3,9,9,256]{3,2,1,0:T(8,128)(2,1)S(1)}, u32[]{:S(2)}) copy-start(bf16[3,9,9,256]{3,2,1,0:T(8,128)(2,1)S(1)} %get-tuple-element.152) | copy-start | bytes 373252
  141.8 12.8 %copy-start.35 = (bf16[3,9,9,256]{3,2,1,0:T(8,128)(2,1)}, bf16[3,9,9,256]{3,2,1,0:T(8,128)(2,1)S(1)}, u32[]{:S(2)}) copy-start(bf16[3,9,9,256]{3,2,1,0:T(8,128)(2,1)S(1)} %get-tuple-element.153) | copy-start | bytes 373252
  141.8 13.6 %copy-start.33 = (bf16[3,9,9,256]{3,2,1,0:T(8,128)(2,1)}, bf16[3,9,9,256]{3,2,1,0:T(8,128)(2,1)S(1)}, u32[]{:S(2)}) copy-start(bf16[3,9,9,256]{3,2,1,0:T(8,128)(2,1)S(1)} %get-tuple-element.154) | copy-start | bytes 373252
  141.8 14.3 %copy-start.31 = (bf16[3,9,9,256]{3,2,1,0:T(8,128)(2,1)}, bf16[3,9,9,256]{3,2,1,0:T(8,128)(2,1)S(1)}, u32[]{:S(2)}) copy-start(bf16[3,9,9,256]{3,2,1,0:T(8,128)(2,1)S(1)} %get-tuple-element.148) | copy-start | bytes 373252
  157.0 6.9 copy-start.136
  168.1 7.1 copy-start.74
  168.1 7.2 copy-start.76
  168.1 7.2 copy-start.78
  168.1 9.4 %copy-start.72 = (bf16[6,7,7,256]{3,2,1,0:T(8,128)(2,1)}, bf16[6,7,7,256]{3,2,1,0:T(8,128)(2,1)S(1)}, u32[]{:S(2)}) copy-start(bf16[6,7,7,256]{3,2,1,0:T(8,128)(2,1)S(1)} %get-tuple-element.192) | copy-start | bytes 451588
  168.1 10.1 %copy-start.70 = (bf16[6,7,7,256]{3,2,1,0:T(8,128)(2,1)}, bf16[6,7,7,256]{3,2,1,0:T(8,128)(2,1)S(1)}, u32[]{:S(2)}) copy-start(bf16[6,7,7,256]{3,2,1,0:T(8,128)(2,1)S(1)} %get-tuple-element.193) | copy-start | bytes 451588
  168.1 10.9 %copy-start.68 = (bf16[6,7,7,256]{3,2,1,0:T(8,128)(2,1)}, bf16[6,7,7,256]{3,2,1,0:T(8,128)(2,1)S(1)}, u32[]{:S(2)}) copy-start(bf16[6,7,7,256]{3,2,1,0:T(8,128)(2,1)S(1)} %get-tuple-element.194) | copy-start | bytes 451588
  168.2 11.6 %copy-start.66 = (bf16[6,7,7,256]{3,2,1,0:T(8,128)(2,1)}, bf16[6,7,7,256]{3,2,1,0:T(8,128)(2,1)S(1)}, u32[]{:S(2)}) copy-start(bf16[6,7,7,256]{3,2,1,0:T(8,128)(2,1)S(1)} %get-tuple-element.188) | copy-start | bytes 451588
  184.5 9.0 %copy-start.48 = (bf16[3,9,9,256]{3,2,1,0:T(8,128)(2,1)}, bf16[3,9,9,256]{3,2,1,0:T(8,128)(2,1)S(1)}, u32[]{:S(2)}) copy-start(bf16[3,9,9,256]{3,2,1,0:T(8,128)(2,1)S(1)} %get-tuple-element.160) | copy-start | bytes 373252
  184.5 9.7 %copy-start.47 = (bf16[3,9,9,256]{3,2,1,0:T(8,128)(2,1)}, bf16[3,9,9,256]{3,2,1,0:T(8,128)(2,1)S(1)}, u32[]{:S(2)}) copy-start(bf16[3,9,9,256]{3,2,1,0:T(8,128)(2,1)S(1)} %get-tuple-element.161) | copy-start | bytes 373252
  184.5 10.4 %copy-start.45 = (bf16[3,9,9,256]{3,2,1,0:T(8,128)(2,1)}, bf16[3,9,9,256]{3,2,1,0:T(8,128)(2,1)S(1)}, u32[]{:S(2)}) copy-start(bf16[3,9,9,256]{3,2,1,0:T(8,128)(2,1)S(1)} %get-tuple-element.162) | copy-start | bytes 373252
  184.5 11.1 %copy-start.43 = (bf16[3,9,9,256]{3,2,1,0:T(8,128)(2,1)}, bf16[3,9,9,256]{3,2,1,0:T(8,128)(2,1)S(1)}, u32[]{:S(2)}) copy-start(bf16[3,9,9,256]{3,2,1,0:T(8,128)(2,1)S(1)} %get-tuple-element.156) | copy-start | bytes 373252
  197.2 26.2 %copy-start.22 = (f32[150,256]{1,0:T(8,128)}, f32[150,256]{1,0:T(8,128)S(1)}, u32[]{:S(2)}) copy-start(f32[150,256]{1,0:T(8,128)S(1)} %convolution_add_fusion.92) | copy-start | bytes 460804
  198.6 24.8 %copy-start.6 = (f32[294,256]{1,0:T(8,128)}, f32[294,256]{1,0:T(8,128)S(1)}, u32[]{:S(2)}) copy-start(f32[294,256]{1,0:T(8,128)S(1)} %convolution_add_fusion.28) | copy-start | bytes 903172
  200.9 22.5 %copy-start.24 = (f32[150,256]{1,0:T(8,128)}, f32[150,256]{1,0:T(8,128)S(1)}, u32[]{:S(2)}) copy-start(f32[150,256]{1,0:T(8,128)S(1)} %convolution_add_fusion.84) | copy-start | bytes 460804
  202.2 21.2 %copy-start.8 = (f32[294,256]{1,0:T(8,128)}, f32[294,256]{1,0:T(8,128)S(1)}, u32[]{:S(2)}) copy-start(f32[294,256]{1,0:T(8,128)S(1)} %convolution_add_fusion.20) | copy-start | bytes 903172
  203.2 18.2 %copy-start.294 = (f32[256]{0:T(256)S(1)}, f32[256]{0:T(256)}, u32[]{:S(2)}) copy-start(f32[256]{0:T(256)} %param.27) | copy-start | bytes 3076
  203.2 20.2 %copy-start.310 = (f32[256]{0:T(256)S(1)}, f32[256]{0:T(256)}, u32[]{:S(2)}) copy-start(f32[256]{0:T(256)} %param.28) | copy-start | bytes 3076
  203.4 21.5 %copy-start.10 = (f32[243,256]{1,0:T(8,128)}, f32[243,256]{1,0:T(8,128)S(1)}, u32[]{:S(2)}) copy-start(f32[243,256]{1,0:T(8,128)S(1)} %convolution_add_fusion.52) | copy-start | bytes 746500
  225.0 44.7 %all-gather.15.cloned.1.call-start = ((), (), s32[]{:S(2)}) async-start(), calls=%async_computation.5 | async-start | bytes 1761280 | tf_op jit(solution)/shard_map/all_gather | solution.py:177
  227.8 24.4 %all-to-all-start = ((bf16[256,4,512]{0,2,1:T(8,128)(2,1)}), bf16[256,4,512]{0,2,1:T(8,128)(2,1)S(1)}, u32[]{:S(2)}, u32[]{:S(2)}) async-start(bf16[256,4,512]{0,2,1:T(8,128)(2,1)} %bitcast.592), calls=%async_computation | async-start | bytes 2097152 | tf_op jit(solution)/shard_map/all_to_all | solution.py:131
  231.3 158.1 %all-gather.21.cloned.1.call-start = ((), (), s32[]{:S(2)}) async-start(), calls=%async_computation.8 | async-start | bytes 3522560 | tf_op jit(solution)/shard_map/all_gather | solution.py:206
  253.5 16.1 %copy-start.153 = (bf16[4,256,512]{2,1,0:T(8,128)(2,1)S(1)}, bf16[4,256,512]{2,1,0:T(8,128)(2,1)}, u32[]{:S(2)}) copy-start(bf16[4,256,512]{2,1,0:T(8,128)(2,1)} %copy.220) | copy-start | bytes 3145732
  257.3 37.3 %copy-start.293 = (f32[512]{0:T(512)S(1)}, f32[512]{0:T(512)}, u32[]{:S(2)}) copy-start(f32[512]{0:T(512)} %param.29) | copy-start | bytes 6148
  296.6 9.4 %copy-start.266 = (f32[512]{0:T(512)}, f32[512]{0:T(512)S(1)}, u32[]{:S(2)}) copy-start(f32[512]{0:T(512)S(1)} %get-tuple-element.125) | copy-start | bytes 6148
  296.6 9.4 %copy-start.267 = (f32[512]{0:T(512)}, f32[512]{0:T(512)S(1)}, u32[]{:S(2)}) copy-start(f32[512]{0:T(512)S(1)} %get-tuple-element.235) | copy-start | bytes 6148
  296.6 9.4 %copy-start.268 = (f32[512]{0:T(512)}, f32[512]{0:T(512)S(1)}, u32[]{:S(2)}) copy-start(f32[512]{0:T(512)S(1)} %get-tuple-element.237) | copy-start | bytes 6148
  296.6 9.4 %copy-start.269 = (f32[512]{0:T(512)}, f32[512]{0:T(512)S(1)}, u32[]{:S(2)}) copy-start(f32[512]{0:T(512)S(1)} %get-tuple-element.238) | copy-start | bytes 6148
  306.0 21.4 %copy-start.3 = (f32[687,512]{1,0:T(8,128)}, f32[687,512]{1,0:T(8,128)S(1)}, u32[]{:S(2)}) copy-start(f32[687,512]{1,0:T(8,128)S(1)} %get-tuple-element.231) | copy-start | bytes 4220932
  327.4 66.2 %all-gather.17.cloned.1.call-start = ((), (), s32[]{:S(2)}) async-start(), calls=%async_computation.6 | async-start | bytes 3522560 | tf_op jit(solution)/shard_map/all_gather | solution.py:206
  331.2 293.3 %all-gather.19.cloned.1.call-start = ((), (), s32[]{:S(2)}) async-start(), calls=%async_computation.7 | async-start | bytes 1761280 | tf_op jit(solution)/shard_map/all_gather | solution.py:251
  393.7 23.8 %copy-start.307 = (f32[256]{0:T(256)S(1)}, f32[256]{0:T(256)}, u32[]{:S(2)}) copy-start(f32[256]{0:T(256)} %get-tuple-element.117) | copy-start | bytes 3076
  446.8 6.8 copy-start.157
  468.5 9.2 %copy-start.13 = (bf16[687,256]{1,0:T(8,128)(2,1)S(1)}, bf16[687,256]{1,0:T(8,128)(2,1)}, u32[]{:S(2)}) copy-start(bf16[687,256]{1,0:T(8,128)(2,1)} %copy-done.12) | copy-start | bytes 1055236
  475.4 7.6 copy-start.170
  512.2 7.6 copy-start.171
  529.7 18.2 %copy-start.297 = (f32[256]{0:T(256)S(1)}, f32[256]{0:T(256)}, u32[]{:S(2)}) copy-start(f32[256]{0:T(256)} %get-tuple-element.110) | copy-start | bytes 3076
  530.7 19.5 %copy-start.163 = (bf16[294,256]{0,1:T(8,128)(2,1)S(1)}, bf16[294,256]{0,1:T(8,128)(2,1)}, u32[]{:S(2)}) copy-start(bf16[294,256]{0,1:T(8,128)(2,1)} %copy.234) | copy-start | bytes 451588
  549.6 78.6 %all-gather.23.cloned.1.call-start = ((), (), s32[]{:S(2)}) async-start(), calls=%async_computation.9 | async-start | bytes 1761280 | tf_op jit(solution)/shard_map/all_gather | solution.py:251
  580.4 210.5 %all-reduce.21.cloned.1.call-start = ((), (), s32[]{:S(2)}) async-start(), calls=%async_computation.10 | async-start | bytes 10747904 | tf_op jit(solution)/shard_map/psum | solution.py:264
  (261 other events, 662.7 us)
Sparse Core Ops, SparseCore 0:
  16.2 29.3 all-gather.8
  47.7 26.6 all-gather.12
  225.0 22.2 all-gather.10
  248.8 20.8 all-gather.14
  327.6 24.4 all-gather.20
  354.0 26.6 all-gather.16
  549.8 16.7 all-gather.18
  580.5 16.7 all-gather.22
  602.5 188.4 all-reduce.20
where the time goes:
time: 817 us; the launch traced here: 804 us
  local copies, waits for them, and re-layouts  274 us (34%)
  waiting for transfers between devices  198 us (24%)
  blocking collectives  133 us (16%)
  matrix products  122 us (15%)
  other arithmetic  50.3 us (6%)
  between operations  21.4 us (3%)
    psum x1, waiting for transfers between devices, per_device(): lax.psum((reduce_acc, group_acc, expand_acc), 'batch')  150 us
    reshape x96, local copies, waits for them, and re-layouts, tap_conv(): window = padded[:, row_start:row_start + edge_size, col_start:col_start +...  104 us
    dot_general x108, matrix products, tap_conv(): jnp.dot(window, matrices[tap_index], preferred_element_type=jnp.float32)  63.5 us
    reshape x48, local copies, waits for them, and re-layouts, kernel_grad(): window = padded[:, row_start:row_start + edge_size, col_start:col_start +...  52.8 us
    all_gather x2, waiting for transfers between devices, per_device(): full_maps = lax.all_gather(local_maps, 'tensor', axis=1, tiled=True)  35.8 us
    unnamed x635, local copies, waits for them, and re-layouts  32.4 us
    dot_general x54, matrix products, kernel_grad(): jnp.einsum('pgi,pgo->gio', window, grad_part, preferred_element_type=jnp....  23.1 us
    slice x12, local copies, waits for them, and re-layouts, tap_conv(): padded[:, row_start:row_start + edge_size, col_start:col_start + edge_siz...  23.1 us
  transfers between devices with their start and end apart: 10, of which 4 were waited for; matrix products, arithmetic and copies ran while one was open for 22% of the time, Pallas kernels for 0%

commit v1 on v0

v1 whole, which is shorter than its diff:
```python
import functools

import jax
import jax.numpy as jnp
import numpy as np
from jax import lax
from jax.experimental import pallas as pl
from jax.experimental.pallas import tpu as pltpu
from jax.sharding import PartitionSpec as P

EPSILON = 1e-05
LANES = 128
SUBLANES = 8
PACKED = 16
HALO = 32
STEP = 48
F32 = jnp.float32
BF16 = jnp.bfloat16
VMEM_LIMIT = 48 * 1024 * 1024


class Layout:
    def __init__(self, edges, slots, micro):
        self.edges, self.slots, self.micro = edges, slots, micro
        self.live = [micro * n * e * e for e, n in zip(edges, slots)]
        self.padded = [-(-n // PACKED) * PACKED for n in self.live]
        self.starts = [sum(self.padded[:k]) for k in range(len(edges))]
        self.rows = sum(self.padded)
        self.parts = next(k for k in (3, 2, 1) if self.rows % (k * PACKED) == 0)
        self.part = self.rows // self.parts

    def segments(self):
        return list(zip(self.edges, self.starts, self.padded))

    def tap_bits(self):
        bits = np.zeros((self.rows, LANES), np.int32)
        for e, n, start in zip(self.edges, self.slots, self.starts):
            h, w = np.meshgrid(np.arange(e), np.arange(e), indexing="ij")
            found = np.zeros((e, e), np.int32)
            for tap in range(9):
                y, x = h + tap // 3 - 1, w + tap % 3 - 1
                found |= ((y >= 0) & (y < e) & (x >= 0) & (x < e)).astype(np.int32) << tap
            per_row = np.repeat(np.tile(found.ravel(), n), self.micro)
            bits[start : start + per_row.size] = per_row[:, None]
        return bits

    def live_mask(self, counts):
        pieces = []
        for k, (e, n) in enumerate(zip(self.edges, self.slots)):
            image = np.repeat(np.arange(n), e * e * self.micro)
            image = np.concatenate([image, np.full(self.padded[k] - image.size, n)])
            which = np.arange(image.size) % self.micro
            limit = jnp.where(jnp.asarray(which == 0), counts[0, 0, k], counts[1, 0, k])
            pieces.append((jnp.asarray(image, jnp.int32) < limit).astype(F32))
        return jnp.broadcast_to(jnp.concatenate(pieces)[:, None], (self.rows, LANES))

    def flatten(self, pieces):
        flat = []
        for piece, padded, live in zip(pieces, self.padded, self.live):
            rows = jnp.transpose(piece, (1, 2, 3, 0, 4)).reshape(live, piece.shape[-1])
            flat.append(jnp.pad(rows, ((0, padded - live), (0, 0))))
        return jnp.concatenate(flat, 0)

    def split(self, flat):
        found = []
        for e, n, start, live in zip(self.edges, self.slots, self.starts, self.live):
            piece = flat[start : start + live].reshape(n, e, e, self.micro, flat.shape[-1])
            found.append(jnp.transpose(piece, (3, 0, 1, 2, 4)))
        return found


def fold(x):
    y = x + pltpu.roll(x, 4, 0)
    return y + pltpu.roll(y, 2, 0)


def slots_of(shape):
    return lax.shift_right_logical(lax.broadcasted_iota(jnp.int32, shape, 0), 1)


def pack(first, second, third):
    slot = slots_of(first.shape)
    found = jnp.where(slot == 0, fold(first), jnp.where(slot == 1, fold(second), 0.0))
    return jnp.where(slot == 2, third, found)


def pick(total, index):
    return fold(jnp.where(slots_of(total.shape) == index, total, 0.0))


def widen(x, width):
    return jnp.concatenate([x] * (width // x.shape[-1]), axis=-1)


def moments(received):
    total = jnp.sum(received[...], axis=0)
    count = pick(total, 2)
    mean = pick(total, 0) / count
    variance = pick(total, 1) / count - mean * mean
    return mean, lax.rsqrt(variance + EPSILON), count


def spread(out_ref, tile):
    out_ref[...] = jnp.broadcast_to(tile[None], out_ref.shape)


def tiles(x):
    return x.reshape(x.shape[0] // SUBLANES, SUBLANES, x.shape[1])


def flat(x):
    return x.reshape(x.shape[0] * SUBLANES, x.shape[2])


def slope_of(values):
    s = jax.nn.sigmoid(values)
    return s * (1.0 + values * (1.0 - s))


def at(start, size, align=PACKED):
    return pl.ds(pl.multiple_of(start, align), size)


def mm(a, b):
    return jnp.dot(a, b, preferred_element_type=F32)


def mm_nt(a, b):
    return lax.dot_general(a, b, (((1,), (1,)), ((), ())), preferred_element_type=F32)


def mm_tn(a, b):
    return lax.dot_general(a, b, (((0,), (0,)), ((), ())), preferred_element_type=F32)


def both(total):
    return (total + pltpu.roll(total, 1, 0))[0:1]


def masked_sums(values, others, mask, carry):
    masked = values * mask
    return carry[0] + jnp.sum(masked, 0), carry[1] + jnp.sum(masked * others, 0)


def zeros_pair(width):
    return (jnp.zeros((SUBLANES, width), F32), jnp.zeros((SUBLANES, width), F32))


def reduce_kernel(lay, me, x0, x1, x2, x3, weight, mask, count, z_out, sums_out):
    t = me[0]
    width = z_out.shape[1]

    def step(part, carry):
        rows = at(part * lay.part, lay.part)
        acc = mm(x0[rows, :], weight[t])
        for k, x in ((1, x1), (2, x2), (3, x3)):
            acc = acc + mm(x[rows, :], weight[jnp.bitwise_xor(t, k)])
        z_out[rows, :] = acc
        z = tiles(acc)
        return masked_sums(z, z, widen(tiles(mask[rows, :]), width), carry)

    sums, squares = lax.fori_loop(0, lay.parts, step, zeros_pair(width))
    spread(sums_out, pack(sums, squares, widen(count[...], width)))


def windows(lay, slabs, bits, image, sign):
    groups = slabs.shape[0]
    for edge, start, size in lay.segments():
        for tap in range(9):
            shift = sign * lay.micro * ((tap // 3 - 1) * edge + tap % 3 - 1)
            which = tap if sign > 0 else 8 - tap
            valid = jnp.bitwise_and(bits[start : start + size, :], 1 << which) != 0
            for group in range(groups):
                low = HALO + start + shift
                moved = slabs[group, low : low + size, :]
                column = (tap * groups + group) * LANES
                image[start : start + size, column : column + LANES] = jnp.where(
                    valid, moved, 0.0
                ).astype(BF16)


def clear_halo(lay, slabs):
    empty = jnp.zeros((slabs.shape[0], HALO, LANES), F32)
    slabs[:, 0:HALO, :] = empty
    slabs[:, HALO + lay.rows : 2 * HALO + lay.rows, :] = empty


def to_slabs(slabs, i, values):
    for group in range(slabs.shape[0]):
        slabs[group, at(HALO + i * STEP, STEP), :] = values[:, group * LANES : (group + 1) * LANES]


def conv_kernel(
    lay, z1, sums1, gain, bias, mask, count, bits, weight, z2_out, sums_out, act_out, slabs, image
):
    width = z1.shape[1]
    mean, inverse, _ = moments(sums1)
    clear_halo(lay, slabs)

    def activate(i, _):
        rows = at(i * STEP, STEP)
        u = gain[...] * ((tiles(z1[rows, :]) - mean) * inverse) + bias[...]
        a = flat(widen(tiles(mask[rows, :]), width) * (u * jax.nn.sigmoid(u))).astype(BF16)
        act_out[rows, :] = a
        to_slabs(slabs, i, a.astype(F32))
        return 0

    lax.fori_loop(0, lay.rows // STEP, activate, 0)
    windows(lay, slabs, bits, image, 1)

    def step(part, carry):
        rows = at(part * lay.part, lay.part)
        acc = mm(image[rows, :], weight[...])
        z2_out[rows, :] = acc
        z = tiles(acc)
        return masked_sums(z, z, widen(tiles(mask[rows, :]), width), carry)

    sums, squares = lax.fori_loop(0, lay.parts, step, zeros_pair(width))
    spread(sums_out, pack(sums, squares, widen(count[...], width)))


def second_kernel(lay, z2, sums2, gain, bias, mask, act_out):
    width = z2.shape[1]
    mean, inverse, _ = moments(sums2)

    def activate(i, _):
        rows = at(i * STEP, STEP)
        u = gain[...] * ((tiles(z2[rows, :]) - mean) * inverse) + bias[...]
        a = widen(tiles(mask[rows, :]), width) * (u * jax.nn.sigmoid(u))
        act_out[rows, :] = flat(a).astype(BF16)
        return 0

    lax.fori_loop(0, lay.rows // STEP, activate, 0)


def expand_kernel(lay, a0, a1, a2, a3, w0, w1, w2, w3, mask, count, z_out, sums_out):
    width = z_out.shape[1]

    def step(part, carry):
        rows = at(part * lay.part, lay.part)
        acc = mm(a0[rows, :], w0[...])
        for a, w in ((a1, w1), (a2, w2), (a3, w3)):
            acc = acc + mm(a[rows, :], w[...])
        z_out[rows, :] = acc
        z = tiles(acc)
        return masked_sums(z, z, widen(tiles(mask[rows, :]), width), carry)

    sums, squares = lax.fori_loop(0, lay.parts, step, zeros_pair(width))
    spread(sums_out, pack(sums, squares, widen(count[...], width)))


def output_kernel(lay, z3, sums3, gain, bias, mask, x, dy, result_out, grad_out, sums_out):
    width = z3.shape[1]
    mean, inverse, _ = moments(sums3)

    def step(i, carry):
        rows = at(i * STEP, STEP)
        live = widen(tiles(mask[rows, :]), width)
        normed = (tiles(z3[rows, :]) - mean) * inverse
        u = gain[...] * normed + bias[...] + tiles(x[rows, :].astype(F32))
        s = jax.nn.sigmoid(u)
        result_out[rows, :] = flat(live * (u * s)).astype(BF16)
        grad = live * tiles(dy[rows, :].astype(F32)) * (s * (1.0 + u * (1.0 - s)))
        grad_out[rows, :] = flat(grad)
        return carry[0] + jnp.sum(grad, 0), carry[1] + jnp.sum(grad * normed, 0)

    first, cross = lax.fori_loop(0, lay.rows // STEP, step, zeros_pair(width))
    spread(sums_out, pack(first, cross, jnp.zeros_like(first)))


def grad_sums(received):
    total = jnp.sum(received[...], axis=0)
    return pick(total, 0), pick(total, 1)


def norm_back_loop(lay, grad, z, mask, gain, stats, sums, store):
    mean, inverse, count = stats
    first, cross = sums
    width = z.shape[1]
    scale = inverse * gain[...]
    first, cross = first / count, cross / count

    def step(i, _):
        rows = at(i * STEP, STEP)
        live = widen(tiles(mask[rows, :]), width)
        normed = (tiles(z[rows, :]) - mean) * inverse
        dz = scale * (tiles(grad[rows, :]) - live * (first + normed * cross))
        store(i, rows, flat(dz))
        return 0

    lax.fori_loop(0, lay.rows // STEP, step, 0)


def third_back_kernel(
    lay, du3, z3, sums3, sums4, gain, mask, w0, w1, w2, w3,
    dz_out, own_out, peer_out, send_out, bias_out, gain_out,
):
    sums = grad_sums(sums4)
    bias_out[...] = both(sums[0])
    gain_out[...] = both(sums[1])

    def store(i, rows, dz):
        dz_out[rows, :] = dz.astype(BF16)

    norm_back_loop(lay, du3, z3, mask, gain, moments(sums3), sums, store)

    def step(part, _):
        rows = at(part * lay.part, lay.part)
        dz = dz_out[rows, :]
        send_out[0, rows, :] = mm_nt(dz, w1[...]).astype(BF16)
        send_out[1, rows, :] = mm_nt(dz, w3[...]).astype(BF16)
        peer_out[rows, :] = mm_nt(dz, w2[...])
        own_out[rows, :] = mm_nt(dz, w0[...])
        return 0

    lax.fori_loop(0, lay.parts, step, 0)


def second_back_kernel(lay, own, near, far, z2, sums2, gain, bias, mask, grad_out, sums_out):
    width = z2.shape[1]
    mean, inverse, _ = moments(sums2)

    def step(i, carry):
        rows = at(i * STEP, STEP)
        live = widen(tiles(mask[rows, :]), width)
        normed = (tiles(z2[rows, :]) - mean) * inverse
        u = gain[...] * normed + bias[...]
        da = own[rows, :] + near[0, rows, :].astype(F32) + far[rows, :].astype(F32)
        grad = live * tiles(da) * slope_of(u)
        grad_out[rows, :] = flat(grad)
        return carry[0] + jnp.sum(grad, 0), carry[1] + jnp.sum(grad * normed, 0)

    first, cross = lax.fori_loop(0, lay.rows // STEP, step, zeros_pair(width))
    spread(sums_out, pack(first, cross, jnp.zeros_like(first)))


def conv_back_kernel(
    lay, groups, du2, z2, sums2, sums5, gain2, mask, bits, weight, act, z1, sums1, gain1, bias1, block, choose,
    grad_out, sums_out, group_out, bias_out, gain_out, slabs, image, wide,
):
    width = z2.shape[1]
    sums = grad_sums(sums5)
    bias_out[...] = both(sums[0])
    gain_out[...] = both(sums[1])
    clear_halo(lay, slabs)

    def store(i, rows, dz):
        to_slabs(slabs, i, dz.astype(BF16).astype(F32))

    norm_back_loop(lay, du2, z2, mask, gain2, moments(sums2), sums, store)
    windows(lay, slabs, bits, image, -1)
    mean, inverse, _ = moments(sums1)

    def step(part, carry):
        rows = at(part * lay.part, lay.part)
        da = mm(image[rows, :], weight[...])
        live = widen(tiles(mask[rows, :]), width)
        normed = (tiles(z1[rows, :]) - mean) * inverse
        u = gain1[...] * normed + bias1[...]
        grad = live * tiles(da) * slope_of(u)
        grad_out[rows, :] = flat(grad)
        return carry[0] + jnp.sum(grad, 0), carry[1] + jnp.sum(grad * normed, 0)

    first, cross = lax.fori_loop(0, lay.parts, step, zeros_pair(width))
    spread(sums_out, pack(first, cross, jnp.zeros_like(first)))
    for tap in range(9):
        columns = slice(tap * width, (tap + 1) * width)
        found = mm_tn(act[...], image[:, columns])
        wide[:, columns] = (found * block[...]).astype(BF16)
    group_out[...] = mm(wide[...], choose[...]).astype(BF16)


def first_back_kernel(
    lay, me, du1, z1, sums1, sums6, gain, mask, x0, x1, x2, x3,
    dz_out, weight_out, bias_out, gain_out,
):
    t = me[0]
    sums = grad_sums(sums6)
    bias_out[...] = both(sums[0])
    gain_out[...] = both(sums[1])

    def store(i, rows, dz):
        dz_out[rows, :] = dz.astype(BF16)

    norm_back_loop(lay, du1, z1, mask, gain, moments(sums1), sums, store)
    for k, x in ((0, x0), (1, x1), (2, x2), (3, x3)):
        weight_out[jnp.bitwise_xor(t, k)] = mm_tn(dz_out[...], x[...]).astype(BF16)


def input_kernel(lay, du3, d0, d1, d2, d3, w0, w1, w2, w3, out):
    def step(part, _):
        rows = at(part * lay.part, lay.part)
        acc = du3[rows, :]
        for d, w in ((d0, w0), (d1, w1), (d2, w2), (d3, w3)):
            acc = acc + mm_nt(d[rows, :], w[...])
        out[rows, :] = acc
        return 0

    lax.fori_loop(0, lay.parts, step, 0)


def expand_grad_kernel(lay, me, a0, a1, a2, a3, dz, out):
    t = me[0]
    for k, a in ((0, a0), (1, a1), (2, a2), (3, a3)):
        out[jnp.bitwise_xor(t, k)] = mm_tn(a[...], dz[...]).astype(BF16)


def run(kernel, args, outs, scratch=(), scalars=0, flops=0):
    size = sum(a.size * a.dtype.itemsize for a in args) + sum(
        int(np.prod(o.shape)) * o.dtype.itemsize for o in outs
    )
    specs = [
        pl.BlockSpec(memory_space=pltpu.SMEM if k < scalars else pltpu.VMEM)
        for k in range(len(args))
    ]
    return pl.pallas_call(
        kernel,
        out_shape=list(outs),
        in_specs=specs,
        out_specs=[pl.BlockSpec(memory_space=pltpu.VMEM)] * len(outs),
        scratch_shapes=list(scratch),
        compiler_params=pltpu.CompilerParams(vmem_limit_bytes=VMEM_LIMIT),
        cost_estimate=pl.CostEstimate(flops=flops, bytes_accessed=size, transcendentals=0),
    )(*args)


def like(shape, dtype):
    return jax.ShapeDtypeStruct(shape, dtype)


def per_device(
    ranks,
    maps_five,
    maps_seven,
    maps_nine,
    upstream_five,
    upstream_seven,
    upstream_nine,
    reduce_weight,
    group_weight,
    expand_weight,
    first_gain,
    first_bias,
    second_gain,
    second_bias,
    third_gain,
    third_bias,
    image_counts,
):
    all_maps = (maps_five, maps_seven, maps_nine)
    all_upstream = (upstream_five, upstream_seven, upstream_nine)
    lay = Layout(
        tuple(p.shape[2] for p in all_maps), tuple(p.shape[1] for p in all_maps), maps_five.shape[0]
    )
    rows = lay.rows
    chan = maps_five.shape[-1]
    group_count, group_width = group_weight.shape[2], group_weight.shape[3]
    inner = group_count * group_width
    shards = reduce_weight.shape[0] // chan
    t = lax.axis_index("tensor").astype(jnp.int32)
    me = t.reshape(1)

    def swap(x, k):
        return lax.ppermute(x, "tensor", [(i, i ^ k) for i in range(shards)])

    def everyone(x):
        return lax.all_to_all(x, "batch", split_axis=0, concat_axis=0, tiled=True)

    def gather(x):
        near = swap(x, 1)
        far = swap(x, 2)
        return x, near, far, swap(far, 1)

    def row(v):
        return v.reshape(1, v.shape[0])

    g1, b1, g2, b2, g3, b3 = map(
        row, (first_gain, first_bias, second_gain, second_bias, third_gain, third_bias)
    )
    mask = lay.live_mask(image_counts)
    areas = jnp.asarray([e * e for e in lay.edges], jnp.int32)
    live_pixels = jnp.sum(image_counts[:, 0, :] * areas[None, :], axis=1).astype(F32)
    count = jnp.broadcast_to(
        jnp.tile(live_pixels, SUBLANES // lay.micro)[:, None], (SUBLANES, LANES)
    )
    bits = jnp.asarray(lay.tap_bits())

    maps = lay.flatten(all_maps)
    xs = gather(maps)
    ids = np.arange(inner) // group_width
    block = jnp.asarray(ids[:, None] == ids[None, :])

    def dense(w):
        tiled = jnp.tile(w.reshape(9, inner, group_width), (1, 1, group_count))
        return jnp.where(block[None], tiled, jnp.zeros((), BF16)).reshape(9 * inner, inner)

    forward_weight = dense(group_weight)
    backward_weight = dense(jnp.transpose(group_weight, (0, 1, 2, 4, 3)))
    choose = np.zeros((9 * inner, 3 * LANES), np.float32)
    for tap in range(9):
        for c in range(inner):
            choose[tap * inner + c, tap * group_width + c % group_width] = 1.0
    choose = jnp.asarray(choose, BF16)

    def columns(k):
        return lax.dynamic_slice_in_dim(expand_weight, jnp.bitwise_xor(t, k) * chan, chan, 1)

    def weight_rows(k):
        return lax.dynamic_slice_in_dim(reduce_weight, jnp.bitwise_xor(t, k) * chan, chan, 0)

    expand_parts = [columns(0)] + [swap(columns(k), k) for k in (1, 2, 3)]
    reduce_parts = [weight_rows(0)] + [swap(weight_rows(k), k) for k in (1, 2, 3)]

    upstream = lay.flatten(all_upstream)
    tile1 = like((ranks, SUBLANES, inner), F32)
    tile3 = like((ranks, SUBLANES, chan), F32)
    slabs = pltpu.VMEM((inner // LANES, rows + 2 * HALO, LANES), F32)
    image = pltpu.VMEM((rows, 9 * inner), BF16)
    full_flops = 2 * rows * chan * shards * inner

    z1, s1 = run(
        functools.partial(reduce_kernel, lay),
        (me, *xs, reduce_weight.reshape(shards, chan, inner), mask, count),
        (like((rows, inner), F32), tile1),
        scalars=1,
        flops=full_flops,
    )
    s1 = everyone(s1)
    z2, s2, act1 = run(
        functools.partial(conv_kernel, lay),
        (z1, s1, g1, b1, mask, count, bits, forward_weight),
        (like((rows, inner), F32), tile1, like((rows, inner), BF16)),
        scratch=(slabs, image),
        flops=full_flops,
    )
    s2 = everyone(s2)
    (act2,) = run(
        functools.partial(second_kernel, lay),
        (z2, s2, g2, b2, mask),
        (like((rows, inner), BF16),),
        flops=20 * rows * inner,
    )
    acts = gather(act2)
    z3, s3 = run(
        functools.partial(expand_kernel, lay),
        (*acts, *expand_parts, mask, count),
        (like((rows, chan), F32), tile3),
        flops=full_flops,
    )
    s3 = everyone(s3)
    output, du3, s4 = run(
        functools.partial(output_kernel, lay),
        (z3, s3, g3, b3, mask, maps, upstream),
        (like((rows, chan), BF16), like((rows, chan), F32), tile3),
        flops=40 * rows * chan,
    )
    s4 = everyone(s4)
    dz3, own, peer, send, bias_three, gain_three = run(
        functools.partial(third_back_kernel, lay),
        (du3, z3, s3, s4, g3, mask, *expand_parts),
        (
            like((rows, chan), BF16),
            like((rows, inner), F32),
            like((rows, inner), F32),
            like((2, rows, inner), BF16),
            like((1, chan), F32),
            like((1, chan), F32),
        ),
        flops=full_flops,
    )
    near = swap(send, 1)
    far = swap((peer + near[1].astype(F32)).astype(BF16), 2)
    (expand_local,) = run(
        functools.partial(expand_grad_kernel, lay),
        (me, *acts, dz3),
        (like((shards, inner, chan), BF16),),
        scalars=1,
        flops=full_flops,
    )
    du2, s5 = run(
        functools.partial(second_back_kernel, lay),
        (own, near, far, z2, s2, g2, b2, mask),
        (like((rows, inner), F32), tile1),
        flops=40 * rows * inner,
    )
    s5 = everyone(s5)
    du1, s6, group_local, bias_two, gain_two = run(
        functools.partial(conv_back_kernel, lay, group_count),
        (
            du2, z2, s2, s5, g2, mask, bits, backward_weight, act1, z1, s1, g1, b1,
            block.astype(F32), choose,
        ),
        (
            like((rows, inner), F32),
            tile1,
            like((inner, choose.shape[1]), BF16),
            like((1, inner), F32),
            like((1, inner), F32),
        ),
        scratch=(slabs, image, pltpu.VMEM((inner, 9 * inner), BF16)),
        flops=2 * full_flops,
    )
    s6 = everyone(s6)
    dz1, reduce_local, bias_one, gain_one = run(
        functools.partial(first_back_kernel, lay),
        (me, du1, z1, s1, s6, g1, mask, *xs),
        (
            like((rows, inner), BF16),
            like((shards, inner, chan), BF16),
            like((1, inner), F32),
            like((1, inner), F32),
        ),
        scalars=1,
        flops=full_flops,
    )
    grads = gather(dz1)
    (backprop,) = run(
        functools.partial(input_kernel, lay),
        (du3, *grads, *reduce_parts),
        (like((rows, chan), F32),),
        flops=full_flops,
    )

    if inner % (ranks * PACKED) == 0 and ranks * LANES <= shards * chan:
        piece = inner // ranks
        sent = expand_local.reshape(shards, ranks, piece, chan).transpose(1, 0, 2, 3)
        mine = jnp.sum(everyone(sent).astype(F32), 0).astype(BF16)
        mine = lax.all_to_all(mine, "tensor", split_axis=0, concat_axis=0, tiled=True)
        whole = everyone(jnp.broadcast_to(mine[None], (ranks, *mine.shape)))
        expand_grad = whole.transpose(0, 2, 1, 3).reshape(inner, shards * chan).astype(F32)

        wide = shards * chan // ranks
        sent = reduce_local.transpose(0, 2, 1).reshape(ranks, wide, inner)
        extra = group_local.reshape(ranks, piece, choose.shape[1])
        extra = jnp.concatenate(
            [extra[:, :, :inner], jnp.pad(extra[:, :, inner:], ((0, 0), (0, 0), (0, 2 * inner - extra.shape[2])))],
            1,
        )
        sent = jnp.concatenate([sent, extra], 1)
        mine = jnp.sum(everyone(sent).astype(F32), 0).astype(BF16)
        whole = everyone(jnp.broadcast_to(mine[None], (ranks, *mine.shape)))
        reduce_grad = whole[:, :wide].reshape(shards * chan, inner).astype(F32)
        group_flat = jnp.concatenate(
            [whole[:, wide : wide + piece], whole[:, wide + piece :]], 2
        ).reshape(inner, 2 * inner)
    else:
        summed = lax.psum(
            (expand_local.astype(F32), reduce_local.astype(F32), group_local.astype(F32)), "batch"
        )
        expand_grad = lax.all_to_all(summed[0], "tensor", split_axis=0, concat_axis=0, tiled=True)
        expand_grad = expand_grad.transpose(1, 0, 2).reshape(inner, shards * chan)
        reduce_grad = summed[1].transpose(0, 2, 1).reshape(shards * chan, inner)
        group_flat = summed[2]
    group_grad = (
        group_flat[:, : 9 * group_width]
        .astype(F32)
        .reshape(group_count, group_width, 9, group_width)
        .transpose(2, 0, 1, 3)
        .reshape(3, 3, group_count, group_width, group_width)
    )
    return (
        *lay.split(output),
        *lay.split(backprop),
        reduce_grad,
        group_grad,
        expand_grad,
        gain_one[0],
        bias_one[0],
        gain_two[0],
        bias_two[0],
        gain_three[0],
        bias_three[0],
    )


def solution(mesh):
    maps_spec = P(None, "batch", None, None, "tensor")
    in_specs = (
        *([maps_spec] * 6),
        P(None, "tensor"),
        P(None, None, "tensor", None, None),
        P("tensor", None),
        *([P("tensor")] * 6),
        P(None, "batch", None),
    )
    out_specs = (
        *([maps_spec] * 6),
        P(None, "tensor"),
        P(None, None, "tensor", None, None),
        P("tensor", None),
        *([P("tensor")] * 6),
    )
    return jax.shard_map(
        functools.partial(per_device, mesh.shape["batch"]),
        mesh=mesh,
        in_specs=in_specs,
        out_specs=out_specs,
        check_vma=False,
    )
```

time: 817 us -> 388 us (0.47); the launches traced: 804 us -> 386 us
  local copies, waits for them, and re-layouts: 274 us -> 70 us
  matrix products: 122 us -> 0 us
  blocking collectives: 133 us -> 22.5 us
  Pallas kernels: 0 us -> 59.9 us
  starting transfers between devices: 4.7 us -> 48.3 us
  waiting for transfers between devices: 198 us -> 165 us
  other arithmetic: 50.3 us -> 19.1 us
  between operations: 21.4 us -> 1.23 us
    psum x1 -> x0, waiting for transfers between devices: 150 us -> none  [per_device(): lax.psum((reduce_acc, group_acc, expand_acc), 'batch')]
    reshape x163 -> x14, local copies, waits for them, and re-layouts: 170 us -> 21.5 us  [the longest x6 10.6 us: flatten(): rows = jnp.transpose(piece, (1, 2, 3, 0, 4)).reshape(live, piece.shape[-1])]
    dot_general x174 -> x0, matrix products: 122 us -> none  [the longest x108 63.5 us: tap_conv(): jnp.dot(window, matrices[tap_index], preferred_element_type=jnp.float32)]
    psum x6 -> x0, blocking collectives: 117 us -> none  [the longest x1 22.4 us: per_device(): lax.psum((jnp.sum(live_mask * first, 0), jnp.sum(live_mask * first * firs...]
    ppermute x0 -> x17, waiting for transfers between devices: none -> 88.3 us  [swap(): return lax.ppermute(x, 'tensor', [(i, i ^ k) for i in range(shards)])]
    all_to_all x1 -> x9, waiting for transfers between devices: 0.01 us -> 76.6 us  [the longest x8 76.6 us: everyone(): return lax.all_to_all(x, 'batch', split_axis=0, concat_axis=0, tiled=True)]
    pallas_call x0 -> x11, Pallas kernels: none -> 59.9 us  [run(): pl.pallas_call(kernel, out_shape=list(outs), in_specs=specs, out_specs=[p...]
    slice x57 -> x15, local copies, waits for them, and re-layouts: 57.1 us -> 7.33 us  [the longest x9 2.67 us: split(): flat[start:start + live].reshape(n, e, e, self.micro, flat.shape[-1])]
  transfers between devices with their start and end apart: 10 -> 26, of which waited for: 4 -> 14; matrix products, arithmetic and copies ran while one was open for 22% -> 15% of each run, Pallas kernels for 0% -> 7%
where the time goes in v1:
time: 388 us; the launch traced here: 386 us
  waiting for transfers between devices  165 us (43%)
  local copies, waits for them, and re-layouts  70 us (18%)
  Pallas kernels  59.9 us (15%)
  starting transfers between devices  48.3 us (12%)
  blocking collectives  22.5 us (6%)
  other arithmetic  19.1 us (5%)
    ppermute x17, waiting for transfers between devices, swap(): return lax.ppermute(x, 'tensor', [(i, i ^ k) for i in range(shards)])  88.3 us
    all_to_all x8, waiting for transfers between devices, everyone(): return lax.all_to_all(x, 'batch', split_axis=0, concat_axis=0, tiled=True)  76.6 us
    pallas_call x11, Pallas kernels, run(): pl.pallas_call(kernel, out_shape=list(outs), in_specs=specs, out_specs=[p...  59.9 us
    all_to_all x8, starting transfers between devices, everyone(): return lax.all_to_all(x, 'batch', split_axis=0, concat_axis=0, tiled=True)  32.9 us
    all_to_all x2, blocking collectives, everyone(): return lax.all_to_all(x, 'batch', split_axis=0, concat_axis=0, tiled=True)  22.5 us
    unnamed x94, local copies, waits for them, and re-layouts  22.4 us
    ppermute x17, starting transfers between devices, swap(): return lax.ppermute(x, 'tensor', [(i, i ^ k) for i in range(shards)])  11.4 us
    reshape x6, local copies, waits for them, and re-layouts, flatten(): rows = jnp.transpose(piece, (1, 2, 3, 0, 4)).reshape(live, piece.shape[-1])  10.6 us
  transfers between devices with their start and end apart: 26, of which 14 were waited for; matrix products, arithmetic and copies ran while one was open for 15% of the time, Pallas kernels for 7%

profile of v1, /device:TPU:0, one launch (start us, length us, event | category | flops | bytes accessed | tf_op | source)
XLA Modules:
  0.0 385.8 jit_solution(5847159561744395481)
XLA Ops:
  0.7 2.0 reshape.146
  2.7 2.0 reshape.145
  6.2 3.0 collective-permute-start.1
  9.2 31.3 %collective-permute-done.1.x2 = bf16[1392,512]{1,0:T(8,128)(2,1)} collective-permute-done((bf16[1392,512]{1,0:T(8,128)(2,1)S(1)}, bf16[1392,512]{1,0:T(8,128)(2,1)}, u32[]{:S(2)}, u32[]{:S(2)}) %collective-permute-start.1) | collective-permute-done | bytes 1425440 | tf_op jit(solution)/shard_map/ppermute | solution.py:464
  45.8 4.8 %shard_map.361 = (f32[1392,256]{1,0:T(8,128)S(1)}, f32[8,8,256]{2,1,0:T(8,128)}) custom-call(s32[1]{0:T(128)} %bitcast.me, bf16[1392,512]{1,0:T(8,128)(2,1)S(1)} %fusion.9.x0.x, bf16[1392,512]{1,0:T(8,128)(2,1)} %collective-permute-done.x1, bf16[1392,512]{1,0:T(8,128)(2,1)} %collective-permute-done.1.x2, bf16[1392,512]{1,0:T(8,128)(2,1)} %collective-permute-done.2.x3, ...), custom_call_target="tpu_custom_call" | custom-call | flops 1459617792 | bytes 8957956 | tf_op jit(solution)/shard_map/pallas_call | solution.py:416
  51.7 6.1 %all-to-all-start = ((f32[8,8,256]{2,1,0:T(8,128)}), f32[8,8,256]{2,1,0:T(8,128)S(1)}, u32[]{:S(2)}, u32[]{:S(2)}) async-start(f32[8,8,256]{2,1,0:T(8,128)} %get-tuple-element.43), calls=%async_computation | async-start | bytes 131072 | tf_op jit(solution)/shard_map/all_to_all | solution.py:467
  57.8 2.1 copy.79
  59.9 1.5 reshape.178
  61.6 1.6 copy.84
  63.2 2.4 copy.72
  66.3 1.5 copy.68
  67.9 1.6 copy.83
  69.5 2.4 copy.69
  71.9 3.2 bitcast_select_fusion
  77.6 6.2 %shard_map.362 = (f32[1392,256]{1,0:T(8,128)S(1)}, f32[8,8,256]{2,1,0:T(8,128)S(1)}, bf16[1392,256]{1,0:T(8,128)(2,1)S(1)}) custom-call(f32[1392,256]{1,0:T(8,128)} %copy-done.4, f32[8,8,256]{2,1,0:T(8,128)S(1)} %all-to-all-done.sums1, f32[1,256]{1,0:T(1,128)S(1)} %bitcast.90, f32[1,256]{1,0:T(1,128)S(1)} %bitcast.93, ...), custom_call_target="tpu_custom_call" | custom-call | flops 1459617792 | bytes 6305792 | tf_op jit(solution)/shard_map/pallas_call | solution.py:416
  83.8 12.7 %all_to_all.55.sums2 = f32[8,8,256]{2,1,0:T(8,128)S(1)} all-to-all(f32[8,8,256]{2,1,0:T(8,128)S(1)} %get-tuple-element.45), channel_id=1, replica_groups=mesh['batch'=8,'tensor'=4] {'batch'}, dimensions={0} | all-to-all | bytes 131072 | tf_op jit(solution)/shard_map/all_to_all | solution.py:467
  96.5 1.6 shard_map.363.a0
  98.1 1.5 collective-permute-start.4
  99.6 15.2 %collective-permute-done.4.a2 = bf16[1392,256]{1,0:T(8,128)(2,1)} collective-permute-done((bf16[1392,256]{1,0:T(8,128)(2,1)}, bf16[1392,256]{1,0:T(8,128)(2,1)}, u32[]{:S(2)}, u32[]{:S(2)}) %collective-permute-start.4) | collective-permute-done | bytes 712736 | tf_op jit(solution)/shard_map/ppermute | solution.py:464
  114.8 2.1 constant_dynamic-slice_fusion.4
  117.4 1.5 collective-permute-start.7
  118.9 2.0 reshape.156
  120.9 2.6 reshape.155
  123.5 1.8 reshape.154
  125.3 1.5 collective-permute-done.7.w2
  126.9 3.8 collective-permute-done.8.w3
  130.7 5.5 %shard_map.364 = (f32[1392,512]{1,0:T(8,128)}, f32[8,8,512]{2,1,0:T(8,128)S(1)}) custom-call(bf16[1392,256]{1,0:T(8,128)(2,1)} %shard_map.363.a0, bf16[1392,256]{1,0:T(8,128)(2,1)} %collective-permute-done.3.a1, bf16[1392,256]{1,0:T(8,128)(2,1)} %collective-permute-done.4.a2, bf16[1392,256]{1,0:T(8,128)(2,1)} %collective-permute-done.5.a3, ...), custom_call_target="tpu_custom_call" | custom-call | flops 1459617792 | bytes 7598080 | tf_op jit(solution)/shard_map/pallas_call | solution.py:416
  136.9 3.4 all-to-all-start.2
  140.3 2.5 fusion.11.dy
  142.8 5.6 %all-to-all-done.2.sums3 = f32[8,8,512]{2,1,0:T(8,128)S(1)} async-done(((f32[8,8,512]{2,1,0:T(8,128)}), f32[8,8,512]{2,1,0:T(8,128)S(1)}, u32[]{:S(2)}, u32[]{:S(2)}) %all-to-all-start.2) | async-done | bytes 131104 | tf_op jit(solution)/shard_map/all_to_all | solution.py:467
  149.7 5.8 %shard_map.365 = (bf16[1392,512]{1,0:T(8,128)(2,1)S(1)}, f32[1392,512]{1,0:T(8,128)}, f32[8,8,512]{2,1,0:T(8,128)S(1)}) custom-call(f32[1392,512]{1,0:T(8,128)} %get-tuple-element.46.z3, f32[8,8,512]{2,1,0:T(8,128)S(1)} %all-to-all-done.2.sums3, f32[1,512]{1,0:T(1,128)S(1)} %bitcast.82, f32[1,512]{1,0:T(1,128)S(1)} %bitcast.89, ...), custom_call_target="tpu_custom_call" | custom-call | flops 28508160 | bytes 10956800 | tf_op jit(solution)/shard_map/pallas_call | solution.py:416
  155.5 9.8 %all_to_all.56.sums4 = f32[8,8,512]{2,1,0:T(8,128)S(1)} all-to-all(f32[8,8,512]{2,1,0:T(8,128)S(1)} %get-tuple-element.50), channel_id=1, replica_groups=mesh['batch'=8,'tensor'=4] {'batch'}, dimensions={0} | all-to-all | bytes 262144 | tf_op jit(solution)/shard_map/all_to_all | solution.py:467
  165.3 7.1 %shard_map.366 = (bf16[1392,512]{1,0:T(8,128)(2,1)S(1)}, f32[1392,256]{1,0:T(8,128)S(1)}, f32[1392,256]{1,0:T(8,128)}, bf16[2,1392,256]{2,1,0:T(8,128)(2,1)}, f32[1,512]{1,0:T(1,128)}, /*index=5*/f32[1,512]{1,0:T(1,128)}) custom-call(f32[1392,512]{1,0:T(8,128)} %get-tuple-element.49.du3, f32[1392,512]{1,0:T(8,128)} %get-tuple-element.46.z3, ...), custom_call_target="tpu_custom_call" | custom-call | flops 1459617792 | bytes 13432832 | tf_op jit(solution)/shard_map/pallas_call | solution.py:416
  172.5 3.4 collective-permute-done.9.near
  175.9 1.6 fusion.12
  177.4 1.6 collective-permute-start.10
  179.0 16.5 %collective-permute-done.10.far = bf16[1392,256]{1,0:T(8,128)(2,1)S(1)} collective-permute-done((bf16[1392,256]{1,0:T(8,128)(2,1)S(1)}, bf16[1392,256]{1,0:T(8,128)(2,1)S(1)}, u32[]{:S(2)}, u32[]{:S(2)}) %collective-permute-start.10) | collective-permute-done | bytes 712736 | tf_op jit(solution)/shard_map/ppermute | solution.py:464
  195.5 3.3 shard_map.367
  199.9 3.4 all-to-all-start.4
  203.3 3.6 shard_map.371
  207.9 2.2 all-to-all-done.4.sums5
  210.1 4.3 %all-to-all-start.8 = ((bf16[8,4,32,512]{3,2,1,0:T(8,128)(2,1)}), bf16[8,4,32,512]{3,2,1,0:T(8,128)(2,1)}, u32[]{:S(2)}, u32[]{:S(2)}) async-start(bf16[8,4,32,512]{3,2,1,0:T(8,128)(2,1)} %bitcast.101), calls=%async_computation.8 | async-start | bytes 2097152 | tf_op jit(solution)/shard_map/all_to_all | solution.py:467
  217.6 11.0 %shard_map.368 = (f32[1392,256]{1,0:T(8,128)S(1)}, f32[8,8,256]{2,1,0:T(8,128)}, bf16[256,384]{1,0:T(8,128)(2,1)S(1)}, f32[1,256]{1,0:T(1,128)}, f32[1,256]{1,0:T(1,128)}) custom-call(f32[1392,256]{1,0:T(8,128)} %copy-done.26, f32[1392,256]{1,0:T(8,128)} %copy-done.1, f32[8,8,256]{2,1,0:T(8,128)S(1)} %all_to_all.55.sums2, ...), custom_call_target="tpu_custom_call" | custom-call | flops 2919235584 | bytes 11514880 | tf_op jit(solution)/shard_map/pallas_call | solution.py:416
  230.4 8.9 %all-to-all-done.8 = bf16[8,4,32,512]{3,2,1,0:T(8,128)(2,1)} async-done(((bf16[8,4,32,512]{3,2,1,0:T(8,128)(2,1)}), bf16[8,4,32,512]{3,2,1,0:T(8,128)(2,1)}, u32[]{:S(2)}, u32[]{:S(2)}) %all-to-all-start.8) | async-done | bytes 1048608 | tf_op jit(solution)/shard_map/all_to_all | solution.py:467
  239.3 3.4 all-to-all-start.5
  242.7 2.1 reduce_sum.35
  246.5 3.1 all-to-all-done.5.sums6
  249.6 3.9 %all-to-all-start.9 = ((bf16[4,32,512]{2,1,0:T(8,128)(2,1)}), bf16[4,32,512]{2,1,0:T(8,128)(2,1)}, u32[]{:S(2)}, u32[]{:S(2)}) async-start(bf16[4,32,512]{2,1,0:T(8,128)(2,1)} %reduce_sum.35), calls=%async_computation.9 | async-start | bytes 262144 | tf_op jit(solution)/shard_map/all_to_all | solution.py:628
  254.9 5.1 %shard_map.369 = (bf16[1392,256]{1,0:T(8,128)(2,1)S(1)}, bf16[4,256,512]{2,1,0:T(8,128)(2,1)S(1)}, f32[1,256]{1,0:T(1,128)}, f32[1,256]{1,0:T(1,128)}) custom-call(s32[1]{0:T(128)} %bitcast.me, f32[1392,256]{1,0:T(8,128)S(1)} %copy-done.7, f32[1392,256]{1,0:T(8,128)S(1)} %copy-done.5, f32[8,8,256]{2,1,0:T(8,128)S(1)} %copy-done.18, ...), custom_call_target="tpu_custom_call" | custom-call | flops 1459617792 | bytes 11160580 | tf_op jit(solution)/shard_map/pallas_call | solution.py:416
  264.5 3.6 all-to-all-start.6
  269.1 31.2 %all-to-all-done.6 = bf16[8,320,256]{2,1,0:T(8,128)(2,1)S(1)} async-done(((bf16[8,320,256]{2,1,0:T(8,128)(2,1)}), bf16[8,320,256]{2,1,0:T(8,128)(2,1)S(1)}, u32[]{:S(2)}, u32[]{:S(2)}) %all-to-all-start.6) | async-done | bytes 1310752 | tf_op jit(solution)/shard_map/all_to_all | solution.py:467
  301.5 4.2 %all-to-all-start.10 = ((bf16[8,4,32,512]{3,1,2,0:T(4,128)(2,1)}), bf16[8,4,32,512]{3,1,2,0:T(4,128)(2,1)}, u32[]{:S(2)}, u32[]{:S(2)}) async-start(bf16[8,4,32,512]{3,1,2,0:T(4,128)(2,1)} %broadcast_in_dim.83), calls=%async_computation.10 | async-start | bytes 2097152 | tf_op jit(solution)/shard_map/all_to_all | solution.py:467
  306.0 25.7 %all-to-all-done.10 = bf16[8,4,32,512]{3,1,2,0:T(4,128)(2,1)} async-done(((bf16[8,4,32,512]{3,1,2,0:T(4,128)(2,1)}), bf16[8,4,32,512]{3,1,2,0:T(4,128)(2,1)}, u32[]{:S(2)}, u32[]{:S(2)}) %all-to-all-start.10) | async-done | bytes 1048608 | tf_op jit(solution)/shard_map/all_to_all | solution.py:467
  332.9 4.6 %all-to-all-start.7 = ((bf16[8,320,256]{2,1,0:T(8,128)(2,1)}), bf16[8,320,256]{2,1,0:T(8,128)(2,1)}, u32[]{:S(2)}, u32[]{:S(2)}) async-start(bf16[8,320,256]{2,1,0:T(8,128)(2,1)} %broadcast_in_dim.82), calls=%async_computation.7 | async-start | bytes 2621440 | tf_op jit(solution)/shard_map/all_to_all | solution.py:467
  337.5 1.5 collective-permute-start.12
  339.0 15.3 %collective-permute-done.12.d2 = bf16[1392,256]{1,0:T(8,128)(2,1)S(1)} collective-permute-done((bf16[1392,256]{1,0:T(8,128)(2,1)S(1)}, bf16[1392,256]{1,0:T(8,128)(2,1)S(1)}, u32[]{:S(2)}, u32[]{:S(2)}) %collective-permute-start.12) | collective-permute-done | bytes 712736 | tf_op jit(solution)/shard_map/ppermute | solution.py:464
  358.7 1.9 reshape.157
  361.7 2.1 reshape.159
  363.9 1.5 convert_element_type.66
  365.4 2.2 copy.85
  368.8 5.8 %shard_map.370 = f32[1392,512]{1,0:T(8,128)} custom-call(f32[1392,512]{1,0:T(8,128)} %get-tuple-element.49.du3, bf16[1392,256]{1,0:T(8,128)(2,1)S(1)} %copy-done.16, bf16[1392,256]{1,0:T(8,128)(2,1)} %collective-permute-done.11.d1, bf16[1392,256]{1,0:T(8,128)(2,1)S(1)} %collective-permute-done.12.d2, bf16[1392,256]{1,0:T(8,128)(2,1)} %collective-permute-done.13.d3, ...), custom_call_target="tpu_custom_call" | custom-call | flops 1459617792 | bytes 9601024 | tf_op jit(solution)/shard_map/pallas_call | solution.py:416
  376.9 1.7 reshape.161
  378.6 1.5 reshape.162
  381.5 1.5 bitcast_convert_fusion
  (158 shorter events, 45.1 us)
Async XLA Ops:
  0.6 4.1 %copy-start.33 = (bf16[2,6,5,5,512]{4,0,3,2,1:T(2,128)(2,1)S(1)}, bf16[2,6,5,5,512]{4,0,3,2,1:T(2,128)(2,1)}, u32[]{:S(2)}) copy-start(bf16[2,6,5,5,512]{4,0,3,2,1:T(2,128)(2,1)} %param.26) | copy-start | bytes 921604
  4.8 35.7 %copy-start.36 = (s32[2,1,3]{2,1,0:T(1,128)S(1)}, s32[2,1,3]{2,1,0:T(1,128)}, u32[]{:S(2)}) copy-start(s32[2,1,3]{2,1,0:T(1,128)} %param.41) | copy-start | bytes 76
  4.9 36.3 %copy-start.39 = (s32[304]{0:T(512)S(1)}, s32[304]{0:T(512)}, u32[]{:S(2)}) copy-start(s32[304]{0:T(512)} %constant.43.clone) | copy-start | bytes 3652
  4.9 36.3 %copy-start.43 = (pred[304]{0:T(512)(128)(4,1)S(1)}, pred[304]{0:T(512)(128)(4,1)}, u32[]{:S(2)}) copy-start(pred[304]{0:T(512)(128)(4,1)} %constant.42.clone) | copy-start | bytes 916
  4.9 37.6 %copy-start.38 = (s32[496]{0:T(512)S(1)}, s32[496]{0:T(512)}, u32[]{:S(2)}) copy-start(s32[496]{0:T(512)} %constant.47.clone) | copy-start | bytes 5956
  4.9 37.6 %copy-start.42 = (pred[496]{0:T(512)(128)(4,1)S(1)}, pred[496]{0:T(512)(128)(4,1)}, u32[]{:S(2)}) copy-start(pred[496]{0:T(512)(128)(4,1)} %constant.46.clone) | copy-start | bytes 1492
  4.9 38.9 %copy-start.37 = (s32[592]{0:T(1024)S(1)}, s32[592]{0:T(1024)}, u32[]{:S(2)}) copy-start(s32[592]{0:T(1024)} %constant.45.clone) | copy-start | bytes 7108
  4.9 38.9 %copy-start.40 = (pred[592]{0:T(1024)(128)(4,1)S(1)}, pred[592]{0:T(1024)(128)(4,1)}, u32[]{:S(2)}) copy-start(pred[592]{0:T(1024)(128)(4,1)} %constant.44.clone) | copy-start | bytes 1780
  4.9 40.3 %copy-start.41 = (s32[3]{0:T(128)S(1)}, s32[3]{0:T(128)}, u32[]{:S(2)}) copy-start(s32[3]{0:T(128)} %constant.48.clone) | copy-start | bytes 40
  4.9 40.8 %copy-start.3 = (bf16[2048,256]{1,0:T(8,128)(2,1)S(1)}, bf16[2048,256]{1,0:T(8,128)(2,1)}, u32[]{:S(2)}) copy-start(bf16[2048,256]{1,0:T(8,128)(2,1)} %param.32) | copy-start | bytes 3145732
  6.2 142.2 %copy-start = (bf16[1392,512]{1,0:T(8,128)(2,1)}, bf16[1392,512]{1,0:T(8,128)(2,1)S(1)}, u32[]{:S(2)}) copy-start(bf16[1392,512]{1,0:T(8,128)(2,1)S(1)} %fusion.9.x0.x) | copy-start | bytes 4276228
  6.2 34.3 %collective-permute-start.1 = (bf16[1392,512]{1,0:T(8,128)(2,1)S(1)}, bf16[1392,512]{1,0:T(8,128)(2,1)}, u32[]{:S(2)}, u32[]{:S(2)}) collective-permute-start(bf16[1392,512]{1,0:T(8,128)(2,1)S(1)} %fusion.9.x0.x), channel_id=1, source_target_pairs={{0,2},{1,3},{2,0},{3,1},{4,6},{5,7},{6,4},{7,5},{8,10},{9,11},{10,... | collective-permute-start | bytes 4276232 | tf_op jit(solution)/shard_map/ppermute | solution.py:464
  9.2 36.2 %collective-permute-start = (bf16[1392,512]{1,0:T(8,128)(2,1)S(1)}, bf16[1392,512]{1,0:T(8,128)(2,1)}, u32[]{:S(2)}, u32[]{:S(2)}) collective-permute-start(bf16[1392,512]{1,0:T(8,128)(2,1)S(1)} %fusion.9.x0.x), channel_id=1, source_target_pairs={{0,1},{1,0},{2,3},{3,2},{4,5},{5,4},{6,7},{7,6},{8,9},{9,8},{10,11... | collective-permute-start | bytes 4276232 | tf_op jit(solution)/shard_map/ppermute | solution.py:464
  40.5 4.9 %collective-permute-start.2 = (bf16[1392,512]{1,0:T(8,128)(2,1)}, bf16[1392,512]{1,0:T(8,128)(2,1)}, u32[]{:S(2)}, u32[]{:S(2)}) collective-permute-start(bf16[1392,512]{1,0:T(8,128)(2,1)} %collective-permute-done.1.x2), channel_id=1, source_target_pairs={{0,1},{1,0},{2,3},{3,2},{4,5},{5,4},{6,7},{7,6},{8,9},{9,8},{10,11... | collective-permute-start | bytes 4276232 | tf_op jit(solution)/shard_map/ppermute | solution.py:464
  51.7 23.4 %all-to-all-start = ((f32[8,8,256]{2,1,0:T(8,128)}), f32[8,8,256]{2,1,0:T(8,128)S(1)}, u32[]{:S(2)}, u32[]{:S(2)}) async-start(f32[8,8,256]{2,1,0:T(8,128)} %get-tuple-element.43), calls=%async_computation | async-start | bytes 131072 | tf_op jit(solution)/shard_map/all_to_all | solution.py:467
  63.2 2.4 copy-start.35
  69.5 2.4 copy-start.34
  71.9 3.2 copy-start.25
  71.9 3.2 copy-start.27
  75.1 8.6 %copy-start.17 = (f32[8,8,256]{2,1,0:T(8,128)}, f32[8,8,256]{2,1,0:T(8,128)S(1)}, u32[]{:S(2)}) copy-start(f32[8,8,256]{2,1,0:T(8,128)S(1)} %all-to-all-done.sums1) | copy-start | bytes 196612
  75.2 1.3 copy-start.11
  77.6 18.9 %copy-start.22 = (f32[256]{0:T(256)S(1)}, f32[256]{0:T(256)}, u32[]{:S(2)}) copy-start(f32[256]{0:T(256)} %param.38) | copy-start | bytes 3076
  77.6 18.9 %copy-start.23 = (f32[256]{0:T(256)S(1)}, f32[256]{0:T(256)}, u32[]{:S(2)}) copy-start(f32[256]{0:T(256)} %param.37) | copy-start | bytes 3076
  83.8 14.3 %copy-start.1 = (f32[1392,256]{1,0:T(8,128)}, f32[1392,256]{1,0:T(8,128)S(1)}, u32[]{:S(2)}) copy-start(f32[1392,256]{1,0:T(8,128)S(1)} %get-tuple-element.44.z2) | copy-start | bytes 4276228
  83.8 14.3 %copy-start.31 = (bf16[1392,256]{1,0:T(8,128)(2,1)}, bf16[1392,256]{1,0:T(8,128)(2,1)S(1)}, u32[]{:S(2)}) copy-start(bf16[1392,256]{1,0:T(8,128)(2,1)S(1)} %get-tuple-element.56.act) | copy-start | bytes 2138116
  98.1 16.7 %collective-permute-start.4 = (bf16[1392,256]{1,0:T(8,128)(2,1)}, bf16[1392,256]{1,0:T(8,128)(2,1)}, u32[]{:S(2)}, u32[]{:S(2)}) collective-permute-start(bf16[1392,256]{1,0:T(8,128)(2,1)} %shard_map.363.a0), channel_id=1, source_target_pairs={{0,2},{1,3},{2,0},{3,1},{4,6},{5,7},{6,4},{7,5},{8,10},{9,11},{10,... | collective-permute-start | bytes 2138120 | tf_op jit(solution)/shard_map/ppermute | solution.py:464
  99.6 31.1 %collective-permute-start.3 = (bf16[1392,256]{1,0:T(8,128)(2,1)}, bf16[1392,256]{1,0:T(8,128)(2,1)}, u32[]{:S(2)}, u32[]{:S(2)}) collective-permute-start(bf16[1392,256]{1,0:T(8,128)(2,1)} %shard_map.363.a0), channel_id=1, source_target_pairs={{0,1},{1,0},{2,3},{3,2},{4,5},{5,4},{6,7},{7,6},{8,9},{9,8},{10,11... | collective-permute-start | bytes 2138120 | tf_op jit(solution)/shard_map/ppermute | solution.py:464
  114.8 15.9 %collective-permute-start.5 = (bf16[1392,256]{1,0:T(8,128)(2,1)}, bf16[1392,256]{1,0:T(8,128)(2,1)}, u32[]{:S(2)}, u32[]{:S(2)}) collective-permute-start(bf16[1392,256]{1,0:T(8,128)(2,1)} %collective-permute-done.4.a2), channel_id=1, source_target_pairs={{0,1},{1,0},{2,3},{3,2},{4,5},{5,4},{6,7},{7,6},{8,9},{9,8},{10,11... | collective-permute-start | bytes 2138120 | tf_op jit(solution)/shard_map/ppermute | solution.py:464
  116.9 19.3 %copy-start.12 = (bf16[256,512]{1,0:T(8,128)(2,1)}, bf16[256,512]{1,0:T(8,128)(2,1)S(1)}, u32[]{:S(2)}) copy-start(bf16[256,512]{1,0:T(8,128)(2,1)S(1)} %get-tuple-element.137.w0) | copy-start | bytes 786436
  116.9 8.4 %collective-permute-start.6 = (bf16[256,512]{1,0:T(8,128)(2,1)}, bf16[256,512]{1,0:T(8,128)(2,1)}, u32[]{:S(2)}, u32[]{:S(2)}) collective-permute-start(bf16[256,512]{1,0:T(8,128)(2,1)} %get-tuple-element.136), channel_id=1, source_target_pairs={{0,1},{1,0},{2,3},{3,2},{4,5},{5,4},{6,7},{7,6},{8,9},{9,8},{10,11... | collective-permute-start | bytes 786440 | tf_op jit(solution)/shard_map/ppermute | solution.py:464
  117.4 9.5 %collective-permute-start.7 = (bf16[256,512]{1,0:T(8,128)(2,1)}, bf16[256,512]{1,0:T(8,128)(2,1)}, u32[]{:S(2)}, u32[]{:S(2)}) collective-permute-start(bf16[256,512]{1,0:T(8,128)(2,1)} %get-tuple-element.138), channel_id=1, source_target_pairs={{0,2},{1,3},{2,0},{3,1},{4,6},{5,7},{6,4},{7,5},{8,10},{9,11},{10,... | collective-permute-start | bytes 786440 | tf_op jit(solution)/shard_map/ppermute | solution.py:464
  118.9 11.8 %collective-permute-start.8 = (bf16[256,512]{1,0:T(8,128)(2,1)}, bf16[256,512]{1,0:T(8,128)(2,1)}, u32[]{:S(2)}, u32[]{:S(2)}) collective-permute-start(bf16[256,512]{1,0:T(8,128)(2,1)} %get-tuple-element.135), channel_id=1, source_target_pairs={{0,3},{1,2},{2,1},{3,0},{4,7},{5,6},{6,5},{7,4},{8,11},{9,10},{10,... | collective-permute-start | bytes 786440 | tf_op jit(solution)/shard_map/ppermute | solution.py:464
  136.9 11.5 %all-to-all-start.2 = ((f32[8,8,512]{2,1,0:T(8,128)}), f32[8,8,512]{2,1,0:T(8,128)S(1)}, u32[]{:S(2)}, u32[]{:S(2)}) async-start(f32[8,8,512]{2,1,0:T(8,128)} %copy-done.20), calls=%async_computation.2 | async-start | bytes 262144 | tf_op jit(solution)/shard_map/all_to_all | solution.py:467
  140.2 8.1 %copy-start.21 = (f32[512]{0:T(512)S(1)}, f32[512]{0:T(512)}, u32[]{:S(2)}) copy-start(f32[512]{0:T(512)} %param.39) | copy-start | bytes 6148
  140.2 8.1 %copy-start.24 = (f32[512]{0:T(512)S(1)}, f32[512]{0:T(512)}, u32[]{:S(2)}) copy-start(f32[512]{0:T(512)} %param.40) | copy-start | bytes 6148
  148.4 1.4 copy-start.2
  149.7 15.6 %copy-start.13 = (bf16[256,512]{1,0:T(8,128)(2,1)S(1)}, bf16[256,512]{1,0:T(8,128)(2,1)}, u32[]{:S(2)}) copy-start(bf16[256,512]{1,0:T(8,128)(2,1)} %copy-done.12) | copy-start | bytes 786436
  155.5 17.0 %copy-start.8 = (bf16[1392,512]{1,0:T(8,128)(2,1)}, bf16[1392,512]{1,0:T(8,128)(2,1)S(1)}, u32[]{:S(2)}) copy-start(bf16[1392,512]{1,0:T(8,128)(2,1)S(1)} %get-tuple-element.48) | copy-start | bytes 4276228
  172.5 3.4 collective-permute-start.9
  177.4 18.1 %collective-permute-start.10 = (bf16[1392,256]{1,0:T(8,128)(2,1)S(1)}, bf16[1392,256]{1,0:T(8,128)(2,1)S(1)}, u32[]{:S(2)}, u32[]{:S(2)}) collective-permute-start(bf16[1392,256]{1,0:T(8,128)(2,1)S(1)} %fusion.12), channel_id=1, source_target_pairs={{0,2},{1,3},{2,0},{3,1},{4,6},{5,7},{6,4},{7,5},{8,10},{9,11},{10,... | collective-permute-start | bytes 2138120 | tf_op jit(solution)/shard_map/ppermute | solution.py:464
  198.8 1.1 copy-start.26
  199.9 10.2 %all-to-all-start.4 = ((f32[8,8,256]{2,1,0:T(8,128)}), f32[8,8,256]{2,1,0:T(8,128)S(1)}, u32[]{:S(2)}, u32[]{:S(2)}) async-start(f32[8,8,256]{2,1,0:T(8,128)} %get-tuple-element.55), calls=%async_computation.4 | async-start | bytes 131072 | tf_op jit(solution)/shard_map/all_to_all | solution.py:467
  207.9 6.5 %copy-start.10 = (bf16[2304,256]{1,0:T(8,128)(2,1)S(1)}, bf16[2304,256]{1,0:T(8,128)(2,1)}, u32[]{:S(2)}) copy-start(bf16[2304,256]{1,0:T(8,128)(2,1)} %get-tuple-element.139.weight) | copy-start | bytes 3538948
  207.9 6.5 %copy-start.18 = (f32[8,8,256]{2,1,0:T(8,128)S(1)}, f32[8,8,256]{2,1,0:T(8,128)}, u32[]{:S(2)}) copy-start(f32[8,8,256]{2,1,0:T(8,128)} %copy-done.17) | copy-start | bytes 196612
  210.1 29.2 %all-to-all-start.8 = ((bf16[8,4,32,512]{3,2,1,0:T(8,128)(2,1)}), bf16[8,4,32,512]{3,2,1,0:T(8,128)(2,1)}, u32[]{:S(2)}, u32[]{:S(2)}) async-start(bf16[8,4,32,512]{3,2,1,0:T(8,128)(2,1)} %bitcast.101), calls=%async_computation.8 | async-start | bytes 2097152 | tf_op jit(solution)/shard_map/all_to_all | solution.py:467
  214.4 1.1 copy-start.29
  228.6 1.1 copy-start.6
  230.4 23.2 %copy-start.5 = (f32[1392,256]{1,0:T(8,128)S(1)}, f32[1392,256]{1,0:T(8,128)}, u32[]{:S(2)}) copy-start(f32[1392,256]{1,0:T(8,128)} %copy-done.4) | copy-start | bytes 4276228
  239.3 10.3 %all-to-all-start.5 = ((f32[8,8,256]{2,1,0:T(8,128)}), f32[8,8,256]{2,1,0:T(8,128)S(1)}, u32[]{:S(2)}, u32[]{:S(2)}) async-start(f32[8,8,256]{2,1,0:T(8,128)} %get-tuple-element.58), calls=%async_computation.5 | async-start | bytes 131072 | tf_op jit(solution)/shard_map/all_to_all | solution.py:467
  249.6 14.9 %all-to-all-start.9 = ((bf16[4,32,512]{2,1,0:T(8,128)(2,1)}), bf16[4,32,512]{2,1,0:T(8,128)(2,1)}, u32[]{:S(2)}, u32[]{:S(2)}) async-start(bf16[4,32,512]{2,1,0:T(8,128)(2,1)} %reduce_sum.35), calls=%async_computation.9 | async-start | bytes 262144 | tf_op jit(solution)/shard_map/all_to_all | solution.py:628
  253.6 1.4 copy-start.7
  264.5 35.8 %all-to-all-start.6 = ((bf16[8,320,256]{2,1,0:T(8,128)(2,1)}), bf16[8,320,256]{2,1,0:T(8,128)(2,1)S(1)}, u32[]{:S(2)}, u32[]{:S(2)}) async-start(bf16[8,320,256]{2,1,0:T(8,128)(2,1)} %fusion.13), calls=%async_computation.6 | async-start | bytes 2621440 | tf_op jit(solution)/shard_map/all_to_all | solution.py:467
  301.5 30.1 %all-to-all-start.10 = ((bf16[8,4,32,512]{3,1,2,0:T(4,128)(2,1)}), bf16[8,4,32,512]{3,1,2,0:T(4,128)(2,1)}, u32[]{:S(2)}, u32[]{:S(2)}) async-start(bf16[8,4,32,512]{3,1,2,0:T(4,128)(2,1)} %broadcast_in_dim.83), calls=%async_computation.10 | async-start | bytes 2097152 | tf_op jit(solution)/shard_map/all_to_all | solution.py:467
  332.9 4.7 %copy-start.16 = (bf16[1392,256]{1,0:T(8,128)(2,1)S(1)}, bf16[1392,256]{1,0:T(8,128)(2,1)}, u32[]{:S(2)}) copy-start(bf16[1392,256]{1,0:T(8,128)(2,1)} %copy-done.15) | copy-start | bytes 2138116
  332.9 47.3 %all-to-all-start.7 = ((bf16[8,320,256]{2,1,0:T(8,128)(2,1)}), bf16[8,320,256]{2,1,0:T(8,128)(2,1)}, u32[]{:S(2)}, u32[]{:S(2)}) async-start(bf16[8,320,256]{2,1,0:T(8,128)(2,1)} %broadcast_in_dim.82), calls=%async_computation.7 | async-start | bytes 2621440 | tf_op jit(solution)/shard_map/all_to_all | solution.py:467
  337.5 19.6 %copy-start.9 = (bf16[1392,512]{1,0:T(8,128)(2,1)S(1)}, bf16[1392,512]{1,0:T(8,128)(2,1)}, u32[]{:S(2)}) copy-start(bf16[1392,512]{1,0:T(8,128)(2,1)} %copy-done.8) | copy-start | bytes 4276228
  337.5 16.8 %collective-permute-start.12 = (bf16[1392,256]{1,0:T(8,128)(2,1)S(1)}, bf16[1392,256]{1,0:T(8,128)(2,1)S(1)}, u32[]{:S(2)}, u32[]{:S(2)}) collective-permute-start(bf16[1392,256]{1,0:T(8,128)(2,1)S(1)} %copy-done.16), channel_id=1, source_target_pairs={{0,2},{1,3},{2,0},{3,1},{4,6},{5,7},{6,4},{7,5},{8,10},{9,11},{10,... | collective-permute-start | bytes 2138120 | tf_op jit(solution)/shard_map/ppermute | solution.py:464
  339.0 29.8 %collective-permute-start.11 = (bf16[1392,256]{1,0:T(8,128)(2,1)S(1)}, bf16[1392,256]{1,0:T(8,128)(2,1)}, u32[]{:S(2)}, u32[]{:S(2)}) collective-permute-start(bf16[1392,256]{1,0:T(8,128)(2,1)S(1)} %copy-done.16), channel_id=1, source_target_pairs={{0,1},{1,0},{2,3},{3,2},{4,5},{5,4},{6,7},{7,6},{8,9},{9,8},{10,11... | collective-permute-start | bytes 2138120 | tf_op jit(solution)/shard_map/ppermute | solution.py:464
  354.3 14.5 %collective-permute-start.13 = (bf16[1392,256]{1,0:T(8,128)(2,1)S(1)}, bf16[1392,256]{1,0:T(8,128)(2,1)}, u32[]{:S(2)}, u32[]{:S(2)}) collective-permute-start(bf16[1392,256]{1,0:T(8,128)(2,1)S(1)} %collective-permute-done.12.d2), channel_id=1, source_target_pairs={{0,1},{1,0},{2,3},{3,2},{4,5},{5,4},{6,7},{7,6},{8,9},{9,8},{10,11... | collective-permute-start | bytes 2138120 | tf_op jit(solution)/shard_map/ppermute | solution.py:464
  355.2 12.4 %collective-permute-start.14 = (bf16[512,256]{1,0:T(8,128)(2,1)}, bf16[512,256]{1,0:T(8,128)(2,1)S(1)}, u32[]{:S(2)}, u32[]{:S(2)}) collective-permute-start(bf16[512,256]{1,0:T(8,128)(2,1)} %get-tuple-element.132), channel_id=1, source_target_pairs={{0,1},{1,0},{2,3},{3,2},{4,5},{5,4},{6,7},{7,6},{8,9},{9,8},{10,11... | collective-permute-start | bytes 786440 | tf_op jit(solution)/shard_map/ppermute | solution.py:464
  355.7 11.9 %collective-permute-start.15 = (bf16[512,256]{1,0:T(8,128)(2,1)}, bf16[512,256]{1,0:T(8,128)(2,1)S(1)}, u32[]{:S(2)}, u32[]{:S(2)}) collective-permute-start(bf16[512,256]{1,0:T(8,128)(2,1)} %get-tuple-element.134), channel_id=1, source_target_pairs={{0,2},{1,3},{2,0},{3,1},{4,6},{5,7},{6,4},{7,5},{8,10},{9,11},{10,... | collective-permute-start | bytes 786440 | tf_op jit(solution)/shard_map/ppermute | solution.py:464
  357.0 11.8 %collective-permute-start.16 = (bf16[512,256]{1,0:T(8,128)(2,1)}, bf16[512,256]{1,0:T(8,128)(2,1)S(1)}, u32[]{:S(2)}, u32[]{:S(2)}) collective-permute-start(bf16[512,256]{1,0:T(8,128)(2,1)} %get-tuple-element.131), channel_id=1, source_target_pairs={{0,3},{1,2},{2,1},{3,0},{4,7},{5,6},{6,5},{7,4},{8,11},{9,10},{10,... | collective-permute-start | bytes 786440 | tf_op jit(solution)/shard_map/ppermute | solution.py:464
  374.6 2.3 slice-start.1
  376.9 1.7 slice-start.2
  (9 other events, 8.5 us)

commit v2 on v1

--- a/solution.py
+++ b/solution.py
@@ -16,7 +16,9 @@
 STEP = 48
 F32 = jnp.float32
 BF16 = jnp.bfloat16
-VMEM_LIMIT = 48 * 1024 * 1024
+MIB = 1024 * 1024
+COST = 1 << 20
+BLOCKS = 8
 
 
 class Layout:
@@ -61,12 +63,42 @@
             flat.append(jnp.pad(rows, ((0, padded - live), (0, 0))))
         return jnp.concatenate(flat, 0)
 
-    def split(self, flat):
+    def pixel_shapes(self, width, dtype):
+        return tuple(
+            jax.ShapeDtypeStruct((n // self.micro, self.micro, width), dtype) for n in self.live
+        )
+
+    def split(self, pieces):
         found = []
-        for e, n, start, live in zip(self.edges, self.slots, self.starts, self.live):
-            piece = flat[start : start + live].reshape(n, e, e, self.micro, flat.shape[-1])
+        for e, n, piece in zip(self.edges, self.slots, pieces):
+            piece = piece.reshape(n, e, e, self.micro, piece.shape[-1])
             found.append(jnp.transpose(piece, (3, 0, 1, 2, 4)))
         return found
+
+    def sweep(self, body, carry):
+        for k, (start, padded, live) in enumerate(zip(self.starts, self.padded, self.live)):
+            many = live // STEP
+
+            def step(i, carry, k=k, start=start):
+                def store(refs, values):
+                    pixels = values.shape[0] // self.micro
+                    found = values.reshape(pixels, self.micro, values.shape[1])
+                    refs[k][pl.ds(i * (STEP // self.micro), pixels)] = found.astype(refs[k].dtype)
+
+                return body(at(start + i * STEP, STEP), store, carry)
+
+            carry = lax.fori_loop(0, many, step, carry)
+            rest, left = padded - many * STEP, live - many * STEP
+
+            def store_rest(refs, values, k=k, many=many, left=left):
+                pixels = left // self.micro
+                found = values[:left].reshape(pixels, self.micro, values.shape[1])
+                first = many * STEP // self.micro
+                refs[k][first : first + pixels] = found.astype(refs[k].dtype)
+
+            if rest:
+                carry = body(slice(start + many * STEP, start + padded), store_rest, carry)
+        return carry
 
 
 def fold(x):
@@ -92,16 +124,18 @@
     return jnp.concatenate([x] * (width // x.shape[-1]), axis=-1)
 
 
+def tree_sum(tiles):
+    while len(tiles) > 1:
+        tiles = [tiles[k] + tiles[k + 1] for k in range(0, len(tiles), 2)]
+    return tiles[0]
+
+
 def moments(received):
-    total = jnp.sum(received[...], axis=0)
+    total = tree_sum([tile[...] for tile in received])
     count = pick(total, 2)
     mean = pick(total, 0) / count
     variance = pick(total, 1) / count - mean * mean
     return mean, lax.rsqrt(variance + EPSILON), count
-
-
-def spread(out_ref, tile):
-    out_ref[...] = jnp.broadcast_to(tile[None], out_ref.shape)
 
 
 def tiles(x):
@@ -160,7 +194,7 @@
         return masked_sums(z, z, widen(tiles(mask[rows, :]), width), carry)
 
     sums, squares = lax.fori_loop(0, lay.parts, step, zeros_pair(width))
-    spread(sums_out, pack(sums, squares, widen(count[...], width)))
+    sums_out[...] = pack(sums, squares, widen(count[...], width))
 
 
 def windows(lay, slabs, bits, image, sign):
@@ -216,7 +250,7 @@
         return masked_sums(z, z, widen(tiles(mask[rows, :]), width), carry)
 
     sums, squares = lax.fori_loop(0, lay.parts, step, zeros_pair(width))
-    spread(sums_out, pack(sums, squares, widen(count[...], width)))
+    sums_out[...] = pack(sums, squares, widen(count[...], width))
 
 
 def second_kernel(lay, z2, sums2, gain, bias, mask, act_out):
@@ -246,30 +280,29 @@
         return masked_sums(z, z, widen(tiles(mask[rows, :]), width), carry)
 
     sums, squares = lax.fori_loop(0, lay.parts, step, zeros_pair(width))
-    spread(sums_out, pack(sums, squares, widen(count[...], width)))
-
-
-def output_kernel(lay, z3, sums3, gain, bias, mask, x, dy, result_out, grad_out, sums_out):
+    sums_out[...] = pack(sums, squares, widen(count[...], width))
+
+
+def output_kernel(lay, z3, sums3, gain, bias, mask, x, dy, out5, out7, out9, grad_out, sums_out):
     width = z3.shape[1]
     mean, inverse, _ = moments(sums3)
 
-    def step(i, carry):
-        rows = at(i * STEP, STEP)
+    def step(rows, store, carry):
         live = widen(tiles(mask[rows, :]), width)
         normed = (tiles(z3[rows, :]) - mean) * inverse
         u = gain[...] * normed + bias[...] + tiles(x[rows, :].astype(F32))
         s = jax.nn.sigmoid(u)
-        result_out[rows, :] = flat(live * (u * s)).astype(BF16)
+        store((out5, out7, out9), flat(live * (u * s)))
         grad = live * tiles(dy[rows, :].astype(F32)) * (s * (1.0 + u * (1.0 - s)))
         grad_out[rows, :] = flat(grad)
         return carry[0] + jnp.sum(grad, 0), carry[1] + jnp.sum(grad * normed, 0)
 
-    first, cross = lax.fori_loop(0, lay.rows // STEP, step, zeros_pair(width))
-    spread(sums_out, pack(first, cross, jnp.zeros_like(first)))
+    first, cross = lay.sweep(step, zeros_pair(width))
+    sums_out[...] = pack(first, cross, jnp.zeros_like(first))
 
 
 def grad_sums(received):
-    total = jnp.sum(received[...], axis=0)
+    total = tree_sum([tile[...] for tile in received])
     return pick(total, 0), pick(total, 1)
 
 
@@ -331,12 +364,12 @@
         return carry[0] + jnp.sum(grad, 0), carry[1] + jnp.sum(grad * normed, 0)
 
     first, cross = lax.fori_loop(0, lay.rows // STEP, step, zeros_pair(width))
-    spread(sums_out, pack(first, cross, jnp.zeros_like(first)))
+    sums_out[...] = pack(first, cross, jnp.zeros_like(first))
 
 
 def conv_back_kernel(
-    lay, groups, du2, z2, sums2, sums5, gain2, mask, bits, weight, act, z1, sums1, gain1, bias1, block, choose,
-    grad_out, sums_out, group_out, bias_out, gain_out, slabs, image, wide,
+    lay, du2, z2, sums2, sums5, gain2, mask, bits, weight, z1, sums1, gain1, bias1,
+    grad_out, sums_out, dz_out, bias_out, gain_out, slabs, image,
 ):
     width = z2.shape[1]
     sums = grad_sums(sums5)
@@ -345,7 +378,9 @@
     clear_halo(lay, slabs)
 
     def store(i, rows, dz):
-        to_slabs(slabs, i, dz.astype(BF16).astype(F32))
+        rounded = dz.astype(BF16)
+        dz_out[rows, :] = rounded
+        to_slabs(slabs, i, rounded.astype(F32))
 
     norm_back_loop(lay, du2, z2, mask, gain2, moments(sums2), sums, store)
     windows(lay, slabs, bits, image, -1)
@@ -362,7 +397,26 @@
         return carry[0] + jnp.sum(grad, 0), carry[1] + jnp.sum(grad * normed, 0)
 
     first, cross = lax.fori_loop(0, lay.parts, step, zeros_pair(width))
-    spread(sums_out, pack(first, cross, jnp.zeros_like(first)))
+    sums_out[...] = pack(first, cross, jnp.zeros_like(first))
+
+
+def deal(rank, held, keep, send, lead=()):
+    piece = held.shape[0] // (2 * keep.shape[0])
+    for j in range(keep.shape[0]):
+        for ref, other in ((keep, 2 * j), (send, 2 * j + 1)):
+            ref[(j, *lead)] = held[at(jnp.bitwise_xor(rank, other) * piece, piece), :]
+
+
+def group_kernel(lay, act, dz, bits, block, choose, group_out, slabs, image, wide):
+    width = act.shape[1]
+    clear_halo(lay, slabs)
+
+    def copy(i, _):
+        to_slabs(slabs, i, dz[at(i * STEP, STEP), :].astype(F32))
+        return 0
+
+    lax.fori_loop(0, lay.rows // STEP, copy, 0)
+    windows(lay, slabs, bits, image, -1)
     for tap in range(9):
         columns = slice(tap * width, (tap + 1) * width)
         found = mm_tn(act[...], image[:, columns])
@@ -371,10 +425,10 @@
 
 
 def first_back_kernel(
-    lay, me, du1, z1, sums1, sums6, gain, mask, x0, x1, x2, x3,
-    dz_out, weight_out, bias_out, gain_out,
+    lay, ids, du1, z1, sums1, sums6, gain, mask, group, x0, x1, x2, x3,
+    dz_out, bias_out, gain_out, keep, send, held,
 ):
-    t = me[0]
+    t, rank = ids[0], ids[1]
     sums = grad_sums(sums6)
     bias_out[...] = both(sums[0])
     gain_out[...] = both(sums[1])
@@ -384,34 +438,89 @@
 
     norm_back_loop(lay, du1, z1, mask, gain, moments(sums1), sums, store)
     for k, x in ((0, x0), (1, x1), (2, x2), (3, x3)):
-        weight_out[jnp.bitwise_xor(t, k)] = mm_tn(dz_out[...], x[...]).astype(BF16)
-
-
-def input_kernel(lay, du3, d0, d1, d2, d3, w0, w1, w2, w3, out):
+        found = mm_tn(dz_out[...], x[...]).astype(BF16)
+        wide = held.shape[2]
+        many = found.shape[1] // wide
+        for i in range(many):
+            held[jnp.bitwise_xor(t, k) * many + i] = found[:, i * wide : (i + 1) * wide]
+    low, piece = held.shape[1], group.shape[0] // held.shape[0]
+    for j in range(keep.shape[0]):
+        for ref, other in ((keep, 2 * j), (send, 2 * j + 1)):
+            other = jnp.bitwise_xor(rank, other)
+            ref[j, :low, :] = held[other]
+            rows = group[at(other * piece, piece), :]
+            ref[j, low : low + piece, :] = rows[:, :wide]
+            high = low + piece
+            ref[j, high:, :LANES] = rows[: piece // 2, wide:]
+            ref[j, high:, LANES:] = rows[piece // 2 :, wide:]
+
+
+def turn_kernel(*refs):
+    total = refs[0][...].astype(F32)
+    for ref in refs[1:-1]:
+        total = total + ref[...].astype(F32)
+    width = total.shape[1]
+    refs[-1][:width, :] = total[:width].T.astype(BF16)
+    refs[-1][width:, :] = total[width:].astype(BF16)
+
+
+def place_kernel(ids, *refs):
+    reduce_out, group_out, group = refs[-3:]
+    width = reduce_out.shape[1]
+    piece = group.shape[0] // (len(refs) - 3)
+    for r, ref in enumerate(refs[:-3]):
+        other = jnp.bitwise_xor(ids[1], r)
+        reduce_out[at(other * width, width), :] = ref[:width, :].astype(F32)
+        rows = ref[width:, :].astype(F32)
+        group[at(other * piece, piece), :width] = rows[:piece]
+        group[at(other * piece, piece // 2), width:] = rows[piece:, :LANES]
+        group[at(other * piece + piece // 2, piece // 2), width:] = rows[piece:, LANES:]
+    size = group_out.shape[-1]
+    for tap in range(group_out.shape[0]):
+        found = group[:, tap * size : (tap + 1) * size]
+        group_out[tap] = found.reshape(group_out.shape[1:])
+
+
+def input_kernel(lay, du3, d0, d1, d2, d3, w0, w1, w2, w3, out5, out7, out9, held):
     def step(part, _):
         rows = at(part * lay.part, lay.part)
         acc = du3[rows, :]
         for d, w in ((d0, w0), (d1, w1), (d2, w2), (d3, w3)):
             acc = acc + mm_nt(d[rows, :], w[...])
-        out[rows, :] = acc
+        held[rows, :] = acc
         return 0
 
     lax.fori_loop(0, lay.parts, step, 0)
 
-
-def expand_grad_kernel(lay, me, a0, a1, a2, a3, dz, out):
-    t = me[0]
-    for k, a in ((0, a0), (1, a1), (2, a2), (3, a3)):
-        out[jnp.bitwise_xor(t, k)] = mm_tn(a[...], dz[...]).astype(BF16)
-
-
-def run(kernel, args, outs, scratch=(), scalars=0, flops=0):
-    size = sum(a.size * a.dtype.itemsize for a in args) + sum(
-        int(np.prod(o.shape)) * o.dtype.itemsize for o in outs
-    )
+    def move(rows, store, carry):
+        store((out5, out7, out9), held[rows, :])
+        return carry
+
+    lay.sweep(move, 0)
+
+
+def expand_grad_kernel(lay, ids, a0, a1, a2, a3, dz, keep, send, held):
+    for k, a in enumerate((a0, a1, a2, a3)):
+        held[...] = mm_tn(a[...], dz[...]).astype(BF16)
+        deal(ids[1], held, keep, send, (k,))
+
+
+def expand_place_kernel(ids, *refs):
+    t, rank = ids[0], ids[1]
+    out = refs[-1]
+    for r, ref in enumerate(refs[:-1]):
+        piece, chan = ref.shape[1], ref.shape[2]
+        for k in range(ref.shape[0]):
+            rows = at(jnp.bitwise_xor(rank, r) * piece, piece)
+            out[rows, at(jnp.bitwise_xor(t, k) * chan, chan, LANES)] = ref[k].astype(F32)
+
+
+def run(kernel, args, outs, scratch=(), scalars=0, limit=8):
     specs = [
-        pl.BlockSpec(memory_space=pltpu.SMEM if k < scalars else pltpu.VMEM)
-        for k in range(len(args))
+        jax.tree.map(
+            lambda _, k=k: pl.BlockSpec(memory_space=pltpu.SMEM if k < scalars else pltpu.VMEM), a
+        )
+        for k, a in enumerate(args)
     ]
     return pl.pallas_call(
         kernel,
@@ -419,8 +528,8 @@
         in_specs=specs,
         out_specs=[pl.BlockSpec(memory_space=pltpu.VMEM)] * len(outs),
         scratch_shapes=list(scratch),
-        compiler_params=pltpu.CompilerParams(vmem_limit_bytes=VMEM_LIMIT),
-        cost_estimate=pl.CostEstimate(flops=flops, bytes_accessed=size, transcendentals=0),
+        compiler_params=pltpu.CompilerParams(vmem_limit_bytes=limit * MIB),
+        cost_estimate=pl.CostEstimate(flops=COST, bytes_accessed=0, transcendentals=0),
     )(*args)
 
 
@@ -458,13 +567,42 @@
     inner = group_count * group_width
     shards = reduce_weight.shape[0] // chan
     t = lax.axis_index("tensor").astype(jnp.int32)
-    me = t.reshape(1)
+    rank = lax.axis_index("batch").astype(jnp.int32)
+    fast = ranks == BLOCKS
+    ids = jnp.stack([t, rank if fast else jnp.zeros_like(rank)])
+    hold = lax.optimization_barrier
 
     def swap(x, k):
         return lax.ppermute(x, "tensor", [(i, i ^ k) for i in range(shards)])
 
-    def everyone(x):
-        return lax.all_to_all(x, "batch", split_axis=0, concat_axis=0, tiled=True)
+    def pass_on(x, k):
+        return lax.ppermute(x, "batch", [(i, i ^ k) for i in range(ranks)])
+
+    def allsum(tile):
+        found = [tile]
+        bits_left = ranks.bit_length() - 1
+        while bits_left:
+            low = bits_left - 2 if bits_left % 2 == 0 or bits_left > 2 else 0
+            tile = tree_sum(found)
+            steps = [k << low for k in range(1, 1 << (bits_left - low))]
+            found = [tile] + [pass_on(tile, k) for k in steps]
+            bits_left = low
+        return tuple(found)
+
+    def halve(keep, send):
+        half = ranks // 2
+        passed = pass_on(send, 1)
+        sums = [total(keep[j], passed[j]).astype(BF16) for j in range(half)]
+        return sums
+
+    def scatter(sums):
+        return [sums[0]] + [pass_on(sums[j], 2 * j) for j in range(1, ranks // 2)]
+
+    def collect_far(mine):
+        return [mine] + [pass_on(mine, 2 * j) for j in range(1, ranks // 2)]
+
+    def collect_near(blocks):
+        return [part for w in blocks for part in (w, pass_on(w, 1))]
 
     def gather(x):
         near = swap(x, 1)
@@ -473,6 +611,12 @@
 
     def row(v):
         return v.reshape(1, v.shape[0])
+
+    def total(*parts):
+        found = parts[0].astype(F32)
+        for part in parts[1:]:
+            found = found + part.astype(F32)
+        return found
 
     g1, b1, g2, b2, g3, b3 = map(
         row, (first_gain, first_bias, second_gain, second_bias, third_gain, third_bias)
@@ -486,9 +630,9 @@
     bits = jnp.asarray(lay.tap_bits())
 
     maps = lay.flatten(all_maps)
-    xs = gather(maps)
-    ids = np.arange(inner) // group_width
-    block = jnp.asarray(ids[:, None] == ids[None, :])
+    maps_near, maps_far = swap(maps, 1), swap(maps, 2)
+    owner = np.arange(inner) // group_width
+    block = jnp.asarray(owner[:, None] == owner[None, :])
 
     def dense(w):
         tiled = jnp.tile(w.reshape(9, inner, group_width), (1, 1, group_count))
@@ -501,6 +645,7 @@
         for c in range(inner):
             choose[tap * inner + c, tap * group_width + c % group_width] = 1.0
     choose = jnp.asarray(choose, BF16)
+    upstream = lay.flatten(all_upstream)
 
     def columns(k):
         return lax.dynamic_slice_in_dim(expand_weight, jnp.bitwise_xor(t, k) * chan, chan, 1)
@@ -508,53 +653,55 @@
     def weight_rows(k):
         return lax.dynamic_slice_in_dim(reduce_weight, jnp.bitwise_xor(t, k) * chan, chan, 0)
 
-    expand_parts = [columns(0)] + [swap(columns(k), k) for k in (1, 2, 3)]
-    reduce_parts = [weight_rows(0)] + [swap(weight_rows(k), k) for k in (1, 2, 3)]
-
-    upstream = lay.flatten(all_upstream)
-    tile1 = like((ranks, SUBLANES, inner), F32)
-    tile3 = like((ranks, SUBLANES, chan), F32)
+    expand_parts = [columns(k) for k in range(shards)]
+    reduce_parts = [weight_rows(k) for k in range(shards)]
+    maps_far, mask, count, forward_weight, backward_weight, upstream, expand_parts, reduce_parts = hold(
+        (maps_far, mask, count, forward_weight, backward_weight, upstream, expand_parts, reduce_parts)
+    )
+    xs = (maps, maps_near, maps_far, swap(maps_far, 1))
+    expand_parts = [w if k == 0 else swap(w, k) for k, w in enumerate(expand_parts)]
+    reduce_parts = [w if k == 0 else swap(w, k) for k, w in enumerate(reduce_parts)]
+
+    tile1 = like((SUBLANES, inner), F32)
+    tile3 = like((SUBLANES, chan), F32)
     slabs = pltpu.VMEM((inner // LANES, rows + 2 * HALO, LANES), F32)
     image = pltpu.VMEM((rows, 9 * inner), BF16)
-    full_flops = 2 * rows * chan * shards * inner
 
     z1, s1 = run(
         functools.partial(reduce_kernel, lay),
-        (me, *xs, reduce_weight.reshape(shards, chan, inner), mask, count),
+        (ids, *xs, reduce_weight.reshape(shards, chan, inner), mask, count),
         (like((rows, inner), F32), tile1),
         scalars=1,
-        flops=full_flops,
-    )
-    s1 = everyone(s1)
+    )
+    s1 = allsum(s1)
+    s1, expand_parts = hold((s1, expand_parts))
     z2, s2, act1 = run(
         functools.partial(conv_kernel, lay),
         (z1, s1, g1, b1, mask, count, bits, forward_weight),
         (like((rows, inner), F32), tile1, like((rows, inner), BF16)),
         scratch=(slabs, image),
-        flops=full_flops,
-    )
-    s2 = everyone(s2)
+        limit=16,
+    )
+    s2 = allsum(s2)
+    s2, reduce_parts = hold((s2, reduce_parts))
     (act2,) = run(
         functools.partial(second_kernel, lay),
         (z2, s2, g2, b2, mask),
         (like((rows, inner), BF16),),
-        flops=20 * rows * inner,
     )
     acts = gather(act2)
     z3, s3 = run(
         functools.partial(expand_kernel, lay),
         (*acts, *expand_parts, mask, count),
         (like((rows, chan), F32), tile3),
-        flops=full_flops,
-    )
-    s3 = everyone(s3)
-    output, du3, s4 = run(
+    )
+    s3 = allsum(s3)
+    *output, du3, s4 = run(
         functools.partial(output_kernel, lay),
         (z3, s3, g3, b3, mask, maps, upstream),
-        (like((rows, chan), BF16), like((rows, chan), F32), tile3),
-        flops=40 * rows * chan,
-    )
-    s4 = everyone(s4)
+        (*lay.pixel_shapes(chan, BF16), like((rows, chan), F32), tile3),
+    )
+    s4 = allsum(s4)
     dz3, own, peer, send, bias_three, gain_three = run(
         functools.partial(third_back_kernel, lay),
         (du3, z3, s3, s4, g3, mask, *expand_parts),
@@ -566,98 +713,122 @@
             like((1, chan), F32),
             like((1, chan), F32),
         ),
-        flops=full_flops,
     )
     near = swap(send, 1)
-    far = swap((peer + near[1].astype(F32)).astype(BF16), 2)
-    (expand_local,) = run(
+    piece = inner // BLOCKS
+    half = BLOCKS // 2
+    expand_keep, expand_send = run(
         functools.partial(expand_grad_kernel, lay),
-        (me, *acts, dz3),
-        (like((shards, inner, chan), BF16),),
+        (ids, *acts, dz3),
+        (like((half, shards, piece, chan), BF16),) * 2,
+        scratch=(pltpu.VMEM((inner, chan), BF16),),
         scalars=1,
-        flops=full_flops,
-    )
+    )
+    if fast:
+        sums = halve(expand_keep, expand_send)
+    far = swap(total(peer, near[1]).astype(BF16), 2)
+    if fast:
+        arrived = scatter(sums)
+        far, arrived[1] = hold((far, arrived[1]))
     du2, s5 = run(
         functools.partial(second_back_kernel, lay),
         (own, near, far, z2, s2, g2, b2, mask),
         (like((rows, inner), F32), tile1),
-        flops=40 * rows * inner,
-    )
-    s5 = everyone(s5)
-    du1, s6, group_local, bias_two, gain_two = run(
-        functools.partial(conv_back_kernel, lay, group_count),
-        (
-            du2, z2, s2, s5, g2, mask, bits, backward_weight, act1, z1, s1, g1, b1,
-            block.astype(F32), choose,
-        ),
+    )
+    s5 = allsum(s5)
+    if fast:
+        s5, arrived = hold((s5, arrived))
+        mine = total(*arrived).astype(BF16)
+        mine = jnp.stack([mine[0]] + [swap(mine[k], k) for k in range(1, shards)])
+    du1, s6, dz2, bias_two, gain_two = run(
+        functools.partial(conv_back_kernel, lay),
+        (du2, z2, s2, s5, g2, mask, bits, backward_weight, z1, s1, g1, b1),
         (
             like((rows, inner), F32),
             tile1,
-            like((inner, choose.shape[1]), BF16),
+            like((rows, inner), BF16),
             like((1, inner), F32),
             like((1, inner), F32),
         ),
+        scratch=(slabs, image),
+        limit=16,
+    )
+    s6 = allsum(s6)
+    lanes = choose.shape[1]
+    (group_local,) = run(
+        functools.partial(group_kernel, lay),
+        (act1, dz2, bits, block.astype(F32), choose),
+        (like((inner, lanes), BF16),),
         scratch=(slabs, image, pltpu.VMEM((inner, 9 * inner), BF16)),
-        flops=2 * full_flops,
-    )
-    s6 = everyone(s6)
-    dz1, reduce_local, bias_one, gain_one = run(
+        limit=24,
+    )
+    if fast:
+        s6, group_local, mine = hold((s6, group_local, mine))
+    wide = shards * chan // BLOCKS
+    deep = wide + piece + piece * (lanes - wide) // wide
+    dz1, bias_one, gain_one, reduce_keep, reduce_send = run(
         functools.partial(first_back_kernel, lay),
-        (me, du1, z1, s1, s6, g1, mask, *xs),
+        (ids, du1, z1, s1, s6, g1, mask, group_local, *xs),
         (
             like((rows, inner), BF16),
-            like((shards, inner, chan), BF16),
             like((1, inner), F32),
             like((1, inner), F32),
+            like((half, deep, inner), BF16),
+            like((half, deep, inner), BF16),
         ),
+        scratch=(pltpu.VMEM((BLOCKS, inner, wide), BF16),),
         scalars=1,
-        flops=full_flops,
-    )
-    grads = gather(dz1)
-    (backprop,) = run(
+    )
+
+    def summed(keep, send):
+        both_sums = lax.psum((keep.astype(F32), send.astype(F32)), "batch")
+        return [both_sums[r % 2][r // 2].astype(BF16) for r in range(BLOCKS)]
+
+    block_shape = (like((deep, inner), BF16),)
+    if fast:
+        reduce_keep, reduce_send, dz1, mine = hold((reduce_keep, reduce_send, dz1, mine))
+        passed = pass_on(reduce_send, 1)
+        dz_near, dz_far = swap(dz1, 1), swap(dz1, 2)
+        whole = collect_far(mine)
+        sums = [total(reduce_keep[j], passed[j]).astype(BF16) for j in range(half)]
+        sums, dz_far, whole = hold((sums, dz_far, whole))
+        parts = scatter(sums)
+        dz_cross = swap(dz_far, 1)
+        crossed = pass_on(jnp.stack(whole), 1)
+        whole = [w for j in range(half) for w in (whole[j], crossed[j])]
+    else:
+        dz_near, dz_far = swap(dz1, 1), swap(dz1, 2)
+        dz_cross = swap(dz_far, 1)
+    backprop = run(
         functools.partial(input_kernel, lay),
-        (du3, *grads, *reduce_parts),
-        (like((rows, chan), F32),),
-        flops=full_flops,
-    )
-
-    if inner % (ranks * PACKED) == 0 and ranks * LANES <= shards * chan:
-        piece = inner // ranks
-        sent = expand_local.reshape(shards, ranks, piece, chan).transpose(1, 0, 2, 3)
-        mine = jnp.sum(everyone(sent).astype(F32), 0).astype(BF16)
-        mine = lax.all_to_all(mine, "tensor", split_axis=0, concat_axis=0, tiled=True)
-        whole = everyone(jnp.broadcast_to(mine[None], (ranks, *mine.shape)))
-        expand_grad = whole.transpose(0, 2, 1, 3).reshape(inner, shards * chan).astype(F32)
-
-        wide = shards * chan // ranks
-        sent = reduce_local.transpose(0, 2, 1).reshape(ranks, wide, inner)
-        extra = group_local.reshape(ranks, piece, choose.shape[1])
-        extra = jnp.concatenate(
-            [extra[:, :, :inner], jnp.pad(extra[:, :, inner:], ((0, 0), (0, 0), (0, 2 * inner - extra.shape[2])))],
-            1,
-        )
-        sent = jnp.concatenate([sent, extra], 1)
-        mine = jnp.sum(everyone(sent).astype(F32), 0).astype(BF16)
-        whole = everyone(jnp.broadcast_to(mine[None], (ranks, *mine.shape)))
-        reduce_grad = whole[:, :wide].reshape(shards * chan, inner).astype(F32)
-        group_flat = jnp.concatenate(
-            [whole[:, wide : wide + piece], whole[:, wide + piece :]], 2
-        ).reshape(inner, 2 * inner)
+        (du3, dz1, dz_near, dz_far, dz_cross, *reduce_parts),
+        lay.pixel_shapes(chan, F32),
+        scratch=(pltpu.VMEM((rows, chan), F32),),
+    )
+    if fast:
+        parts, backprop = hold((parts, backprop))
+        (mine,) = run(turn_kernel, tuple(parts), block_shape)
+        blocks = collect_near(collect_far(mine))
     else:
-        summed = lax.psum(
-            (expand_local.astype(F32), reduce_local.astype(F32), group_local.astype(F32)), "batch"
-        )
-        expand_grad = lax.all_to_all(summed[0], "tensor", split_axis=0, concat_axis=0, tiled=True)
-        expand_grad = expand_grad.transpose(1, 0, 2).reshape(inner, shards * chan)
-        reduce_grad = summed[1].transpose(0, 2, 1).reshape(shards * chan, inner)
-        group_flat = summed[2]
-    group_grad = (
-        group_flat[:, : 9 * group_width]
-        .astype(F32)
-        .reshape(group_count, group_width, 9, group_width)
-        .transpose(2, 0, 1, 3)
-        .reshape(3, 3, group_count, group_width, group_width)
-    )
+        blocks = [run(turn_kernel, (b,), block_shape)[0] for b in summed(reduce_keep, reduce_send)]
+        whole = [
+            jnp.stack([b[0]] + [swap(b[k], k) for k in range(1, shards)])
+            for b in summed(expand_keep, expand_send)
+        ]
+    (expand_grad,) = run(
+        expand_place_kernel, (ids, *whole), (like((inner, shards * chan), F32),), scalars=1
+    )
+    reduce_grad, group_grad = run(
+        place_kernel,
+        (ids, *blocks),
+        (
+            like((shards * chan, inner), F32),
+            like((9, group_count, group_width, group_width), F32),
+        ),
+        scratch=(pltpu.VMEM((inner, lanes), F32),),
+        scalars=1,
+    )
+    group_grad = group_grad.reshape(3, 3, group_count, group_width, group_width)
     return (
         *lay.split(output),
         *lay.split(backprop),

time: 388 us -> 257 us (0.66)
  waiting for transfers between devices: 165 us -> 110 us
  local copies, waits for them, and re-layouts: 70 us -> 19.3 us
  blocking collectives: 22.5 us -> 0 us
  starting transfers between devices: 48.3 us -> 67.4 us
  Pallas kernels: 59.9 us -> 49.1 us
  other arithmetic: 19.1 us -> 8.98 us
    ppermute x0 -> x43, waiting for transfers between devices: none -> 82.4 us  [pass_on(): return lax.ppermute(x, 'batch', [(i, i ^ k) for i in range(ranks)])]
    all_to_all x9 -> x0, waiting for transfers between devices: 76.6 us -> none  [the longest x8 76.6 us: everyone(): return lax.all_to_all(x, 'batch', split_axis=0, concat_axis=0, tiled=True)]
    ppermute x17 -> x20, waiting for transfers between devices: 88.3 us -> 27.7 us  [swap(): return lax.ppermute(x, 'tensor', [(i, i ^ k) for i in range(shards)])]
    ppermute x0 -> x43, starting transfers between devices: none -> 55.2 us  [pass_on(): return lax.ppermute(x, 'batch', [(i, i ^ k) for i in range(ranks)])]
    all_to_all x9 -> x0, starting transfers between devices: 36.9 us -> none  [the longest x8 32.9 us: everyone(): return lax.all_to_all(x, 'batch', split_axis=0, concat_axis=0, tiled=True)]
    all_to_all x2 -> x0, blocking collectives: 22.5 us -> none  [everyone(): return lax.all_to_all(x, 'batch', split_axis=0, concat_axis=0, tiled=True)]
    unnamed x94 -> x69, local copies, waits for them, and re-layouts: 22.4 us -> 4.51 us
    reshape x8 -> x0, local copies, waits for them, and re-layouts: 11 us -> none  [the longest x6 9.65 us: split(): flat[start:start + live].reshape(n, e, e, self.micro, flat.shape[-1])]
  transfers between devices with their start and end apart: 26 -> 63, of which waited for: 14 -> 34; matrix products, arithmetic and copies ran while one was open for 15% -> 9% of each run, Pallas kernels for 7% -> 8%
where the time goes in v2:
time: 257 us; the launch traced here: 256 us
  waiting for transfers between devices  110 us (43%)
  starting transfers between devices  67.4 us (26%)
  Pallas kernels  49.1 us (19%)
  local copies, waits for them, and re-layouts  19.3 us (8%)
  other arithmetic  8.98 us (3%)
    ppermute x43, waiting for transfers between devices, pass_on(): return lax.ppermute(x, 'batch', [(i, i ^ k) for i in range(ranks)])  82.4 us
    ppermute x43, starting transfers between devices, pass_on(): return lax.ppermute(x, 'batch', [(i, i ^ k) for i in range(ranks)])  55.2 us
    pallas_call x15, Pallas kernels, run(): pl.pallas_call(kernel, out_shape=list(outs), in_specs=specs, out_specs=[p...  49.1 us
    ppermute x20, waiting for transfers between devices, swap(): return lax.ppermute(x, 'tensor', [(i, i ^ k) for i in range(shards)])  27.7 us
    ppermute x20, starting transfers between devices, swap(): return lax.ppermute(x, 'tensor', [(i, i ^ k) for i in range(shards)])  12.2 us
    another operation x7, local copies, waits for them, and re-layouts, dense(): tiled = jnp.tile(w.reshape(9, inner, group_width), (1, 1, group_count))  6.15 us
    reshape x6, local copies, waits for them, and re-layouts, flatten(): rows = jnp.transpose(piece, (1, 2, 3, 0, 4)).reshape(live, piece.shape[-1])  5.6 us
  transfers between devices with their start and end apart: 63, of which 34 were waited for; matrix products, arithmetic and copies ran while one was open for 9% of the time, Pallas kernels for 8%

profile of v2, /device:TPU:0, one launch (start us, length us, event | category | flops | bytes accessed | tf_op | source)
XLA Modules:
  0.0 256.2 jit_solution(13981438453422861891)
XLA Ops:
  3.5 3.0 %collective-permute-start.1 = (bf16[1392,512]{1,0:T(8,128)(2,1)S(1)}, bf16[1392,512]{1,0:T(8,128)(2,1)}, u32[]{:S(2)}, u32[]{:S(2)}) collective-permute-start(bf16[1392,512]{1,0:T(8,128)(2,1)S(1)} %fusion.8.x0.x), channel_id=1, source_target_pairs={{0,2},{1,3},{2,0},{3,1},{4,6},{5,7},{6,4},{7,5},{8,10},{9,11},{10,... | collective-permute-start | bytes 4276232 | tf_op jit(solution)/shard_map/ppermute | solution.py:576
  13.4 1.8 reshape.148
  17.9 1.6 copy.45
  21.2 1.4 copy.42
  22.6 2.9 %bitcast_select_fusion = (bf16[2304,256]{1,0:T(8,128)(2,1)S(1)}, bf16[2304,256]{1,0:T(8,128)(2,1)}) fusion(bf16[2304,256]{1,0:T(8,128)(2,1)} %copy.45, pred[256,256]{1,0:T(8,128)(4,1)S(1)} %copy.50, bf16[2304,256]{1,0:T(8,128)(2,1)} %copy.42), kind=kLoop, calls=%fused_computation.2 | loop fusion | flops 1179648 | bytes 4784128 | tf_op jit(solution)/shard_map/jit(_where)/select_n | solution.py:639
  29.8 8.1 %collective-permute-done.1.x2 = bf16[1392,512]{1,0:T(8,128)(2,1)} collective-permute-done((bf16[1392,512]{1,0:T(8,128)(2,1)S(1)}, bf16[1392,512]{1,0:T(8,128)(2,1)}, u32[]{:S(2)}, u32[]{:S(2)}) %collective-permute-start.1) | collective-permute-done | bytes 1425440 | tf_op jit(solution)/shard_map/ppermute | solution.py:576
  38.7 1.7 collective-permute-start.8
  43.0 4.4 %shard_map.361 = (f32[1392,256]{1,0:T(8,128)S(1)}, f32[8,256]{1,0:T(8,128)S(1)}) custom-call(s32[2]{0:T(128)S(1)} %pad_add_fusion.me.ids, bf16[1392,512]{1,0:T(8,128)(2,1)S(1)} %fusion.8.x0.x, bf16[1392,512]{1,0:T(8,128)(2,1)} %collective-permute-done.x1, bf16[1392,512]{1,0:T(8,128)(2,1)} %collective-permute-done.1.x2, ...), custom_call_target="tpu_custom_call" | custom-call | flops 1048576 | tf_op jit(solution)/shard_map/pallas_call | solution.py:525
  47.4 3.9 %collective-permute-start.5 = (f32[8,256]{1,0:T(8,128)S(1)}, f32[8,256]{1,0:T(8,128)S(1)}, u32[]{:S(2)}, u32[]{:S(2)}) collective-permute-start(f32[8,256]{1,0:T(8,128)S(1)} %get-tuple-element.114), channel_id=1, source_target_pairs={{0,24},{4,28},{8,16},{12,20},{16,8},{20,12},{24,0},{28,4},{1,25},{... | collective-permute-start | bytes 24584 | tf_op jit(solution)/shard_map/ppermute | solution.py:579
  53.0 2.9 %collective-permute-done.4 = f32[8,256]{1,0:T(8,128)S(1)} collective-permute-done((f32[8,256]{1,0:T(8,128)S(1)}, f32[8,256]{1,0:T(8,128)S(1)}, u32[]{:S(2)}, u32[]{:S(2)}) %collective-permute-start.4) | collective-permute-done | bytes 8224 | tf_op jit(solution)/shard_map/ppermute | solution.py:579
  55.9 1.5 collective-permute-start.15
  57.4 1.6 collective-permute-start.6
  59.0 2.1 collective-permute-done.6.sums1_1_
  61.2 4.8 %shard_map.362 = (f32[1392,256]{1,0:T(8,128)S(1)}, f32[8,256]{1,0:T(8,128)S(1)}, bf16[1392,256]{1,0:T(8,128)(2,1)S(1)}) custom-call(f32[1392,256]{1,0:T(8,128)S(1)} %get-tuple-element.113.z1, f32[8,256]{1,0:T(8,128)S(1)} %add_add_fusion.5.sums1_0_, f32[8,256]{1,0:T(8,128)S(1)} %collective-permute-done.6.sums1_1_, f32[1,256]{1,0:T(1,128)S(1)} %bitcast.113, ...), custom_call_target="tpu_custom_call" | custom-call | flops 1048576 | tf_op jit(solution)/shard_map/pallas_call | solution.py:525
  67.4 4.2 %collective-permute-done.12 = f32[8,256]{1,0:T(8,128)S(1)} collective-permute-done((f32[8,256]{1,0:T(8,128)S(1)}, f32[8,256]{1,0:T(8,128)S(1)}, u32[]{:S(2)}, u32[]{:S(2)}) %collective-permute-start.12) | collective-permute-done | bytes 8224 | tf_op jit(solution)/shard_map/ppermute | solution.py:579
  71.9 3.3 %collective-permute-done.10 = f32[8,256]{1,0:T(8,128)S(1)} collective-permute-done((f32[8,256]{1,0:T(8,128)S(1)}, f32[8,256]{1,0:T(8,128)S(1)}, u32[]{:S(2)}, u32[]{:S(2)}) %collective-permute-start.10) | collective-permute-done | bytes 8224 | tf_op jit(solution)/shard_map/ppermute | solution.py:579
  75.2 1.5 collective-permute-start.13
  76.7 2.1 collective-permute-done.13.sums2_1_
  80.2 13.8 %collective-permute-done.18.a2 = bf16[1392,256]{1,0:T(8,128)(2,1)S(1)} collective-permute-done((bf16[1392,256]{1,0:T(8,128)(2,1)S(1)}, bf16[1392,256]{1,0:T(8,128)(2,1)S(1)}, u32[]{:S(2)}, u32[]{:S(2)}) %collective-permute-start.18) | collective-permute-done | bytes 712736 | tf_op jit(solution)/shard_map/ppermute | solution.py:576
  94.0 2.2 collective-permute-done.19.a3
  96.2 2.9 %shard_map.364 = (f32[1392,512]{1,0:T(8,128)S(1)}, f32[8,512]{1,0:T(8,128)S(1)}) custom-call(bf16[1392,256]{1,0:T(8,128)(2,1)S(1)} %shard_map.363.a0, bf16[1392,256]{1,0:T(8,128)(2,1)S(1)} %collective-permute-done.17.a1, bf16[1392,256]{1,0:T(8,128)(2,1)S(1)} %collective-permute-done.18.a2, bf16[1392,256]{1,0:T(8,128)(2,1)S(1)} %collective-permute-done.19.a3, ...), custom_call_target="tpu_custom_call" | custom-call | flops 1048576 | tf_op jit(solution)/shard_map/pallas_call | solution.py:525
  100.8 2.8 %collective-permute-start.20 = (f32[8,512]{1,0:T(8,128)S(1)}, f32[8,512]{1,0:T(8,128)S(1)}, u32[]{:S(2)}, u32[]{:S(2)}) collective-permute-start(f32[8,512]{1,0:T(8,128)S(1)} %get-tuple-element.135), channel_id=1, source_target_pairs={{0,8},{4,12},{8,0},{12,4},{16,24},{20,28},{24,16},{28,20},{1,9},{5... | collective-permute-start | bytes 49160 | tf_op jit(solution)/shard_map/ppermute | solution.py:579
  105.3 1.6 collective-permute-start.23
  106.9 2.2 collective-permute-done.23.sums3_1_
  109.1 4.7 %shard_map.365 = (bf16[150,2,512]{2,1,0:T(2,128)(2,1)}, bf16[294,2,512]{2,1,0:T(2,128)(2,1)}, bf16[243,2,512]{2,1,0:T(2,128)(2,1)}, f32[1392,512]{1,0:T(8,128)S(1)}, f32[8,512]{1,0:T(8,128)S(1)}) custom-call(f32[1392,512]{1,0:T(8,128)S(1)} %get-tuple-element.134.z3, f32[8,512]{1,0:T(8,128)S(1)} %add_add_fusion.1.sums3_0_, ...), custom_call_target="tpu_custom_call" | custom-call | flops 1048576 | tf_op jit(solution)/shard_map/pallas_call | solution.py:525
  113.8 2.4 collective-permute-start.26
  119.3 1.5 collective-permute-done.25
  121.0 1.6 collective-permute-start.27
  122.6 2.2 collective-permute-done.27.sums4_1_
  124.8 4.3 %shard_map.366 = (bf16[1392,512]{1,0:T(8,128)(2,1)S(1)}, f32[1392,256]{1,0:T(8,128)S(1)}, f32[1392,256]{1,0:T(8,128)S(1)}, bf16[2,1392,256]{2,1,0:T(8,128)(2,1)S...) custom-call(f32[1392,512]{1,0:T(8,128)S(1)} %get-tuple-element.140.du3, f32[1392,512]{1,0:T(8,128)S(1)} %get-tuple-element.134.z3, ...), custom_call_target="tpu_custom_call" | custom-call | flops 1048576 | tf_op jit(solution)/shard_map/pallas_call | solution.py:525
  129.2 2.4 shard_map.367
  131.6 1.6 collective-permute-start.30
  133.4 1.4 collective-permute-start.29
  134.8 11.2 %collective-permute-done.30 = bf16[4,4,32,512]{3,2,1,0:T(8,128)(2,1)S(1)} collective-permute-done((bf16[4,4,32,512]{3,2,1,0:T(8,128)(2,1)S(1)}, bf16[4,4,32,512]{3,2,1,0:T(8,128)(2,1)S(1)}, u32[]{:S(2)}, u32[]{:S(2)}) %collective-permute-start.30) | collective-permute-done | bytes 524320 | tf_op jit(solution)/shard_map/ppermute | solution.py:579
  147.1 4.2 %collective-permute-done.31 = bf16[4,32,512]{2,1,0:T(8,128)(2,1)S(1)} collective-permute-done((bf16[4,32,512]{2,1,0:T(8,128)(2,1)S(1)}, bf16[4,32,512]{2,1,0:T(8,128)(2,1)S(1)}, u32[]{:S(2)}, u32[]{:S(2)}) %collective-permute-start.31) | collective-permute-done | bytes 131104 | tf_op jit(solution)/shard_map/ppermute | solution.py:579
  152.8 1.5 collective-permute-start.34
  155.2 2.0 collective-permute-start.32
  157.3 1.4 collective-permute-start.37
  158.9 1.5 collective-permute-start.35
  160.5 4.1 %collective-permute-done.37 = bf16[4,32,512]{2,1,0:T(8,128)(2,1)S(1)} collective-permute-done((bf16[4,32,512]{2,1,0:T(8,128)(2,1)S(1)}, bf16[4,32,512]{2,1,0:T(8,128)(2,1)S(1)}, u32[]{:S(2)}, u32[]{:S(2)}) %collective-permute-start.37) | collective-permute-done | bytes 131104 | tf_op jit(solution)/shard_map/ppermute | solution.py:579
  164.6 5.5 %collective-permute-done.36 = bf16[4,32,512]{2,1,0:T(8,128)(2,1)S(1)} collective-permute-done((bf16[4,32,512]{2,1,0:T(8,128)(2,1)S(1)}, bf16[4,32,512]{2,1,0:T(8,128)(2,1)S(1)}, u32[]{:S(2)}, u32[]{:S(2)}) %collective-permute-start.36) | collective-permute-done | bytes 131104 | tf_op jit(solution)/shard_map/ppermute | solution.py:579
  170.1 5.8 %shard_map.369 = (f32[1392,256]{1,0:T(8,128)S(1)}, f32[8,256]{1,0:T(8,128)S(1)}, bf16[1392,256]{1,0:T(8,128)(2,1)S(1)}, f32[1,256]{1,0:T(1,128)}, f32[1,256]{1,0:T(1,128)}) custom-call(f32[1392,256]{1,0:T(8,128)S(1)} %get-tuple-element.149.du2, f32[1392,256]{1,0:T(8,128)S(1)} %get-tuple-element.122.z2, f32[8,256]{1,0:T(8,128)S(1)} %add_add_fusion.4.sums2_0_, ...), custom_call_target="tpu_custom_call" | custom-call | flops 1048576 | tf_op jit(solution)/shard_map/pallas_call | solution.py:525
  175.9 1.6 collective-permute-start.40
  177.4 2.8 %collective-permute-start.38 = (f32[8,256]{1,0:T(8,128)S(1)}, f32[8,256]{1,0:T(8,128)S(1)}, u32[]{:S(2)}, u32[]{:S(2)}) collective-permute-start(f32[8,256]{1,0:T(8,128)S(1)} %get-tuple-element.156), channel_id=1, source_target_pairs={{0,8},{4,12},{8,0},{12,4},{16,24},{20,28},{24,16},{28,20},{1,9},{5... | collective-permute-start | bytes 24584 | tf_op jit(solution)/shard_map/ppermute | solution.py:579
  180.4 1.4 collective-permute-start.43
  181.9 3.7 %shard_map.370.group = bf16[256,384]{1,0:T(8,128)(2,1)S(1)} custom-call(bf16[1392,256]{1,0:T(8,128)(2,1)S(1)} %get-tuple-element.157.act, bf16[1392,256]{1,0:T(8,128)(2,1)S(1)} %get-tuple-element.158.dz, s32[1392,128]{1,0:T(8,128)S(1)} %copy-done, f32[256,256]{1,0:T(8,128)S(1)} %copy-done.8, bf16[2304,384]{1,0:T(8,128)(2,1)S(1)} %copy-done.6), custom_call_target="tpu_custom_call" | custom-call | flops 1048576 | tf_op jit(solution)/shard_map/pallas_call | solution.py:525
  187.0 2.8 %collective-permute-done.41.sums6_1_ = f32[8,256]{1,0:T(8,128)S(1)} collective-permute-done((f32[8,256]{1,0:T(8,128)S(1)}, f32[8,256]{1,0:T(8,128)S(1)}, u32[]{:S(2)}, u32[]{:S(2)}) %collective-permute-start.41) | collective-permute-done | bytes 8224 | tf_op jit(solution)/shard_map/ppermute | solution.py:579
  189.8 5.3 %shard_map.371 = (bf16[1392,256]{1,0:T(8,128)(2,1)S(1)}, f32[1,256]{1,0:T(1,128)}, f32[1,256]{1,0:T(1,128)}, bf16[4,304,256]{2,1,0:T(8,128)(2,1)S(1)}, bf16[4,304,256]{2,1,0:T(8,128)(2,1)S(1)}) custom-call(s32[2]{0:T(128)S(1)} %pad_add_fusion.me.ids, f32[1392,256]{1,0:T(8,128)S(1)} %get-tuple-element.155.du1, f32[1392,256]{1,0:T(8,128)S(1)} %get-tuple-element.113.z1, ...), custom_call_target="tpu_custom_call" | custom-call | flops 1048576 | tf_op jit(solution)/shard_map/pallas_call | solution.py:525
  197.2 1.7 collective-permute-start.49
  198.9 2.7 %collective-permute-start.47 = (bf16[4,32,512]{2,1,0:T(8,128)(2,1)S(1)}, bf16[4,32,512]{2,1,0:T(8,128)(2,1)S(1)}, u32[]{:S(2)}, u32[]{:S(2)}) collective-permute-start(bf16[4,32,512]{2,1,0:T(8,128)(2,1)S(1)} %pad_maximum_fusion.1.refs_0_), channel_id=1, source_target_pairs={{0,8},{4,12},{8,0},{12,4},{16,24},{20,28},{24,16},{28,20},{1,9},{5... | collective-permute-start | bytes 393224 | tf_op jit(solution)/shard_map/ppermute | solution.py:579
  201.6 8.4 %collective-permute-done.45 = bf16[4,304,256]{2,1,0:T(8,128)(2,1)S(1)} collective-permute-done((bf16[4,304,256]{2,1,0:T(8,128)(2,1)S(1)}, bf16[4,304,256]{2,1,0:T(8,128)(2,1)S(1)}, u32[]{:S(2)}, u32[]{:S(2)}) %collective-permute-start.45) | collective-permute-done | bytes 622624 | tf_op jit(solution)/shard_map/ppermute | solution.py:579
  210.2 2.2 collective-permute-done.46.d2
  213.8 2.1 collective-permute-start.51
  215.9 2.3 collective-permute-start.52
  218.2 4.0 %shard_map.372 = (f32[150,2,512]{2,1,0:T(2,128)}, f32[294,2,512]{2,1,0:T(2,128)}, f32[243,2,512]{2,1,0:T(2,128)}) custom-call(f32[1392,512]{1,0:T(8,128)S(1)} %get-tuple-element.140.du3, bf16[1392,256]{1,0:T(8,128)(2,1)S(1)} %get-tuple-element.172.d0, bf16[1392,256]{1,0:T(8,128)(2,1)S(1)} %collective-permute-done.53.d1, ...), custom_call_target="tpu_custom_call" | custom-call | flops 1048576 | tf_op jit(solution)/shard_map/pallas_call | solution.py:525
  222.3 6.0 %collective-permute-done.51.refs_2_ = bf16[304,256]{1,0:T(8,128)(2,1)S(1)} collective-permute-done((bf16[304,256]{1,0:T(8,128)(2,1)S(1)}, bf16[304,256]{1,0:T(8,128)(2,1)S(1)}, u32[]{:S(2)}, u32[]{:S(2)}) %collective-permute-start.51) | collective-permute-done | bytes 155680 | tf_op jit(solution)/shard_map/ppermute | solution.py:579
  228.4 1.6 collective-permute-start.60
  230.0 3.1 %collective-permute-start.58 = (bf16[304,256]{1,0:T(8,128)(2,1)S(1)}, bf16[304,256]{1,0:T(8,128)(2,1)S(1)}, u32[]{:S(2)}, u32[]{:S(2)}) collective-permute-start(bf16[304,256]{1,0:T(8,128)(2,1)S(1)} %shard_map.373.refs_0_), channel_id=1, source_target_pairs={{0,16},{4,20},{8,24},{12,28},{16,0},{20,4},{24,8},{28,12},{1,17},{... | collective-permute-start | bytes 466952 | tf_op jit(solution)/shard_map/ppermute | solution.py:579
  233.9 2.9 %collective-permute-done.60.refs_6_ = bf16[304,256]{1,0:T(8,128)(2,1)S(1)} collective-permute-done((bf16[304,256]{1,0:T(8,128)(2,1)S(1)}, bf16[304,256]{1,0:T(8,128)(2,1)S(1)}, u32[]{:S(2)}, u32[]{:S(2)}) %collective-permute-start.60) | collective-permute-done | bytes 155680 | tf_op jit(solution)/shard_map/ppermute | solution.py:579
  237.4 7.5 %collective-permute-done.58.refs_4_ = bf16[304,256]{1,0:T(8,128)(2,1)S(1)} collective-permute-done((bf16[304,256]{1,0:T(8,128)(2,1)S(1)}, bf16[304,256]{1,0:T(8,128)(2,1)S(1)}, u32[]{:S(2)}, u32[]{:S(2)}) %collective-permute-start.58) | collective-permute-done | bytes 155680 | tf_op jit(solution)/shard_map/ppermute | solution.py:579
  247.0 2.0 shard_map.375
  249.0 2.9 %collective-permute-done.59.refs_5_ = bf16[304,256]{1,0:T(8,128)(2,1)S(1)} collective-permute-done((bf16[304,256]{1,0:T(8,128)(2,1)S(1)}, bf16[304,256]{1,0:T(8,128)(2,1)S(1)}, u32[]{:S(2)}, u32[]{:S(2)}) %collective-permute-start.59) | collective-permute-done | bytes 155680 | tf_op jit(solution)/shard_map/ppermute | solution.py:579
  251.9 1.7 collective-permute-done.57.refs_3_
  253.5 2.6 %shard_map.374 = (f32[2048,256]{1,0:T(8,128)}, f32[9,8,32,32]{3,2,1,0:T(8,128)}) custom-call(s32[2]{0:T(128)S(1)} %pad_add_fusion.me.ids, bf16[304,256]{1,0:T(8,128)(2,1)S(1)} %shard_map.373.refs_0_, bf16[304,256]{1,0:T(8,128)(2,1)S(1)} %collective-permute-done.55.refs_1_, bf16[304,256]{1,0:T(8,128)(2,1)S(1)} %collective-permute-done.56.refs_2_, ...), custom_call_target="tpu_custom_call" | custom-call | flops 1048576 | tf_op jit(solution)/shard_map/pallas_call | solution.py:525
  (191 shorter events, 46.0 us)
Async XLA Ops:
  3.5 34.3 %collective-permute-start.1 = (bf16[1392,512]{1,0:T(8,128)(2,1)S(1)}, bf16[1392,512]{1,0:T(8,128)(2,1)}, u32[]{:S(2)}, u32[]{:S(2)}) collective-permute-start(bf16[1392,512]{1,0:T(8,128)(2,1)S(1)} %fusion.8.x0.x), channel_id=1, source_target_pairs={{0,2},{1,3},{2,0},{3,1},{4,6},{5,7},{6,4},{7,5},{8,10},{9,11},{10,... | collective-permute-start | bytes 4276232 | tf_op jit(solution)/shard_map/ppermute | solution.py:576
  6.5 34.1 %collective-permute-start = (bf16[1392,512]{1,0:T(8,128)(2,1)S(1)}, bf16[1392,512]{1,0:T(8,128)(2,1)}, u32[]{:S(2)}, u32[]{:S(2)}) collective-permute-start(bf16[1392,512]{1,0:T(8,128)(2,1)S(1)} %fusion.8.x0.x), channel_id=1, source_target_pairs={{0,1},{1,0},{2,3},{3,2},{4,5},{5,4},{6,7},{7,6},{8,9},{9,8},{10,11... | collective-permute-start | bytes 4276232 | tf_op jit(solution)/shard_map/ppermute | solution.py:576
  38.2 3.6 %collective-permute-start.2 = (bf16[1392,512]{1,0:T(8,128)(2,1)}, bf16[1392,512]{1,0:T(8,128)(2,1)}, u32[]{:S(2)}, u32[]{:S(2)}) collective-permute-start(bf16[1392,512]{1,0:T(8,128)(2,1)} %collective-permute-done.1.x2), channel_id=1, source_target_pairs={{0,1},{1,0},{2,3},{3,2},{4,5},{5,4},{6,7},{7,6},{8,9},{9,8},{10,11... | collective-permute-start | bytes 4276232 | tf_op jit(solution)/shard_map/ppermute | solution.py:576
  38.2 13.1 %collective-permute-start.7 = (bf16[256,512]{1,0:T(8,128)(2,1)}, bf16[256,512]{1,0:T(8,128)(2,1)}, u32[]{:S(2)}, u32[]{:S(2)}) collective-permute-start(bf16[256,512]{1,0:T(8,128)(2,1)} %get-tuple-element.116), channel_id=1, source_target_pairs={{0,1},{1,0},{2,3},{3,2},{4,5},{5,4},{6,7},{7,6},{8,9},{9,8},{10,11... | collective-permute-start | bytes 786440 | tf_op jit(solution)/shard_map/ppermute | solution.py:576
  38.7 18.7 %collective-permute-start.8 = (bf16[256,512]{1,0:T(8,128)(2,1)}, bf16[256,512]{1,0:T(8,128)(2,1)S(1)}, u32[]{:S(2)}, u32[]{:S(2)}) collective-permute-start(bf16[256,512]{1,0:T(8,128)(2,1)} %get-tuple-element.117), channel_id=1, source_target_pairs={{0,2},{1,3},{2,0},{3,1},{4,6},{5,7},{6,4},{7,5},{8,10},{9,11},{10,... | collective-permute-start | bytes 786440 | tf_op jit(solution)/shard_map/ppermute | solution.py:576
  40.5 18.5 %collective-permute-start.9 = (bf16[256,512]{1,0:T(8,128)(2,1)}, bf16[256,512]{1,0:T(8,128)(2,1)S(1)}, u32[]{:S(2)}, u32[]{:S(2)}) collective-permute-start(bf16[256,512]{1,0:T(8,128)(2,1)} %get-tuple-element.118), channel_id=1, source_target_pairs={{0,3},{1,2},{2,1},{3,0},{4,7},{5,6},{6,5},{7,4},{8,11},{9,10},{10,... | collective-permute-start | bytes 786440 | tf_op jit(solution)/shard_map/ppermute | solution.py:576
  47.4 5.5 %collective-permute-start.5 = (f32[8,256]{1,0:T(8,128)S(1)}, f32[8,256]{1,0:T(8,128)S(1)}, u32[]{:S(2)}, u32[]{:S(2)}) collective-permute-start(f32[8,256]{1,0:T(8,128)S(1)} %get-tuple-element.114), channel_id=1, source_target_pairs={{0,24},{4,28},{8,16},{12,20},{16,8},{20,12},{24,0},{28,4},{1,25},{... | collective-permute-start | bytes 24584 | tf_op jit(solution)/shard_map/ppermute | solution.py:579
  51.3 4.5 %collective-permute-start.4 = (f32[8,256]{1,0:T(8,128)S(1)}, f32[8,256]{1,0:T(8,128)S(1)}, u32[]{:S(2)}, u32[]{:S(2)}) collective-permute-start(f32[8,256]{1,0:T(8,128)S(1)} %get-tuple-element.114), channel_id=1, source_target_pairs={{0,16},{4,20},{8,24},{12,28},{16,0},{20,4},{24,8},{28,12},{1,17},{... | collective-permute-start | bytes 24584 | tf_op jit(solution)/shard_map/ppermute | solution.py:579
  51.4 6.0 %collective-permute-start.3 = (f32[8,256]{1,0:T(8,128)S(1)}, f32[8,256]{1,0:T(8,128)S(1)}, u32[]{:S(2)}, u32[]{:S(2)}) collective-permute-start(f32[8,256]{1,0:T(8,128)S(1)} %get-tuple-element.114), channel_id=1, source_target_pairs={{0,8},{4,12},{8,0},{12,4},{16,24},{20,28},{24,16},{28,20},{1,9},{5... | collective-permute-start | bytes 24584 | tf_op jit(solution)/shard_map/ppermute | solution.py:579
  53.0 23.7 %collective-permute-start.14 = (bf16[512,256]{1,0:T(8,128)(2,1)S(1)}, bf16[512,256]{1,0:T(8,128)(2,1)S(1)}, u32[]{:S(2)}, u32[]{:S(2)}) collective-permute-start(bf16[512,256]{1,0:T(8,128)(2,1)S(1)} %copy-done.24), channel_id=1, source_target_pairs={{0,1},{1,0},{2,3},{3,2},{4,5},{5,4},{6,7},{7,6},{8,9},{9,8},{10,11... | collective-permute-start | bytes 786440 | tf_op jit(solution)/shard_map/ppermute | solution.py:576
  55.9 20.8 %collective-permute-start.15 = (bf16[512,256]{1,0:T(8,128)(2,1)S(1)}, bf16[512,256]{1,0:T(8,128)(2,1)S(1)}, u32[]{:S(2)}, u32[]{:S(2)}) collective-permute-start(bf16[512,256]{1,0:T(8,128)(2,1)S(1)} %copy-done.23), channel_id=1, source_target_pairs={{0,2},{1,3},{2,0},{3,1},{4,6},{5,7},{6,4},{7,5},{8,10},{9,11},{10,... | collective-permute-start | bytes 786440 | tf_op jit(solution)/shard_map/ppermute | solution.py:576
  57.4 19.3 %collective-permute-start.16 = (bf16[512,256]{1,0:T(8,128)(2,1)S(1)}, bf16[512,256]{1,0:T(8,128)(2,1)S(1)}, u32[]{:S(2)}, u32[]{:S(2)}) collective-permute-start(bf16[512,256]{1,0:T(8,128)(2,1)S(1)} %copy-done.22), channel_id=1, source_target_pairs={{0,3},{1,2},{2,1},{3,0},{4,7},{5,6},{6,5},{7,4},{8,11},{9,10},{10,... | collective-permute-start | bytes 786440 | tf_op jit(solution)/shard_map/ppermute | solution.py:576
  57.4 3.7 %collective-permute-start.6 = (f32[8,256]{1,0:T(8,128)S(1)}, f32[8,256]{1,0:T(8,128)S(1)}, u32[]{:S(2)}, u32[]{:S(2)}) collective-permute-start(f32[8,256]{1,0:T(8,128)S(1)} %add_add_fusion.5.sums1_0_), channel_id=1, source_target_pairs={{0,4},{4,0},{8,12},{12,8},{16,20},{20,16},{24,28},{28,24},{1,5},{5... | collective-permute-start | bytes 24584 | tf_op jit(solution)/shard_map/ppermute | solution.py:579
  66.0 5.5 %collective-permute-start.12 = (f32[8,256]{1,0:T(8,128)S(1)}, f32[8,256]{1,0:T(8,128)S(1)}, u32[]{:S(2)}, u32[]{:S(2)}) collective-permute-start(f32[8,256]{1,0:T(8,128)S(1)} %get-tuple-element.123), channel_id=1, source_target_pairs={{0,24},{4,28},{8,16},{12,20},{16,8},{20,12},{24,0},{28,4},{1,25},{... | collective-permute-start | bytes 24584 | tf_op jit(solution)/shard_map/ppermute | solution.py:579
  67.4 4.5 %collective-permute-start.11 = (f32[8,256]{1,0:T(8,128)S(1)}, f32[8,256]{1,0:T(8,128)S(1)}, u32[]{:S(2)}, u32[]{:S(2)}) collective-permute-start(f32[8,256]{1,0:T(8,128)S(1)} %get-tuple-element.123), channel_id=1, source_target_pairs={{0,16},{4,20},{8,24},{12,28},{16,0},{20,4},{24,8},{28,12},{1,17},{... | collective-permute-start | bytes 24584 | tf_op jit(solution)/shard_map/ppermute | solution.py:579
  71.5 3.7 %collective-permute-start.10 = (f32[8,256]{1,0:T(8,128)S(1)}, f32[8,256]{1,0:T(8,128)S(1)}, u32[]{:S(2)}, u32[]{:S(2)}) collective-permute-start(f32[8,256]{1,0:T(8,128)S(1)} %get-tuple-element.123), channel_id=1, source_target_pairs={{0,8},{4,12},{8,0},{12,4},{16,24},{20,28},{24,16},{28,20},{1,9},{5... | collective-permute-start | bytes 24584 | tf_op jit(solution)/shard_map/ppermute | solution.py:579
  75.2 3.7 %collective-permute-start.13 = (f32[8,256]{1,0:T(8,128)S(1)}, f32[8,256]{1,0:T(8,128)S(1)}, u32[]{:S(2)}, u32[]{:S(2)}) collective-permute-start(f32[8,256]{1,0:T(8,128)S(1)} %add_add_fusion.4.sums2_0_), channel_id=1, source_target_pairs={{0,4},{4,0},{8,12},{12,8},{16,20},{20,16},{24,28},{28,24},{1,5},{5... | collective-permute-start | bytes 24584 | tf_op jit(solution)/shard_map/ppermute | solution.py:579
  79.6 29.5 %copy-start.1 = (bf16[1392,512]{1,0:T(8,128)(2,1)S(1)}, bf16[1392,512]{1,0:T(8,128)(2,1)}, u32[]{:S(2)}) copy-start(bf16[1392,512]{1,0:T(8,128)(2,1)} %fusion.10.dy) | copy-start | bytes 4276228
  79.6 14.4 %collective-permute-start.18 = (bf16[1392,256]{1,0:T(8,128)(2,1)S(1)}, bf16[1392,256]{1,0:T(8,128)(2,1)S(1)}, u32[]{:S(2)}, u32[]{:S(2)}) collective-permute-start(bf16[1392,256]{1,0:T(8,128)(2,1)S(1)} %shard_map.363.a0), channel_id=1, source_target_pairs={{0,2},{1,3},{2,0},{3,1},{4,6},{5,7},{6,4},{7,5},{8,10},{9,11},{10,... | collective-permute-start | bytes 2138120 | tf_op jit(solution)/shard_map/ppermute | solution.py:576
  80.2 13.8 %collective-permute-start.17 = (bf16[1392,256]{1,0:T(8,128)(2,1)S(1)}, bf16[1392,256]{1,0:T(8,128)(2,1)S(1)}, u32[]{:S(2)}, u32[]{:S(2)}) collective-permute-start(bf16[1392,256]{1,0:T(8,128)(2,1)S(1)} %shard_map.363.a0), channel_id=1, source_target_pairs={{0,1},{1,0},{2,3},{3,2},{4,5},{5,4},{6,7},{7,6},{8,9},{9,8},{10,11... | collective-permute-start | bytes 2138120 | tf_op jit(solution)/shard_map/ppermute | solution.py:576
  94.0 2.2 collective-permute-start.19
  99.1 5.8 %collective-permute-start.22 = (f32[8,512]{1,0:T(8,128)S(1)}, f32[8,512]{1,0:T(8,128)S(1)}, u32[]{:S(2)}, u32[]{:S(2)}) collective-permute-start(f32[8,512]{1,0:T(8,128)S(1)} %get-tuple-element.135), channel_id=1, source_target_pairs={{0,24},{4,28},{8,16},{12,20},{16,8},{20,12},{24,0},{28,4},{1,25},{... | collective-permute-start | bytes 49160 | tf_op jit(solution)/shard_map/ppermute | solution.py:579
  100.0 4.8 %collective-permute-start.21 = (f32[8,512]{1,0:T(8,128)S(1)}, f32[8,512]{1,0:T(8,128)S(1)}, u32[]{:S(2)}, u32[]{:S(2)}) collective-permute-start(f32[8,512]{1,0:T(8,128)S(1)} %get-tuple-element.135), channel_id=1, source_target_pairs={{0,16},{4,20},{8,24},{12,28},{16,0},{20,4},{24,8},{28,12},{1,17},{... | collective-permute-start | bytes 49160 | tf_op jit(solution)/shard_map/ppermute | solution.py:579
  100.8 4.5 %collective-permute-start.20 = (f32[8,512]{1,0:T(8,128)S(1)}, f32[8,512]{1,0:T(8,128)S(1)}, u32[]{:S(2)}, u32[]{:S(2)}) collective-permute-start(f32[8,512]{1,0:T(8,128)S(1)} %get-tuple-element.135), channel_id=1, source_target_pairs={{0,8},{4,12},{8,0},{12,4},{16,24},{20,28},{24,16},{28,20},{1,9},{5... | collective-permute-start | bytes 49160 | tf_op jit(solution)/shard_map/ppermute | solution.py:579
  105.3 3.8 %collective-permute-start.23 = (f32[8,512]{1,0:T(8,128)S(1)}, f32[8,512]{1,0:T(8,128)S(1)}, u32[]{:S(2)}, u32[]{:S(2)}) collective-permute-start(f32[8,512]{1,0:T(8,128)S(1)} %add_add_fusion.1.sums3_0_), channel_id=1, source_target_pairs={{0,4},{4,0},{8,12},{12,8},{16,20},{20,16},{24,28},{28,24},{1,5},{5... | collective-permute-start | bytes 49160 | tf_op jit(solution)/shard_map/ppermute | solution.py:579
  113.8 5.5 %collective-permute-start.26 = (f32[8,512]{1,0:T(8,128)S(1)}, f32[8,512]{1,0:T(8,128)S(1)}, u32[]{:S(2)}, u32[]{:S(2)}) collective-permute-start(f32[8,512]{1,0:T(8,128)S(1)} %get-tuple-element.141), channel_id=1, source_target_pairs={{0,24},{4,28},{8,16},{12,20},{16,8},{20,12},{24,0},{28,4},{1,25},{... | collective-permute-start | bytes 49160 | tf_op jit(solution)/shard_map/ppermute | solution.py:579
  116.2 4.6 %collective-permute-start.25 = (f32[8,512]{1,0:T(8,128)S(1)}, f32[8,512]{1,0:T(8,128)S(1)}, u32[]{:S(2)}, u32[]{:S(2)}) collective-permute-start(f32[8,512]{1,0:T(8,128)S(1)} %get-tuple-element.141), channel_id=1, source_target_pairs={{0,16},{4,20},{8,24},{12,28},{16,0},{20,4},{24,8},{28,12},{1,17},{... | collective-permute-start | bytes 49160 | tf_op jit(solution)/shard_map/ppermute | solution.py:579
  117.3 3.7 %collective-permute-start.24 = (f32[8,512]{1,0:T(8,128)S(1)}, f32[8,512]{1,0:T(8,128)S(1)}, u32[]{:S(2)}, u32[]{:S(2)}) collective-permute-start(f32[8,512]{1,0:T(8,128)S(1)} %get-tuple-element.141), channel_id=1, source_target_pairs={{0,8},{4,12},{8,0},{12,4},{16,24},{20,28},{24,16},{28,20},{1,9},{5... | collective-permute-start | bytes 49160 | tf_op jit(solution)/shard_map/ppermute | solution.py:579
  121.0 3.8 %collective-permute-start.27 = (f32[8,512]{1,0:T(8,128)S(1)}, f32[8,512]{1,0:T(8,128)S(1)}, u32[]{:S(2)}, u32[]{:S(2)}) collective-permute-start(f32[8,512]{1,0:T(8,128)S(1)} %add_add_fusion.sums4_0_), channel_id=1, source_target_pairs={{0,4},{4,0},{8,12},{12,8},{16,20},{20,16},{24,28},{28,24},{1,5},{5... | collective-permute-start | bytes 49160 | tf_op jit(solution)/shard_map/ppermute | solution.py:579
  129.2 4.0 %collective-permute-start.28 = (bf16[2,1392,256]{2,1,0:T(8,128)(2,1)S(1)}, bf16[2,1392,256]{2,1,0:T(8,128)(2,1)S(1)}, u32[]{:S(2)}, u32[]{:S(2)}) collective-permute-start(bf16[2,1392,256]{2,1,0:T(8,128)(2,1)S(1)} %get-tuple-element.143), channel_id=1, source_target_pairs={{0,1},{1,0},{2,3},{3,2},{4,5},{5,4},{6,7},{7,6},{8,9},{9,8},{10,11... | collective-permute-start | bytes 4276232 | tf_op jit(solution)/shard_map/ppermute | solution.py:576
  131.6 14.4 %collective-permute-start.30 = (bf16[4,4,32,512]{3,2,1,0:T(8,128)(2,1)S(1)}, bf16[4,4,32,512]{3,2,1,0:T(8,128)(2,1)S(1)}, u32[]{:S(2)}, u32[]{:S(2)}) collective-permute-start(bf16[4,4,32,512]{3,2,1,0:T(8,128)(2,1)S(1)} %get-tuple-element.147), channel_id=1, source_target_pairs={{0,4},{4,0},{8,12},{12,8},{16,20},{20,16},{24,28},{28,24},{1,5},{5... | collective-permute-start | bytes 1572872 | tf_op jit(solution)/shard_map/ppermute | solution.py:579
  133.4 18.2 %collective-permute-start.29 = (bf16[1392,256]{1,0:T(8,128)(2,1)S(1)}, bf16[1392,256]{1,0:T(8,128)(2,1)S(1)}, u32[]{:S(2)}, u32[]{:S(2)}) collective-permute-start(bf16[1392,256]{1,0:T(8,128)(2,1)S(1)} %fusion.11), channel_id=1, source_target_pairs={{0,2},{1,3},{2,0},{3,1},{4,6},{5,7},{6,4},{7,5},{8,10},{9,11},{10,... | collective-permute-start | bytes 2138120 | tf_op jit(solution)/shard_map/ppermute | solution.py:576
  146.1 5.2 %collective-permute-start.31 = (bf16[4,32,512]{2,1,0:T(8,128)(2,1)S(1)}, bf16[4,32,512]{2,1,0:T(8,128)(2,1)S(1)}, u32[]{:S(2)}, u32[]{:S(2)}) collective-permute-start(bf16[4,32,512]{2,1,0:T(8,128)(2,1)S(1)} %get-tuple-element.212), channel_id=1, source_target_pairs={{0,8},{4,12},{8,0},{12,4},{16,24},{20,28},{24,16},{28,20},{1,9},{5... | collective-permute-start | bytes 393224 | tf_op jit(solution)/shard_map/ppermute | solution.py:579
  152.8 5.9 %collective-permute-start.34 = (f32[8,256]{1,0:T(8,128)S(1)}, f32[8,256]{1,0:T(8,128)S(1)}, u32[]{:S(2)}, u32[]{:S(2)}) collective-permute-start(f32[8,256]{1,0:T(8,128)S(1)} %get-tuple-element.150), channel_id=1, source_target_pairs={{0,24},{4,28},{8,16},{12,20},{16,8},{20,12},{24,0},{28,4},{1,25},{... | collective-permute-start | bytes 24584 | tf_op jit(solution)/shard_map/ppermute | solution.py:579
  154.3 4.6 %collective-permute-start.33 = (f32[8,256]{1,0:T(8,128)S(1)}, f32[8,256]{1,0:T(8,128)S(1)}, u32[]{:S(2)}, u32[]{:S(2)}) collective-permute-start(f32[8,256]{1,0:T(8,128)S(1)} %get-tuple-element.150), channel_id=1, source_target_pairs={{0,16},{4,20},{8,24},{12,28},{16,0},{20,4},{24,8},{28,12},{1,17},{... | collective-permute-start | bytes 24584 | tf_op jit(solution)/shard_map/ppermute | solution.py:579
  155.2 3.7 %collective-permute-start.32 = (f32[8,256]{1,0:T(8,128)S(1)}, f32[8,256]{1,0:T(8,128)S(1)}, u32[]{:S(2)}, u32[]{:S(2)}) collective-permute-start(f32[8,256]{1,0:T(8,128)S(1)} %get-tuple-element.150), channel_id=1, source_target_pairs={{0,8},{4,12},{8,0},{12,4},{16,24},{20,28},{24,16},{28,20},{1,9},{5... | collective-permute-start | bytes 24584 | tf_op jit(solution)/shard_map/ppermute | solution.py:579
  157.3 7.3 %collective-permute-start.37 = (bf16[4,32,512]{2,1,0:T(8,128)(2,1)S(1)}, bf16[4,32,512]{2,1,0:T(8,128)(2,1)S(1)}, u32[]{:S(2)}, u32[]{:S(2)}) collective-permute-start(bf16[4,32,512]{2,1,0:T(8,128)(2,1)S(1)} %get-tuple-element.209), channel_id=1, source_target_pairs={{0,24},{4,28},{8,16},{12,20},{16,8},{20,12},{24,0},{28,4},{1,25},{... | collective-permute-start | bytes 393224 | tf_op jit(solution)/shard_map/ppermute | solution.py:579
  158.7 11.4 %collective-permute-start.36 = (bf16[4,32,512]{2,1,0:T(8,128)(2,1)S(1)}, bf16[4,32,512]{2,1,0:T(8,128)(2,1)S(1)}, u32[]{:S(2)}, u32[]{:S(2)}) collective-permute-start(bf16[4,32,512]{2,1,0:T(8,128)(2,1)S(1)} %get-tuple-element.210), channel_id=1, source_target_pairs={{0,16},{4,20},{8,24},{12,28},{16,0},{20,4},{24,8},{28,12},{1,17},{... | collective-permute-start | bytes 393224 | tf_op jit(solution)/shard_map/ppermute | solution.py:579
  158.9 11.1 %collective-permute-start.35 = (f32[8,256]{1,0:T(8,128)S(1)}, f32[8,256]{1,0:T(8,128)S(1)}, u32[]{:S(2)}, u32[]{:S(2)}) collective-permute-start(f32[8,256]{1,0:T(8,128)S(1)} %add_add_fusion.3.sums5_0_), channel_id=1, source_target_pairs={{0,4},{4,0},{8,12},{12,8},{16,20},{20,16},{24,28},{28,24},{1,5},{5... | collective-permute-start | bytes 24584 | tf_op jit(solution)/shard_map/ppermute | solution.py:579
  175.9 9.8 %collective-permute-start.40 = (f32[8,256]{1,0:T(8,128)S(1)}, f32[8,256]{1,0:T(8,128)S(1)}, u32[]{:S(2)}, u32[]{:S(2)}) collective-permute-start(f32[8,256]{1,0:T(8,128)S(1)} %get-tuple-element.156), channel_id=1, source_target_pairs={{0,24},{4,28},{8,16},{12,20},{16,8},{20,12},{24,0},{28,4},{1,25},{... | collective-permute-start | bytes 24584 | tf_op jit(solution)/shard_map/ppermute | solution.py:579
  177.4 8.7 %collective-permute-start.39 = (f32[8,256]{1,0:T(8,128)S(1)}, f32[8,256]{1,0:T(8,128)S(1)}, u32[]{:S(2)}, u32[]{:S(2)}) collective-permute-start(f32[8,256]{1,0:T(8,128)S(1)} %get-tuple-element.156), channel_id=1, source_target_pairs={{0,16},{4,20},{8,24},{12,28},{16,0},{20,4},{24,8},{28,12},{1,17},{... | collective-permute-start | bytes 24584 | tf_op jit(solution)/shard_map/ppermute | solution.py:579
  177.4 8.7 %collective-permute-start.38 = (f32[8,256]{1,0:T(8,128)S(1)}, f32[8,256]{1,0:T(8,128)S(1)}, u32[]{:S(2)}, u32[]{:S(2)}) collective-permute-start(f32[8,256]{1,0:T(8,128)S(1)} %get-tuple-element.156), channel_id=1, source_target_pairs={{0,8},{4,12},{8,0},{12,4},{16,24},{20,28},{24,16},{28,20},{1,9},{5... | collective-permute-start | bytes 24584 | tf_op jit(solution)/shard_map/ppermute | solution.py:579
  180.3 6.6 %collective-permute-start.44 = (bf16[32,512]{1,0:T(8,128)(2,1)S(1)}, bf16[32,512]{1,0:T(8,128)(2,1)S(1)}, u32[]{:S(2)}, u32[]{:S(2)}) collective-permute-start(bf16[32,512]{1,0:T(8,128)(2,1)S(1)} %get-tuple-element.226), channel_id=1, source_target_pairs={{0,3},{1,2},{2,1},{3,0},{4,7},{5,6},{6,5},{7,4},{8,11},{9,10},{10,... | collective-permute-start | bytes 98312 | tf_op jit(solution)/shard_map/ppermute | solution.py:576
  180.4 6.5 %collective-permute-start.43 = (bf16[32,512]{1,0:T(8,128)(2,1)S(1)}, bf16[32,512]{1,0:T(8,128)(2,1)S(1)}, u32[]{:S(2)}, u32[]{:S(2)}) collective-permute-start(bf16[32,512]{1,0:T(8,128)(2,1)S(1)} %get-tuple-element.227), channel_id=1, source_target_pairs={{0,2},{1,3},{2,0},{3,1},{4,6},{5,7},{6,4},{7,5},{8,10},{9,11},{10,... | collective-permute-start | bytes 98312 | tf_op jit(solution)/shard_map/ppermute | solution.py:576
  185.6 1.3 collective-permute-start.42
  186.1 3.7 %collective-permute-start.41 = (f32[8,256]{1,0:T(8,128)S(1)}, f32[8,256]{1,0:T(8,128)S(1)}, u32[]{:S(2)}, u32[]{:S(2)}) collective-permute-start(f32[8,256]{1,0:T(8,128)S(1)} %add_add_fusion.2.sums6_0_), channel_id=1, source_target_pairs={{0,4},{4,0},{8,12},{12,8},{16,20},{20,16},{24,28},{28,24},{1,5},{5... | collective-permute-start | bytes 24584 | tf_op jit(solution)/shard_map/ppermute | solution.py:579
  195.1 14.9 %collective-permute-start.45 = (bf16[4,304,256]{2,1,0:T(8,128)(2,1)S(1)}, bf16[4,304,256]{2,1,0:T(8,128)(2,1)S(1)}, u32[]{:S(2)}, u32[]{:S(2)}) collective-permute-start(bf16[4,304,256]{2,1,0:T(8,128)(2,1)S(1)} %get-tuple-element.171), channel_id=1, source_target_pairs={{0,4},{4,0},{8,12},{12,8},{16,20},{20,16},{24,28},{28,24},{1,5},{5... | collective-permute-start | bytes 1867784 | tf_op jit(solution)/shard_map/ppermute | solution.py:579
  195.8 16.5 %collective-permute-start.46 = (bf16[1392,256]{1,0:T(8,128)(2,1)S(1)}, bf16[1392,256]{1,0:T(8,128)(2,1)S(1)}, u32[]{:S(2)}, u32[]{:S(2)}) collective-permute-start(bf16[1392,256]{1,0:T(8,128)(2,1)S(1)} %get-tuple-element.172.d0), channel_id=1, source_target_pairs={{0,2},{1,3},{2,0},{3,1},{4,6},{5,7},{6,4},{7,5},{8,10},{9,11},{10,... | collective-permute-start | bytes 2138120 | tf_op jit(solution)/shard_map/ppermute | solution.py:576
  197.2 12.9 %collective-permute-start.49 = (bf16[4,32,512]{2,1,0:T(8,128)(2,1)S(1)}, bf16[4,32,512]{2,1,0:T(8,128)(2,1)S(1)}, u32[]{:S(2)}, u32[]{:S(2)}) collective-permute-start(bf16[4,32,512]{2,1,0:T(8,128)(2,1)S(1)} %pad_maximum_fusion.1.refs_0_), channel_id=1, source_target_pairs={{0,24},{4,28},{8,16},{12,20},{16,8},{20,12},{24,0},{28,4},{1,25},{... | collective-permute-start | bytes 393224 | tf_op jit(solution)/shard_map/ppermute | solution.py:579
  198.9 11.3 %collective-permute-start.48 = (bf16[4,32,512]{2,1,0:T(8,128)(2,1)S(1)}, bf16[4,32,512]{2,1,0:T(8,128)(2,1)S(1)}, u32[]{:S(2)}, u32[]{:S(2)}) collective-permute-start(bf16[4,32,512]{2,1,0:T(8,128)(2,1)S(1)} %pad_maximum_fusion.1.refs_0_), channel_id=1, source_target_pairs={{0,16},{4,20},{8,24},{12,28},{16,0},{20,4},{24,8},{28,12},{1,17},{... | collective-permute-start | bytes 393224 | tf_op jit(solution)/shard_map/ppermute | solution.py:579
  198.9 11.3 %collective-permute-start.47 = (bf16[4,32,512]{2,1,0:T(8,128)(2,1)S(1)}, bf16[4,32,512]{2,1,0:T(8,128)(2,1)S(1)}, u32[]{:S(2)}, u32[]{:S(2)}) collective-permute-start(bf16[4,32,512]{2,1,0:T(8,128)(2,1)S(1)} %pad_maximum_fusion.1.refs_0_), channel_id=1, source_target_pairs={{0,8},{4,12},{8,0},{12,4},{16,24},{20,28},{24,16},{28,20},{1,9},{5... | collective-permute-start | bytes 393224 | tf_op jit(solution)/shard_map/ppermute | solution.py:579
  210.0 6.0 %collective-permute-start.53 = (bf16[1392,256]{1,0:T(8,128)(2,1)S(1)}, bf16[1392,256]{1,0:T(8,128)(2,1)S(1)}, u32[]{:S(2)}, u32[]{:S(2)}) collective-permute-start(bf16[1392,256]{1,0:T(8,128)(2,1)S(1)} %get-tuple-element.172.d0), channel_id=1, source_target_pairs={{0,1},{1,0},{2,3},{3,2},{4,5},{5,4},{6,7},{7,6},{8,9},{9,8},{10,11... | collective-permute-start | bytes 2138120 | tf_op jit(solution)/shard_map/ppermute | solution.py:576
  212.4 5.8 %collective-permute-start.54 = (bf16[1392,256]{1,0:T(8,128)(2,1)S(1)}, bf16[1392,256]{1,0:T(8,128)(2,1)S(1)}, u32[]{:S(2)}, u32[]{:S(2)}) collective-permute-start(bf16[1392,256]{1,0:T(8,128)(2,1)S(1)} %collective-permute-done.46.d2), channel_id=1, source_target_pairs={{0,1},{1,0},{2,3},{3,2},{4,5},{5,4},{6,7},{7,6},{8,9},{9,8},{10,11... | collective-permute-start | bytes 2138120 | tf_op jit(solution)/shard_map/ppermute | solution.py:576
  212.4 34.5 %collective-permute-start.62 = (bf16[4,4,32,512]{3,2,1,0:T(8,128)(2,1)S(1)}, bf16[4,4,32,512]{3,2,1,0:T(8,128)(2,1)S(1)}, u32[]{:S(2)}, u32[]{:S(2)}) collective-permute-start(bf16[4,4,32,512]{3,2,1,0:T(8,128)(2,1)S(1)} %pad_maximum_fusion), channel_id=1, source_target_pairs={{0,4},{4,0},{8,12},{12,8},{16,20},{20,16},{24,28},{28,24},{1,5},{5... | collective-permute-start | bytes 1572872 | tf_op jit(solution)/shard_map/ppermute | solution.py:579
  213.8 8.5 %collective-permute-start.50 = (bf16[304,256]{1,0:T(8,128)(2,1)S(1)}, bf16[304,256]{1,0:T(8,128)(2,1)S(1)}, u32[]{:S(2)}, u32[]{:S(2)}) collective-permute-start(bf16[304,256]{1,0:T(8,128)(2,1)S(1)} %get-tuple-element.175), channel_id=1, source_target_pairs={{0,8},{4,12},{8,0},{12,4},{16,24},{20,28},{24,16},{28,20},{1,9},{5... | collective-permute-start | bytes 466952 | tf_op jit(solution)/shard_map/ppermute | solution.py:579
  213.8 14.5 %collective-permute-start.51 = (bf16[304,256]{1,0:T(8,128)(2,1)S(1)}, bf16[304,256]{1,0:T(8,128)(2,1)S(1)}, u32[]{:S(2)}, u32[]{:S(2)}) collective-permute-start(bf16[304,256]{1,0:T(8,128)(2,1)S(1)} %get-tuple-element.176), channel_id=1, source_target_pairs={{0,16},{4,20},{8,24},{12,28},{16,0},{20,4},{24,8},{28,12},{1,17},{... | collective-permute-start | bytes 466952 | tf_op jit(solution)/shard_map/ppermute | solution.py:579
  215.9 12.3 %collective-permute-start.52 = (bf16[304,256]{1,0:T(8,128)(2,1)S(1)}, bf16[304,256]{1,0:T(8,128)(2,1)S(1)}, u32[]{:S(2)}, u32[]{:S(2)}) collective-permute-start(bf16[304,256]{1,0:T(8,128)(2,1)S(1)} %get-tuple-element.177), channel_id=1, source_target_pairs={{0,24},{4,28},{8,16},{12,20},{16,8},{20,12},{24,0},{28,4},{1,25},{... | collective-permute-start | bytes 466952 | tf_op jit(solution)/shard_map/ppermute | solution.py:579
  228.4 8.4 %collective-permute-start.60 = (bf16[304,256]{1,0:T(8,128)(2,1)S(1)}, bf16[304,256]{1,0:T(8,128)(2,1)S(1)}, u32[]{:S(2)}, u32[]{:S(2)}) collective-permute-start(bf16[304,256]{1,0:T(8,128)(2,1)S(1)} %shard_map.373.refs_0_), channel_id=1, source_target_pairs={{0,24},{4,28},{8,16},{12,20},{16,8},{20,12},{24,0},{28,4},{1,25},{... | collective-permute-start | bytes 466952 | tf_op jit(solution)/shard_map/ppermute | solution.py:579
  230.0 14.9 %collective-permute-start.58 = (bf16[304,256]{1,0:T(8,128)(2,1)S(1)}, bf16[304,256]{1,0:T(8,128)(2,1)S(1)}, u32[]{:S(2)}, u32[]{:S(2)}) collective-permute-start(bf16[304,256]{1,0:T(8,128)(2,1)S(1)} %shard_map.373.refs_0_), channel_id=1, source_target_pairs={{0,16},{4,20},{8,24},{12,28},{16,0},{20,4},{24,8},{28,12},{1,17},{... | collective-permute-start | bytes 466952 | tf_op jit(solution)/shard_map/ppermute | solution.py:579
  233.1 12.5 %collective-permute-start.56 = (bf16[304,256]{1,0:T(8,128)(2,1)S(1)}, bf16[304,256]{1,0:T(8,128)(2,1)S(1)}, u32[]{:S(2)}, u32[]{:S(2)}) collective-permute-start(bf16[304,256]{1,0:T(8,128)(2,1)S(1)} %shard_map.373.refs_0_), channel_id=1, source_target_pairs={{0,8},{4,12},{8,0},{12,4},{16,24},{20,28},{24,16},{28,20},{1,9},{5... | collective-permute-start | bytes 466952 | tf_op jit(solution)/shard_map/ppermute | solution.py:579
  233.1 15.9 %collective-permute-start.55 = (bf16[304,256]{1,0:T(8,128)(2,1)S(1)}, bf16[304,256]{1,0:T(8,128)(2,1)S(1)}, u32[]{:S(2)}, u32[]{:S(2)}) collective-permute-start(bf16[304,256]{1,0:T(8,128)(2,1)S(1)} %shard_map.373.refs_0_), channel_id=1, source_target_pairs={{0,4},{4,0},{8,12},{12,8},{16,20},{20,16},{24,28},{28,24},{1,5},{5... | collective-permute-start | bytes 466952 | tf_op jit(solution)/shard_map/ppermute | solution.py:579
  236.8 12.2 %collective-permute-start.61 = (bf16[304,256]{1,0:T(8,128)(2,1)S(1)}, bf16[304,256]{1,0:T(8,128)(2,1)S(1)}, u32[]{:S(2)}, u32[]{:S(2)}) collective-permute-start(bf16[304,256]{1,0:T(8,128)(2,1)S(1)} %collective-permute-done.60.refs_6_), channel_id=1, source_target_pairs={{0,4},{4,0},{8,12},{12,8},{16,20},{20,16},{24,28},{28,24},{1,5},{5... | collective-permute-start | bytes 466952 | tf_op jit(solution)/shard_map/ppermute | solution.py:579
  244.9 6.9 %collective-permute-start.59 = (bf16[304,256]{1,0:T(8,128)(2,1)S(1)}, bf16[304,256]{1,0:T(8,128)(2,1)S(1)}, u32[]{:S(2)}, u32[]{:S(2)}) collective-permute-start(bf16[304,256]{1,0:T(8,128)(2,1)S(1)} %collective-permute-done.58.refs_4_), channel_id=1, source_target_pairs={{0,4},{4,0},{8,12},{12,8},{16,20},{20,16},{24,28},{28,24},{1,5},{5... | collective-permute-start | bytes 466952 | tf_op jit(solution)/shard_map/ppermute | solution.py:579
  245.7 7.9 %collective-permute-start.57 = (bf16[304,256]{1,0:T(8,128)(2,1)S(1)}, bf16[304,256]{1,0:T(8,128)(2,1)S(1)}, u32[]{:S(2)}, u32[]{:S(2)}) collective-permute-start(bf16[304,256]{1,0:T(8,128)(2,1)S(1)} %collective-permute-done.56.refs_2_), channel_id=1, source_target_pairs={{0,4},{4,0},{8,12},{12,8},{16,20},{20,16},{24,28},{28,24},{1,5},{5... | collective-permute-start | bytes 466952 | tf_op jit(solution)/shard_map/ppermute | solution.py:579
  (32 other events, 339.9 us)

commit v3 on v2

--- a/solution.py
+++ b/solution.py
@@ -13,6 +13,7 @@
 SUBLANES = 8
 PACKED = 16
 HALO = 32
+IMAGE_BIT = 16
 STEP = 48
 F32 = jnp.float32
 BF16 = jnp.bfloat16
@@ -30,38 +31,30 @@
         self.rows = sum(self.padded)
         self.parts = next(k for k in (3, 2, 1) if self.rows % (k * PACKED) == 0)
         self.part = self.rows // self.parts
+        self.cut = self.starts[-1]
 
     def segments(self):
         return list(zip(self.edges, self.starts, self.padded))
 
-    def tap_bits(self):
-        bits = np.zeros((self.rows, LANES), np.int32)
-        for e, n, start in zip(self.edges, self.slots, self.starts):
+    def row_facts(self):
+        facts = np.zeros((self.rows, LANES), np.int32)
+        for e, n, start, size in zip(self.edges, self.slots, self.starts, self.padded):
             h, w = np.meshgrid(np.arange(e), np.arange(e), indexing="ij")
             found = np.zeros((e, e), np.int32)
             for tap in range(9):
                 y, x = h + tap // 3 - 1, w + tap % 3 - 1
                 found |= ((y >= 0) & (y < e) & (x >= 0) & (x < e)).astype(np.int32) << tap
-            per_row = np.repeat(np.tile(found.ravel(), n), self.micro)
-            bits[start : start + per_row.size] = per_row[:, None]
-        return bits
-
-    def live_mask(self, counts):
-        pieces = []
-        for k, (e, n) in enumerate(zip(self.edges, self.slots)):
-            image = np.repeat(np.arange(n), e * e * self.micro)
-            image = np.concatenate([image, np.full(self.padded[k] - image.size, n)])
-            which = np.arange(image.size) % self.micro
-            limit = jnp.where(jnp.asarray(which == 0), counts[0, 0, k], counts[1, 0, k])
-            pieces.append((jnp.asarray(image, jnp.int32) < limit).astype(F32))
-        return jnp.broadcast_to(jnp.concatenate(pieces)[:, None], (self.rows, LANES))
-
-    def flatten(self, pieces):
-        flat = []
-        for piece, padded, live in zip(pieces, self.padded, self.live):
-            rows = jnp.transpose(piece, (1, 2, 3, 0, 4)).reshape(live, piece.shape[-1])
-            flat.append(jnp.pad(rows, ((0, padded - live), (0, 0))))
-        return jnp.concatenate(flat, 0)
+            found = found.ravel()[None, :] | (np.arange(n, dtype=np.int32) << IMAGE_BIT)[:, None]
+            per_row = np.full(size, n << IMAGE_BIT, np.int32)
+            per_row[: self.micro * found.size] = np.repeat(found.ravel(), self.micro)
+            facts[start : start + size] = per_row[:, None]
+        return facts
+
+    def by_pixel(self, pieces):
+        return [
+            jnp.transpose(p, (1, 2, 3, 0, 4)).reshape(n // self.micro, self.micro, p.shape[-1])
+            for p, n in zip(pieces, self.live)
+        ]
 
     def pixel_shapes(self, width, dtype):
         return tuple(
@@ -180,20 +173,104 @@
     return (jnp.zeros((SUBLANES, width), F32), jnp.zeros((SUBLANES, width), F32))
 
 
-def reduce_kernel(lay, me, x0, x1, x2, x3, weight, mask, count, z_out, sums_out):
-    t = me[0]
+def prepare_kernel(lay, counts, facts, weight, repeat, block, mask_out, count_out, forward_out, backward_out):
+    def by_micro(shape, pair):
+        odd = jnp.bitwise_and(lax.broadcasted_iota(jnp.int32, shape, 0), 1)
+        return jnp.where(odd == 0, pair[0], pair[1])
+
+    pixels = [jnp.int32(0), jnp.int32(0)]
+    for k, (edge, start, size) in enumerate(lay.segments()):
+        limits = [counts[m, 0, k] for m in range(2)]
+        pixels = [p + c * (edge * edge) for p, c in zip(pixels, limits)]
+        image = lax.shift_right_logical(facts[start : start + size, :], IMAGE_BIT)
+        live = image < by_micro(image.shape, limits)
+        mask_out[start : start + size, :] = jnp.where(live, 1.0, 0.0)
+    count_out[...] = by_micro(count_out.shape, pixels).astype(F32)
+    size = weight.shape[1]
+    for tap in range(weight.shape[0]):
+        full = mm(weight[tap], repeat[...]) * block[...]
+        forward_out[tap * size : (tap + 1) * size, :] = full.astype(BF16)
+        backward_out[tap * size : (tap + 1) * size, :] = full.T.astype(BF16)
+
+
+def to_rows(lay, which, pixels, out):
+    base = lay.starts[which[0]]
+    width = out.shape[1]
+    for k, ref in zip(which, pixels):
+        start, padded, live = lay.starts[k] - base, lay.padded[k], lay.live[k]
+        many = live // STEP
+        step_pixels = STEP // lay.micro
+
+        def step(i, _, ref=ref, start=start):
+            found = ref[pl.ds(i * step_pixels, step_pixels)].reshape(STEP, width)
+            out[at(start + i * STEP, STEP), :] = found
+            return 0
+
+        lax.fori_loop(0, many, step, 0)
+        rest, left = padded - many * STEP, live - many * STEP
+        if rest:
+            first = many * step_pixels
+            tail = ref[first : first + left // lay.micro].astype(F32).reshape(left, width)
+            tail = jnp.concatenate([tail, jnp.zeros((rest - left, width), F32)], 0)
+            out[start + many * STEP : start + padded, :] = tail.astype(BF16)
+
+
+def rows_kernel(lay, *refs):
+    to_rows(lay, range(len(lay.edges)), refs[:-1], refs[-1])
+
+
+def reduce_begin_kernel(lay, ids, own, near, weight, z_out):
+    t = ids[0]
+
+    def step(part, _):
+        rows = at(part * lay.part, lay.part)
+        acc = mm(own[rows, :], weight[t])
+        z_out[rows, :] = acc + mm(near[rows, :], weight[jnp.bitwise_xor(t, 1)])
+        return 0
+
+    lax.fori_loop(0, lay.parts, step, 0)
+
+
+def reduce_last_kernel(lay, ids, far, cross, weight, z, mask, far_out, cross_out, z_out, part_out):
+    last = (len(lay.edges) - 1,)
+    to_rows(lay, last, far, far_out)
+    to_rows(lay, last, cross, cross_out)
+    acc = z[lay.cut :, :] + mm(far_out[...], weight[jnp.bitwise_xor(ids[0], 2)])
+    acc = acc + mm(cross_out[...], weight[jnp.bitwise_xor(ids[0], 3)])
+    z_out[...] = acc
+    found = tiles(acc)
+    live = widen(tiles(mask[lay.cut :, :]), acc.shape[1])
+    part_out[0], part_out[1] = masked_sums(found, found, live, zeros_pair(acc.shape[1]))
+
+
+def reduce_more_kernel(lay, ids, far, weight, z, far_out, z_out):
+    to_rows(lay, range(len(lay.edges) - 1), far, far_out)
+    half = lay.cut // 2
+
+    def step(part, _):
+        rows = at(part * half, half)
+        z_out[rows, :] = z[rows, :] + mm(far_out[rows, :], weight[jnp.bitwise_xor(ids[0], 2)])
+        return 0
+
+    lax.fori_loop(0, 2, step, 0)
+
+
+def reduce_end_kernel(
+    lay, ids, cross, weight, z, z_last, part, mask, count, cross_out, z_out, sums_out
+):
+    to_rows(lay, range(len(lay.edges) - 1), cross, cross_out)
     width = z_out.shape[1]
-
-    def step(part, carry):
-        rows = at(part * lay.part, lay.part)
-        acc = mm(x0[rows, :], weight[t])
-        for k, x in ((1, x1), (2, x2), (3, x3)):
-            acc = acc + mm(x[rows, :], weight[jnp.bitwise_xor(t, k)])
+    half = lay.cut // 2
+    z_out[lay.cut :, :] = z_last[...]
+
+    def step(k, carry):
+        rows = at(k * half, half)
+        acc = z[rows, :] + mm(cross_out[rows, :], weight[jnp.bitwise_xor(ids[0], 3)])
         z_out[rows, :] = acc
-        z = tiles(acc)
-        return masked_sums(z, z, widen(tiles(mask[rows, :]), width), carry)
-
-    sums, squares = lax.fori_loop(0, lay.parts, step, zeros_pair(width))
+        found = tiles(acc)
+        return masked_sums(found, found, widen(tiles(mask[rows, :]), width), carry)
+
+    sums, squares = lax.fori_loop(0, 2, step, (part[0], part[1]))
     sums_out[...] = pack(sums, squares, widen(count[...], width))
 
 
@@ -225,7 +302,8 @@
 
 
 def conv_kernel(
-    lay, z1, sums1, gain, bias, mask, count, bits, weight, z2_out, sums_out, act_out, slabs, image
+    lay, z1, sums1, gain, bias, mask, count, bits, weight,
+    z2_out, sums_out, act_out, near_out, offset_out, slabs, image,
 ):
     width = z1.shape[1]
     mean, inverse, _ = moments(sums1)
@@ -250,31 +328,55 @@
         return masked_sums(z, z, widen(tiles(mask[rows, :]), width), carry)
 
     sums, squares = lax.fori_loop(0, lay.parts, step, zeros_pair(width))
-    sums_out[...] = pack(sums, squares, widen(count[...], width))
-
-
-def second_kernel(lay, z2, sums2, gain, bias, mask, act_out):
-    width = z2.shape[1]
-    mean, inverse, _ = moments(sums2)
-
-    def activate(i, _):
+    local = widen(count[...], width)
+    sums_out[...] = pack(sums, squares, local)
+    offset = fold(sums) / jnp.maximum(local, 1.0)
+    offset_out[...] = offset
+
+    def centre(i, _):
         rows = at(i * STEP, STEP)
-        u = gain[...] * ((tiles(z2[rows, :]) - mean) * inverse) + bias[...]
-        a = widen(tiles(mask[rows, :]), width) * (u * jax.nn.sigmoid(u))
-        act_out[rows, :] = flat(a).astype(BF16)
+        near_out[rows, :] = flat(tiles(z2_out[rows, :]) - offset).astype(BF16)
         return 0
 
-    lax.fori_loop(0, lay.rows // STEP, activate, 0)
-
-
-def expand_kernel(lay, a0, a1, a2, a3, w0, w1, w2, w3, mask, count, z_out, sums_out):
+    lax.fori_loop(0, lay.rows // STEP, centre, 0)
+
+
+def stat_kernel(sums, offset, gain, bias, out):
+    out[:SUBLANES, :] = tree_sum([tile[...] for tile in sums])
+    out[SUBLANES : 2 * SUBLANES, :] = offset[...]
+    row = lax.broadcasted_iota(jnp.int32, offset.shape, 0)
+    out[2 * SUBLANES :, :] = jnp.where(row == 0, gain[...], bias[...])
+
+
+def expand_kernel(lay, zs, stats, ws, mask, count, z_out, sums_out, *acts):
     width = z_out.shape[1]
+    inner = zs[0].shape[1]
+    for z, stat, act in zip(zs, stats, acts):
+        mean, inverse, _ = moments((stat.at[:SUBLANES, :],))
+        scale = stat[2 * SUBLANES : 2 * SUBLANES + 1, :] * inverse
+        shift = stat[2 * SUBLANES + 1 : 2 * SUBLANES + 2, :] + scale * (
+            stat[SUBLANES : 2 * SUBLANES, :] - mean
+        )
+
+        def activate(i, _, z=z, act=act, scale=scale, shift=shift):
+            rows = at(i * STEP, STEP)
+            u = scale * tiles(z[rows, :].astype(F32)) + shift
+            a = widen(tiles(mask[rows, :]), inner) * (u * jax.nn.sigmoid(u))
+            act[rows, :] = flat(a).astype(BF16)
+            return 0
+
+        lax.fori_loop(0, lay.rows // STEP, activate, 0)
 
     def step(part, carry):
         rows = at(part * lay.part, lay.part)
-        acc = mm(a0[rows, :], w0[...])
-        for a, w in ((a1, w1), (a2, w2), (a3, w3)):
-            acc = acc + mm(a[rows, :], w[...])
+        halves = [
+            functools.reduce(
+                jnp.add,
+                [mm(a[rows, :], w[low : low + inner, :]) for a, w in zip(acts, ws)],
+            )
+            for low in range(0, width, inner)
+        ]
+        acc = jnp.concatenate(halves, 1)
         z_out[rows, :] = acc
         z = tiles(acc)
         return masked_sums(z, z, widen(tiles(mask[rows, :]), width), carry)
@@ -283,22 +385,31 @@
     sums_out[...] = pack(sums, squares, widen(count[...], width))
 
 
-def output_kernel(lay, z3, sums3, gain, bias, mask, x, dy, out5, out7, out9, grad_out, sums_out):
+def output_kernel(lay, z3, sums3, gain, bias, mask, x, dy, result_out, grad_out, sums_out):
     width = z3.shape[1]
     mean, inverse, _ = moments(sums3)
 
-    def step(rows, store, carry):
+    def step(i, carry):
+        rows = at(i * STEP, STEP)
         live = widen(tiles(mask[rows, :]), width)
         normed = (tiles(z3[rows, :]) - mean) * inverse
         u = gain[...] * normed + bias[...] + tiles(x[rows, :].astype(F32))
         s = jax.nn.sigmoid(u)
-        store((out5, out7, out9), flat(live * (u * s)))
+        result_out[rows, :] = flat(live * (u * s)).astype(BF16)
         grad = live * tiles(dy[rows, :].astype(F32)) * (s * (1.0 + u * (1.0 - s)))
         grad_out[rows, :] = flat(grad)
         return carry[0] + jnp.sum(grad, 0), carry[1] + jnp.sum(grad * normed, 0)
 
-    first, cross = lay.sweep(step, zeros_pair(width))
+    first, cross = lax.fori_loop(0, lay.rows // STEP, step, zeros_pair(width))
     sums_out[...] = pack(first, cross, jnp.zeros_like(first))
+
+
+def move_kernel(lay, source, *outs):
+    def move(rows, store, carry):
+        store(outs, source[rows, :].astype(F32))
+        return carry
+
+    lay.sweep(move, 0)
 
 
 def grad_sums(received):
@@ -324,10 +435,18 @@
     lax.fori_loop(0, lay.rows // STEP, step, 0)
 
 
+def back_through(dz, w, inner):
+    found = [
+        mm_nt(dz[:, low : low + inner], w[low : low + inner, :])
+        for low in range(0, dz.shape[1], inner)
+    ]
+    return functools.reduce(jnp.add, found)
+
+
 def third_back_kernel(
-    lay, du3, z3, sums3, sums4, gain, mask, w0, w1, w2, w3,
-    dz_out, own_out, peer_out, send_out, bias_out, gain_out,
+    lay, du3, z3, sums3, sums4, gain, mask, w1, w3, dz_out, send_out, bias_out, gain_out
 ):
+    inner = send_out.shape[2]
     sums = grad_sums(sums4)
     bias_out[...] = both(sums[0])
     gain_out[...] = both(sums[1])
@@ -339,11 +458,20 @@
 
     def step(part, _):
         rows = at(part * lay.part, lay.part)
-        dz = dz_out[rows, :]
-        send_out[0, rows, :] = mm_nt(dz, w1[...]).astype(BF16)
-        send_out[1, rows, :] = mm_nt(dz, w3[...]).astype(BF16)
-        peer_out[rows, :] = mm_nt(dz, w2[...])
-        own_out[rows, :] = mm_nt(dz, w0[...])
+        send_out[0, rows, :] = back_through(dz_out[rows, :], w1, inner).astype(BF16)
+        send_out[1, rows, :] = back_through(dz_out[rows, :], w3, inner).astype(BF16)
+        return 0
+
+    lax.fori_loop(0, lay.parts, step, 0)
+
+
+def stay_kernel(lay, dz, w0, w2, own_out, peer_out):
+    inner = own_out.shape[1]
+
+    def step(part, _):
+        rows = at(part * lay.part, lay.part)
+        peer_out[rows, :] = back_through(dz[rows, :], w2, inner)
+        own_out[rows, :] = back_through(dz[rows, :], w0, inner)
         return 0
 
     lax.fori_loop(0, lay.parts, step, 0)
@@ -400,13 +528,6 @@
     sums_out[...] = pack(first, cross, jnp.zeros_like(first))
 
 
-def deal(rank, held, keep, send, lead=()):
-    piece = held.shape[0] // (2 * keep.shape[0])
-    for j in range(keep.shape[0]):
-        for ref, other in ((keep, 2 * j), (send, 2 * j + 1)):
-            ref[(j, *lead)] = held[at(jnp.bitwise_xor(rank, other) * piece, piece), :]
-
-
 def group_kernel(lay, act, dz, bits, block, choose, group_out, slabs, image, wide):
     width = act.shape[1]
     clear_halo(lay, slabs)
@@ -424,11 +545,31 @@
     group_out[...] = mm(wide[...], choose[...]).astype(BF16)
 
 
+def weight_blocks(ids, flip, dz, group, xs, out, held):
+    t, rank = ids[0], ids[1]
+    wide = held.shape[2]
+    piece = group.shape[0] // (2 * held.shape[0])
+    start = jnp.bitwise_xor(jnp.bitwise_and(rank, 1), flip) * wide
+    for k, pieces in enumerate(xs):
+        found, low = None, 0
+        for x in pieces:
+            high = low + x.shape[0]
+            more = mm_tn(dz[low:high, :], x[:, at(start, wide, LANES)])
+            found, low = more if found is None else found + more, high
+        held[jnp.bitwise_xor(t, k)] = found.astype(BF16)
+    for j in range(out.shape[0]):
+        other = jnp.bitwise_xor(rank, 2 * j + flip)
+        out[j, :wide, :] = held[lax.shift_right_logical(other, 1)]
+        rows = group[at(other * piece, piece), :]
+        out[j, wide : wide + piece, :] = rows[:, :wide]
+        out[j, wide + piece :, :LANES] = rows[: piece // 2, wide:]
+        out[j, wide + piece :, LANES:] = rows[piece // 2 :, wide:]
+
+
 def first_back_kernel(
-    lay, ids, du1, z1, sums1, sums6, gain, mask, group, x0, x1, x2, x3,
-    dz_out, bias_out, gain_out, keep, send, held,
+    lay, ids, du1, z1, sums1, sums6, gain, mask, group, xs,
+    dz_out, bias_out, gain_out, send, held,
 ):
-    t, rank = ids[0], ids[1]
     sums = grad_sums(sums6)
     bias_out[...] = both(sums[0])
     gain_out[...] = both(sums[1])
@@ -437,22 +578,11 @@
         dz_out[rows, :] = dz.astype(BF16)
 
     norm_back_loop(lay, du1, z1, mask, gain, moments(sums1), sums, store)
-    for k, x in ((0, x0), (1, x1), (2, x2), (3, x3)):
-        found = mm_tn(dz_out[...], x[...]).astype(BF16)
-        wide = held.shape[2]
-        many = found.shape[1] // wide
-        for i in range(many):
-            held[jnp.bitwise_xor(t, k) * many + i] = found[:, i * wide : (i + 1) * wide]
-    low, piece = held.shape[1], group.shape[0] // held.shape[0]
-    for j in range(keep.shape[0]):
-        for ref, other in ((keep, 2 * j), (send, 2 * j + 1)):
-            other = jnp.bitwise_xor(rank, other)
-            ref[j, :low, :] = held[other]
-            rows = group[at(other * piece, piece), :]
-            ref[j, low : low + piece, :] = rows[:, :wide]
-            high = low + piece
-            ref[j, high:, :LANES] = rows[: piece // 2, wide:]
-            ref[j, high:, LANES:] = rows[piece // 2 :, wide:]
+    weight_blocks(ids, 1, dz_out, group, xs, send, held)
+
+
+def keep_kernel(ids, dz, group, xs, keep, held):
+    weight_blocks(ids, 0, dz, group, xs, keep, held)
 
 
 def turn_kernel(*refs):
@@ -499,10 +629,16 @@
     lay.sweep(move, 0)
 
 
-def expand_grad_kernel(lay, ids, a0, a1, a2, a3, dz, keep, send, held):
-    for k, a in enumerate((a0, a1, a2, a3)):
+def expand_grad_kernel(lay, ids, acts, dz, keep_low, keep_high, send_low, send_high, held):
+    half = keep_low.shape[0]
+    piece = keep_low.shape[2]
+    for k, a in enumerate(acts):
         held[...] = mm_tn(a[...], dz[...]).astype(BF16)
-        deal(ids[1], held, keep, send, (k,))
+        for flip, low, high in ((0, keep_low, keep_high), (1, send_low, send_high)):
+            for j in range(2 * half):
+                ref, place = (low, j) if j < half else (high, j - half)
+                other = jnp.bitwise_xor(ids[1], 2 * j + flip)
+                ref[place, k] = held[at(other * piece, piece), :]
 
 
 def expand_place_kernel(ids, *refs):
@@ -589,14 +725,17 @@
             bits_left = low
         return tuple(found)
 
-    def halve(keep, send):
-        half = ranks // 2
-        passed = pass_on(send, 1)
-        sums = [total(keep[j], passed[j]).astype(BF16) for j in range(half)]
-        return sums
-
-    def scatter(sums):
-        return [sums[0]] + [pass_on(sums[j], 2 * j) for j in range(1, ranks // 2)]
+    def halve(keep_low, keep_high, send_low, send_high):
+        def add(keep, passed):
+            return [total(keep[j], passed[j]).astype(BF16) for j in range(keep.shape[0])]
+
+        passed = pass_on(send_high, 1)
+        send_low, passed = hold((send_low, passed))
+        return add(keep_low, pass_on(send_low, 1)), add(keep_high, passed)
+
+    def scatter(low, high):
+        far_parts = [pass_on(w, 2 * (j + len(low))) for j, w in enumerate(high)]
+        return [low[0], *(pass_on(w, 2 * j) for j, w in enumerate(low) if j), *far_parts]
 
     def collect_far(mine):
         return [mine] + [pass_on(mine, 2 * j) for j in range(1, ranks // 2)]
@@ -621,128 +760,195 @@
     g1, b1, g2, b2, g3, b3 = map(
         row, (first_gain, first_bias, second_gain, second_bias, third_gain, third_bias)
     )
-    mask = lay.live_mask(image_counts)
-    areas = jnp.asarray([e * e for e in lay.edges], jnp.int32)
-    live_pixels = jnp.sum(image_counts[:, 0, :] * areas[None, :], axis=1).astype(F32)
-    count = jnp.broadcast_to(
-        jnp.tile(live_pixels, SUBLANES // lay.micro)[:, None], (SUBLANES, LANES)
-    )
-    bits = jnp.asarray(lay.tap_bits())
-
-    maps = lay.flatten(all_maps)
-    maps_near, maps_far = swap(maps, 1), swap(maps, 2)
+    facts = jnp.asarray(lay.row_facts())
+    def as_rows(pixels):
+        (found,) = run(functools.partial(rows_kernel, lay), pixels, (like((rows, chan), BF16),))
+        return found
+
+    map_pixels = lay.by_pixel(all_maps)
+    far_pixels = [swap(p, 2) for p in map_pixels]
+    maps = as_rows(map_pixels)
+    maps_near = swap(maps, 1)
     owner = np.arange(inner) // group_width
-    block = jnp.asarray(owner[:, None] == owner[None, :])
-
-    def dense(w):
-        tiled = jnp.tile(w.reshape(9, inner, group_width), (1, 1, group_count))
-        return jnp.where(block[None], tiled, jnp.zeros((), BF16)).reshape(9 * inner, inner)
-
-    forward_weight = dense(group_weight)
-    backward_weight = dense(jnp.transpose(group_weight, (0, 1, 2, 4, 3)))
+    block = jnp.asarray(owner[:, None] == owner[None, :], F32)
+    repeat = np.arange(inner)[None, :] % group_width == np.arange(group_width)[:, None]
+    mask, count, forward_weight, backward_weight = run(
+        functools.partial(prepare_kernel, lay),
+        (
+            image_counts,
+            facts,
+            group_weight.reshape(9, inner, group_width),
+            jnp.asarray(repeat, BF16),
+            block,
+        ),
+        (
+            like((rows, LANES), F32),
+            like((SUBLANES, LANES), F32),
+            like((9 * inner, inner), BF16),
+            like((9 * inner, inner), BF16),
+        ),
+        scalars=1,
+    )
     choose = np.zeros((9 * inner, 3 * LANES), np.float32)
     for tap in range(9):
         for c in range(inner):
             choose[tap * inner + c, tap * group_width + c % group_width] = 1.0
     choose = jnp.asarray(choose, BF16)
-    upstream = lay.flatten(all_upstream)
+    upstream = as_rows(lay.by_pixel(all_upstream))
 
     def columns(k):
-        return lax.dynamic_slice_in_dim(expand_weight, jnp.bitwise_xor(t, k) * chan, chan, 1)
+        start = jnp.bitwise_xor(t, k) * chan
+        return jnp.concatenate(
+            [
+                lax.dynamic_slice_in_dim(expand_weight, start + low, inner, 1)
+                for low in range(0, chan, inner)
+            ],
+            0,
+        )
 
     def weight_rows(k):
         return lax.dynamic_slice_in_dim(reduce_weight, jnp.bitwise_xor(t, k) * chan, chan, 0)
 
-    expand_parts = [columns(k) for k in range(shards)]
-    reduce_parts = [weight_rows(k) for k in range(shards)]
-    maps_far, mask, count, forward_weight, backward_weight, upstream, expand_parts, reduce_parts = hold(
-        (maps_far, mask, count, forward_weight, backward_weight, upstream, expand_parts, reduce_parts)
-    )
-    xs = (maps, maps_near, maps_far, swap(maps_far, 1))
-    expand_parts = [w if k == 0 else swap(w, k) for k, w in enumerate(expand_parts)]
-    reduce_parts = [w if k == 0 else swap(w, k) for k, w in enumerate(reduce_parts)]
+    weight_blocks = reduce_weight.reshape(shards, chan, inner)
+    (z1,) = run(
+        functools.partial(reduce_begin_kernel, lay),
+        (ids, maps, maps_near, weight_blocks),
+        (like((rows, inner), F32),),
+        scalars=1,
+    )
+    weights = [columns(k) for k in range(shards)]
+    weights_back = [weight_rows(k) for k in range(shards)]
+    (far_last, mask, count, forward_weight, backward_weight, upstream, weights, weights_back, z1) = hold(
+        (far_pixels[-1], mask, count, forward_weight, backward_weight, upstream, weights, weights_back, z1)
+    )
+    last_rows = like((rows - lay.cut, chan), BF16)
+    more_rows = like((lay.cut, chan), BF16)
+    last_far, last_cross, z1_last, s1 = run(
+        functools.partial(reduce_last_kernel, lay),
+        (ids, (far_last,), (swap(far_last, 1),), weight_blocks, z1, mask),
+        (
+            last_rows,
+            last_rows,
+            like((rows - lay.cut, inner), F32),
+            like((2, SUBLANES, inner), F32),
+        ),
+        scalars=1,
+    )
+    far_more, z1_last = hold((far_pixels[:-1], z1_last))
+    cross_more = [swap(p, 1) for p in far_more]
+    weights, _ = hold((weights, far_more))
+    weights = [w if k == 0 else swap(w, k) for k, w in enumerate(weights)]
 
     tile1 = like((SUBLANES, inner), F32)
     tile3 = like((SUBLANES, chan), F32)
     slabs = pltpu.VMEM((inner // LANES, rows + 2 * HALO, LANES), F32)
     image = pltpu.VMEM((rows, 9 * inner), BF16)
 
-    z1, s1 = run(
-        functools.partial(reduce_kernel, lay),
-        (ids, *xs, reduce_weight.reshape(shards, chan, inner), mask, count),
-        (like((rows, inner), F32), tile1),
+    more_far, z1 = run(
+        functools.partial(reduce_more_kernel, lay),
+        (ids, far_more, weight_blocks, z1),
+        (more_rows, like((lay.cut, inner), F32)),
         scalars=1,
     )
+    more_cross, z1, s1 = run(
+        functools.partial(reduce_end_kernel, lay),
+        (ids, cross_more, weight_blocks, z1, z1_last, s1, mask, count),
+        (more_rows, like((rows, inner), F32), tile1),
+        scalars=1,
+    )
+    xs = ((maps,), (maps_near,), (more_far, last_far), (more_cross, last_cross))
     s1 = allsum(s1)
-    s1, expand_parts = hold((s1, expand_parts))
-    z2, s2, act1 = run(
+    s1, weights = hold((s1, weights))
+    z2, s2, act1, z2_sent, offset = run(
         functools.partial(conv_kernel, lay),
-        (z1, s1, g1, b1, mask, count, bits, forward_weight),
-        (like((rows, inner), F32), tile1, like((rows, inner), BF16)),
+        (z1, s1, g1, b1, mask, count, facts, forward_weight),
+        (
+            like((rows, inner), F32),
+            tile1,
+            like((rows, inner), BF16),
+            like((rows, inner), BF16),
+            tile1,
+        ),
         scratch=(slabs, image),
         limit=16,
     )
+    z2_near, z2_far = swap(z2_sent, 1), swap(z2_sent, 2)
     s2 = allsum(s2)
-    s2, reduce_parts = hold((s2, reduce_parts))
-    (act2,) = run(
-        functools.partial(second_kernel, lay),
-        (z2, s2, g2, b2, mask),
-        (like((rows, inner), BF16),),
-    )
-    acts = gather(act2)
-    z3, s3 = run(
+    (stat,) = run(stat_kernel, (s2, offset, g2, b2), (like((3 * SUBLANES, inner), F32),))
+    stats = [stat] + [swap(stat, k) for k in range(1, shards)]
+    z2_far, stats[1] = hold((z2_far, stats[1]))
+    z3, s3, *acts = run(
         functools.partial(expand_kernel, lay),
-        (*acts, *expand_parts, mask, count),
-        (like((rows, chan), F32), tile3),
-    )
+        (
+            (z2_sent, z2_near, z2_far, swap(z2_far, 1)),
+            stats,
+            weights,
+            mask,
+            count,
+        ),
+        (like((rows, chan), F32), tile3, *([like((rows, inner), BF16)] * shards)),
+    )
+    weights_back[1:3], s3 = hold((weights_back[1:3], s3))
+    weights_back[1], weights_back[2] = swap(weights_back[1], 1), swap(weights_back[2], 2)
     s3 = allsum(s3)
-    *output, du3, s4 = run(
+    weights_back[1:3], s3 = hold((weights_back[1:3], s3))
+    output, du3, s4 = run(
         functools.partial(output_kernel, lay),
         (z3, s3, g3, b3, mask, maps, upstream),
-        (*lay.pixel_shapes(chan, BF16), like((rows, chan), F32), tile3),
-    )
+        (like((rows, chan), BF16), like((rows, chan), F32), tile3),
+    )
+    weights_back[3], s4 = hold((weights_back[3], s4))
+    weights_back[3] = swap(weights_back[3], 3)
     s4 = allsum(s4)
-    dz3, own, peer, send, bias_three, gain_three = run(
+    weights_back[3], s4 = hold((weights_back[3], s4))
+    dz3, send, bias_three, gain_three = run(
         functools.partial(third_back_kernel, lay),
-        (du3, z3, s3, s4, g3, mask, *expand_parts),
+        (du3, z3, s3, s4, g3, mask, weights[1], weights[3]),
         (
             like((rows, chan), BF16),
-            like((rows, inner), F32),
-            like((rows, inner), F32),
             like((2, rows, inner), BF16),
             like((1, chan), F32),
             like((1, chan), F32),
         ),
     )
     near = swap(send, 1)
+    own, peer = run(
+        functools.partial(stay_kernel, lay),
+        (dz3, weights[0], weights[2]),
+        (like((rows, inner), F32),) * 2,
+    )
     piece = inner // BLOCKS
     half = BLOCKS // 2
-    expand_keep, expand_send = run(
+    keep_low, keep_high, send_low, send_high = run(
         functools.partial(expand_grad_kernel, lay),
-        (ids, *acts, dz3),
-        (like((half, shards, piece, chan), BF16),) * 2,
+        (ids, acts, dz3),
+        (like((half // 2, shards, piece, chan), BF16),) * 4,
         scratch=(pltpu.VMEM((inner, chan), BF16),),
         scalars=1,
     )
+    expand_local = (keep_low, keep_high, send_low, send_high)
+    far = swap(total(peer, near[1]).astype(BF16), 2)
+    output = run(functools.partial(move_kernel, lay), (output,), lay.pixel_shapes(chan, BF16))
+    far, output = hold((far, output))
     if fast:
-        sums = halve(expand_keep, expand_send)
-    far = swap(total(peer, near[1]).astype(BF16), 2)
-    if fast:
-        arrived = scatter(sums)
-        far, arrived[1] = hold((far, arrived[1]))
+        arrived = scatter(*halve(*expand_local))
+        far, arrived = hold((far, arrived))
     du2, s5 = run(
         functools.partial(second_back_kernel, lay),
         (own, near, far, z2, s2, g2, b2, mask),
         (like((rows, inner), F32), tile1),
     )
+    if fast:
+        mine = total(*arrived).astype(BF16)
+        s5, mine = hold((s5, mine))
+        moved = [swap(mine[k], k) for k in range(1, shards)]
     s5 = allsum(s5)
     if fast:
-        s5, arrived = hold((s5, arrived))
-        mine = total(*arrived).astype(BF16)
-        mine = jnp.stack([mine[0]] + [swap(mine[k], k) for k in range(1, shards)])
+        s5, moved = hold((s5, moved))
+        mine = jnp.stack([mine[0], *moved])
     du1, s6, dz2, bias_two, gain_two = run(
         functools.partial(conv_back_kernel, lay),
-        (du2, z2, s2, s5, g2, mask, bits, backward_weight, z1, s1, g1, b1),
+        (du2, z2, s2, s5, g2, mask, facts, backward_weight, z1, s1, g1, b1),
         (
             like((rows, inner), F32),
             tile1,
@@ -754,10 +960,11 @@
         limit=16,
     )
     s6 = allsum(s6)
+    dz2, s6 = hold((dz2, s6[0]))[0], s6
     lanes = choose.shape[1]
     (group_local,) = run(
         functools.partial(group_kernel, lay),
-        (act1, dz2, bits, block.astype(F32), choose),
+        (act1, dz2, facts, block, choose),
         (like((inner, lanes), BF16),),
         scratch=(slabs, image, pltpu.VMEM((inner, 9 * inner), BF16)),
         limit=24,
@@ -766,17 +973,25 @@
         s6, group_local, mine = hold((s6, group_local, mine))
     wide = shards * chan // BLOCKS
     deep = wide + piece + piece * (lanes - wide) // wide
-    dz1, bias_one, gain_one, reduce_keep, reduce_send = run(
+    weight_part = like((half, deep, inner), BF16)
+    weight_scratch = (pltpu.VMEM((shards, inner, wide), BF16),)
+    dz1, bias_one, gain_one, send = run(
         functools.partial(first_back_kernel, lay),
-        (ids, du1, z1, s1, s6, g1, mask, group_local, *xs),
+        (ids, du1, z1, s1, s6, g1, mask, group_local, xs),
         (
             like((rows, inner), BF16),
             like((1, inner), F32),
             like((1, inner), F32),
-            like((half, deep, inner), BF16),
-            like((half, deep, inner), BF16),
+            weight_part,
         ),
-        scratch=(pltpu.VMEM((BLOCKS, inner, wide), BF16),),
+        scratch=weight_scratch,
+        scalars=1,
+    )
+    (keep,) = run(
+        keep_kernel,
+        (ids, dz1, group_local, xs),
+        (weight_part,),
+        scratch=weight_scratch,
         scalars=1,
     )
 
@@ -785,36 +1000,37 @@
         return [both_sums[r % 2][r // 2].astype(BF16) for r in range(BLOCKS)]
 
     block_shape = (like((deep, inner), BF16),)
+    def gradient_of_maps(near, far, cross):
+        return run(
+            functools.partial(input_kernel, lay),
+            (du3, dz1, near, far, cross, *weights_back),
+            lay.pixel_shapes(chan, F32),
+            scratch=(pltpu.VMEM((rows, chan), F32),),
+        )
+
     if fast:
-        reduce_keep, reduce_send, dz1, mine = hold((reduce_keep, reduce_send, dz1, mine))
-        passed = pass_on(reduce_send, 1)
-        dz_near, dz_far = swap(dz1, 1), swap(dz1, 2)
+        send, dz1, mine = hold((send, dz1, mine))
+        passed = pass_on(send, 1)
+        dz_far = swap(dz1, 2)
         whole = collect_far(mine)
-        sums = [total(reduce_keep[j], passed[j]).astype(BF16) for j in range(half)]
-        sums, dz_far, whole = hold((sums, dz_far, whole))
-        parts = scatter(sums)
-        dz_cross = swap(dz_far, 1)
+        sums = [total(keep[j], passed[j]).astype(BF16) for j in range(half)]
+        sums, whole = hold((sums, whole))
         crossed = pass_on(jnp.stack(whole), 1)
         whole = [w for j in range(half) for w in (whole[j], crossed[j])]
+        parts = scatter(sums[:1], sums[1:])
+        dz1, dz_far, _ = hold((dz1, dz_far, sums[0]))
+        backprop = gradient_of_maps(swap(dz1, 1), dz_far, swap(dz_far, 1))
+        parts, backprop = hold((parts, backprop))
+        (mine,) = run(turn_kernel, tuple(parts), block_shape)
+        blocks = collect_far(mine)
+        blocks = collect_near(blocks)
     else:
         dz_near, dz_far = swap(dz1, 1), swap(dz1, 2)
-        dz_cross = swap(dz_far, 1)
-    backprop = run(
-        functools.partial(input_kernel, lay),
-        (du3, dz1, dz_near, dz_far, dz_cross, *reduce_parts),
-        lay.pixel_shapes(chan, F32),
-        scratch=(pltpu.VMEM((rows, chan), F32),),
-    )
-    if fast:
-        parts, backprop = hold((parts, backprop))
-        (mine,) = run(turn_kernel, tuple(parts), block_shape)
-        blocks = collect_near(collect_far(mine))
-    else:
-        blocks = [run(turn_kernel, (b,), block_shape)[0] for b in summed(reduce_keep, reduce_send)]
-        whole = [
-            jnp.stack([b[0]] + [swap(b[k], k) for k in range(1, shards)])
-            for b in summed(expand_keep, expand_send)
-        ]
+        backprop = gradient_of_maps(dz_near, dz_far, swap(dz_far, 1))
+        found = summed(keep, send)
+        blocks = [run(turn_kernel, (b,), block_shape)[0] for b in found]
+        found = summed(jnp.concatenate(expand_local[:2], 0), jnp.concatenate(expand_local[2:], 0))
+        whole = [jnp.stack([b[0]] + [swap(b[k], k) for k in range(1, shards)]) for b in found]
     (expand_grad,) = run(
         expand_place_kernel, (ids, *whole), (like((inner, shards * chan), F32),), scalars=1
     )

time: 257 us -> 233 us (0.907)
  waiting for transfers between devices: 110 us -> 90.9 us
  local copies, waits for them, and re-layouts: 19.3 us -> 5.39 us
  starting transfers between devices: 67.4 us -> 80.3 us
  other arithmetic: 8.98 us -> 0.82 us
  Pallas kernels: 49.1 us -> 53.8 us
    ppermute x43 -> x44, waiting for transfers between devices: 82.4 us -> 63.8 us  [pass_on(): return lax.ppermute(x, 'batch', [(i, i ^ k) for i in range(ranks)])]
    ppermute x43 -> x44, starting transfers between devices: 55.2 us -> 62.7 us  [pass_on(): return lax.ppermute(x, 'batch', [(i, i ^ k) for i in range(ranks)])]
    another operation x8 -> x0, local copies, waits for them, and re-layouts: 6.16 us -> none  [the longest x7 6.15 us: dense(): tiled = jnp.tile(w.reshape(9, inner, group_width), (1, 1, group_count))]
    reshape x6 -> x0, local copies, waits for them, and re-layouts: 5.6 us -> none  [flatten(): rows = jnp.transpose(piece, (1, 2, 3, 0, 4)).reshape(live, piece.shape[-1])]
    ppermute x20 -> x27, starting transfers between devices: 12.2 us -> 17.6 us  [swap(): return lax.ppermute(x, 'tensor', [(i, i ^ k) for i in range(shards)])]
    pallas_call x15 -> x24, Pallas kernels: 49.1 us -> 53.8 us  [run(): pl.pallas_call(kernel, out_shape=list(outs), in_specs=specs, out_specs=[p...]
    lt x3 -> x0, other arithmetic: 3.9 us -> none  [live_mask(): pieces.append((jnp.asarray(image, jnp.int32) < limit).astype(F32))]
    select_n x1 -> x0, other arithmetic: 2.89 us -> none  [dense(): jnp.where(block[None], tiled, jnp.zeros((), BF16)).reshape(9 * inner, inner)]
  transfers between devices with their start and end apart: 63 -> 71, of which waited for: 34 -> 38; matrix products, arithmetic and copies ran while one was open for 9% -> 0% of each run, Pallas kernels for 8% -> 11%
where the time goes in v3:
time: 233 us; the launch traced here: 232 us
  waiting for transfers between devices  90.9 us (39%)
  starting transfers between devices  80.3 us (34%)
  Pallas kernels  53.8 us (23%)
  local copies, waits for them, and re-layouts  5.39 us (2%)
    ppermute x44, waiting for transfers between devices, pass_on(): return lax.ppermute(x, 'batch', [(i, i ^ k) for i in range(ranks)])  63.8 us
    ppermute x44, starting transfers between devices, pass_on(): return lax.ppermute(x, 'batch', [(i, i ^ k) for i in range(ranks)])  62.7 us
    pallas_call x24, Pallas kernels, run(): pl.pallas_call(kernel, out_shape=list(outs), in_specs=specs, out_specs=[p...  53.8 us
    ppermute x27, waiting for transfers between devices, swap(): return lax.ppermute(x, 'tensor', [(i, i ^ k) for i in range(shards)])  27.1 us
    ppermute x27, starting transfers between devices, swap(): return lax.ppermute(x, 'tensor', [(i, i ^ k) for i in range(shards)])  17.6 us
    unnamed x38, local copies, waits for them, and re-layouts  5.11 us
  transfers between devices with their start and end apart: 71, of which 38 were waited for; matrix products, arithmetic and copies ran while one was open for 0% of the time, Pallas kernels for 11%

profile of v3, /device:TPU:0, one launch (start us, length us, event | category | flops | bytes accessed | tf_op | source)
XLA Modules:
  0.0 232.3 jit_solution(9289220495618500980)
XLA Ops:
  3.6 2.6 %collective-permute-start.2 = (bf16[243,2,512]{2,1,0:T(2,128)(2,1)}, bf16[243,2,512]{2,1,0:T(2,128)(2,1)}, u32[]{:S(2)}, u32[]{:S(2)}) collective-permute-start(bf16[243,2,512]{2,1,0:T(2,128)(2,1)} %bitcast.7.refs_2_), channel_id=1, source_target_pairs={{0,2},{1,3},{2,0},{3,1},{4,6},{5,7},{6,4},{7,5},{8,10},{9,11},{10,... | collective-permute-start | bytes 1493000 | tf_op jit(solution)/shard_map/ppermute | solution.py:712
  12.4 1.8 shard_map.310.z
  14.2 4.5 %collective-permute-done.2.far_0_ = bf16[243,2,512]{2,1,0:T(2,128)(2,1)} collective-permute-done((bf16[243,2,512]{2,1,0:T(2,128)(2,1)}, bf16[243,2,512]{2,1,0:T(2,128)(2,1)}, u32[]{:S(2)}, u32[]{:S(2)}) %collective-permute-start.2) | collective-permute-done | bytes 497696 | tf_op jit(solution)/shard_map/ppermute | solution.py:712
  18.7 1.9 collective-permute-start
  20.8 1.7 shard_map.311
  22.5 15.4 %collective-permute-done.far_0_ = bf16[150,2,512]{2,1,0:T(2,128)(2,1)S(1)} collective-permute-done((bf16[150,2,512]{2,1,0:T(2,128)(2,1)S(1)}, bf16[150,2,512]{2,1,0:T(2,128)(2,1)S(1)}, u32[]{:S(2)}, u32[]{:S(2)}) %collective-permute-start) | collective-permute-done | bytes 307232 | tf_op jit(solution)/shard_map/ppermute | solution.py:712
  38.4 1.8 collective-permute-start.12
  40.3 1.8 shard_map.312
  43.5 3.9 %collective-permute-start.9 = (f32[8,256]{1,0:T(8,128)S(1)}, f32[8,256]{1,0:T(8,128)S(1)}, u32[]{:S(2)}, u32[]{:S(2)}) collective-permute-start(f32[8,256]{1,0:T(8,128)S(1)} %get-tuple-element.171), channel_id=1, source_target_pairs={{0,24},{4,28},{8,16},{12,20},{16,8},{20,12},{24,0},{28,4},{1,25},{... | collective-permute-start | bytes 24584 | tf_op jit(solution)/shard_map/ppermute | solution.py:715
  47.3 1.6 collective-permute-done.9
  49.0 2.9 %collective-permute-done.8 = f32[8,256]{1,0:T(8,128)S(1)} collective-permute-done((f32[8,256]{1,0:T(8,128)S(1)}, f32[8,256]{1,0:T(8,128)S(1)}, u32[]{:S(2)}, u32[]{:S(2)}) %collective-permute-start.8) | collective-permute-done | bytes 8224 | tf_op jit(solution)/shard_map/ppermute | solution.py:715
  52.6 1.7 collective-permute-start.10
  54.4 1.9 collective-permute-done.10.sums1_1_
  56.3 5.0 %shard_map.314 = (f32[1392,256]{1,0:T(8,128)S(1)}, f32[8,256]{1,0:T(8,128)S(1)}, bf16[1392,256]{1,0:T(8,128)(2,1)S(1)}, bf16[1392,256]{1,0:T(8,128)(2,1)S(1)}, f32[8,256]{1,0:T(8,128)S(1)}) custom-call(f32[1392,256]{1,0:T(8,128)S(1)} %get-tuple-element.170.z1, f32[8,256]{1,0:T(8,128)S(1)} %add_add_fusion.5.sums1_0_, ...), custom_call_target="tpu_custom_call" | custom-call | flops 1048576 | tf_op jit(solution)/shard_map/pallas_call | solution.py:661
  61.3 1.8 collective-permute-start.15
  63.1 3.6 %collective-permute-start.18 = (f32[8,256]{1,0:T(8,128)S(1)}, f32[8,256]{1,0:T(8,128)S(1)}, u32[]{:S(2)}, u32[]{:S(2)}) collective-permute-start(f32[8,256]{1,0:T(8,128)S(1)} %get-tuple-element.184), channel_id=1, source_target_pairs={{0,24},{4,28},{8,16},{12,20},{16,8},{20,12},{24,0},{28,4},{1,25},{... | collective-permute-start | bytes 24584 | tf_op jit(solution)/shard_map/ppermute | solution.py:715
  68.5 2.7 %collective-permute-done.17 = f32[8,256]{1,0:T(8,128)S(1)} collective-permute-done((f32[8,256]{1,0:T(8,128)S(1)}, f32[8,256]{1,0:T(8,128)S(1)}, u32[]{:S(2)}, u32[]{:S(2)}) %collective-permute-start.17) | collective-permute-done | bytes 8224 | tf_op jit(solution)/shard_map/ppermute | solution.py:715
  71.2 1.6 collective-permute-start.19
  72.8 2.1 collective-permute-done.19.sums_1_.sums2_1_
  76.6 1.6 collective-permute-start.23
  79.9 2.2 collective-permute-done.22.stats_2_
  82.1 4.8 %shard_map.316 = (f32[1392,512]{1,0:T(8,128)S(1)}, f32[8,512]{1,0:T(8,128)S(1)}, bf16[1392,256]{1,0:T(8,128)(2,1)S(1)}, bf16[1392,256]{1,0:T(8,128)(2,1)S(1)}, b...) custom-call(bf16[1392,256]{1,0:T(8,128)(2,1)S(1)} %get-tuple-element.183.zs_0_, ...), custom_call_target="tpu_custom_call" | custom-call | flops 1048576 | tf_op jit(solution)/shard_map/pallas_call | solution.py:661
  87.6 3.5 %collective-permute-start.28 = (f32[8,512]{1,0:T(8,128)S(1)}, f32[8,512]{1,0:T(8,128)S(1)}, u32[]{:S(2)}, u32[]{:S(2)}) collective-permute-start(f32[8,512]{1,0:T(8,128)S(1)} %get-tuple-element.198), channel_id=1, source_target_pairs={{0,24},{4,28},{8,16},{12,20},{16,8},{20,12},{24,0},{28,4},{1,25},{... | collective-permute-start | bytes 49160 | tf_op jit(solution)/shard_map/ppermute | solution.py:715
  93.1 2.6 %collective-permute-done.27 = f32[8,512]{1,0:T(8,128)S(1)} collective-permute-done((f32[8,512]{1,0:T(8,128)S(1)}, f32[8,512]{1,0:T(8,128)S(1)}, u32[]{:S(2)}, u32[]{:S(2)}) %collective-permute-start.27) | collective-permute-done | bytes 16416 | tf_op jit(solution)/shard_map/ppermute | solution.py:715
  95.8 1.6 collective-permute-start.29
  97.3 2.2 collective-permute-done.29.sums3_1_
  99.6 2.3 %shard_map.317 = (bf16[1392,512]{1,0:T(8,128)(2,1)S(1)}, f32[1392,512]{1,0:T(8,128)S(1)}, f32[8,512]{1,0:T(8,128)S(1)}) custom-call(f32[1392,512]{1,0:T(8,128)S(1)} %get-tuple-element.192.z3, f32[8,512]{1,0:T(8,128)S(1)} %add_add_fusion.1.sums3_0_, f32[8,512]{1,0:T(8,128)S(1)} %collective-permute-done.29.sums3_1_, f32[1,512]{1,0:T(1,128)S(1)} %bitcast.115, ...), custom_call_target="tpu_custom_call" | custom-call | flops 1048576 | tf_op jit(solution)/shard_map/pallas_call | solution.py:661
  102.0 1.5 collective-permute-start.33
  104.2 2.3 collective-permute-start.31
  108.9 1.6 collective-permute-start.34
  110.4 2.2 collective-permute-done.34.sums4_1_
  112.7 2.6 %shard_map.318 = (bf16[1392,512]{1,0:T(8,128)(2,1)S(1)}, bf16[2,1392,256]{2,1,0:T(8,128)(2,1)S(1)}, f32[1,512]{1,0:T(1,128)}, f32[1,512]{1,0:T(1,128)}) custom-call(f32[1392,512]{1,0:T(8,128)S(1)} %get-tuple-element.202.du3, f32[1392,512]{1,0:T(8,128)S(1)} %get-tuple-element.192.z3, f32[8,512]{1,0:T(8,128)S(1)} %add_add_fusion.1.sums3_0_, ...), custom_call_target="tpu_custom_call" | custom-call | flops 1048576 | tf_op jit(solution)/shard_map/pallas_call | solution.py:661
  115.3 2.4 %shard_map.321 = (bf16[2,4,32,512]{3,2,1,0:T(8,128)(2,1)S(1)}, bf16[2,4,32,512]{3,2,1,0:T(8,128)(2,1)S(1)}, bf16[2,4,32,512]{3,2,1,0:T(8,128)(2,1)S(1)}, bf16[2,4,32,512]{3,2,1,0:T(8,128)(2,1)S(1)}) custom-call(s32[2]{0:T(128)S(1)} %pad_add_fusion.ids, bf16[1392,256]{1,0:T(8,128)(2,1)S(1)} %get-tuple-element.221.acts_0_, ...), custom_call_target="tpu_custom_call" | custom-call | flops 1048576 | tf_op jit(solution)/shard_map/pallas_call | solution.py:661
  117.7 1.6 collective-permute-start.37
  121.9 4.6 %collective-permute-done.37 = bf16[2,4,32,512]{3,2,1,0:T(8,128)(2,1)S(1)} collective-permute-done((bf16[2,4,32,512]{3,2,1,0:T(8,128)(2,1)S(1)}, bf16[2,4,32,512]{3,2,1,0:T(8,128)(2,1)S(1)}, u32[]{:S(2)}, u32[]{:S(2)}) %collective-permute-start.37) | collective-permute-done | bytes 262176 | tf_op jit(solution)/shard_map/ppermute | solution.py:715
  128.0 2.3 %collective-permute-start.41 = (bf16[4,32,512]{2,1,0:T(8,128)(2,1)S(1)}, bf16[4,32,512]{2,1,0:T(8,128)(2,1)S(1)}, u32[]{:S(2)}, u32[]{:S(2)}) collective-permute-start(bf16[4,32,512]{2,1,0:T(8,128)(2,1)S(1)} %get-tuple-element.317), channel_id=1, source_target_pairs={{0,24},{4,28},{8,16},{12,20},{16,8},{20,12},{24,0},{28,4},{1,25},{... | collective-permute-start | bytes 393224 | tf_op jit(solution)/shard_map/ppermute | solution.py:715
  131.1 3.3 %collective-permute-done.38 = bf16[2,4,32,512]{3,2,1,0:T(8,128)(2,1)S(1)} collective-permute-done((bf16[2,4,32,512]{3,2,1,0:T(8,128)(2,1)S(1)}, bf16[2,4,32,512]{3,2,1,0:T(8,128)(2,1)S(1)}, u32[]{:S(2)}, u32[]{:S(2)}) %collective-permute-start.38) | collective-permute-done | bytes 262176 | tf_op jit(solution)/shard_map/ppermute | solution.py:715
  134.5 1.6 collective-permute-start.39
  136.1 2.5 %shard_map.320 = (bf16[150,2,512]{2,1,0:T(2,128)(2,1)}, bf16[294,2,512]{2,1,0:T(2,128)(2,1)}, bf16[243,2,512]{2,1,0:T(2,128)(2,1)}) custom-call(bf16[1392,512]{1,0:T(8,128)(2,1)S(1)} %get-tuple-element.212.source), custom_call_target="tpu_custom_call" | custom-call | flops 1048576 | tf_op jit(solution)/shard_map/pallas_call | solution.py:661
  139.0 3.4 %collective-permute-done.40 = bf16[4,32,512]{2,1,0:T(8,128)(2,1)S(1)} collective-permute-done((bf16[4,32,512]{2,1,0:T(8,128)(2,1)S(1)}, bf16[4,32,512]{2,1,0:T(8,128)(2,1)S(1)}, u32[]{:S(2)}, u32[]{:S(2)}) %collective-permute-start.40) | collective-permute-done | bytes 131104 | tf_op jit(solution)/shard_map/ppermute | solution.py:715
  143.9 2.1 collective-permute-start.44
  145.9 2.4 %collective-permute-start.42 = (f32[8,256]{1,0:T(8,128)S(1)}, f32[8,256]{1,0:T(8,128)S(1)}, u32[]{:S(2)}, u32[]{:S(2)}) collective-permute-start(f32[8,256]{1,0:T(8,128)S(1)} %get-tuple-element.239), channel_id=1, source_target_pairs={{0,8},{4,12},{8,0},{12,4},{16,24},{20,28},{24,16},{28,20},{1,9},{5... | collective-permute-start | bytes 24584 | tf_op jit(solution)/shard_map/ppermute | solution.py:715
  151.6 2.6 %collective-permute-done.45.sums5_1_ = f32[8,256]{1,0:T(8,128)S(1)} collective-permute-done((f32[8,256]{1,0:T(8,128)S(1)}, f32[8,256]{1,0:T(8,128)S(1)}, u32[]{:S(2)}, u32[]{:S(2)}) %collective-permute-start.45) | collective-permute-done | bytes 8224 | tf_op jit(solution)/shard_map/ppermute | solution.py:715
  154.2 5.5 %shard_map.323 = (f32[1392,256]{1,0:T(8,128)S(1)}, f32[8,256]{1,0:T(8,128)S(1)}, bf16[1392,256]{1,0:T(8,128)(2,1)S(1)}, f32[1,256]{1,0:T(1,128)}, f32[1,256]{1,0:T(1,128)}) custom-call(f32[1392,256]{1,0:T(8,128)S(1)} %get-tuple-element.233.du2, f32[1392,256]{1,0:T(8,128)S(1)} %get-tuple-element.232.z2, f32[8,256]{1,0:T(8,128)S(1)} %add_add_fusion.4.sums_0_.sums2_0_, ...), custom_call_target="tpu_custom_call" | custom-call | flops 1048576 | tf_op jit(solution)/shard_map/pallas_call | solution.py:661
  159.7 1.8 collective-permute-start.51
  167.5 3.6 %shard_map.324.group = bf16[256,384]{1,0:T(8,128)(2,1)S(1)} custom-call(bf16[1392,256]{1,0:T(8,128)(2,1)S(1)} %get-tuple-element.246.act, bf16[1392,256]{1,0:T(8,128)(2,1)S(1)} %get-tuple-element.248.dz, s32[1392,128]{1,0:T(8,128)S(1)} %copy-done.1, f32[256,256]{1,0:T(8,128)S(1)} %copy-done.3, bf16[2304,384]{1,0:T(8,128)(2,1)S(1)} %copy-done.2), custom_call_target="tpu_custom_call" | custom-call | flops 1048576 | tf_op jit(solution)/shard_map/pallas_call | solution.py:661
  171.1 2.4 %shard_map.325 = (bf16[1392,256]{1,0:T(8,128)(2,1)S(1)}, f32[1,256]{1,0:T(1,128)}, f32[1,256]{1,0:T(1,128)}, bf16[4,304,256]{2,1,0:T(8,128)(2,1)S(1)}) custom-call(s32[2]{0:T(128)S(1)} %pad_add_fusion.ids, f32[1392,256]{1,0:T(8,128)S(1)} %get-tuple-element.244.du1, f32[1392,256]{1,0:T(8,128)S(1)} %get-tuple-element.170.z1, ...), custom_call_target="tpu_custom_call" | custom-call | flops 1048576 | tf_op jit(solution)/shard_map/pallas_call | solution.py:661
  175.6 1.8 collective-permute-start.56
  178.3 1.6 collective-permute-start.54
  180.0 1.6 shard_map.326
  181.6 4.6 %collective-permute-done.53 = bf16[4,304,256]{2,1,0:T(8,128)(2,1)S(1)} collective-permute-done((bf16[4,304,256]{2,1,0:T(8,128)(2,1)S(1)}, bf16[4,304,256]{2,1,0:T(8,128)(2,1)S(1)}, u32[]{:S(2)}, u32[]{:S(2)}) %collective-permute-start.53) | collective-permute-done | bytes 622624 | tf_op jit(solution)/shard_map/ppermute | solution.py:715
  186.7 2.2 collective-permute-done.60.d2
  190.5 1.5 collective-permute-start.57
  193.1 1.8 collective-permute-start.59
  194.9 4.0 %shard_map.327 = (f32[150,2,512]{2,1,0:T(2,128)}, f32[294,2,512]{2,1,0:T(2,128)}, f32[243,2,512]{2,1,0:T(2,128)}) custom-call(f32[1392,512]{1,0:T(8,128)S(1)} %get-tuple-element.202.du3, bf16[1392,256]{1,0:T(8,128)(2,1)S(1)} %get-tuple-element.269.dz.d0, bf16[1392,256]{1,0:T(8,128)(2,1)S(1)} %collective-permute-done.61.d1, ...), custom_call_target="tpu_custom_call" | custom-call | flops 1048576 | tf_op jit(solution)/shard_map/pallas_call | solution.py:661
  198.9 7.5 %collective-permute-done.58.refs_2_ = bf16[304,256]{1,0:T(8,128)(2,1)S(1)} collective-permute-done((bf16[304,256]{1,0:T(8,128)(2,1)S(1)}, bf16[304,256]{1,0:T(8,128)(2,1)S(1)}, u32[]{:S(2)}, u32[]{:S(2)}) %collective-permute-start.58) | collective-permute-done | bytes 155680 | tf_op jit(solution)/shard_map/ppermute | solution.py:715
  206.6 2.0 collective-permute-start.68
  208.6 3.8 %collective-permute-start.66 = (bf16[304,256]{1,0:T(8,128)(2,1)S(1)}, bf16[304,256]{1,0:T(8,128)(2,1)S(1)}, u32[]{:S(2)}, u32[]{:S(2)}) collective-permute-start(bf16[304,256]{1,0:T(8,128)(2,1)S(1)} %shard_map.328.refs_0_), channel_id=1, source_target_pairs={{0,16},{4,20},{8,24},{12,28},{16,0},{20,4},{24,8},{28,12},{1,17},{... | collective-permute-start | bytes 466952 | tf_op jit(solution)/shard_map/ppermute | solution.py:715
  213.3 2.1 collective-permute-done.68.refs_6_
  216.2 5.5 %collective-permute-done.66.refs_4_ = bf16[304,256]{1,0:T(8,128)(2,1)S(1)} collective-permute-done((bf16[304,256]{1,0:T(8,128)(2,1)S(1)}, bf16[304,256]{1,0:T(8,128)(2,1)S(1)}, u32[]{:S(2)}, u32[]{:S(2)}) %collective-permute-start.66) | collective-permute-done | bytes 155680 | tf_op jit(solution)/shard_map/ppermute | solution.py:715
  223.8 2.0 shard_map.330
  225.8 2.2 collective-permute-done.67.refs_5_
  228.0 1.7 collective-permute-done.65.refs_3_
  229.6 2.6 %shard_map.329 = (f32[2048,256]{1,0:T(8,128)}, f32[9,8,32,32]{3,2,1,0:T(8,128)}) custom-call(s32[2]{0:T(128)S(1)} %pad_add_fusion.ids, bf16[304,256]{1,0:T(8,128)(2,1)S(1)} %shard_map.328.refs_0_, bf16[304,256]{1,0:T(8,128)(2,1)S(1)} %collective-permute-done.63.refs_1_, bf16[304,256]{1,0:T(8,128)(2,1)S(1)} %collective-permute-done.64.refs_2_, ...), custom_call_target="tpu_custom_call" | custom-call | flops 1048576 | tf_op jit(solution)/shard_map/pallas_call | solution.py:661
  (160 shorter events, 49.5 us)
Async XLA Ops:
  3.1 9.3 %collective-permute-start.3 = (bf16[1392,512]{1,0:T(8,128)(2,1)S(1)}, bf16[1392,512]{1,0:T(8,128)(2,1)S(1)}, u32[]{:S(2)}, u32[]{:S(2)}) collective-permute-start(bf16[1392,512]{1,0:T(8,128)(2,1)S(1)} %shard_map.309.own.x.xs_0__0_), channel_id=1, source_target_pairs={{0,1},{1,0},{2,3},{3,2},{4,5},{5,4},{6,7},{7,6},{8,9},{9,8},{10,11... | collective-permute-start | bytes 4276232 | tf_op jit(solution)/shard_map/ppermute | solution.py:712
  3.6 15.1 %collective-permute-start.2 = (bf16[243,2,512]{2,1,0:T(2,128)(2,1)}, bf16[243,2,512]{2,1,0:T(2,128)(2,1)}, u32[]{:S(2)}, u32[]{:S(2)}) collective-permute-start(bf16[243,2,512]{2,1,0:T(2,128)(2,1)} %bitcast.7.refs_2_), channel_id=1, source_target_pairs={{0,2},{1,3},{2,0},{3,1},{4,6},{5,7},{6,4},{7,5},{8,10},{9,11},{10,... | collective-permute-start | bytes 1493000 | tf_op jit(solution)/shard_map/ppermute | solution.py:712
  6.2 31.6 %collective-permute-start.1 = (bf16[294,2,512]{2,1,0:T(2,128)(2,1)}, bf16[294,2,512]{2,1,0:T(2,128)(2,1)}, u32[]{:S(2)}, u32[]{:S(2)}) collective-permute-start(bf16[294,2,512]{2,1,0:T(2,128)(2,1)} %bitcast.5.refs_1_), channel_id=1, source_target_pairs={{0,2},{1,3},{2,0},{3,1},{4,6},{5,7},{6,4},{7,5},{8,10},{9,11},{10,... | collective-permute-start | bytes 1806344 | tf_op jit(solution)/shard_map/ppermute | solution.py:712
  18.7 19.1 %collective-permute-start = (bf16[150,2,512]{2,1,0:T(2,128)(2,1)S(1)}, bf16[150,2,512]{2,1,0:T(2,128)(2,1)S(1)}, u32[]{:S(2)}, u32[]{:S(2)}) collective-permute-start(bf16[150,2,512]{2,1,0:T(2,128)(2,1)S(1)} %bitcast.108), channel_id=1, source_target_pairs={{0,2},{1,3},{2,0},{3,1},{4,6},{5,7},{6,4},{7,5},{8,10},{9,11},{10,... | collective-permute-start | bytes 921608 | tf_op jit(solution)/shard_map/ppermute | solution.py:712
  37.9 4.2 %collective-permute-start.6 = (bf16[294,2,512]{2,1,0:T(2,128)(2,1)}, bf16[294,2,512]{2,1,0:T(2,128)(2,1)S(1)}, u32[]{:S(2)}, u32[]{:S(2)}) collective-permute-start(bf16[294,2,512]{2,1,0:T(2,128)(2,1)} %collective-permute-done.1.far_1_), channel_id=1, source_target_pairs={{0,1},{1,0},{2,3},{3,2},{4,5},{5,4},{6,7},{7,6},{8,9},{9,8},{10,11... | collective-permute-start | bytes 1806344 | tf_op jit(solution)/shard_map/ppermute | solution.py:712
  37.9 4.2 %collective-permute-start.5 = (bf16[150,2,512]{2,1,0:T(2,128)(2,1)S(1)}, bf16[150,2,512]{2,1,0:T(2,128)(2,1)S(1)}, u32[]{:S(2)}, u32[]{:S(2)}) collective-permute-start(bf16[150,2,512]{2,1,0:T(2,128)(2,1)S(1)} %collective-permute-done.far_0_), channel_id=1, source_target_pairs={{0,1},{1,0},{2,3},{3,2},{4,5},{5,4},{6,7},{7,6},{8,9},{9,8},{10,11... | collective-permute-start | bytes 921608 | tf_op jit(solution)/shard_map/ppermute | solution.py:712
  38.4 16.0 %collective-permute-start.11 = (bf16[512,256]{1,0:T(8,128)(2,1)S(1)}, bf16[512,256]{1,0:T(8,128)(2,1)S(1)}, u32[]{:S(2)}, u32[]{:S(2)}) collective-permute-start(bf16[512,256]{1,0:T(8,128)(2,1)S(1)} %get-tuple-element.177), channel_id=1, source_target_pairs={{0,1},{1,0},{2,3},{3,2},{4,5},{5,4},{6,7},{7,6},{8,9},{9,8},{10,11... | collective-permute-start | bytes 786440 | tf_op jit(solution)/shard_map/ppermute | solution.py:712
  38.4 16.0 %collective-permute-start.12 = (bf16[512,256]{1,0:T(8,128)(2,1)S(1)}, bf16[512,256]{1,0:T(8,128)(2,1)S(1)}, u32[]{:S(2)}, u32[]{:S(2)}) collective-permute-start(bf16[512,256]{1,0:T(8,128)(2,1)S(1)} %get-tuple-element.178), channel_id=1, source_target_pairs={{0,2},{1,3},{2,0},{3,1},{4,6},{5,7},{6,4},{7,5},{8,10},{9,11},{10,... | collective-permute-start | bytes 786440 | tf_op jit(solution)/shard_map/ppermute | solution.py:712
  40.1 14.2 %collective-permute-start.13 = (bf16[512,256]{1,0:T(8,128)(2,1)S(1)}, bf16[512,256]{1,0:T(8,128)(2,1)S(1)}, u32[]{:S(2)}, u32[]{:S(2)}) collective-permute-start(bf16[512,256]{1,0:T(8,128)(2,1)S(1)} %get-tuple-element.179), channel_id=1, source_target_pairs={{0,3},{1,2},{2,1},{3,0},{4,7},{5,6},{6,5},{7,4},{8,11},{9,10},{10,... | collective-permute-start | bytes 786440 | tf_op jit(solution)/shard_map/ppermute | solution.py:712
  43.5 5.5 %collective-permute-start.9 = (f32[8,256]{1,0:T(8,128)S(1)}, f32[8,256]{1,0:T(8,128)S(1)}, u32[]{:S(2)}, u32[]{:S(2)}) collective-permute-start(f32[8,256]{1,0:T(8,128)S(1)} %get-tuple-element.171), channel_id=1, source_target_pairs={{0,24},{4,28},{8,16},{12,20},{16,8},{20,12},{24,0},{28,4},{1,25},{... | collective-permute-start | bytes 24584 | tf_op jit(solution)/shard_map/ppermute | solution.py:715
  47.3 4.5 %collective-permute-start.8 = (f32[8,256]{1,0:T(8,128)S(1)}, f32[8,256]{1,0:T(8,128)S(1)}, u32[]{:S(2)}, u32[]{:S(2)}) collective-permute-start(f32[8,256]{1,0:T(8,128)S(1)} %get-tuple-element.171), channel_id=1, source_target_pairs={{0,16},{4,20},{8,24},{12,28},{16,0},{20,4},{24,8},{28,12},{1,17},{... | collective-permute-start | bytes 24584 | tf_op jit(solution)/shard_map/ppermute | solution.py:715
  61.3 15.4 %collective-permute-start.15 = (bf16[1392,256]{1,0:T(8,128)(2,1)S(1)}, bf16[1392,256]{1,0:T(8,128)(2,1)S(1)}, u32[]{:S(2)}, u32[]{:S(2)}) collective-permute-start(bf16[1392,256]{1,0:T(8,128)(2,1)S(1)} %get-tuple-element.183.zs_0_), channel_id=1, source_target_pairs={{0,2},{1,3},{2,0},{3,1},{4,6},{5,7},{6,4},{7,5},{8,10},{9,11},{10,... | collective-permute-start | bytes 2138120 | tf_op jit(solution)/shard_map/ppermute | solution.py:712
  63.1 5.4 %collective-permute-start.18 = (f32[8,256]{1,0:T(8,128)S(1)}, f32[8,256]{1,0:T(8,128)S(1)}, u32[]{:S(2)}, u32[]{:S(2)}) collective-permute-start(f32[8,256]{1,0:T(8,128)S(1)} %get-tuple-element.184), channel_id=1, source_target_pairs={{0,24},{4,28},{8,16},{12,20},{16,8},{20,12},{24,0},{28,4},{1,25},{... | collective-permute-start | bytes 24584 | tf_op jit(solution)/shard_map/ppermute | solution.py:715
  66.7 4.5 %collective-permute-start.17 = (f32[8,256]{1,0:T(8,128)S(1)}, f32[8,256]{1,0:T(8,128)S(1)}, u32[]{:S(2)}, u32[]{:S(2)}) collective-permute-start(f32[8,256]{1,0:T(8,128)S(1)} %get-tuple-element.184), channel_id=1, source_target_pairs={{0,16},{4,20},{8,24},{12,28},{16,0},{20,4},{24,8},{28,12},{1,17},{... | collective-permute-start | bytes 24584 | tf_op jit(solution)/shard_map/ppermute | solution.py:715
  66.7 4.5 %collective-permute-start.16 = (f32[8,256]{1,0:T(8,128)S(1)}, f32[8,256]{1,0:T(8,128)S(1)}, u32[]{:S(2)}, u32[]{:S(2)}) collective-permute-start(f32[8,256]{1,0:T(8,128)S(1)} %get-tuple-element.184), channel_id=1, source_target_pairs={{0,8},{4,12},{8,0},{12,4},{16,24},{20,28},{24,16},{28,20},{1,9},{5... | collective-permute-start | bytes 24584 | tf_op jit(solution)/shard_map/ppermute | solution.py:715
  71.2 3.7 %collective-permute-start.19 = (f32[8,256]{1,0:T(8,128)S(1)}, f32[8,256]{1,0:T(8,128)S(1)}, u32[]{:S(2)}, u32[]{:S(2)}) collective-permute-start(f32[8,256]{1,0:T(8,128)S(1)} %add_add_fusion.4.sums_0_.sums2_0_), channel_id=1, source_target_pairs={{0,4},{4,0},{8,12},{12,8},{16,20},{20,16},{24,28},{28,24},{1,5},{5... | collective-permute-start | bytes 24584 | tf_op jit(solution)/shard_map/ppermute | solution.py:715
  75.1 7.0 %collective-permute-start.14 = (bf16[1392,256]{1,0:T(8,128)(2,1)S(1)}, bf16[1392,256]{1,0:T(8,128)(2,1)S(1)}, u32[]{:S(2)}, u32[]{:S(2)}) collective-permute-start(bf16[1392,256]{1,0:T(8,128)(2,1)S(1)} %get-tuple-element.183.zs_0_), channel_id=1, source_target_pairs={{0,1},{1,0},{2,3},{3,2},{4,5},{5,4},{6,7},{7,6},{8,9},{9,8},{10,11... | collective-permute-start | bytes 2138120 | tf_op jit(solution)/shard_map/ppermute | solution.py:712
  76.6 5.4 %collective-permute-start.21 = (bf16[1392,256]{1,0:T(8,128)(2,1)S(1)}, bf16[1392,256]{1,0:T(8,128)(2,1)S(1)}, u32[]{:S(2)}, u32[]{:S(2)}) collective-permute-start(bf16[1392,256]{1,0:T(8,128)(2,1)S(1)} %collective-permute-done.15.zs_2_), channel_id=1, source_target_pairs={{0,1},{1,0},{2,3},{3,2},{4,5},{5,4},{6,7},{7,6},{8,9},{9,8},{10,11... | collective-permute-start | bytes 2138120 | tf_op jit(solution)/shard_map/ppermute | solution.py:712
  78.2 3.8 %collective-permute-start.22 = (f32[24,256]{1,0:T(8,128)S(1)}, f32[24,256]{1,0:T(8,128)S(1)}, u32[]{:S(2)}, u32[]{:S(2)}) collective-permute-start(f32[24,256]{1,0:T(8,128)S(1)} %shard_map.315.stats_0_), channel_id=1, source_target_pairs={{0,2},{1,3},{2,0},{3,1},{4,6},{5,7},{6,4},{7,5},{8,10},{9,11},{10,... | collective-permute-start | bytes 73736 | tf_op jit(solution)/shard_map/ppermute | solution.py:712
  86.9 12.7 %collective-permute-start.24 = (bf16[512,256]{1,0:T(8,128)(2,1)S(1)}, bf16[512,256]{1,0:T(8,128)(2,1)S(1)}, u32[]{:S(2)}, u32[]{:S(2)}) collective-permute-start(bf16[512,256]{1,0:T(8,128)(2,1)S(1)} %get-tuple-element.196), channel_id=1, source_target_pairs={{0,1},{1,0},{2,3},{3,2},{4,5},{5,4},{6,7},{7,6},{8,9},{9,8},{10,11... | collective-permute-start | bytes 786440 | tf_op jit(solution)/shard_map/ppermute | solution.py:712
  87.0 12.6 %collective-permute-start.25 = (bf16[512,256]{1,0:T(8,128)(2,1)S(1)}, bf16[512,256]{1,0:T(8,128)(2,1)S(1)}, u32[]{:S(2)}, u32[]{:S(2)}) collective-permute-start(bf16[512,256]{1,0:T(8,128)(2,1)S(1)} %get-tuple-element.197), channel_id=1, source_target_pairs={{0,2},{1,3},{2,0},{3,1},{4,6},{5,7},{6,4},{7,5},{8,10},{9,11},{10,... | collective-permute-start | bytes 786440 | tf_op jit(solution)/shard_map/ppermute | solution.py:712
  87.6 5.5 %collective-permute-start.28 = (f32[8,512]{1,0:T(8,128)S(1)}, f32[8,512]{1,0:T(8,128)S(1)}, u32[]{:S(2)}, u32[]{:S(2)}) collective-permute-start(f32[8,512]{1,0:T(8,128)S(1)} %get-tuple-element.198), channel_id=1, source_target_pairs={{0,24},{4,28},{8,16},{12,20},{16,8},{20,12},{24,0},{28,4},{1,25},{... | collective-permute-start | bytes 49160 | tf_op jit(solution)/shard_map/ppermute | solution.py:715
  91.1 4.6 %collective-permute-start.27 = (f32[8,512]{1,0:T(8,128)S(1)}, f32[8,512]{1,0:T(8,128)S(1)}, u32[]{:S(2)}, u32[]{:S(2)}) collective-permute-start(f32[8,512]{1,0:T(8,128)S(1)} %get-tuple-element.198), channel_id=1, source_target_pairs={{0,16},{4,20},{8,24},{12,28},{16,0},{20,4},{24,8},{28,12},{1,17},{... | collective-permute-start | bytes 49160 | tf_op jit(solution)/shard_map/ppermute | solution.py:715
  91.1 4.6 %collective-permute-start.26 = (f32[8,512]{1,0:T(8,128)S(1)}, f32[8,512]{1,0:T(8,128)S(1)}, u32[]{:S(2)}, u32[]{:S(2)}) collective-permute-start(f32[8,512]{1,0:T(8,128)S(1)} %get-tuple-element.198), channel_id=1, source_target_pairs={{0,8},{4,12},{8,0},{12,4},{16,24},{20,28},{24,16},{28,20},{1,9},{5... | collective-permute-start | bytes 49160 | tf_op jit(solution)/shard_map/ppermute | solution.py:715
  95.8 3.8 %collective-permute-start.29 = (f32[8,512]{1,0:T(8,128)S(1)}, f32[8,512]{1,0:T(8,128)S(1)}, u32[]{:S(2)}, u32[]{:S(2)}) collective-permute-start(f32[8,512]{1,0:T(8,128)S(1)} %add_add_fusion.1.sums3_0_), channel_id=1, source_target_pairs={{0,4},{4,0},{8,12},{12,8},{16,20},{20,16},{24,28},{28,24},{1,5},{5... | collective-permute-start | bytes 49160 | tf_op jit(solution)/shard_map/ppermute | solution.py:715
  101.9 10.7 %collective-permute-start.30 = (bf16[512,256]{1,0:T(8,128)(2,1)S(1)}, bf16[512,256]{1,0:T(8,128)(2,1)S(1)}, u32[]{:S(2)}, u32[]{:S(2)}) collective-permute-start(bf16[512,256]{1,0:T(8,128)(2,1)S(1)} %get-tuple-element.205), channel_id=1, source_target_pairs={{0,3},{1,2},{2,1},{3,0},{4,7},{5,6},{6,5},{7,4},{8,11},{9,10},{10,... | collective-permute-start | bytes 786440 | tf_op jit(solution)/shard_map/ppermute | solution.py:712
  102.0 5.6 %collective-permute-start.33 = (f32[8,512]{1,0:T(8,128)S(1)}, f32[8,512]{1,0:T(8,128)S(1)}, u32[]{:S(2)}, u32[]{:S(2)}) collective-permute-start(f32[8,512]{1,0:T(8,128)S(1)} %get-tuple-element.206), channel_id=1, source_target_pairs={{0,24},{4,28},{8,16},{12,20},{16,8},{20,12},{24,0},{28,4},{1,25},{... | collective-permute-start | bytes 49160 | tf_op jit(solution)/shard_map/ppermute | solution.py:715
  103.5 4.9 %collective-permute-start.32 = (f32[8,512]{1,0:T(8,128)S(1)}, f32[8,512]{1,0:T(8,128)S(1)}, u32[]{:S(2)}, u32[]{:S(2)}) collective-permute-start(f32[8,512]{1,0:T(8,128)S(1)} %get-tuple-element.206), channel_id=1, source_target_pairs={{0,16},{4,20},{8,24},{12,28},{16,0},{20,4},{24,8},{28,12},{1,17},{... | collective-permute-start | bytes 49160 | tf_op jit(solution)/shard_map/ppermute | solution.py:715
  104.2 4.7 %collective-permute-start.31 = (f32[8,512]{1,0:T(8,128)S(1)}, f32[8,512]{1,0:T(8,128)S(1)}, u32[]{:S(2)}, u32[]{:S(2)}) collective-permute-start(f32[8,512]{1,0:T(8,128)S(1)} %get-tuple-element.206), channel_id=1, source_target_pairs={{0,8},{4,12},{8,0},{12,4},{16,24},{20,28},{24,16},{28,20},{1,9},{5... | collective-permute-start | bytes 49160 | tf_op jit(solution)/shard_map/ppermute | solution.py:715
  108.9 3.8 %collective-permute-start.34 = (f32[8,512]{1,0:T(8,128)S(1)}, f32[8,512]{1,0:T(8,128)S(1)}, u32[]{:S(2)}, u32[]{:S(2)}) collective-permute-start(f32[8,512]{1,0:T(8,128)S(1)} %add_add_fusion.sums4_0_), channel_id=1, source_target_pairs={{0,4},{4,0},{8,12},{12,8},{16,20},{20,16},{24,28},{28,24},{1,5},{5... | collective-permute-start | bytes 49160 | tf_op jit(solution)/shard_map/ppermute | solution.py:715
  115.3 5.3 %collective-permute-start.35 = (bf16[2,1392,256]{2,1,0:T(8,128)(2,1)S(1)}, bf16[2,1392,256]{2,1,0:T(8,128)(2,1)S(1)}, u32[]{:S(2)}, u32[]{:S(2)}) collective-permute-start(bf16[2,1392,256]{2,1,0:T(8,128)(2,1)S(1)} %get-tuple-element.211), channel_id=1, source_target_pairs={{0,1},{1,0},{2,3},{3,2},{4,5},{5,4},{6,7},{7,6},{8,9},{9,8},{10,11... | collective-permute-start | bytes 4276232 | tf_op jit(solution)/shard_map/ppermute | solution.py:712
  117.7 8.8 %collective-permute-start.37 = (bf16[2,4,32,512]{3,2,1,0:T(8,128)(2,1)S(1)}, bf16[2,4,32,512]{3,2,1,0:T(8,128)(2,1)S(1)}, u32[]{:S(2)}, u32[]{:S(2)}) collective-permute-start(bf16[2,4,32,512]{3,2,1,0:T(8,128)(2,1)S(1)} %get-tuple-element.227), channel_id=1, source_target_pairs={{0,4},{4,0},{8,12},{12,8},{16,20},{20,16},{24,28},{28,24},{1,5},{5... | collective-permute-start | bytes 786440 | tf_op jit(solution)/shard_map/ppermute | solution.py:715
  120.8 18.2 %collective-permute-start.36 = (bf16[1392,256]{1,0:T(8,128)(2,1)S(1)}, bf16[1392,256]{1,0:T(8,128)(2,1)S(1)}, u32[]{:S(2)}, u32[]{:S(2)}) collective-permute-start(bf16[1392,256]{1,0:T(8,128)(2,1)S(1)} %fusion), channel_id=1, source_target_pairs={{0,2},{1,3},{2,0},{3,1},{4,6},{5,7},{6,4},{7,5},{8,10},{9,11},{10,... | collective-permute-start | bytes 2138120 | tf_op jit(solution)/shard_map/ppermute | solution.py:712
  126.5 7.9 %collective-permute-start.38 = (bf16[2,4,32,512]{3,2,1,0:T(8,128)(2,1)S(1)}, bf16[2,4,32,512]{3,2,1,0:T(8,128)(2,1)S(1)}, u32[]{:S(2)}, u32[]{:S(2)}) collective-permute-start(bf16[2,4,32,512]{3,2,1,0:T(8,128)(2,1)S(1)} %get-tuple-element.228), channel_id=1, source_target_pairs={{0,4},{4,0},{8,12},{12,8},{16,20},{20,16},{24,28},{28,24},{1,5},{5... | collective-permute-start | bytes 786440 | tf_op jit(solution)/shard_map/ppermute | solution.py:715
  128.0 10.9 %collective-permute-start.41 = (bf16[4,32,512]{2,1,0:T(8,128)(2,1)S(1)}, bf16[4,32,512]{2,1,0:T(8,128)(2,1)S(1)}, u32[]{:S(2)}, u32[]{:S(2)}) collective-permute-start(bf16[4,32,512]{2,1,0:T(8,128)(2,1)S(1)} %get-tuple-element.317), channel_id=1, source_target_pairs={{0,24},{4,28},{8,16},{12,20},{16,8},{20,12},{24,0},{28,4},{1,25},{... | collective-permute-start | bytes 393224 | tf_op jit(solution)/shard_map/ppermute | solution.py:715
  130.4 12.0 %collective-permute-start.40 = (bf16[4,32,512]{2,1,0:T(8,128)(2,1)S(1)}, bf16[4,32,512]{2,1,0:T(8,128)(2,1)S(1)}, u32[]{:S(2)}, u32[]{:S(2)}) collective-permute-start(bf16[4,32,512]{2,1,0:T(8,128)(2,1)S(1)} %get-tuple-element.318), channel_id=1, source_target_pairs={{0,16},{4,20},{8,24},{12,28},{16,0},{20,4},{24,8},{28,12},{1,17},{... | collective-permute-start | bytes 393224 | tf_op jit(solution)/shard_map/ppermute | solution.py:715
  134.5 7.9 %collective-permute-start.39 = (bf16[4,32,512]{2,1,0:T(8,128)(2,1)S(1)}, bf16[4,32,512]{2,1,0:T(8,128)(2,1)S(1)}, u32[]{:S(2)}, u32[]{:S(2)}) collective-permute-start(bf16[4,32,512]{2,1,0:T(8,128)(2,1)S(1)} %get-tuple-element.319), channel_id=1, source_target_pairs={{0,8},{4,12},{8,0},{12,4},{16,24},{20,28},{24,16},{28,20},{1,9},{5... | collective-permute-start | bytes 393224 | tf_op jit(solution)/shard_map/ppermute | solution.py:715
  143.9 5.9 %collective-permute-start.44 = (f32[8,256]{1,0:T(8,128)S(1)}, f32[8,256]{1,0:T(8,128)S(1)}, u32[]{:S(2)}, u32[]{:S(2)}) collective-permute-start(f32[8,256]{1,0:T(8,128)S(1)} %get-tuple-element.239), channel_id=1, source_target_pairs={{0,24},{4,28},{8,16},{12,20},{16,8},{20,12},{24,0},{28,4},{1,25},{... | collective-permute-start | bytes 24584 | tf_op jit(solution)/shard_map/ppermute | solution.py:715
  145.9 4.5 %collective-permute-start.43 = (f32[8,256]{1,0:T(8,128)S(1)}, f32[8,256]{1,0:T(8,128)S(1)}, u32[]{:S(2)}, u32[]{:S(2)}) collective-permute-start(f32[8,256]{1,0:T(8,128)S(1)} %get-tuple-element.239), channel_id=1, source_target_pairs={{0,16},{4,20},{8,24},{12,28},{16,0},{20,4},{24,8},{28,12},{1,17},{... | collective-permute-start | bytes 24584 | tf_op jit(solution)/shard_map/ppermute | solution.py:715
  145.9 4.5 %collective-permute-start.42 = (f32[8,256]{1,0:T(8,128)S(1)}, f32[8,256]{1,0:T(8,128)S(1)}, u32[]{:S(2)}, u32[]{:S(2)}) collective-permute-start(f32[8,256]{1,0:T(8,128)S(1)} %get-tuple-element.239), channel_id=1, source_target_pairs={{0,8},{4,12},{8,0},{12,4},{16,24},{20,28},{24,16},{28,20},{1,9},{5... | collective-permute-start | bytes 24584 | tf_op jit(solution)/shard_map/ppermute | solution.py:715
  148.4 5.9 %collective-permute-start.48 = (bf16[32,512]{1,0:T(8,128)(2,1)S(1)}, bf16[32,512]{1,0:T(8,128)(2,1)S(1)}, u32[]{:S(2)}, u32[]{:S(2)}) collective-permute-start(bf16[32,512]{1,0:T(8,128)(2,1)S(1)} %get-tuple-element.322), channel_id=1, source_target_pairs={{0,3},{1,2},{2,1},{3,0},{4,7},{5,6},{6,5},{7,4},{8,11},{9,10},{10,... | collective-permute-start | bytes 98312 | tf_op jit(solution)/shard_map/ppermute | solution.py:712
  148.4 5.8 %collective-permute-start.47 = (bf16[32,512]{1,0:T(8,128)(2,1)S(1)}, bf16[32,512]{1,0:T(8,128)(2,1)S(1)}, u32[]{:S(2)}, u32[]{:S(2)}) collective-permute-start(bf16[32,512]{1,0:T(8,128)(2,1)S(1)} %get-tuple-element.323), channel_id=1, source_target_pairs={{0,2},{1,3},{2,0},{3,1},{4,6},{5,7},{6,4},{7,5},{8,10},{9,11},{10,... | collective-permute-start | bytes 98312 | tf_op jit(solution)/shard_map/ppermute | solution.py:712
  149.8 4.4 %collective-permute-start.46 = (bf16[32,512]{1,0:T(8,128)(2,1)S(1)}, bf16[32,512]{1,0:T(8,128)(2,1)S(1)}, u32[]{:S(2)}, u32[]{:S(2)}) collective-permute-start(bf16[32,512]{1,0:T(8,128)(2,1)S(1)} %get-tuple-element.324), channel_id=1, source_target_pairs={{0,1},{1,0},{2,3},{3,2},{4,5},{5,4},{6,7},{7,6},{8,9},{9,8},{10,11... | collective-permute-start | bytes 98312 | tf_op jit(solution)/shard_map/ppermute | solution.py:712
  159.7 5.4 %collective-permute-start.51 = (f32[8,256]{1,0:T(8,128)S(1)}, f32[8,256]{1,0:T(8,128)S(1)}, u32[]{:S(2)}, u32[]{:S(2)}) collective-permute-start(f32[8,256]{1,0:T(8,128)S(1)} %get-tuple-element.245), channel_id=1, source_target_pairs={{0,24},{4,28},{8,16},{12,20},{16,8},{20,12},{24,0},{28,4},{1,25},{... | collective-permute-start | bytes 24584 | tf_op jit(solution)/shard_map/ppermute | solution.py:715
  161.5 4.5 %collective-permute-start.50 = (f32[8,256]{1,0:T(8,128)S(1)}, f32[8,256]{1,0:T(8,128)S(1)}, u32[]{:S(2)}, u32[]{:S(2)}) collective-permute-start(f32[8,256]{1,0:T(8,128)S(1)} %get-tuple-element.245), channel_id=1, source_target_pairs={{0,16},{4,20},{8,24},{12,28},{16,0},{20,4},{24,8},{28,12},{1,17},{... | collective-permute-start | bytes 24584 | tf_op jit(solution)/shard_map/ppermute | solution.py:715
  166.3 4.8 %collective-permute-start.52 = (f32[8,256]{1,0:T(8,128)S(1)}, f32[8,256]{1,0:T(8,128)S(1)}, u32[]{:S(2)}, u32[]{:S(2)}) collective-permute-start(f32[8,256]{1,0:T(8,128)S(1)} %add_add_fusion.2.sums6_0_), channel_id=1, source_target_pairs={{0,4},{4,0},{8,12},{12,8},{16,20},{20,16},{24,28},{28,24},{1,5},{5... | collective-permute-start | bytes 24584 | tf_op jit(solution)/shard_map/ppermute | solution.py:715
  173.4 12.8 %collective-permute-start.53 = (bf16[4,304,256]{2,1,0:T(8,128)(2,1)S(1)}, bf16[4,304,256]{2,1,0:T(8,128)(2,1)S(1)}, u32[]{:S(2)}, u32[]{:S(2)}) collective-permute-start(bf16[4,304,256]{2,1,0:T(8,128)(2,1)S(1)} %get-tuple-element.262), channel_id=1, source_target_pairs={{0,4},{4,0},{8,12},{12,8},{16,20},{20,16},{24,28},{28,24},{1,5},{5... | collective-permute-start | bytes 1867784 | tf_op jit(solution)/shard_map/ppermute | solution.py:715
  174.3 14.6 %collective-permute-start.60 = (bf16[1392,256]{1,0:T(8,128)(2,1)S(1)}, bf16[1392,256]{1,0:T(8,128)(2,1)S(1)}, u32[]{:S(2)}, u32[]{:S(2)}) collective-permute-start(bf16[1392,256]{1,0:T(8,128)(2,1)S(1)} %get-tuple-element.269.dz.d0), channel_id=1, source_target_pairs={{0,2},{1,3},{2,0},{3,1},{4,6},{5,7},{6,4},{7,5},{8,10},{9,11},{10,... | collective-permute-start | bytes 2138120 | tf_op jit(solution)/shard_map/ppermute | solution.py:712
  175.6 10.8 %collective-permute-start.56 = (bf16[4,32,512]{2,1,0:T(8,128)(2,1)S(1)}, bf16[4,32,512]{2,1,0:T(8,128)(2,1)S(1)}, u32[]{:S(2)}, u32[]{:S(2)}) collective-permute-start(bf16[4,32,512]{2,1,0:T(8,128)(2,1)S(1)} %pad_maximum_fusion.5.refs_0_), channel_id=1, source_target_pairs={{0,24},{4,28},{8,16},{12,20},{16,8},{20,12},{24,0},{28,4},{1,25},{... | collective-permute-start | bytes 393224 | tf_op jit(solution)/shard_map/ppermute | solution.py:715
  177.3 9.3 %collective-permute-start.55 = (bf16[4,32,512]{2,1,0:T(8,128)(2,1)S(1)}, bf16[4,32,512]{2,1,0:T(8,128)(2,1)S(1)}, u32[]{:S(2)}, u32[]{:S(2)}) collective-permute-start(bf16[4,32,512]{2,1,0:T(8,128)(2,1)S(1)} %pad_maximum_fusion.5.refs_0_), channel_id=1, source_target_pairs={{0,16},{4,20},{8,24},{12,28},{16,0},{20,4},{24,8},{28,12},{1,17},{... | collective-permute-start | bytes 393224 | tf_op jit(solution)/shard_map/ppermute | solution.py:715
  178.3 8.3 %collective-permute-start.54 = (bf16[4,32,512]{2,1,0:T(8,128)(2,1)S(1)}, bf16[4,32,512]{2,1,0:T(8,128)(2,1)S(1)}, u32[]{:S(2)}, u32[]{:S(2)}) collective-permute-start(bf16[4,32,512]{2,1,0:T(8,128)(2,1)S(1)} %pad_maximum_fusion.5.refs_0_), channel_id=1, source_target_pairs={{0,8},{4,12},{8,0},{12,4},{16,24},{20,28},{24,16},{28,20},{1,9},{5... | collective-permute-start | bytes 393224 | tf_op jit(solution)/shard_map/ppermute | solution.py:715
  188.9 4.2 %collective-permute-start.61 = (bf16[1392,256]{1,0:T(8,128)(2,1)S(1)}, bf16[1392,256]{1,0:T(8,128)(2,1)S(1)}, u32[]{:S(2)}, u32[]{:S(2)}) collective-permute-start(bf16[1392,256]{1,0:T(8,128)(2,1)S(1)} %get-tuple-element.269.dz.d0), channel_id=1, source_target_pairs={{0,1},{1,0},{2,3},{3,2},{4,5},{5,4},{6,7},{7,6},{8,9},{9,8},{10,11... | collective-permute-start | bytes 2138120 | tf_op jit(solution)/shard_map/ppermute | solution.py:712
  188.9 6.1 %collective-permute-start.62 = (bf16[1392,256]{1,0:T(8,128)(2,1)S(1)}, bf16[1392,256]{1,0:T(8,128)(2,1)S(1)}, u32[]{:S(2)}, u32[]{:S(2)}) collective-permute-start(bf16[1392,256]{1,0:T(8,128)(2,1)S(1)} %collective-permute-done.60.d2), channel_id=1, source_target_pairs={{0,1},{1,0},{2,3},{3,2},{4,5},{5,4},{6,7},{7,6},{8,9},{9,8},{10,11... | collective-permute-start | bytes 2138120 | tf_op jit(solution)/shard_map/ppermute | solution.py:712
  189.4 34.3 %collective-permute-start.70 = (bf16[4,4,32,512]{3,2,1,0:T(8,128)(2,1)S(1)}, bf16[4,4,32,512]{3,2,1,0:T(8,128)(2,1)S(1)}, u32[]{:S(2)}, u32[]{:S(2)}) collective-permute-start(bf16[4,4,32,512]{3,2,1,0:T(8,128)(2,1)S(1)} %pad_maximum_fusion), channel_id=1, source_target_pairs={{0,4},{4,0},{8,12},{12,8},{16,20},{20,16},{24,28},{28,24},{1,5},{5... | collective-permute-start | bytes 1572872 | tf_op jit(solution)/shard_map/ppermute | solution.py:715
  190.5 8.4 %collective-permute-start.57 = (bf16[304,256]{1,0:T(8,128)(2,1)S(1)}, bf16[304,256]{1,0:T(8,128)(2,1)S(1)}, u32[]{:S(2)}, u32[]{:S(2)}) collective-permute-start(bf16[304,256]{1,0:T(8,128)(2,1)S(1)} %get-tuple-element.265), channel_id=1, source_target_pairs={{0,8},{4,12},{8,0},{12,4},{16,24},{20,28},{24,16},{28,20},{1,9},{5... | collective-permute-start | bytes 466952 | tf_op jit(solution)/shard_map/ppermute | solution.py:715
  192.1 14.4 %collective-permute-start.58 = (bf16[304,256]{1,0:T(8,128)(2,1)S(1)}, bf16[304,256]{1,0:T(8,128)(2,1)S(1)}, u32[]{:S(2)}, u32[]{:S(2)}) collective-permute-start(bf16[304,256]{1,0:T(8,128)(2,1)S(1)} %get-tuple-element.266), channel_id=1, source_target_pairs={{0,16},{4,20},{8,24},{12,28},{16,0},{20,4},{24,8},{28,12},{1,17},{... | collective-permute-start | bytes 466952 | tf_op jit(solution)/shard_map/ppermute | solution.py:715
  193.1 13.3 %collective-permute-start.59 = (bf16[304,256]{1,0:T(8,128)(2,1)S(1)}, bf16[304,256]{1,0:T(8,128)(2,1)S(1)}, u32[]{:S(2)}, u32[]{:S(2)}) collective-permute-start(bf16[304,256]{1,0:T(8,128)(2,1)S(1)} %get-tuple-element.267), channel_id=1, source_target_pairs={{0,24},{4,28},{8,16},{12,20},{16,8},{20,12},{24,0},{28,4},{1,25},{... | collective-permute-start | bytes 466952 | tf_op jit(solution)/shard_map/ppermute | solution.py:715
  206.6 8.8 %collective-permute-start.68 = (bf16[304,256]{1,0:T(8,128)(2,1)S(1)}, bf16[304,256]{1,0:T(8,128)(2,1)S(1)}, u32[]{:S(2)}, u32[]{:S(2)}) collective-permute-start(bf16[304,256]{1,0:T(8,128)(2,1)S(1)} %shard_map.328.refs_0_), channel_id=1, source_target_pairs={{0,24},{4,28},{8,16},{12,20},{16,8},{20,12},{24,0},{28,4},{1,25},{... | collective-permute-start | bytes 466952 | tf_op jit(solution)/shard_map/ppermute | solution.py:715
  208.6 13.2 %collective-permute-start.66 = (bf16[304,256]{1,0:T(8,128)(2,1)S(1)}, bf16[304,256]{1,0:T(8,128)(2,1)S(1)}, u32[]{:S(2)}, u32[]{:S(2)}) collective-permute-start(bf16[304,256]{1,0:T(8,128)(2,1)S(1)} %shard_map.328.refs_0_), channel_id=1, source_target_pairs={{0,16},{4,20},{8,24},{12,28},{16,0},{20,4},{24,8},{28,12},{1,17},{... | collective-permute-start | bytes 466952 | tf_op jit(solution)/shard_map/ppermute | solution.py:715
  212.4 10.2 %collective-permute-start.64 = (bf16[304,256]{1,0:T(8,128)(2,1)S(1)}, bf16[304,256]{1,0:T(8,128)(2,1)S(1)}, u32[]{:S(2)}, u32[]{:S(2)}) collective-permute-start(bf16[304,256]{1,0:T(8,128)(2,1)S(1)} %shard_map.328.refs_0_), channel_id=1, source_target_pairs={{0,8},{4,12},{8,0},{12,4},{16,24},{20,28},{24,16},{28,20},{1,9},{5... | collective-permute-start | bytes 466952 | tf_op jit(solution)/shard_map/ppermute | solution.py:715
  212.4 13.4 %collective-permute-start.63 = (bf16[304,256]{1,0:T(8,128)(2,1)S(1)}, bf16[304,256]{1,0:T(8,128)(2,1)S(1)}, u32[]{:S(2)}, u32[]{:S(2)}) collective-permute-start(bf16[304,256]{1,0:T(8,128)(2,1)S(1)} %shard_map.328.refs_0_), channel_id=1, source_target_pairs={{0,4},{4,0},{8,12},{12,8},{16,20},{20,16},{24,28},{28,24},{1,5},{5... | collective-permute-start | bytes 466952 | tf_op jit(solution)/shard_map/ppermute | solution.py:715
  215.3 10.5 %collective-permute-start.69 = (bf16[304,256]{1,0:T(8,128)(2,1)S(1)}, bf16[304,256]{1,0:T(8,128)(2,1)S(1)}, u32[]{:S(2)}, u32[]{:S(2)}) collective-permute-start(bf16[304,256]{1,0:T(8,128)(2,1)S(1)} %collective-permute-done.68.refs_6_), channel_id=1, source_target_pairs={{0,4},{4,0},{8,12},{12,8},{16,20},{20,16},{24,28},{28,24},{1,5},{5... | collective-permute-start | bytes 466952 | tf_op jit(solution)/shard_map/ppermute | solution.py:715
  221.7 6.3 %collective-permute-start.67 = (bf16[304,256]{1,0:T(8,128)(2,1)S(1)}, bf16[304,256]{1,0:T(8,128)(2,1)S(1)}, u32[]{:S(2)}, u32[]{:S(2)}) collective-permute-start(bf16[304,256]{1,0:T(8,128)(2,1)S(1)} %collective-permute-done.66.refs_4_), channel_id=1, source_target_pairs={{0,4},{4,0},{8,12},{12,8},{16,20},{20,16},{24,28},{28,24},{1,5},{5... | collective-permute-start | bytes 466952 | tf_op jit(solution)/shard_map/ppermute | solution.py:715
  222.6 7.1 %collective-permute-start.65 = (bf16[304,256]{1,0:T(8,128)(2,1)S(1)}, bf16[304,256]{1,0:T(8,128)(2,1)S(1)}, u32[]{:S(2)}, u32[]{:S(2)}) collective-permute-start(bf16[304,256]{1,0:T(8,128)(2,1)S(1)} %collective-permute-done.64.refs_2_), channel_id=1, source_target_pairs={{0,4},{4,0},{8,12},{12,8},{16,20},{20,16},{24,28},{28,24},{1,5},{5... | collective-permute-start | bytes 466952 | tf_op jit(solution)/shard_map/ppermute | solution.py:715
  (26 other events, 176.5 us)

commit v4 on v3

--- a/solution.py
+++ b/solution.py
@@ -228,7 +228,7 @@
         z_out[rows, :] = acc + mm(near[rows, :], weight[jnp.bitwise_xor(t, 1)])
         return 0
 
-    lax.fori_loop(0, lay.parts, step, 0)
+    lax.fori_loop(0, lay.parts, step, 0, unroll=True)
 
 
 def reduce_last_kernel(lay, ids, far, cross, weight, z, mask, far_out, cross_out, z_out, part_out):
@@ -252,7 +252,7 @@
         z_out[rows, :] = z[rows, :] + mm(far_out[rows, :], weight[jnp.bitwise_xor(ids[0], 2)])
         return 0
 
-    lax.fori_loop(0, 2, step, 0)
+    lax.fori_loop(0, 2, step, 0, unroll=True)
 
 
 def reduce_end_kernel(
@@ -270,24 +270,25 @@
         found = tiles(acc)
         return masked_sums(found, found, widen(tiles(mask[rows, :]), width), carry)
 
-    sums, squares = lax.fori_loop(0, 2, step, (part[0], part[1]))
+    sums, squares = lax.fori_loop(0, 2, step, (part[0], part[1]), unroll=True)
     sums_out[...] = pack(sums, squares, widen(count[...], width))
 
 
-def windows(lay, slabs, bits, image, sign):
+def windows(lay, slabs, bits, image, sign, low, high, taps=range(9)):
     groups = slabs.shape[0]
     for edge, start, size in lay.segments():
-        for tap in range(9):
+        first, last = max(start, low), min(start + size, high)
+        if first >= last:
+            continue
+        for tap in taps:
             shift = sign * lay.micro * ((tap // 3 - 1) * edge + tap % 3 - 1)
             which = tap if sign > 0 else 8 - tap
-            valid = jnp.bitwise_and(bits[start : start + size, :], 1 << which) != 0
+            valid = jnp.bitwise_and(bits[first:last, :], 1 << which) != 0
             for group in range(groups):
-                low = HALO + start + shift
-                moved = slabs[group, low : low + size, :]
+                moved = slabs[group, HALO + first + shift : HALO + last + shift, :]
                 column = (tap * groups + group) * LANES
-                image[start : start + size, column : column + LANES] = jnp.where(
-                    valid, moved, 0.0
-                ).astype(BF16)
+                found = moved if tap == 4 else jnp.where(valid, moved, 0.0)
+                image[first:last, column : column + LANES] = found.astype(BF16)
 
 
 def clear_halo(lay, slabs):
@@ -317,17 +318,18 @@
         to_slabs(slabs, i, a.astype(F32))
         return 0
 
-    lax.fori_loop(0, lay.rows // STEP, activate, 0)
-    windows(lay, slabs, bits, image, 1)
-
+    lax.fori_loop(0, lay.rows // STEP, activate, 0, unroll=True)
     def step(part, carry):
-        rows = at(part * lay.part, lay.part)
+        rows = slice(part * lay.part, (part + 1) * lay.part)
+        windows(lay, slabs, bits, image, 1, rows.start, rows.stop)
         acc = mm(image[rows, :], weight[...])
         z2_out[rows, :] = acc
         z = tiles(acc)
         return masked_sums(z, z, widen(tiles(mask[rows, :]), width), carry)
 
-    sums, squares = lax.fori_loop(0, lay.parts, step, zeros_pair(width))
+    sums, squares = zeros_pair(width)
+    for part in range(lay.parts):
+        sums, squares = step(part, (sums, squares))
     local = widen(count[...], width)
     sums_out[...] = pack(sums, squares, local)
     offset = fold(sums) / jnp.maximum(local, 1.0)
@@ -338,7 +340,7 @@
         near_out[rows, :] = flat(tiles(z2_out[rows, :]) - offset).astype(BF16)
         return 0
 
-    lax.fori_loop(0, lay.rows // STEP, centre, 0)
+    lax.fori_loop(0, lay.rows // STEP, centre, 0, unroll=True)
 
 
 def stat_kernel(sums, offset, gain, bias, out):
@@ -348,15 +350,19 @@
     out[2 * SUBLANES :, :] = jnp.where(row == 0, gain[...], bias[...])
 
 
+def second_norm(stat):
+    mean, inverse, _ = moments((stat.at[:SUBLANES, :],))
+    mean = mean - stat[SUBLANES : 2 * SUBLANES, :]
+    scale = stat[2 * SUBLANES : 2 * SUBLANES + 1, :] * inverse
+    shift = stat[2 * SUBLANES + 1 : 2 * SUBLANES + 2, :] - scale * mean
+    return mean, inverse, scale, shift
+
+
 def expand_kernel(lay, zs, stats, ws, mask, count, z_out, sums_out, *acts):
     width = z_out.shape[1]
     inner = zs[0].shape[1]
     for z, stat, act in zip(zs, stats, acts):
-        mean, inverse, _ = moments((stat.at[:SUBLANES, :],))
-        scale = stat[2 * SUBLANES : 2 * SUBLANES + 1, :] * inverse
-        shift = stat[2 * SUBLANES + 1 : 2 * SUBLANES + 2, :] + scale * (
-            stat[SUBLANES : 2 * SUBLANES, :] - mean
-        )
+        _, _, scale, shift = second_norm(stat)
 
         def activate(i, _, z=z, act=act, scale=scale, shift=shift):
             rows = at(i * STEP, STEP)
@@ -365,7 +371,7 @@
             act[rows, :] = flat(a).astype(BF16)
             return 0
 
-        lax.fori_loop(0, lay.rows // STEP, activate, 0)
+        lax.fori_loop(0, lay.rows // STEP, activate, 0, unroll=True)
 
     def step(part, carry):
         rows = at(part * lay.part, lay.part)
@@ -381,7 +387,7 @@
         z = tiles(acc)
         return masked_sums(z, z, widen(tiles(mask[rows, :]), width), carry)
 
-    sums, squares = lax.fori_loop(0, lay.parts, step, zeros_pair(width))
+    sums, squares = lax.fori_loop(0, lay.parts, step, zeros_pair(width), unroll=True)
     sums_out[...] = pack(sums, squares, widen(count[...], width))
 
 
@@ -400,7 +406,7 @@
         grad_out[rows, :] = flat(grad)
         return carry[0] + jnp.sum(grad, 0), carry[1] + jnp.sum(grad * normed, 0)
 
-    first, cross = lax.fori_loop(0, lay.rows // STEP, step, zeros_pair(width))
+    first, cross = lax.fori_loop(0, lay.rows // STEP, step, zeros_pair(width), unroll=True)
     sums_out[...] = pack(first, cross, jnp.zeros_like(first))
 
 
@@ -432,7 +438,7 @@
         store(i, rows, flat(dz))
         return 0
 
-    lax.fori_loop(0, lay.rows // STEP, step, 0)
+    lax.fori_loop(0, lay.rows // STEP, step, 0, unroll=True)
 
 
 def back_through(dz, w, inner):
@@ -462,10 +468,31 @@
         send_out[1, rows, :] = back_through(dz_out[rows, :], w3, inner).astype(BF16)
         return 0
 
-    lax.fori_loop(0, lay.parts, step, 0)
-
-
-def stay_kernel(lay, dz, w0, w2, own_out, peer_out):
+    lax.fori_loop(0, lay.parts, step, 0, unroll=True)
+
+
+def share_of_sums(lay, part, z, stat, mask, out):
+    width = out.shape[1]
+    mean, inverse, scale, shift = second_norm(stat)
+
+    def step(i, carry):
+        rows = at(i * STEP, STEP)
+        live = widen(tiles(mask[rows, :]), width)
+        sent = tiles(z[rows, :].astype(F32))
+        grad = live * tiles(part[rows, :].astype(F32)) * slope_of(scale * sent + shift)
+        cross = grad * ((sent - mean) * inverse)
+        return carry[0] + jnp.sum(grad, 0), carry[1] + jnp.sum(cross, 0)
+
+    first, cross = lax.fori_loop(0, lay.rows // STEP, step, zeros_pair(width), unroll=True)
+    out[...] = pack(first, cross, jnp.zeros_like(first))
+
+
+def second_sums_kernel(lay, send, zs, stats, mask, *outs):
+    for k, (z, stat, out) in enumerate(zip(zs, stats, outs)):
+        share_of_sums(lay, send.at[k], z, stat, mask, out)
+
+
+def stay_kernel(lay, dz, w0, w2, zs, stats, mask, own_out, peer_out, own_share, peer_share):
     inner = own_out.shape[1]
 
     def step(part, _):
@@ -474,29 +501,13 @@
         own_out[rows, :] = back_through(dz[rows, :], w0, inner)
         return 0
 
-    lax.fori_loop(0, lay.parts, step, 0)
-
-
-def second_back_kernel(lay, own, near, far, z2, sums2, gain, bias, mask, grad_out, sums_out):
-    width = z2.shape[1]
-    mean, inverse, _ = moments(sums2)
-
-    def step(i, carry):
-        rows = at(i * STEP, STEP)
-        live = widen(tiles(mask[rows, :]), width)
-        normed = (tiles(z2[rows, :]) - mean) * inverse
-        u = gain[...] * normed + bias[...]
-        da = own[rows, :] + near[0, rows, :].astype(F32) + far[rows, :].astype(F32)
-        grad = live * tiles(da) * slope_of(u)
-        grad_out[rows, :] = flat(grad)
-        return carry[0] + jnp.sum(grad, 0), carry[1] + jnp.sum(grad * normed, 0)
-
-    first, cross = lax.fori_loop(0, lay.rows // STEP, step, zeros_pair(width))
-    sums_out[...] = pack(first, cross, jnp.zeros_like(first))
+    lax.fori_loop(0, lay.parts, step, 0, unroll=True)
+    share_of_sums(lay, own_out, zs[0], stats[0], mask, own_share)
+    share_of_sums(lay, peer_out, zs[1], stats[1], mask, peer_share)
 
 
 def conv_back_kernel(
-    lay, du2, z2, sums2, sums5, gain2, mask, bits, weight, z1, sums1, gain1, bias1,
+    lay, own, near, far, z2, sums2, sums5, gain2, bias2, mask, bits, weight, z1, sums1, gain1, bias1,
     grad_out, sums_out, dz_out, bias_out, gain_out, slabs, image,
 ):
     width = z2.shape[1]
@@ -505,17 +516,28 @@
     gain_out[...] = both(sums[1])
     clear_halo(lay, slabs)
 
-    def store(i, rows, dz):
-        rounded = dz.astype(BF16)
+    mean, inverse, count = moments(sums2)
+    scale = inverse * gain2[...]
+    first, cross = sums[0] / count, sums[1] / count
+
+    def back(i, _):
+        rows = at(i * STEP, STEP)
+        live = widen(tiles(mask[rows, :]), width)
+        normed = (tiles(z2[rows, :]) - mean) * inverse
+        da = own[rows, :] + near[0, rows, :].astype(F32) + far[rows, :].astype(F32)
+        slope = slope_of(gain2[...] * normed + bias2[...])
+        dz = scale * live * (tiles(da) * slope - (first + normed * cross))
+        rounded = flat(dz).astype(BF16)
         dz_out[rows, :] = rounded
         to_slabs(slabs, i, rounded.astype(F32))
-
-    norm_back_loop(lay, du2, z2, mask, gain2, moments(sums2), sums, store)
-    windows(lay, slabs, bits, image, -1)
+        return 0
+
+    lax.fori_loop(0, lay.rows // STEP, back, 0)
     mean, inverse, _ = moments(sums1)
 
     def step(part, carry):
-        rows = at(part * lay.part, lay.part)
+        rows = slice(part * lay.part, (part + 1) * lay.part)
+        windows(lay, slabs, bits, image, -1, rows.start, rows.stop)
         da = mm(image[rows, :], weight[...])
         live = widen(tiles(mask[rows, :]), width)
         normed = (tiles(z1[rows, :]) - mean) * inverse
@@ -524,7 +546,9 @@
         grad_out[rows, :] = flat(grad)
         return carry[0] + jnp.sum(grad, 0), carry[1] + jnp.sum(grad * normed, 0)
 
-    first, cross = lax.fori_loop(0, lay.parts, step, zeros_pair(width))
+    first, cross = zeros_pair(width)
+    for part in range(lay.parts):
+        first, cross = step(part, (first, cross))
     sums_out[...] = pack(first, cross, jnp.zeros_like(first))
 
 
@@ -536,9 +560,9 @@
         to_slabs(slabs, i, dz[at(i * STEP, STEP), :].astype(F32))
         return 0
 
-    lax.fori_loop(0, lay.rows // STEP, copy, 0)
-    windows(lay, slabs, bits, image, -1)
+    lax.fori_loop(0, lay.rows // STEP, copy, 0, unroll=True)
     for tap in range(9):
+        windows(lay, slabs, bits, image, -1, 0, lay.rows, (tap,))
         columns = slice(tap * width, (tap + 1) * width)
         found = mm_tn(act[...], image[:, columns])
         wide[:, columns] = (found * block[...]).astype(BF16)
@@ -620,7 +644,7 @@
         held[rows, :] = acc
         return 0
 
-    lax.fori_loop(0, lay.parts, step, 0)
+    lax.fori_loop(0, lay.parts, step, 0, unroll=True)
 
     def move(rows, store, carry):
         store((out5, out7, out9), held[rows, :])
@@ -877,10 +901,11 @@
     (stat,) = run(stat_kernel, (s2, offset, g2, b2), (like((3 * SUBLANES, inner), F32),))
     stats = [stat] + [swap(stat, k) for k in range(1, shards)]
     z2_far, stats[1] = hold((z2_far, stats[1]))
+    zs = (z2_sent, z2_near, z2_far, swap(z2_far, 1))
     z3, s3, *acts = run(
         functools.partial(expand_kernel, lay),
         (
-            (z2_sent, z2_near, z2_far, swap(z2_far, 1)),
+            zs,
             stats,
             weights,
             mask,
@@ -900,6 +925,12 @@
     weights_back[3], s4 = hold((weights_back[3], s4))
     weights_back[3] = swap(weights_back[3], 3)
     s4 = allsum(s4)
+    output = run(
+        functools.partial(move_kernel, lay),
+        (hold((output, s4[0]))[0],),
+        lay.pixel_shapes(chan, BF16),
+    )
+    s4, output = hold((s4, output))
     weights_back[3], s4 = hold((weights_back[3], s4))
     dz3, send, bias_three, gain_three = run(
         functools.partial(third_back_kernel, lay),
@@ -912,10 +943,10 @@
         ),
     )
     near = swap(send, 1)
-    own, peer = run(
+    own, peer, own_share, peer_share = run(
         functools.partial(stay_kernel, lay),
-        (dz3, weights[0], weights[2]),
-        (like((rows, inner), F32),) * 2,
+        (dz3, weights[0], weights[2], (zs[0], zs[2]), (stats[0], stats[2]), mask),
+        (*[like((rows, inner), F32)] * 2, tile1, tile1),
     )
     piece = inner // BLOCKS
     half = BLOCKS // 2
@@ -928,27 +959,21 @@
     )
     expand_local = (keep_low, keep_high, send_low, send_high)
     far = swap(total(peer, near[1]).astype(BF16), 2)
-    output = run(functools.partial(move_kernel, lay), (output,), lay.pixel_shapes(chan, BF16))
-    far, output = hold((far, output))
+    near_share, cross_share = run(
+        functools.partial(second_sums_kernel, lay),
+        (send, (zs[1], zs[3]), (stats[1], stats[3]), mask),
+        (tile1,) * 2,
+    )
+    shares = (own_share, near_share, peer_share, cross_share)
+    s5 = allsum(tree_sum([shares[0], *(swap(shares[k], k) for k in range(1, shards))]))
     if fast:
         arrived = scatter(*halve(*expand_local))
-        far, arrived = hold((far, arrived))
-    du2, s5 = run(
-        functools.partial(second_back_kernel, lay),
-        (own, near, far, z2, s2, g2, b2, mask),
-        (like((rows, inner), F32), tile1),
-    )
-    if fast:
-        mine = total(*arrived).astype(BF16)
-        s5, mine = hold((s5, mine))
-        moved = [swap(mine[k], k) for k in range(1, shards)]
-    s5 = allsum(s5)
-    if fast:
-        s5, moved = hold((s5, moved))
-        mine = jnp.stack([mine[0], *moved])
+        far, arrived[1:3], s5 = hold((far, arrived[1:3], s5))
+    else:
+        far, s5 = hold((far, s5))
     du1, s6, dz2, bias_two, gain_two = run(
         functools.partial(conv_back_kernel, lay),
-        (du2, z2, s2, s5, g2, mask, facts, backward_weight, z1, s1, g1, b1),
+        (own, near, far, z2, s2, s5, g2, b2, mask, facts, backward_weight, z1, s1, g1, b1),
         (
             like((rows, inner), F32),
             tile1,
@@ -959,6 +984,11 @@
         scratch=(slabs, image),
         limit=16,
     )
+    if fast:
+        mine = total(*arrived).astype(BF16)
+        s6, mine = hold((s6, mine))
+        moved = [swap(mine[k], k) for k in range(1, shards)]
+        mine = jnp.stack([mine[0], *moved])
     s6 = allsum(s6)
     dz2, s6 = hold((dz2, s6[0]))[0], s6
     lanes = choose.shape[1]

time: 233 us -> 221 us (0.948)
  Pallas kernels: 53.8 us -> 46.6 us
  waiting for transfers between devices: 90.9 us -> 84.6 us
    pallas_call x24, Pallas kernels: 53.8 us -> 46.6 us  [run(): pl.pallas_call(kernel, out_shape=list(outs), in_specs=specs, out_specs=[p...]
    ppermute x44, waiting for transfers between devices: 63.8 us -> 57.6 us  [pass_on(): return lax.ppermute(x, 'batch', [(i, i ^ k) for i in range(ranks)])]
    ppermute x27 -> x30, starting transfers between devices: 17.6 us -> 19.9 us  [swap(): return lax.ppermute(x, 'tensor', [(i, i ^ k) for i in range(shards)])]
    ppermute x27 -> x30, waiting for transfers between devices: 27.1 us -> 26.9 us  [swap(): return lax.ppermute(x, 'tensor', [(i, i ^ k) for i in range(shards)])]
  transfers between devices with their start and end apart: 71 -> 74, of which waited for: 38 -> 31; matrix products, arithmetic and copies ran while one was open for 0% -> 0% of each run, Pallas kernels for 11% -> 12%
where the time goes in v4:
time: 221 us
  waiting for transfers between devices  84.6 us (38%)
  starting transfers between devices  82.3 us (37%)
  Pallas kernels  46.6 us (21%)
  local copies, waits for them, and re-layouts  5.37 us (2%)
    ppermute x44, starting transfers between devices, pass_on(): return lax.ppermute(x, 'batch', [(i, i ^ k) for i in range(ranks)])  62.4 us
    ppermute x44, waiting for transfers between devices, pass_on(): return lax.ppermute(x, 'batch', [(i, i ^ k) for i in range(ranks)])  57.6 us
    pallas_call x24, Pallas kernels, run(): pl.pallas_call(kernel, out_shape=list(outs), in_specs=specs, out_specs=[p...  46.6 us
    ppermute x30, waiting for transfers between devices, swap(): return lax.ppermute(x, 'tensor', [(i, i ^ k) for i in range(shards)])  26.9 us
    ppermute x30, starting transfers between devices, swap(): return lax.ppermute(x, 'tensor', [(i, i ^ k) for i in range(shards)])  19.9 us
    unnamed x38, local copies, waits for them, and re-layouts  5.1 us
  transfers between devices with their start and end apart: 74, of which 31 were waited for; matrix products, arithmetic and copies ran while one was open for 0% of the time, Pallas kernels for 12%

profile of v4, /device:TPU:0, one launch (start us, length us, event | category | flops | bytes accessed | tf_op | source)
XLA Modules:
  0.0 220.8 jit_solution(16671939944724958123)
XLA Ops:
  1.6 1.5 shard_map.309.own.x.xs_0__0_
  3.6 2.6 %collective-permute-start = (bf16[243,2,512]{2,1,0:T(2,128)(2,1)}, bf16[243,2,512]{2,1,0:T(2,128)(2,1)}, u32[]{:S(2)}, u32[]{:S(2)}) collective-permute-start(bf16[243,2,512]{2,1,0:T(2,128)(2,1)} %bitcast.1.refs_2_), channel_id=1, source_target_pairs={{0,2},{1,3},{2,0},{3,1},{4,6},{5,7},{6,4},{7,5},{8,10},{9,11},{10,... | collective-permute-start | bytes 1493000 | tf_op jit(solution)/shard_map/ppermute | solution.py:736
  12.4 1.4 shard_map.310.z
  13.9 4.8 %collective-permute-done.far_0_ = bf16[243,2,512]{2,1,0:T(2,128)(2,1)} collective-permute-done((bf16[243,2,512]{2,1,0:T(2,128)(2,1)}, bf16[243,2,512]{2,1,0:T(2,128)(2,1)}, u32[]{:S(2)}, u32[]{:S(2)}) %collective-permute-start) | collective-permute-done | bytes 497696 | tf_op jit(solution)/shard_map/ppermute | solution.py:736
  18.7 1.9 collective-permute-start.2
  20.8 1.7 shard_map.311
  22.5 15.4 %collective-permute-done.2.far_0_ = bf16[150,2,512]{2,1,0:T(2,128)(2,1)S(1)} collective-permute-done((bf16[150,2,512]{2,1,0:T(2,128)(2,1)S(1)}, bf16[150,2,512]{2,1,0:T(2,128)(2,1)S(1)}, u32[]{:S(2)}, u32[]{:S(2)}) %collective-permute-start.2) | collective-permute-done | bytes 307232 | tf_op jit(solution)/shard_map/ppermute | solution.py:736
  38.4 1.8 collective-permute-start.12
  40.3 1.6 shard_map.312
  43.3 3.9 %collective-permute-start.9 = (f32[8,256]{1,0:T(8,128)S(1)}, f32[8,256]{1,0:T(8,128)S(1)}, u32[]{:S(2)}, u32[]{:S(2)}) collective-permute-start(f32[8,256]{1,0:T(8,128)S(1)} %get-tuple-element.171), channel_id=1, source_target_pairs={{0,24},{4,28},{8,16},{12,20},{16,8},{20,12},{24,0},{28,4},{1,25},{... | collective-permute-start | bytes 24584 | tf_op jit(solution)/shard_map/ppermute | solution.py:739
  47.2 1.6 collective-permute-done.9
  48.9 2.9 %collective-permute-done.8 = f32[8,256]{1,0:T(8,128)S(1)} collective-permute-done((f32[8,256]{1,0:T(8,128)S(1)}, f32[8,256]{1,0:T(8,128)S(1)}, u32[]{:S(2)}, u32[]{:S(2)}) %collective-permute-start.8) | collective-permute-done | bytes 8224 | tf_op jit(solution)/shard_map/ppermute | solution.py:739
  52.5 1.7 collective-permute-start.10
  54.3 1.9 collective-permute-done.10.sums1_1_
  56.2 2.8 %shard_map.314 = (f32[1392,256]{1,0:T(8,128)S(1)}, f32[8,256]{1,0:T(8,128)S(1)}, bf16[1392,256]{1,0:T(8,128)(2,1)S(1)}, bf16[1392,256]{1,0:T(8,128)(2,1)S(1)}, f32[8,256]{1,0:T(8,128)S(1)}) custom-call(f32[1392,256]{1,0:T(8,128)S(1)} %get-tuple-element.170.z1, f32[8,256]{1,0:T(8,128)S(1)} %add_add_fusion.6.sums1_0_, ...), custom_call_target="tpu_custom_call" | custom-call | flops 1048576 | tf_op jit(solution)/shard_map/pallas_call | solution.py:685
  59.0 1.8 collective-permute-start.15
  60.8 3.6 %collective-permute-start.18 = (f32[8,256]{1,0:T(8,128)S(1)}, f32[8,256]{1,0:T(8,128)S(1)}, u32[]{:S(2)}, u32[]{:S(2)}) collective-permute-start(f32[8,256]{1,0:T(8,128)S(1)} %get-tuple-element.184), channel_id=1, source_target_pairs={{0,24},{4,28},{8,16},{12,20},{16,8},{20,12},{24,0},{28,4},{1,25},{... | collective-permute-start | bytes 24584 | tf_op jit(solution)/shard_map/ppermute | solution.py:739
  66.3 2.7 %collective-permute-done.17 = f32[8,256]{1,0:T(8,128)S(1)} collective-permute-done((f32[8,256]{1,0:T(8,128)S(1)}, f32[8,256]{1,0:T(8,128)S(1)}, u32[]{:S(2)}, u32[]{:S(2)}) %collective-permute-start.17) | collective-permute-done | bytes 8224 | tf_op jit(solution)/shard_map/ppermute | solution.py:739
  69.0 1.6 collective-permute-start.19
  70.6 2.1 collective-permute-done.19.sums_1_.sums2_1_
  74.4 1.6 collective-permute-start.23
  77.6 2.2 collective-permute-done.22.stats_2_.stats_1_
  79.8 2.1 shard_map.316
  82.6 3.5 %collective-permute-start.28 = (f32[8,512]{1,0:T(8,128)S(1)}, f32[8,512]{1,0:T(8,128)S(1)}, u32[]{:S(2)}, u32[]{:S(2)}) collective-permute-start(f32[8,512]{1,0:T(8,128)S(1)} %get-tuple-element.198), channel_id=1, source_target_pairs={{0,24},{4,28},{8,16},{12,20},{16,8},{20,12},{24,0},{28,4},{1,25},{... | collective-permute-start | bytes 49160 | tf_op jit(solution)/shard_map/ppermute | solution.py:739
  88.2 2.6 %collective-permute-done.27 = f32[8,512]{1,0:T(8,128)S(1)} collective-permute-done((f32[8,512]{1,0:T(8,128)S(1)}, f32[8,512]{1,0:T(8,128)S(1)}, u32[]{:S(2)}, u32[]{:S(2)}) %collective-permute-start.27) | collective-permute-done | bytes 16416 | tf_op jit(solution)/shard_map/ppermute | solution.py:739
  90.8 1.6 collective-permute-start.29
  92.4 2.2 %collective-permute-done.29.sums3_1_ = f32[8,512]{1,0:T(8,128)S(1)} collective-permute-done((f32[8,512]{1,0:T(8,128)S(1)}, f32[8,512]{1,0:T(8,128)S(1)}, u32[]{:S(2)}, u32[]{:S(2)}) %collective-permute-start.29) | collective-permute-done | bytes 16416 | tf_op jit(solution)/shard_map/ppermute | solution.py:739
  94.6 2.2 shard_map.317
  96.9 1.5 collective-permute-start.32
  99.1 2.3 %collective-permute-start.30 = (f32[8,512]{1,0:T(8,128)S(1)}, f32[8,512]{1,0:T(8,128)S(1)}, u32[]{:S(2)}, u32[]{:S(2)}) collective-permute-start(f32[8,512]{1,0:T(8,128)S(1)} %get-tuple-element.203), channel_id=1, source_target_pairs={{0,8},{4,12},{8,0},{12,4},{16,24},{20,28},{24,16},{28,20},{1,9},{5... | collective-permute-start | bytes 49160 | tf_op jit(solution)/shard_map/ppermute | solution.py:739
  103.8 1.6 collective-permute-start.33
  105.3 2.5 %shard_map.318 = (bf16[150,2,512]{2,1,0:T(2,128)(2,1)}, bf16[294,2,512]{2,1,0:T(2,128)(2,1)}, bf16[243,2,512]{2,1,0:T(2,128)(2,1)}) custom-call(bf16[1392,512]{1,0:T(8,128)(2,1)S(1)} %get-tuple-element.205.source), custom_call_target="tpu_custom_call" | custom-call | flops 1048576 | tf_op jit(solution)/shard_map/pallas_call | solution.py:685
  107.8 1.6 shard_map.319
  109.4 2.4 %shard_map.321 = (bf16[2,4,32,512]{3,2,1,0:T(8,128)(2,1)S(1)}, bf16[2,4,32,512]{3,2,1,0:T(8,128)(2,1)S(1)}, bf16[2,4,32,512]{3,2,1,0:T(8,128)(2,1)S(1)}, bf16[2,4,32,512]{3,2,1,0:T(8,128)(2,1)S(1)}) custom-call(s32[2]{0:T(128)S(1)} %pad_add_fusion.ids, bf16[1392,256]{1,0:T(8,128)(2,1)S(1)} %get-tuple-element.222.acts_0_, ...), custom_call_target="tpu_custom_call" | custom-call | flops 1048576 | tf_op jit(solution)/shard_map/pallas_call | solution.py:685
  113.1 1.7 shard_map.322
  116.0 1.9 shard_map.320
  119.0 1.6 collective-permute-done.37
  123.1 2.5 %collective-permute-start.46 = (f32[8,256]{1,0:T(8,128)S(1)}, f32[8,256]{1,0:T(8,128)S(1)}, u32[]{:S(2)}, u32[]{:S(2)}) collective-permute-start(f32[8,256]{1,0:T(8,128)S(1)} %add_add_fusion.4), channel_id=1, source_target_pairs={{0,24},{4,28},{8,16},{12,20},{16,8},{20,12},{24,0},{28,4},{1,25},{... | collective-permute-start | bytes 24584 | tf_op jit(solution)/shard_map/ppermute | solution.py:739
  128.5 2.2 %collective-permute-start.48 = (bf16[4,32,512]{2,1,0:T(8,128)(2,1)S(1)}, bf16[4,32,512]{2,1,0:T(8,128)(2,1)S(1)}, u32[]{:S(2)}, u32[]{:S(2)}) collective-permute-start(bf16[4,32,512]{2,1,0:T(8,128)(2,1)S(1)} %get-tuple-element.315), channel_id=1, source_target_pairs={{0,24},{4,28},{8,16},{12,20},{16,8},{20,12},{24,0},{28,4},{1,25},{... | collective-permute-start | bytes 393224 | tf_op jit(solution)/shard_map/ppermute | solution.py:739
  131.6 1.4 collective-permute-start.39
  134.3 2.4 %collective-permute-done.47.sums5_1_ = f32[8,256]{1,0:T(8,128)S(1)} collective-permute-done((f32[8,256]{1,0:T(8,128)S(1)}, f32[8,256]{1,0:T(8,128)S(1)}, u32[]{:S(2)}, u32[]{:S(2)}) %collective-permute-start.47) | collective-permute-done | bytes 8224 | tf_op jit(solution)/shard_map/ppermute | solution.py:739
  136.7 5.4 %collective-permute-done.40 = bf16[4,32,512]{2,1,0:T(8,128)(2,1)S(1)} collective-permute-done((bf16[4,32,512]{2,1,0:T(8,128)(2,1)S(1)}, bf16[4,32,512]{2,1,0:T(8,128)(2,1)S(1)}, u32[]{:S(2)}, u32[]{:S(2)}) %collective-permute-start.40) | collective-permute-done | bytes 131104 | tf_op jit(solution)/shard_map/ppermute | solution.py:739
  142.3 4.6 %shard_map.323 = (f32[1392,256]{1,0:T(8,128)S(1)}, f32[8,256]{1,0:T(8,128)S(1)}, bf16[1392,256]{1,0:T(8,128)(2,1)S(1)}, f32[1,256]{1,0:T(1,128)}, f32[1,256]{1,0:T(1,128)}) custom-call(f32[1392,256]{1,0:T(8,128)S(1)} %get-tuple-element.219.own, bf16[2,1392,256]{2,1,0:T(8,128)(2,1)S(1)} %collective-permute-done.35.near, ...), custom_call_target="tpu_custom_call" | custom-call | flops 1048576 | tf_op jit(solution)/shard_map/pallas_call | solution.py:685
  146.9 1.7 collective-permute-start.51
  148.6 2.7 %collective-permute-start.49 = (f32[8,256]{1,0:T(8,128)S(1)}, f32[8,256]{1,0:T(8,128)S(1)}, u32[]{:S(2)}, u32[]{:S(2)}) collective-permute-start(f32[8,256]{1,0:T(8,128)S(1)} %get-tuple-element.245), channel_id=1, source_target_pairs={{0,8},{4,12},{8,0},{12,4},{16,24},{20,28},{24,16},{28,20},{1,9},{5... | collective-permute-start | bytes 24584 | tf_op jit(solution)/shard_map/ppermute | solution.py:739
  151.4 1.4 collective-permute-start.54
  154.6 3.3 %shard_map.324.group = bf16[256,384]{1,0:T(8,128)(2,1)S(1)} custom-call(bf16[1392,256]{1,0:T(8,128)(2,1)S(1)} %get-tuple-element.246.act, bf16[1392,256]{1,0:T(8,128)(2,1)S(1)} %get-tuple-element.248.dz, s32[1392,128]{1,0:T(8,128)S(1)} %copy-done.1, f32[256,256]{1,0:T(8,128)S(1)} %copy-done.3, bf16[2304,384]{1,0:T(8,128)(2,1)S(1)} %copy-done.2), custom_call_target="tpu_custom_call" | custom-call | flops 1048576 | tf_op jit(solution)/shard_map/pallas_call | solution.py:685
  158.0 2.3 %shard_map.325 = (bf16[1392,256]{1,0:T(8,128)(2,1)S(1)}, f32[1,256]{1,0:T(1,128)}, f32[1,256]{1,0:T(1,128)}, bf16[4,304,256]{2,1,0:T(8,128)(2,1)S(1)}) custom-call(s32[2]{0:T(128)S(1)} %pad_add_fusion.ids, f32[1392,256]{1,0:T(8,128)S(1)} %get-tuple-element.241.du1, f32[1392,256]{1,0:T(8,128)S(1)} %get-tuple-element.170.z1, ...), custom_call_target="tpu_custom_call" | custom-call | flops 1048576 | tf_op jit(solution)/shard_map/pallas_call | solution.py:685
  162.4 2.0 collective-permute-start.59
  166.8 1.6 shard_map.326
  168.4 7.7 %collective-permute-done.56 = bf16[4,304,256]{2,1,0:T(8,128)(2,1)S(1)} collective-permute-done((bf16[4,304,256]{2,1,0:T(8,128)(2,1)S(1)}, bf16[4,304,256]{2,1,0:T(8,128)(2,1)S(1)}, u32[]{:S(2)}, u32[]{:S(2)}) %collective-permute-start.56) | collective-permute-done | bytes 622624 | tf_op jit(solution)/shard_map/ppermute | solution.py:739
  176.3 2.2 collective-permute-done.63.d2
  180.4 2.2 collective-permute-start.61
  182.6 2.2 collective-permute-start.62
  184.8 3.6 %shard_map.327 = (f32[150,2,512]{2,1,0:T(2,128)}, f32[294,2,512]{2,1,0:T(2,128)}, f32[243,2,512]{2,1,0:T(2,128)}) custom-call(f32[1392,512]{1,0:T(8,128)S(1)} %get-tuple-element.212.du3, bf16[1392,256]{1,0:T(8,128)(2,1)S(1)} %get-tuple-element.267.dz.d0, bf16[1392,256]{1,0:T(8,128)(2,1)S(1)} %collective-permute-done.64.d1, ...), custom_call_target="tpu_custom_call" | custom-call | flops 1048576 | tf_op jit(solution)/shard_map/pallas_call | solution.py:685
  188.4 6.5 %collective-permute-done.61.refs_2_ = bf16[304,256]{1,0:T(8,128)(2,1)S(1)} collective-permute-done((bf16[304,256]{1,0:T(8,128)(2,1)S(1)}, bf16[304,256]{1,0:T(8,128)(2,1)S(1)}, u32[]{:S(2)}, u32[]{:S(2)}) %collective-permute-start.61) | collective-permute-done | bytes 155680 | tf_op jit(solution)/shard_map/ppermute | solution.py:739
  195.0 1.7 collective-permute-start.71
  196.7 4.2 %collective-permute-start.69 = (bf16[304,256]{1,0:T(8,128)(2,1)S(1)}, bf16[304,256]{1,0:T(8,128)(2,1)S(1)}, u32[]{:S(2)}, u32[]{:S(2)}) collective-permute-start(bf16[304,256]{1,0:T(8,128)(2,1)S(1)} %shard_map.328.refs_0_), channel_id=1, source_target_pairs={{0,16},{4,20},{8,24},{12,28},{16,0},{20,4},{24,8},{28,12},{1,17},{... | collective-permute-start | bytes 466952 | tf_op jit(solution)/shard_map/ppermute | solution.py:739
  201.6 2.1 collective-permute-done.71.refs_6_
  204.5 5.9 %collective-permute-done.69.refs_4_ = bf16[304,256]{1,0:T(8,128)(2,1)S(1)} collective-permute-done((bf16[304,256]{1,0:T(8,128)(2,1)S(1)}, bf16[304,256]{1,0:T(8,128)(2,1)S(1)}, u32[]{:S(2)}, u32[]{:S(2)}) %collective-permute-start.69) | collective-permute-done | bytes 155680 | tf_op jit(solution)/shard_map/ppermute | solution.py:739
  212.4 2.0 shard_map.330
  214.4 2.1 collective-permute-done.70.refs_5_
  216.5 1.7 collective-permute-done.68.refs_3_
  218.2 2.6 %shard_map.329 = (f32[2048,256]{1,0:T(8,128)}, f32[9,8,32,32]{3,2,1,0:T(8,128)}) custom-call(s32[2]{0:T(128)S(1)} %pad_add_fusion.ids, bf16[304,256]{1,0:T(8,128)(2,1)S(1)} %shard_map.328.refs_0_, bf16[304,256]{1,0:T(8,128)(2,1)S(1)} %collective-permute-done.66.refs_1_, bf16[304,256]{1,0:T(8,128)(2,1)S(1)} %collective-permute-done.67.refs_2_, ...), custom_call_target="tpu_custom_call" | custom-call | flops 1048576 | tf_op jit(solution)/shard_map/pallas_call | solution.py:685
  (167 shorter events, 44.9 us)
Async XLA Ops:
  3.1 9.3 %collective-permute-start.1 = (bf16[1392,512]{1,0:T(8,128)(2,1)S(1)}, bf16[1392,512]{1,0:T(8,128)(2,1)S(1)}, u32[]{:S(2)}, u32[]{:S(2)}) collective-permute-start(bf16[1392,512]{1,0:T(8,128)(2,1)S(1)} %shard_map.309.own.x.xs_0__0_), channel_id=1, source_target_pairs={{0,1},{1,0},{2,3},{3,2},{4,5},{5,4},{6,7},{7,6},{8,9},{9,8},{10,11... | collective-permute-start | bytes 4276232 | tf_op jit(solution)/shard_map/ppermute | solution.py:736
  3.6 15.1 %collective-permute-start = (bf16[243,2,512]{2,1,0:T(2,128)(2,1)}, bf16[243,2,512]{2,1,0:T(2,128)(2,1)}, u32[]{:S(2)}, u32[]{:S(2)}) collective-permute-start(bf16[243,2,512]{2,1,0:T(2,128)(2,1)} %bitcast.1.refs_2_), channel_id=1, source_target_pairs={{0,2},{1,3},{2,0},{3,1},{4,6},{5,7},{6,4},{7,5},{8,10},{9,11},{10,... | collective-permute-start | bytes 1493000 | tf_op jit(solution)/shard_map/ppermute | solution.py:736
  6.2 31.6 %collective-permute-start.3 = (bf16[294,2,512]{2,1,0:T(2,128)(2,1)}, bf16[294,2,512]{2,1,0:T(2,128)(2,1)}, u32[]{:S(2)}, u32[]{:S(2)}) collective-permute-start(bf16[294,2,512]{2,1,0:T(2,128)(2,1)} %bitcast.14.refs_1_), channel_id=1, source_target_pairs={{0,2},{1,3},{2,0},{3,1},{4,6},{5,7},{6,4},{7,5},{8,10},{9,11},{10,... | collective-permute-start | bytes 1806344 | tf_op jit(solution)/shard_map/ppermute | solution.py:736
  18.7 19.1 %collective-permute-start.2 = (bf16[150,2,512]{2,1,0:T(2,128)(2,1)S(1)}, bf16[150,2,512]{2,1,0:T(2,128)(2,1)S(1)}, u32[]{:S(2)}, u32[]{:S(2)}) collective-permute-start(bf16[150,2,512]{2,1,0:T(2,128)(2,1)S(1)} %bitcast.111), channel_id=1, source_target_pairs={{0,2},{1,3},{2,0},{3,1},{4,6},{5,7},{6,4},{7,5},{8,10},{9,11},{10,... | collective-permute-start | bytes 921608 | tf_op jit(solution)/shard_map/ppermute | solution.py:736
  37.9 4.1 %collective-permute-start.6 = (bf16[294,2,512]{2,1,0:T(2,128)(2,1)}, bf16[294,2,512]{2,1,0:T(2,128)(2,1)S(1)}, u32[]{:S(2)}, u32[]{:S(2)}) collective-permute-start(bf16[294,2,512]{2,1,0:T(2,128)(2,1)} %collective-permute-done.3.far_1_), channel_id=1, source_target_pairs={{0,1},{1,0},{2,3},{3,2},{4,5},{5,4},{6,7},{7,6},{8,9},{9,8},{10,11... | collective-permute-start | bytes 1806344 | tf_op jit(solution)/shard_map/ppermute | solution.py:736
  37.9 4.1 %collective-permute-start.5 = (bf16[150,2,512]{2,1,0:T(2,128)(2,1)S(1)}, bf16[150,2,512]{2,1,0:T(2,128)(2,1)S(1)}, u32[]{:S(2)}, u32[]{:S(2)}) collective-permute-start(bf16[150,2,512]{2,1,0:T(2,128)(2,1)S(1)} %collective-permute-done.2.far_0_), channel_id=1, source_target_pairs={{0,1},{1,0},{2,3},{3,2},{4,5},{5,4},{6,7},{7,6},{8,9},{9,8},{10,11... | collective-permute-start | bytes 921608 | tf_op jit(solution)/shard_map/ppermute | solution.py:736
  38.4 15.9 %collective-permute-start.11 = (bf16[512,256]{1,0:T(8,128)(2,1)S(1)}, bf16[512,256]{1,0:T(8,128)(2,1)S(1)}, u32[]{:S(2)}, u32[]{:S(2)}) collective-permute-start(bf16[512,256]{1,0:T(8,128)(2,1)S(1)} %get-tuple-element.177), channel_id=1, source_target_pairs={{0,1},{1,0},{2,3},{3,2},{4,5},{5,4},{6,7},{7,6},{8,9},{9,8},{10,11... | collective-permute-start | bytes 786440 | tf_op jit(solution)/shard_map/ppermute | solution.py:736
  38.4 15.9 %collective-permute-start.12 = (bf16[512,256]{1,0:T(8,128)(2,1)S(1)}, bf16[512,256]{1,0:T(8,128)(2,1)S(1)}, u32[]{:S(2)}, u32[]{:S(2)}) collective-permute-start(bf16[512,256]{1,0:T(8,128)(2,1)S(1)} %get-tuple-element.178), channel_id=1, source_target_pairs={{0,2},{1,3},{2,0},{3,1},{4,6},{5,7},{6,4},{7,5},{8,10},{9,11},{10,... | collective-permute-start | bytes 786440 | tf_op jit(solution)/shard_map/ppermute | solution.py:736
  40.1 14.1 %collective-permute-start.13 = (bf16[512,256]{1,0:T(8,128)(2,1)S(1)}, bf16[512,256]{1,0:T(8,128)(2,1)S(1)}, u32[]{:S(2)}, u32[]{:S(2)}) collective-permute-start(bf16[512,256]{1,0:T(8,128)(2,1)S(1)} %get-tuple-element.179), channel_id=1, source_target_pairs={{0,3},{1,2},{2,1},{3,0},{4,7},{5,6},{6,5},{7,4},{8,11},{9,10},{10,... | collective-permute-start | bytes 786440 | tf_op jit(solution)/shard_map/ppermute | solution.py:736
  43.3 5.5 %collective-permute-start.9 = (f32[8,256]{1,0:T(8,128)S(1)}, f32[8,256]{1,0:T(8,128)S(1)}, u32[]{:S(2)}, u32[]{:S(2)}) collective-permute-start(f32[8,256]{1,0:T(8,128)S(1)} %get-tuple-element.171), channel_id=1, source_target_pairs={{0,24},{4,28},{8,16},{12,20},{16,8},{20,12},{24,0},{28,4},{1,25},{... | collective-permute-start | bytes 24584 | tf_op jit(solution)/shard_map/ppermute | solution.py:739
  47.2 4.5 %collective-permute-start.8 = (f32[8,256]{1,0:T(8,128)S(1)}, f32[8,256]{1,0:T(8,128)S(1)}, u32[]{:S(2)}, u32[]{:S(2)}) collective-permute-start(f32[8,256]{1,0:T(8,128)S(1)} %get-tuple-element.171), channel_id=1, source_target_pairs={{0,16},{4,20},{8,24},{12,28},{16,0},{20,4},{24,8},{28,12},{1,17},{... | collective-permute-start | bytes 24584 | tf_op jit(solution)/shard_map/ppermute | solution.py:739
  59.0 15.3 %collective-permute-start.15 = (bf16[1392,256]{1,0:T(8,128)(2,1)S(1)}, bf16[1392,256]{1,0:T(8,128)(2,1)S(1)}, u32[]{:S(2)}, u32[]{:S(2)}) collective-permute-start(bf16[1392,256]{1,0:T(8,128)(2,1)S(1)} %get-tuple-element.183.zs_0_), channel_id=1, source_target_pairs={{0,2},{1,3},{2,0},{3,1},{4,6},{5,7},{6,4},{7,5},{8,10},{9,11},{10,... | collective-permute-start | bytes 2138120 | tf_op jit(solution)/shard_map/ppermute | solution.py:736
  60.8 5.4 %collective-permute-start.18 = (f32[8,256]{1,0:T(8,128)S(1)}, f32[8,256]{1,0:T(8,128)S(1)}, u32[]{:S(2)}, u32[]{:S(2)}) collective-permute-start(f32[8,256]{1,0:T(8,128)S(1)} %get-tuple-element.184), channel_id=1, source_target_pairs={{0,24},{4,28},{8,16},{12,20},{16,8},{20,12},{24,0},{28,4},{1,25},{... | collective-permute-start | bytes 24584 | tf_op jit(solution)/shard_map/ppermute | solution.py:739
  64.4 4.5 %collective-permute-start.17 = (f32[8,256]{1,0:T(8,128)S(1)}, f32[8,256]{1,0:T(8,128)S(1)}, u32[]{:S(2)}, u32[]{:S(2)}) collective-permute-start(f32[8,256]{1,0:T(8,128)S(1)} %get-tuple-element.184), channel_id=1, source_target_pairs={{0,16},{4,20},{8,24},{12,28},{16,0},{20,4},{24,8},{28,12},{1,17},{... | collective-permute-start | bytes 24584 | tf_op jit(solution)/shard_map/ppermute | solution.py:739
  64.4 4.5 %collective-permute-start.16 = (f32[8,256]{1,0:T(8,128)S(1)}, f32[8,256]{1,0:T(8,128)S(1)}, u32[]{:S(2)}, u32[]{:S(2)}) collective-permute-start(f32[8,256]{1,0:T(8,128)S(1)} %get-tuple-element.184), channel_id=1, source_target_pairs={{0,8},{4,12},{8,0},{12,4},{16,24},{20,28},{24,16},{28,20},{1,9},{5... | collective-permute-start | bytes 24584 | tf_op jit(solution)/shard_map/ppermute | solution.py:739
  72.8 7.0 %collective-permute-start.14 = (bf16[1392,256]{1,0:T(8,128)(2,1)S(1)}, bf16[1392,256]{1,0:T(8,128)(2,1)S(1)}, u32[]{:S(2)}, u32[]{:S(2)}) collective-permute-start(bf16[1392,256]{1,0:T(8,128)(2,1)S(1)} %get-tuple-element.183.zs_0_), channel_id=1, source_target_pairs={{0,1},{1,0},{2,3},{3,2},{4,5},{5,4},{6,7},{7,6},{8,9},{9,8},{10,11... | collective-permute-start | bytes 2138120 | tf_op jit(solution)/shard_map/ppermute | solution.py:736
  74.4 5.4 %collective-permute-start.21 = (bf16[1392,256]{1,0:T(8,128)(2,1)S(1)}, bf16[1392,256]{1,0:T(8,128)(2,1)S(1)}, u32[]{:S(2)}, u32[]{:S(2)}) collective-permute-start(bf16[1392,256]{1,0:T(8,128)(2,1)S(1)} %collective-permute-done.15.zs_2_.zs_1_), channel_id=1, source_target_pairs={{0,1},{1,0},{2,3},{3,2},{4,5},{5,4},{6,7},{7,6},{8,9},{9,8},{10,11... | collective-permute-start | bytes 2138120 | tf_op jit(solution)/shard_map/ppermute | solution.py:736
  82.0 12.7 %collective-permute-start.24 = (bf16[512,256]{1,0:T(8,128)(2,1)S(1)}, bf16[512,256]{1,0:T(8,128)(2,1)S(1)}, u32[]{:S(2)}, u32[]{:S(2)}) collective-permute-start(bf16[512,256]{1,0:T(8,128)(2,1)S(1)} %get-tuple-element.196), channel_id=1, source_target_pairs={{0,1},{1,0},{2,3},{3,2},{4,5},{5,4},{6,7},{7,6},{8,9},{9,8},{10,11... | collective-permute-start | bytes 786440 | tf_op jit(solution)/shard_map/ppermute | solution.py:736
  82.0 12.6 %collective-permute-start.25 = (bf16[512,256]{1,0:T(8,128)(2,1)S(1)}, bf16[512,256]{1,0:T(8,128)(2,1)S(1)}, u32[]{:S(2)}, u32[]{:S(2)}) collective-permute-start(bf16[512,256]{1,0:T(8,128)(2,1)S(1)} %get-tuple-element.197), channel_id=1, source_target_pairs={{0,2},{1,3},{2,0},{3,1},{4,6},{5,7},{6,4},{7,5},{8,10},{9,11},{10,... | collective-permute-start | bytes 786440 | tf_op jit(solution)/shard_map/ppermute | solution.py:736
  82.6 5.5 %collective-permute-start.28 = (f32[8,512]{1,0:T(8,128)S(1)}, f32[8,512]{1,0:T(8,128)S(1)}, u32[]{:S(2)}, u32[]{:S(2)}) collective-permute-start(f32[8,512]{1,0:T(8,128)S(1)} %get-tuple-element.198), channel_id=1, source_target_pairs={{0,24},{4,28},{8,16},{12,20},{16,8},{20,12},{24,0},{28,4},{1,25},{... | collective-permute-start | bytes 49160 | tf_op jit(solution)/shard_map/ppermute | solution.py:739
  86.2 4.6 %collective-permute-start.27 = (f32[8,512]{1,0:T(8,128)S(1)}, f32[8,512]{1,0:T(8,128)S(1)}, u32[]{:S(2)}, u32[]{:S(2)}) collective-permute-start(f32[8,512]{1,0:T(8,128)S(1)} %get-tuple-element.198), channel_id=1, source_target_pairs={{0,16},{4,20},{8,24},{12,28},{16,0},{20,4},{24,8},{28,12},{1,17},{... | collective-permute-start | bytes 49160 | tf_op jit(solution)/shard_map/ppermute | solution.py:739
  86.2 4.6 %collective-permute-start.26 = (f32[8,512]{1,0:T(8,128)S(1)}, f32[8,512]{1,0:T(8,128)S(1)}, u32[]{:S(2)}, u32[]{:S(2)}) collective-permute-start(f32[8,512]{1,0:T(8,128)S(1)} %get-tuple-element.198), channel_id=1, source_target_pairs={{0,8},{4,12},{8,0},{12,4},{16,24},{20,28},{24,16},{28,20},{1,9},{5... | collective-permute-start | bytes 49160 | tf_op jit(solution)/shard_map/ppermute | solution.py:739
  96.8 11.0 %collective-permute-start.34 = (bf16[512,256]{1,0:T(8,128)(2,1)S(1)}, bf16[512,256]{1,0:T(8,128)(2,1)S(1)}, u32[]{:S(2)}, u32[]{:S(2)}) collective-permute-start(bf16[512,256]{1,0:T(8,128)(2,1)S(1)} %get-tuple-element.213), channel_id=1, source_target_pairs={{0,3},{1,2},{2,1},{3,0},{4,7},{5,6},{6,5},{7,4},{8,11},{9,10},{10,... | collective-permute-start | bytes 786440 | tf_op jit(solution)/shard_map/ppermute | solution.py:736
  96.9 5.6 %collective-permute-start.32 = (f32[8,512]{1,0:T(8,128)S(1)}, f32[8,512]{1,0:T(8,128)S(1)}, u32[]{:S(2)}, u32[]{:S(2)}) collective-permute-start(f32[8,512]{1,0:T(8,128)S(1)} %get-tuple-element.203), channel_id=1, source_target_pairs={{0,24},{4,28},{8,16},{12,20},{16,8},{20,12},{24,0},{28,4},{1,25},{... | collective-permute-start | bytes 49160 | tf_op jit(solution)/shard_map/ppermute | solution.py:739
  98.4 4.9 %collective-permute-start.31 = (f32[8,512]{1,0:T(8,128)S(1)}, f32[8,512]{1,0:T(8,128)S(1)}, u32[]{:S(2)}, u32[]{:S(2)}) collective-permute-start(f32[8,512]{1,0:T(8,128)S(1)} %get-tuple-element.203), channel_id=1, source_target_pairs={{0,16},{4,20},{8,24},{12,28},{16,0},{20,4},{24,8},{28,12},{1,17},{... | collective-permute-start | bytes 49160 | tf_op jit(solution)/shard_map/ppermute | solution.py:739
  99.1 4.7 %collective-permute-start.30 = (f32[8,512]{1,0:T(8,128)S(1)}, f32[8,512]{1,0:T(8,128)S(1)}, u32[]{:S(2)}, u32[]{:S(2)}) collective-permute-start(f32[8,512]{1,0:T(8,128)S(1)} %get-tuple-element.203), channel_id=1, source_target_pairs={{0,8},{4,12},{8,0},{12,4},{16,24},{20,28},{24,16},{28,20},{1,9},{5... | collective-permute-start | bytes 49160 | tf_op jit(solution)/shard_map/ppermute | solution.py:739
  109.4 12.4 %collective-permute-start.35 = (bf16[2,1392,256]{2,1,0:T(8,128)(2,1)S(1)}, bf16[2,1392,256]{2,1,0:T(8,128)(2,1)S(1)}, u32[]{:S(2)}, u32[]{:S(2)}) collective-permute-start(bf16[2,1392,256]{2,1,0:T(8,128)(2,1)S(1)} %get-tuple-element.220.send), channel_id=1, source_target_pairs={{0,1},{1,0},{2,3},{3,2},{4,5},{5,4},{6,7},{7,6},{8,9},{9,8},{10,11... | collective-permute-start | bytes 4276232 | tf_op jit(solution)/shard_map/ppermute | solution.py:736
  111.8 8.8 %collective-permute-start.37 = (bf16[2,4,32,512]{3,2,1,0:T(8,128)(2,1)S(1)}, bf16[2,4,32,512]{3,2,1,0:T(8,128)(2,1)S(1)}, u32[]{:S(2)}, u32[]{:S(2)}) collective-permute-start(bf16[2,4,32,512]{3,2,1,0:T(8,128)(2,1)S(1)} %get-tuple-element.228), channel_id=1, source_target_pairs={{0,4},{4,0},{8,12},{12,8},{16,20},{20,16},{24,28},{28,24},{1,5},{5... | collective-permute-start | bytes 786440 | tf_op jit(solution)/shard_map/ppermute | solution.py:739
  114.8 8.3 %collective-permute-start.41 = (f32[8,256]{1,0:T(8,128)S(1)}, f32[8,256]{1,0:T(8,128)S(1)}, u32[]{:S(2)}, u32[]{:S(2)}) collective-permute-start(f32[8,256]{1,0:T(8,128)S(1)} %get-tuple-element.233), channel_id=1, source_target_pairs={{0,1},{1,0},{2,3},{3,2},{4,5},{5,4},{6,7},{7,6},{8,9},{9,8},{10,11... | collective-permute-start | bytes 24584 | tf_op jit(solution)/shard_map/ppermute | solution.py:736
  115.1 8.0 %collective-permute-start.43 = (f32[8,256]{1,0:T(8,128)S(1)}, f32[8,256]{1,0:T(8,128)S(1)}, u32[]{:S(2)}, u32[]{:S(2)}) collective-permute-start(f32[8,256]{1,0:T(8,128)S(1)} %get-tuple-element.235), channel_id=1, source_target_pairs={{0,3},{1,2},{2,1},{3,0},{4,7},{5,6},{6,5},{7,4},{8,11},{9,10},{10,... | collective-permute-start | bytes 24584 | tf_op jit(solution)/shard_map/ppermute | solution.py:736
  117.9 5.2 %collective-permute-start.42 = (f32[8,256]{1,0:T(8,128)S(1)}, f32[8,256]{1,0:T(8,128)S(1)}, u32[]{:S(2)}, u32[]{:S(2)}) collective-permute-start(f32[8,256]{1,0:T(8,128)S(1)} %get-tuple-element.234), channel_id=1, source_target_pairs={{0,2},{1,3},{2,0},{3,1},{4,6},{5,7},{6,4},{7,5},{8,10},{9,11},{10,... | collective-permute-start | bytes 24584 | tf_op jit(solution)/shard_map/ppermute | solution.py:736
  120.6 7.9 %collective-permute-start.38 = (bf16[2,4,32,512]{3,2,1,0:T(8,128)(2,1)S(1)}, bf16[2,4,32,512]{3,2,1,0:T(8,128)(2,1)S(1)}, u32[]{:S(2)}, u32[]{:S(2)}) collective-permute-start(bf16[2,4,32,512]{3,2,1,0:T(8,128)(2,1)S(1)} %get-tuple-element.229), channel_id=1, source_target_pairs={{0,4},{4,0},{8,12},{12,8},{16,20},{20,16},{24,28},{28,24},{1,5},{5... | collective-permute-start | bytes 786440 | tf_op jit(solution)/shard_map/ppermute | solution.py:739
  122.0 20.1 %collective-permute-start.36 = (bf16[1392,256]{1,0:T(8,128)(2,1)S(1)}, bf16[1392,256]{1,0:T(8,128)(2,1)S(1)}, u32[]{:S(2)}, u32[]{:S(2)}) collective-permute-start(bf16[1392,256]{1,0:T(8,128)(2,1)S(1)} %fusion), channel_id=1, source_target_pairs={{0,2},{1,3},{2,0},{3,1},{4,6},{5,7},{6,4},{7,5},{8,10},{9,11},{10,... | collective-permute-start | bytes 2138120 | tf_op jit(solution)/shard_map/ppermute | solution.py:736
  123.1 7.7 %collective-permute-start.46 = (f32[8,256]{1,0:T(8,128)S(1)}, f32[8,256]{1,0:T(8,128)S(1)}, u32[]{:S(2)}, u32[]{:S(2)}) collective-permute-start(f32[8,256]{1,0:T(8,128)S(1)} %add_add_fusion.4), channel_id=1, source_target_pairs={{0,24},{4,28},{8,16},{12,20},{16,8},{20,12},{24,0},{28,4},{1,25},{... | collective-permute-start | bytes 24584 | tf_op jit(solution)/shard_map/ppermute | solution.py:739
  125.6 6.0 %collective-permute-start.45 = (f32[8,256]{1,0:T(8,128)S(1)}, f32[8,256]{1,0:T(8,128)S(1)}, u32[]{:S(2)}, u32[]{:S(2)}) collective-permute-start(f32[8,256]{1,0:T(8,128)S(1)} %add_add_fusion.4), channel_id=1, source_target_pairs={{0,16},{4,20},{8,24},{12,28},{16,0},{20,4},{24,8},{28,12},{1,17},{... | collective-permute-start | bytes 24584 | tf_op jit(solution)/shard_map/ppermute | solution.py:739
  126.5 6.5 %collective-permute-start.44 = (f32[8,256]{1,0:T(8,128)S(1)}, f32[8,256]{1,0:T(8,128)S(1)}, u32[]{:S(2)}, u32[]{:S(2)}) collective-permute-start(f32[8,256]{1,0:T(8,128)S(1)} %add_add_fusion.4), channel_id=1, source_target_pairs={{0,8},{4,12},{8,0},{12,4},{16,24},{20,28},{24,16},{28,20},{1,9},{5... | collective-permute-start | bytes 24584 | tf_op jit(solution)/shard_map/ppermute | solution.py:739
  128.5 13.6 %collective-permute-start.48 = (bf16[4,32,512]{2,1,0:T(8,128)(2,1)S(1)}, bf16[4,32,512]{2,1,0:T(8,128)(2,1)S(1)}, u32[]{:S(2)}, u32[]{:S(2)}) collective-permute-start(bf16[4,32,512]{2,1,0:T(8,128)(2,1)S(1)} %get-tuple-element.315), channel_id=1, source_target_pairs={{0,24},{4,28},{8,16},{12,20},{16,8},{20,12},{24,0},{28,4},{1,25},{... | collective-permute-start | bytes 393224 | tf_op jit(solution)/shard_map/ppermute | solution.py:739
  130.8 11.3 %collective-permute-start.40 = (bf16[4,32,512]{2,1,0:T(8,128)(2,1)S(1)}, bf16[4,32,512]{2,1,0:T(8,128)(2,1)S(1)}, u32[]{:S(2)}, u32[]{:S(2)}) collective-permute-start(bf16[4,32,512]{2,1,0:T(8,128)(2,1)S(1)} %get-tuple-element.316), channel_id=1, source_target_pairs={{0,16},{4,20},{8,24},{12,28},{16,0},{20,4},{24,8},{28,12},{1,17},{... | collective-permute-start | bytes 393224 | tf_op jit(solution)/shard_map/ppermute | solution.py:739
  131.6 10.5 %collective-permute-start.39 = (bf16[4,32,512]{2,1,0:T(8,128)(2,1)S(1)}, bf16[4,32,512]{2,1,0:T(8,128)(2,1)S(1)}, u32[]{:S(2)}, u32[]{:S(2)}) collective-permute-start(bf16[4,32,512]{2,1,0:T(8,128)(2,1)S(1)} %fusion.8), channel_id=1, source_target_pairs={{0,8},{4,12},{8,0},{12,4},{16,24},{20,28},{24,16},{28,20},{1,9},{5... | collective-permute-start | bytes 393224 | tf_op jit(solution)/shard_map/ppermute | solution.py:739
  146.9 6.0 %collective-permute-start.51 = (f32[8,256]{1,0:T(8,128)S(1)}, f32[8,256]{1,0:T(8,128)S(1)}, u32[]{:S(2)}, u32[]{:S(2)}) collective-permute-start(f32[8,256]{1,0:T(8,128)S(1)} %get-tuple-element.245), channel_id=1, source_target_pairs={{0,24},{4,28},{8,16},{12,20},{16,8},{20,12},{24,0},{28,4},{1,25},{... | collective-permute-start | bytes 24584 | tf_op jit(solution)/shard_map/ppermute | solution.py:739
  148.6 4.7 %collective-permute-start.50 = (f32[8,256]{1,0:T(8,128)S(1)}, f32[8,256]{1,0:T(8,128)S(1)}, u32[]{:S(2)}, u32[]{:S(2)}) collective-permute-start(f32[8,256]{1,0:T(8,128)S(1)} %get-tuple-element.245), channel_id=1, source_target_pairs={{0,16},{4,20},{8,24},{12,28},{16,0},{20,4},{24,8},{28,12},{1,17},{... | collective-permute-start | bytes 24584 | tf_op jit(solution)/shard_map/ppermute | solution.py:739
  148.6 4.7 %collective-permute-start.49 = (f32[8,256]{1,0:T(8,128)S(1)}, f32[8,256]{1,0:T(8,128)S(1)}, u32[]{:S(2)}, u32[]{:S(2)}) collective-permute-start(f32[8,256]{1,0:T(8,128)S(1)} %get-tuple-element.245), channel_id=1, source_target_pairs={{0,8},{4,12},{8,0},{12,4},{16,24},{20,28},{24,16},{28,20},{1,9},{5... | collective-permute-start | bytes 24584 | tf_op jit(solution)/shard_map/ppermute | solution.py:739
  151.3 6.6 %collective-permute-start.55 = (bf16[32,512]{1,0:T(8,128)(2,1)S(1)}, bf16[32,512]{1,0:T(8,128)(2,1)S(1)}, u32[]{:S(2)}, u32[]{:S(2)}) collective-permute-start(bf16[32,512]{1,0:T(8,128)(2,1)S(1)} %get-tuple-element.318), channel_id=1, source_target_pairs={{0,3},{1,2},{2,1},{3,0},{4,7},{5,6},{6,5},{7,4},{8,11},{9,10},{10,... | collective-permute-start | bytes 98312 | tf_op jit(solution)/shard_map/ppermute | solution.py:736
  151.4 6.5 %collective-permute-start.54 = (bf16[32,512]{1,0:T(8,128)(2,1)S(1)}, bf16[32,512]{1,0:T(8,128)(2,1)S(1)}, u32[]{:S(2)}, u32[]{:S(2)}) collective-permute-start(bf16[32,512]{1,0:T(8,128)(2,1)S(1)} %get-tuple-element.319), channel_id=1, source_target_pairs={{0,2},{1,3},{2,0},{3,1},{4,6},{5,7},{6,4},{7,5},{8,10},{9,11},{10,... | collective-permute-start | bytes 98312 | tf_op jit(solution)/shard_map/ppermute | solution.py:736
  152.8 5.1 %collective-permute-start.53 = (bf16[32,512]{1,0:T(8,128)(2,1)S(1)}, bf16[32,512]{1,0:T(8,128)(2,1)S(1)}, u32[]{:S(2)}, u32[]{:S(2)}) collective-permute-start(bf16[32,512]{1,0:T(8,128)(2,1)S(1)} %get-tuple-element.320), channel_id=1, source_target_pairs={{0,1},{1,0},{2,3},{3,2},{4,5},{5,4},{6,7},{7,6},{8,9},{9,8},{10,11... | collective-permute-start | bytes 98312 | tf_op jit(solution)/shard_map/ppermute | solution.py:736
  153.3 4.7 %collective-permute-start.52 = (f32[8,256]{1,0:T(8,128)S(1)}, f32[8,256]{1,0:T(8,128)S(1)}, u32[]{:S(2)}, u32[]{:S(2)}) collective-permute-start(f32[8,256]{1,0:T(8,128)S(1)} %add_add_fusion.2.sums6_0_), channel_id=1, source_target_pairs={{0,4},{4,0},{8,12},{12,8},{16,20},{20,16},{24,28},{28,24},{1,5},{5... | collective-permute-start | bytes 24584 | tf_op jit(solution)/shard_map/ppermute | solution.py:739
  160.3 15.7 %collective-permute-start.56 = (bf16[4,304,256]{2,1,0:T(8,128)(2,1)S(1)}, bf16[4,304,256]{2,1,0:T(8,128)(2,1)S(1)}, u32[]{:S(2)}, u32[]{:S(2)}) collective-permute-start(bf16[4,304,256]{2,1,0:T(8,128)(2,1)S(1)} %get-tuple-element.260), channel_id=1, source_target_pairs={{0,4},{4,0},{8,12},{12,8},{16,20},{20,16},{24,28},{28,24},{1,5},{5... | collective-permute-start | bytes 1867784 | tf_op jit(solution)/shard_map/ppermute | solution.py:739
  161.0 17.4 %collective-permute-start.63 = (bf16[1392,256]{1,0:T(8,128)(2,1)S(1)}, bf16[1392,256]{1,0:T(8,128)(2,1)S(1)}, u32[]{:S(2)}, u32[]{:S(2)}) collective-permute-start(bf16[1392,256]{1,0:T(8,128)(2,1)S(1)} %get-tuple-element.267.dz.d0), channel_id=1, source_target_pairs={{0,2},{1,3},{2,0},{3,1},{4,6},{5,7},{6,4},{7,5},{8,10},{9,11},{10,... | collective-permute-start | bytes 2138120 | tf_op jit(solution)/shard_map/ppermute | solution.py:736
  162.4 13.8 %collective-permute-start.59 = (bf16[4,32,512]{2,1,0:T(8,128)(2,1)S(1)}, bf16[4,32,512]{2,1,0:T(8,128)(2,1)S(1)}, u32[]{:S(2)}, u32[]{:S(2)}) collective-permute-start(bf16[4,32,512]{2,1,0:T(8,128)(2,1)S(1)} %pad_maximum_fusion.5.refs_0_), channel_id=1, source_target_pairs={{0,24},{4,28},{8,16},{12,20},{16,8},{20,12},{24,0},{28,4},{1,25},{... | collective-permute-start | bytes 393224 | tf_op jit(solution)/shard_map/ppermute | solution.py:739
  164.4 11.8 %collective-permute-start.58 = (bf16[4,32,512]{2,1,0:T(8,128)(2,1)S(1)}, bf16[4,32,512]{2,1,0:T(8,128)(2,1)S(1)}, u32[]{:S(2)}, u32[]{:S(2)}) collective-permute-start(bf16[4,32,512]{2,1,0:T(8,128)(2,1)S(1)} %pad_maximum_fusion.5.refs_0_), channel_id=1, source_target_pairs={{0,16},{4,20},{8,24},{12,28},{16,0},{20,4},{24,8},{28,12},{1,17},{... | collective-permute-start | bytes 393224 | tf_op jit(solution)/shard_map/ppermute | solution.py:739
  165.5 10.8 %collective-permute-start.57 = (bf16[4,32,512]{2,1,0:T(8,128)(2,1)S(1)}, bf16[4,32,512]{2,1,0:T(8,128)(2,1)S(1)}, u32[]{:S(2)}, u32[]{:S(2)}) collective-permute-start(bf16[4,32,512]{2,1,0:T(8,128)(2,1)S(1)} %pad_maximum_fusion.5.refs_0_), channel_id=1, source_target_pairs={{0,8},{4,12},{8,0},{12,4},{16,24},{20,28},{24,16},{28,20},{1,9},{5... | collective-permute-start | bytes 393224 | tf_op jit(solution)/shard_map/ppermute | solution.py:739
  178.4 4.2 %collective-permute-start.64 = (bf16[1392,256]{1,0:T(8,128)(2,1)S(1)}, bf16[1392,256]{1,0:T(8,128)(2,1)S(1)}, u32[]{:S(2)}, u32[]{:S(2)}) collective-permute-start(bf16[1392,256]{1,0:T(8,128)(2,1)S(1)} %get-tuple-element.267.dz.d0), channel_id=1, source_target_pairs={{0,1},{1,0},{2,3},{3,2},{4,5},{5,4},{6,7},{7,6},{8,9},{9,8},{10,11... | collective-permute-start | bytes 2138120 | tf_op jit(solution)/shard_map/ppermute | solution.py:736
  178.4 6.3 %collective-permute-start.65 = (bf16[1392,256]{1,0:T(8,128)(2,1)S(1)}, bf16[1392,256]{1,0:T(8,128)(2,1)S(1)}, u32[]{:S(2)}, u32[]{:S(2)}) collective-permute-start(bf16[1392,256]{1,0:T(8,128)(2,1)S(1)} %collective-permute-done.63.d2), channel_id=1, source_target_pairs={{0,1},{1,0},{2,3},{3,2},{4,5},{5,4},{6,7},{7,6},{8,9},{9,8},{10,11... | collective-permute-start | bytes 2138120 | tf_op jit(solution)/shard_map/ppermute | solution.py:736
  179.0 33.4 %collective-permute-start.73 = (bf16[4,4,32,512]{3,2,1,0:T(8,128)(2,1)S(1)}, bf16[4,4,32,512]{3,2,1,0:T(8,128)(2,1)S(1)}, u32[]{:S(2)}, u32[]{:S(2)}) collective-permute-start(bf16[4,4,32,512]{3,2,1,0:T(8,128)(2,1)S(1)} %pad_maximum_fusion), channel_id=1, source_target_pairs={{0,4},{4,0},{8,12},{12,8},{16,20},{20,16},{24,28},{28,24},{1,5},{5... | collective-permute-start | bytes 1572872 | tf_op jit(solution)/shard_map/ppermute | solution.py:739
  180.4 8.0 %collective-permute-start.60 = (bf16[304,256]{1,0:T(8,128)(2,1)S(1)}, bf16[304,256]{1,0:T(8,128)(2,1)S(1)}, u32[]{:S(2)}, u32[]{:S(2)}) collective-permute-start(bf16[304,256]{1,0:T(8,128)(2,1)S(1)} %get-tuple-element.263), channel_id=1, source_target_pairs={{0,8},{4,12},{8,0},{12,4},{16,24},{20,28},{24,16},{28,20},{1,9},{5... | collective-permute-start | bytes 466952 | tf_op jit(solution)/shard_map/ppermute | solution.py:739
  180.4 14.5 %collective-permute-start.61 = (bf16[304,256]{1,0:T(8,128)(2,1)S(1)}, bf16[304,256]{1,0:T(8,128)(2,1)S(1)}, u32[]{:S(2)}, u32[]{:S(2)}) collective-permute-start(bf16[304,256]{1,0:T(8,128)(2,1)S(1)} %get-tuple-element.264), channel_id=1, source_target_pairs={{0,16},{4,20},{8,24},{12,28},{16,0},{20,4},{24,8},{28,12},{1,17},{... | collective-permute-start | bytes 466952 | tf_op jit(solution)/shard_map/ppermute | solution.py:739
  182.6 12.3 %collective-permute-start.62 = (bf16[304,256]{1,0:T(8,128)(2,1)S(1)}, bf16[304,256]{1,0:T(8,128)(2,1)S(1)}, u32[]{:S(2)}, u32[]{:S(2)}) collective-permute-start(bf16[304,256]{1,0:T(8,128)(2,1)S(1)} %get-tuple-element.265), channel_id=1, source_target_pairs={{0,24},{4,28},{8,16},{12,20},{16,8},{20,12},{24,0},{28,4},{1,25},{... | collective-permute-start | bytes 466952 | tf_op jit(solution)/shard_map/ppermute | solution.py:739
  195.0 8.7 %collective-permute-start.71 = (bf16[304,256]{1,0:T(8,128)(2,1)S(1)}, bf16[304,256]{1,0:T(8,128)(2,1)S(1)}, u32[]{:S(2)}, u32[]{:S(2)}) collective-permute-start(bf16[304,256]{1,0:T(8,128)(2,1)S(1)} %shard_map.328.refs_0_), channel_id=1, source_target_pairs={{0,24},{4,28},{8,16},{12,20},{16,8},{20,12},{24,0},{28,4},{1,25},{... | collective-permute-start | bytes 466952 | tf_op jit(solution)/shard_map/ppermute | solution.py:739
  196.7 13.6 %collective-permute-start.69 = (bf16[304,256]{1,0:T(8,128)(2,1)S(1)}, bf16[304,256]{1,0:T(8,128)(2,1)S(1)}, u32[]{:S(2)}, u32[]{:S(2)}) collective-permute-start(bf16[304,256]{1,0:T(8,128)(2,1)S(1)} %shard_map.328.refs_0_), channel_id=1, source_target_pairs={{0,16},{4,20},{8,24},{12,28},{16,0},{20,4},{24,8},{28,12},{1,17},{... | collective-permute-start | bytes 466952 | tf_op jit(solution)/shard_map/ppermute | solution.py:739
  200.9 10.2 %collective-permute-start.67 = (bf16[304,256]{1,0:T(8,128)(2,1)S(1)}, bf16[304,256]{1,0:T(8,128)(2,1)S(1)}, u32[]{:S(2)}, u32[]{:S(2)}) collective-permute-start(bf16[304,256]{1,0:T(8,128)(2,1)S(1)} %shard_map.328.refs_0_), channel_id=1, source_target_pairs={{0,8},{4,12},{8,0},{12,4},{16,24},{20,28},{24,16},{28,20},{1,9},{5... | collective-permute-start | bytes 466952 | tf_op jit(solution)/shard_map/ppermute | solution.py:739
  200.9 13.5 %collective-permute-start.66 = (bf16[304,256]{1,0:T(8,128)(2,1)S(1)}, bf16[304,256]{1,0:T(8,128)(2,1)S(1)}, u32[]{:S(2)}, u32[]{:S(2)}) collective-permute-start(bf16[304,256]{1,0:T(8,128)(2,1)S(1)} %shard_map.328.refs_0_), channel_id=1, source_target_pairs={{0,4},{4,0},{8,12},{12,8},{16,20},{20,16},{24,28},{28,24},{1,5},{5... | collective-permute-start | bytes 466952 | tf_op jit(solution)/shard_map/ppermute | solution.py:739
  203.8 10.7 %collective-permute-start.72 = (bf16[304,256]{1,0:T(8,128)(2,1)S(1)}, bf16[304,256]{1,0:T(8,128)(2,1)S(1)}, u32[]{:S(2)}, u32[]{:S(2)}) collective-permute-start(bf16[304,256]{1,0:T(8,128)(2,1)S(1)} %collective-permute-done.71.refs_6_), channel_id=1, source_target_pairs={{0,4},{4,0},{8,12},{12,8},{16,20},{20,16},{24,28},{28,24},{1,5},{5... | collective-permute-start | bytes 466952 | tf_op jit(solution)/shard_map/ppermute | solution.py:739
  210.3 6.2 %collective-permute-start.70 = (bf16[304,256]{1,0:T(8,128)(2,1)S(1)}, bf16[304,256]{1,0:T(8,128)(2,1)S(1)}, u32[]{:S(2)}, u32[]{:S(2)}) collective-permute-start(bf16[304,256]{1,0:T(8,128)(2,1)S(1)} %collective-permute-done.69.refs_4_), channel_id=1, source_target_pairs={{0,4},{4,0},{8,12},{12,8},{16,20},{20,16},{24,28},{28,24},{1,5},{5... | collective-permute-start | bytes 466952 | tf_op jit(solution)/shard_map/ppermute | solution.py:739
  211.1 7.1 %collective-permute-start.68 = (bf16[304,256]{1,0:T(8,128)(2,1)S(1)}, bf16[304,256]{1,0:T(8,128)(2,1)S(1)}, u32[]{:S(2)}, u32[]{:S(2)}) collective-permute-start(bf16[304,256]{1,0:T(8,128)(2,1)S(1)} %collective-permute-done.67.refs_2_), channel_id=1, source_target_pairs={{0,4},{4,0},{8,12},{12,8},{16,20},{20,16},{24,28},{28,24},{1,5},{5... | collective-permute-start | bytes 466952 | tf_op jit(solution)/shard_map/ppermute | solution.py:739
  (29 other events, 177.7 us)

commit v5 on v4

--- a/solution.py
+++ b/solution.py
@@ -80,7 +80,7 @@
 
                 return body(at(start + i * STEP, STEP), store, carry)
 
-            carry = lax.fori_loop(0, many, step, carry)
+            carry = lax.fori_loop(0, many, step, carry, unroll=True)
             rest, left = padded - many * STEP, live - many * STEP
 
             def store_rest(refs, values, k=k, many=many, left=left):
@@ -206,7 +206,7 @@
             out[at(start + i * STEP, STEP), :] = found
             return 0
 
-        lax.fori_loop(0, many, step, 0)
+        lax.fori_loop(0, many, step, 0, unroll=True)
         rest, left = padded - many * STEP, live - many * STEP
         if rest:
             first = many * step_pixels
@@ -968,7 +968,7 @@
     s5 = allsum(tree_sum([shares[0], *(swap(shares[k], k) for k in range(1, shards))]))
     if fast:
         arrived = scatter(*halve(*expand_local))
-        far, arrived[1:3], s5 = hold((far, arrived[1:3], s5))
+        far, arrived[1], s5 = hold((far, arrived[1], s5))
     else:
         far, s5 = hold((far, s5))
     du1, s6, dz2, bias_two, gain_two = run(

time: 221 us -> 219 us (level)
  transfers between devices with their start and end apart: 74 -> 74, of which waited for: 31 -> 35; matrix products, arithmetic and copies ran while one was open for 0% -> 0% of each run, Pallas kernels for 12% -> 11%
where the time goes in v5:
time: 219 us
  waiting for transfers between devices  84.9 us (39%)
  starting transfers between devices  81.6 us (37%)
  Pallas kernels  45 us (21%)
  local copies, waits for them, and re-layouts  5.45 us (2%)
    ppermute x44, starting transfers between devices, pass_on(): return lax.ppermute(x, 'batch', [(i, i ^ k) for i in range(ranks)])  62.1 us
    ppermute x44, waiting for transfers between devices, pass_on(): return lax.ppermute(x, 'batch', [(i, i ^ k) for i in range(ranks)])  58.2 us
    pallas_call x24, Pallas kernels, run(): pl.pallas_call(kernel, out_shape=list(outs), in_specs=specs, out_specs=[p...  45 us
    ppermute x30, waiting for transfers between devices, swap(): return lax.ppermute(x, 'tensor', [(i, i ^ k) for i in range(shards)])  26.7 us
    ppermute x30, starting transfers between devices, swap(): return lax.ppermute(x, 'tensor', [(i, i ^ k) for i in range(shards)])  19.5 us
    unnamed x38, local copies, waits for them, and re-layouts  5.18 us
  transfers between devices with their start and end apart: 74, of which 35 were waited for; matrix products, arithmetic and copies ran while one was open for 0% of the time, Pallas kernels for 11%

profile of v5, /device:TPU:0, one launch (start us, length us, event | category | flops | bytes accessed | tf_op | source)
XLA Modules:
  0.0 219.0 jit_solution(552703026319439789)
XLA Ops:
  3.6 2.6 %collective-permute-start = (bf16[243,2,512]{2,1,0:T(2,128)(2,1)}, bf16[243,2,512]{2,1,0:T(2,128)(2,1)}, u32[]{:S(2)}, u32[]{:S(2)}) collective-permute-start(bf16[243,2,512]{2,1,0:T(2,128)(2,1)} %bitcast.1.refs_2_), channel_id=1, source_target_pairs={{0,2},{1,3},{2,0},{3,1},{4,6},{5,7},{6,4},{7,5},{8,10},{9,11},{10,... | collective-permute-start | bytes 1493000 | tf_op jit(solution)/shard_map/ppermute | solution.py:736
  13.8 4.8 %collective-permute-done.far_0_ = bf16[243,2,512]{2,1,0:T(2,128)(2,1)} collective-permute-done((bf16[243,2,512]{2,1,0:T(2,128)(2,1)}, bf16[243,2,512]{2,1,0:T(2,128)(2,1)}, u32[]{:S(2)}, u32[]{:S(2)}) %collective-permute-start) | collective-permute-done | bytes 497696 | tf_op jit(solution)/shard_map/ppermute | solution.py:736
  18.7 1.9 collective-permute-start.2
  20.7 1.6 shard_map.311
  22.3 15.4 %collective-permute-done.2.far_0_ = bf16[150,2,512]{2,1,0:T(2,128)(2,1)S(1)} collective-permute-done((bf16[150,2,512]{2,1,0:T(2,128)(2,1)S(1)}, bf16[150,2,512]{2,1,0:T(2,128)(2,1)S(1)}, u32[]{:S(2)}, u32[]{:S(2)}) %collective-permute-start.2) | collective-permute-done | bytes 307232 | tf_op jit(solution)/shard_map/ppermute | solution.py:736
  38.3 1.8 collective-permute-start.12
  40.2 1.6 shard_map.312
  43.0 3.9 %collective-permute-start.9 = (f32[8,256]{1,0:T(8,128)S(1)}, f32[8,256]{1,0:T(8,128)S(1)}, u32[]{:S(2)}, u32[]{:S(2)}) collective-permute-start(f32[8,256]{1,0:T(8,128)S(1)} %get-tuple-element.170), channel_id=1, source_target_pairs={{0,24},{4,28},{8,16},{12,20},{16,8},{20,12},{24,0},{28,4},{1,25},{... | collective-permute-start | bytes 24584 | tf_op jit(solution)/shard_map/ppermute | solution.py:739
  46.9 1.6 collective-permute-done.9
  48.5 2.9 %collective-permute-done.8 = f32[8,256]{1,0:T(8,128)S(1)} collective-permute-done((f32[8,256]{1,0:T(8,128)S(1)}, f32[8,256]{1,0:T(8,128)S(1)}, u32[]{:S(2)}, u32[]{:S(2)}) %collective-permute-start.8) | collective-permute-done | bytes 8224 | tf_op jit(solution)/shard_map/ppermute | solution.py:739
  52.1 1.7 collective-permute-start.10
  53.9 1.9 collective-permute-done.10.sums1_1_
  55.8 2.8 %shard_map.314 = (f32[1392,256]{1,0:T(8,128)S(1)}, f32[8,256]{1,0:T(8,128)S(1)}, bf16[1392,256]{1,0:T(8,128)(2,1)S(1)}, bf16[1392,256]{1,0:T(8,128)(2,1)S(1)}, f32[8,256]{1,0:T(8,128)S(1)}) custom-call(f32[1392,256]{1,0:T(8,128)S(1)} %get-tuple-element.169.z1, f32[8,256]{1,0:T(8,128)S(1)} %add_add_fusion.6.sums1_0_, ...), custom_call_target="tpu_custom_call" | custom-call | flops 1048576 | tf_op jit(solution)/shard_map/pallas_call | solution.py:685
  58.7 1.8 collective-permute-start.15
  60.4 3.6 %collective-permute-start.18 = (f32[8,256]{1,0:T(8,128)S(1)}, f32[8,256]{1,0:T(8,128)S(1)}, u32[]{:S(2)}, u32[]{:S(2)}) collective-permute-start(f32[8,256]{1,0:T(8,128)S(1)} %get-tuple-element.183), channel_id=1, source_target_pairs={{0,24},{4,28},{8,16},{12,20},{16,8},{20,12},{24,0},{28,4},{1,25},{... | collective-permute-start | bytes 24584 | tf_op jit(solution)/shard_map/ppermute | solution.py:739
  65.9 2.7 %collective-permute-done.17 = f32[8,256]{1,0:T(8,128)S(1)} collective-permute-done((f32[8,256]{1,0:T(8,128)S(1)}, f32[8,256]{1,0:T(8,128)S(1)}, u32[]{:S(2)}, u32[]{:S(2)}) %collective-permute-start.17) | collective-permute-done | bytes 8224 | tf_op jit(solution)/shard_map/ppermute | solution.py:739
  68.6 1.6 collective-permute-start.19
  70.2 2.1 collective-permute-done.19.sums_1_.sums2_1_
  74.0 1.6 collective-permute-start.23
  77.3 2.2 collective-permute-done.22.stats_2_.stats_1_
  79.4 2.1 shard_map.316
  82.3 3.5 %collective-permute-start.28 = (f32[8,512]{1,0:T(8,128)S(1)}, f32[8,512]{1,0:T(8,128)S(1)}, u32[]{:S(2)}, u32[]{:S(2)}) collective-permute-start(f32[8,512]{1,0:T(8,128)S(1)} %get-tuple-element.197), channel_id=1, source_target_pairs={{0,24},{4,28},{8,16},{12,20},{16,8},{20,12},{24,0},{28,4},{1,25},{... | collective-permute-start | bytes 49160 | tf_op jit(solution)/shard_map/ppermute | solution.py:739
  87.8 2.6 %collective-permute-done.27 = f32[8,512]{1,0:T(8,128)S(1)} collective-permute-done((f32[8,512]{1,0:T(8,128)S(1)}, f32[8,512]{1,0:T(8,128)S(1)}, u32[]{:S(2)}, u32[]{:S(2)}) %collective-permute-start.27) | collective-permute-done | bytes 16416 | tf_op jit(solution)/shard_map/ppermute | solution.py:739
  90.5 1.6 collective-permute-start.29
  92.0 2.2 %collective-permute-done.29.sums3_1_ = f32[8,512]{1,0:T(8,128)S(1)} collective-permute-done((f32[8,512]{1,0:T(8,128)S(1)}, f32[8,512]{1,0:T(8,128)S(1)}, u32[]{:S(2)}, u32[]{:S(2)}) %collective-permute-start.29) | collective-permute-done | bytes 16416 | tf_op jit(solution)/shard_map/ppermute | solution.py:739
  94.3 2.4 %shard_map.317 = (bf16[1392,512]{1,0:T(8,128)(2,1)S(1)}, f32[1392,512]{1,0:T(8,128)S(1)}, f32[8,512]{1,0:T(8,128)S(1)}) custom-call(f32[1392,512]{1,0:T(8,128)S(1)} %get-tuple-element.191.z3, f32[8,512]{1,0:T(8,128)S(1)} %add_add_fusion.1.sums3_0_, f32[8,512]{1,0:T(8,128)S(1)} %collective-permute-done.29.sums3_1_, f32[1,512]{1,0:T(1,128)S(1)} %bitcast.115, ...), custom_call_target="tpu_custom_call" | custom-call | flops 1048576 | tf_op jit(solution)/shard_map/pallas_call | solution.py:685
  96.7 1.5 collective-permute-start.32
  98.9 2.3 %collective-permute-start.30 = (f32[8,512]{1,0:T(8,128)S(1)}, f32[8,512]{1,0:T(8,128)S(1)}, u32[]{:S(2)}, u32[]{:S(2)}) collective-permute-start(f32[8,512]{1,0:T(8,128)S(1)} %get-tuple-element.202), channel_id=1, source_target_pairs={{0,8},{4,12},{8,0},{12,4},{16,24},{20,28},{24,16},{28,20},{1,9},{5... | collective-permute-start | bytes 49160 | tf_op jit(solution)/shard_map/ppermute | solution.py:739
  103.6 1.6 collective-permute-start.33
  105.1 2.1 shard_map.318
  107.4 1.6 shard_map.319
  109.0 2.4 %shard_map.321 = (bf16[2,4,32,512]{3,2,1,0:T(8,128)(2,1)S(1)}, bf16[2,4,32,512]{3,2,1,0:T(8,128)(2,1)S(1)}, bf16[2,4,32,512]{3,2,1,0:T(8,128)(2,1)S(1)}, bf16[2,4,32,512]{3,2,1,0:T(8,128)(2,1)S(1)}) custom-call(s32[2]{0:T(128)S(1)} %pad_add_fusion.ids, bf16[1392,256]{1,0:T(8,128)(2,1)S(1)} %get-tuple-element.221.acts_0_, ...), custom_call_target="tpu_custom_call" | custom-call | flops 1048576 | tf_op jit(solution)/shard_map/pallas_call | solution.py:685
  111.4 1.6 collective-permute-start.37
  112.9 1.7 shard_map.322
  115.8 1.9 shard_map.320
  122.9 2.5 %collective-permute-start.45 = (f32[8,256]{1,0:T(8,128)S(1)}, f32[8,256]{1,0:T(8,128)S(1)}, u32[]{:S(2)}, u32[]{:S(2)}) collective-permute-start(f32[8,256]{1,0:T(8,128)S(1)} %add_add_fusion.4), channel_id=1, source_target_pairs={{0,24},{4,28},{8,16},{12,20},{16,8},{20,12},{24,0},{28,4},{1,25},{... | collective-permute-start | bytes 24584 | tf_op jit(solution)/shard_map/ppermute | solution.py:739
  128.1 1.5 collective-permute-start.47
  129.6 2.4 %collective-permute-start.48 = (bf16[4,32,512]{2,1,0:T(8,128)(2,1)S(1)}, bf16[4,32,512]{2,1,0:T(8,128)(2,1)S(1)}, u32[]{:S(2)}, u32[]{:S(2)}) collective-permute-start(bf16[4,32,512]{2,1,0:T(8,128)(2,1)S(1)} %get-tuple-element.314), channel_id=1, source_target_pairs={{0,24},{4,28},{8,16},{12,20},{16,8},{20,12},{24,0},{28,4},{1,25},{... | collective-permute-start | bytes 393224 | tf_op jit(solution)/shard_map/ppermute | solution.py:739
  132.1 1.6 collective-permute-start.46
  133.7 2.1 collective-permute-done.46.sums5_1_
  135.8 4.4 %collective-permute-done.39 = bf16[4,32,512]{2,1,0:T(8,128)(2,1)S(1)} collective-permute-done((bf16[4,32,512]{2,1,0:T(8,128)(2,1)S(1)}, bf16[4,32,512]{2,1,0:T(8,128)(2,1)S(1)}, u32[]{:S(2)}, u32[]{:S(2)}) %collective-permute-start.39) | collective-permute-done | bytes 131104 | tf_op jit(solution)/shard_map/ppermute | solution.py:739
  140.4 4.5 %shard_map.323 = (f32[1392,256]{1,0:T(8,128)S(1)}, f32[8,256]{1,0:T(8,128)S(1)}, bf16[1392,256]{1,0:T(8,128)(2,1)S(1)}, f32[1,256]{1,0:T(1,128)}, f32[1,256]{1,0:T(1,128)}) custom-call(f32[1392,256]{1,0:T(8,128)S(1)} %get-tuple-element.218.own, bf16[2,1392,256]{2,1,0:T(8,128)(2,1)S(1)} %collective-permute-done.35.near, ...), custom_call_target="tpu_custom_call" | custom-call | flops 1048576 | tf_op jit(solution)/shard_map/pallas_call | solution.py:685
  144.9 2.3 %collective-permute-start.51 = (f32[8,256]{1,0:T(8,128)S(1)}, f32[8,256]{1,0:T(8,128)S(1)}, u32[]{:S(2)}, u32[]{:S(2)}) collective-permute-start(f32[8,256]{1,0:T(8,128)S(1)} %get-tuple-element.243), channel_id=1, source_target_pairs={{0,24},{4,28},{8,16},{12,20},{16,8},{20,12},{24,0},{28,4},{1,25},{... | collective-permute-start | bytes 24584 | tf_op jit(solution)/shard_map/ppermute | solution.py:739
  152.0 1.5 collective-permute-start.52
  153.6 3.3 %shard_map.324.group = bf16[256,384]{1,0:T(8,128)(2,1)S(1)} custom-call(bf16[1392,256]{1,0:T(8,128)(2,1)S(1)} %get-tuple-element.244.act, bf16[1392,256]{1,0:T(8,128)(2,1)S(1)} %get-tuple-element.246.dz, s32[1392,128]{1,0:T(8,128)S(1)} %copy-done.1, f32[256,256]{1,0:T(8,128)S(1)} %copy-done.3, bf16[2304,384]{1,0:T(8,128)(2,1)S(1)} %copy-done.2), custom_call_target="tpu_custom_call" | custom-call | flops 1048576 | tf_op jit(solution)/shard_map/pallas_call | solution.py:685
  157.0 2.3 %shard_map.325 = (bf16[1392,256]{1,0:T(8,128)(2,1)S(1)}, f32[1,256]{1,0:T(1,128)}, f32[1,256]{1,0:T(1,128)}, bf16[4,304,256]{2,1,0:T(8,128)(2,1)S(1)}) custom-call(s32[2]{0:T(128)S(1)} %pad_add_fusion.ids, f32[1392,256]{1,0:T(8,128)S(1)} %get-tuple-element.238.du1, f32[1392,256]{1,0:T(8,128)S(1)} %get-tuple-element.169.z1, ...), custom_call_target="tpu_custom_call" | custom-call | flops 1048576 | tf_op jit(solution)/shard_map/pallas_call | solution.py:685
  160.8 2.4 %collective-permute-start.59 = (bf16[4,32,512]{2,1,0:T(8,128)(2,1)S(1)}, bf16[4,32,512]{2,1,0:T(8,128)(2,1)S(1)}, u32[]{:S(2)}, u32[]{:S(2)}) collective-permute-start(bf16[4,32,512]{2,1,0:T(8,128)(2,1)S(1)} %pad_maximum_fusion.5.refs_0_), channel_id=1, source_target_pairs={{0,24},{4,28},{8,16},{12,20},{16,8},{20,12},{24,0},{28,4},{1,25},{... | collective-permute-start | bytes 393224 | tf_op jit(solution)/shard_map/ppermute | solution.py:739
  163.2 1.9 collective-permute-start.57
  165.1 1.6 shard_map.326
  166.7 7.6 %collective-permute-done.56 = bf16[4,304,256]{2,1,0:T(8,128)(2,1)S(1)} collective-permute-done((bf16[4,304,256]{2,1,0:T(8,128)(2,1)S(1)}, bf16[4,304,256]{2,1,0:T(8,128)(2,1)S(1)}, u32[]{:S(2)}, u32[]{:S(2)}) %collective-permute-start.56) | collective-permute-done | bytes 622624 | tf_op jit(solution)/shard_map/ppermute | solution.py:739
  174.5 1.9 collective-permute-done.63.d2
  177.0 1.7 collective-permute-start.73
  179.7 1.8 collective-permute-start.61
  181.5 1.6 collective-permute-start.62
  183.0 2.8 %shard_map.327 = (f32[150,2,512]{2,1,0:T(2,128)}, f32[294,2,512]{2,1,0:T(2,128)}, f32[243,2,512]{2,1,0:T(2,128)}) custom-call(f32[1392,512]{1,0:T(8,128)S(1)} %get-tuple-element.211.du3, bf16[1392,256]{1,0:T(8,128)(2,1)S(1)} %get-tuple-element.265.dz.d0, bf16[1392,256]{1,0:T(8,128)(2,1)S(1)} %collective-permute-done.64.d1, ...), custom_call_target="tpu_custom_call" | custom-call | flops 1048576 | tf_op jit(solution)/shard_map/pallas_call | solution.py:685
  186.6 7.7 %collective-permute-done.61.refs_2_ = bf16[304,256]{1,0:T(8,128)(2,1)S(1)} collective-permute-done((bf16[304,256]{1,0:T(8,128)(2,1)S(1)}, bf16[304,256]{1,0:T(8,128)(2,1)S(1)}, u32[]{:S(2)}, u32[]{:S(2)}) %collective-permute-start.61) | collective-permute-done | bytes 155680 | tf_op jit(solution)/shard_map/ppermute | solution.py:739
  194.4 2.0 collective-permute-start.71
  196.4 3.6 %collective-permute-start.69 = (bf16[304,256]{1,0:T(8,128)(2,1)S(1)}, bf16[304,256]{1,0:T(8,128)(2,1)S(1)}, u32[]{:S(2)}, u32[]{:S(2)}) collective-permute-start(bf16[304,256]{1,0:T(8,128)(2,1)S(1)} %shard_map.328.refs_0_), channel_id=1, source_target_pairs={{0,16},{4,20},{8,24},{12,28},{16,0},{20,4},{24,8},{28,12},{1,17},{... | collective-permute-start | bytes 466952 | tf_op jit(solution)/shard_map/ppermute | solution.py:739
  200.5 2.7 %collective-permute-done.71.refs_6_ = bf16[304,256]{1,0:T(8,128)(2,1)S(1)} collective-permute-done((bf16[304,256]{1,0:T(8,128)(2,1)S(1)}, bf16[304,256]{1,0:T(8,128)(2,1)S(1)}, u32[]{:S(2)}, u32[]{:S(2)}) %collective-permute-start.71) | collective-permute-done | bytes 155680 | tf_op jit(solution)/shard_map/ppermute | solution.py:739
  203.6 5.7 %collective-permute-done.69.refs_4_ = bf16[304,256]{1,0:T(8,128)(2,1)S(1)} collective-permute-done((bf16[304,256]{1,0:T(8,128)(2,1)S(1)}, bf16[304,256]{1,0:T(8,128)(2,1)S(1)}, u32[]{:S(2)}, u32[]{:S(2)}) %collective-permute-start.69) | collective-permute-done | bytes 155680 | tf_op jit(solution)/shard_map/ppermute | solution.py:739
  209.8 1.6 collective-permute-start.68
  211.4 2.0 shard_map.330
  214.7 1.7 collective-permute-done.68.refs_3_
  216.4 2.6 %shard_map.329 = (f32[2048,256]{1,0:T(8,128)}, f32[9,8,32,32]{3,2,1,0:T(8,128)}) custom-call(s32[2]{0:T(128)S(1)} %pad_add_fusion.ids, bf16[304,256]{1,0:T(8,128)(2,1)S(1)} %shard_map.328.refs_0_, bf16[304,256]{1,0:T(8,128)(2,1)S(1)} %collective-permute-done.66.refs_1_, bf16[304,256]{1,0:T(8,128)(2,1)S(1)} %collective-permute-done.67.refs_2_, ...), custom_call_target="tpu_custom_call" | custom-call | flops 1048576 | tf_op jit(solution)/shard_map/pallas_call | solution.py:685
  (167 shorter events, 45.1 us)
Async XLA Ops:
  3.0 9.3 %collective-permute-start.1 = (bf16[1392,512]{1,0:T(8,128)(2,1)S(1)}, bf16[1392,512]{1,0:T(8,128)(2,1)S(1)}, u32[]{:S(2)}, u32[]{:S(2)}) collective-permute-start(bf16[1392,512]{1,0:T(8,128)(2,1)S(1)} %shard_map.309.own.x.xs_0__0_), channel_id=1, source_target_pairs={{0,1},{1,0},{2,3},{3,2},{4,5},{5,4},{6,7},{7,6},{8,9},{9,8},{10,11... | collective-permute-start | bytes 4276232 | tf_op jit(solution)/shard_map/ppermute | solution.py:736
  3.6 15.1 %collective-permute-start = (bf16[243,2,512]{2,1,0:T(2,128)(2,1)}, bf16[243,2,512]{2,1,0:T(2,128)(2,1)}, u32[]{:S(2)}, u32[]{:S(2)}) collective-permute-start(bf16[243,2,512]{2,1,0:T(2,128)(2,1)} %bitcast.1.refs_2_), channel_id=1, source_target_pairs={{0,2},{1,3},{2,0},{3,1},{4,6},{5,7},{6,4},{7,5},{8,10},{9,11},{10,... | collective-permute-start | bytes 1493000 | tf_op jit(solution)/shard_map/ppermute | solution.py:736
  6.1 31.6 %collective-permute-start.3 = (bf16[294,2,512]{2,1,0:T(2,128)(2,1)}, bf16[294,2,512]{2,1,0:T(2,128)(2,1)}, u32[]{:S(2)}, u32[]{:S(2)}) collective-permute-start(bf16[294,2,512]{2,1,0:T(2,128)(2,1)} %bitcast.14.refs_1_), channel_id=1, source_target_pairs={{0,2},{1,3},{2,0},{3,1},{4,6},{5,7},{6,4},{7,5},{8,10},{9,11},{10,... | collective-permute-start | bytes 1806344 | tf_op jit(solution)/shard_map/ppermute | solution.py:736
  18.7 19.1 %collective-permute-start.2 = (bf16[150,2,512]{2,1,0:T(2,128)(2,1)S(1)}, bf16[150,2,512]{2,1,0:T(2,128)(2,1)S(1)}, u32[]{:S(2)}, u32[]{:S(2)}) collective-permute-start(bf16[150,2,512]{2,1,0:T(2,128)(2,1)S(1)} %bitcast.111), channel_id=1, source_target_pairs={{0,2},{1,3},{2,0},{3,1},{4,6},{5,7},{6,4},{7,5},{8,10},{9,11},{10,... | collective-permute-start | bytes 921608 | tf_op jit(solution)/shard_map/ppermute | solution.py:736
  37.8 4.0 %collective-permute-start.6 = (bf16[294,2,512]{2,1,0:T(2,128)(2,1)}, bf16[294,2,512]{2,1,0:T(2,128)(2,1)S(1)}, u32[]{:S(2)}, u32[]{:S(2)}) collective-permute-start(bf16[294,2,512]{2,1,0:T(2,128)(2,1)} %collective-permute-done.3.far_1_), channel_id=1, source_target_pairs={{0,1},{1,0},{2,3},{3,2},{4,5},{5,4},{6,7},{7,6},{8,9},{9,8},{10,11... | collective-permute-start | bytes 1806344 | tf_op jit(solution)/shard_map/ppermute | solution.py:736
  37.8 4.0 %collective-permute-start.5 = (bf16[150,2,512]{2,1,0:T(2,128)(2,1)S(1)}, bf16[150,2,512]{2,1,0:T(2,128)(2,1)S(1)}, u32[]{:S(2)}, u32[]{:S(2)}) collective-permute-start(bf16[150,2,512]{2,1,0:T(2,128)(2,1)S(1)} %collective-permute-done.2.far_0_), channel_id=1, source_target_pairs={{0,1},{1,0},{2,3},{3,2},{4,5},{5,4},{6,7},{7,6},{8,9},{9,8},{10,11... | collective-permute-start | bytes 921608 | tf_op jit(solution)/shard_map/ppermute | solution.py:736
  38.3 15.6 %collective-permute-start.11 = (bf16[512,256]{1,0:T(8,128)(2,1)S(1)}, bf16[512,256]{1,0:T(8,128)(2,1)S(1)}, u32[]{:S(2)}, u32[]{:S(2)}) collective-permute-start(bf16[512,256]{1,0:T(8,128)(2,1)S(1)} %get-tuple-element.176), channel_id=1, source_target_pairs={{0,1},{1,0},{2,3},{3,2},{4,5},{5,4},{6,7},{7,6},{8,9},{9,8},{10,11... | collective-permute-start | bytes 786440 | tf_op jit(solution)/shard_map/ppermute | solution.py:736
  38.3 15.6 %collective-permute-start.12 = (bf16[512,256]{1,0:T(8,128)(2,1)S(1)}, bf16[512,256]{1,0:T(8,128)(2,1)S(1)}, u32[]{:S(2)}, u32[]{:S(2)}) collective-permute-start(bf16[512,256]{1,0:T(8,128)(2,1)S(1)} %get-tuple-element.177), channel_id=1, source_target_pairs={{0,2},{1,3},{2,0},{3,1},{4,6},{5,7},{6,4},{7,5},{8,10},{9,11},{10,... | collective-permute-start | bytes 786440 | tf_op jit(solution)/shard_map/ppermute | solution.py:736
  40.0 13.9 %collective-permute-start.13 = (bf16[512,256]{1,0:T(8,128)(2,1)S(1)}, bf16[512,256]{1,0:T(8,128)(2,1)S(1)}, u32[]{:S(2)}, u32[]{:S(2)}) collective-permute-start(bf16[512,256]{1,0:T(8,128)(2,1)S(1)} %get-tuple-element.178), channel_id=1, source_target_pairs={{0,3},{1,2},{2,1},{3,0},{4,7},{5,6},{6,5},{7,4},{8,11},{9,10},{10,... | collective-permute-start | bytes 786440 | tf_op jit(solution)/shard_map/ppermute | solution.py:736
  43.0 5.5 %collective-permute-start.9 = (f32[8,256]{1,0:T(8,128)S(1)}, f32[8,256]{1,0:T(8,128)S(1)}, u32[]{:S(2)}, u32[]{:S(2)}) collective-permute-start(f32[8,256]{1,0:T(8,128)S(1)} %get-tuple-element.170), channel_id=1, source_target_pairs={{0,24},{4,28},{8,16},{12,20},{16,8},{20,12},{24,0},{28,4},{1,25},{... | collective-permute-start | bytes 24584 | tf_op jit(solution)/shard_map/ppermute | solution.py:739
  46.9 4.5 %collective-permute-start.8 = (f32[8,256]{1,0:T(8,128)S(1)}, f32[8,256]{1,0:T(8,128)S(1)}, u32[]{:S(2)}, u32[]{:S(2)}) collective-permute-start(f32[8,256]{1,0:T(8,128)S(1)} %get-tuple-element.170), channel_id=1, source_target_pairs={{0,16},{4,20},{8,24},{12,28},{16,0},{20,4},{24,8},{28,12},{1,17},{... | collective-permute-start | bytes 24584 | tf_op jit(solution)/shard_map/ppermute | solution.py:739
  58.7 15.3 %collective-permute-start.15 = (bf16[1392,256]{1,0:T(8,128)(2,1)S(1)}, bf16[1392,256]{1,0:T(8,128)(2,1)S(1)}, u32[]{:S(2)}, u32[]{:S(2)}) collective-permute-start(bf16[1392,256]{1,0:T(8,128)(2,1)S(1)} %get-tuple-element.182.zs_0_), channel_id=1, source_target_pairs={{0,2},{1,3},{2,0},{3,1},{4,6},{5,7},{6,4},{7,5},{8,10},{9,11},{10,... | collective-permute-start | bytes 2138120 | tf_op jit(solution)/shard_map/ppermute | solution.py:736
  60.4 5.4 %collective-permute-start.18 = (f32[8,256]{1,0:T(8,128)S(1)}, f32[8,256]{1,0:T(8,128)S(1)}, u32[]{:S(2)}, u32[]{:S(2)}) collective-permute-start(f32[8,256]{1,0:T(8,128)S(1)} %get-tuple-element.183), channel_id=1, source_target_pairs={{0,24},{4,28},{8,16},{12,20},{16,8},{20,12},{24,0},{28,4},{1,25},{... | collective-permute-start | bytes 24584 | tf_op jit(solution)/shard_map/ppermute | solution.py:739
  64.0 4.5 %collective-permute-start.17 = (f32[8,256]{1,0:T(8,128)S(1)}, f32[8,256]{1,0:T(8,128)S(1)}, u32[]{:S(2)}, u32[]{:S(2)}) collective-permute-start(f32[8,256]{1,0:T(8,128)S(1)} %get-tuple-element.183), channel_id=1, source_target_pairs={{0,16},{4,20},{8,24},{12,28},{16,0},{20,4},{24,8},{28,12},{1,17},{... | collective-permute-start | bytes 24584 | tf_op jit(solution)/shard_map/ppermute | solution.py:739
  64.0 4.5 %collective-permute-start.16 = (f32[8,256]{1,0:T(8,128)S(1)}, f32[8,256]{1,0:T(8,128)S(1)}, u32[]{:S(2)}, u32[]{:S(2)}) collective-permute-start(f32[8,256]{1,0:T(8,128)S(1)} %get-tuple-element.183), channel_id=1, source_target_pairs={{0,8},{4,12},{8,0},{12,4},{16,24},{20,28},{24,16},{28,20},{1,9},{5... | collective-permute-start | bytes 24584 | tf_op jit(solution)/shard_map/ppermute | solution.py:739
  72.4 7.0 %collective-permute-start.14 = (bf16[1392,256]{1,0:T(8,128)(2,1)S(1)}, bf16[1392,256]{1,0:T(8,128)(2,1)S(1)}, u32[]{:S(2)}, u32[]{:S(2)}) collective-permute-start(bf16[1392,256]{1,0:T(8,128)(2,1)S(1)} %get-tuple-element.182.zs_0_), channel_id=1, source_target_pairs={{0,1},{1,0},{2,3},{3,2},{4,5},{5,4},{6,7},{7,6},{8,9},{9,8},{10,11... | collective-permute-start | bytes 2138120 | tf_op jit(solution)/shard_map/ppermute | solution.py:736
  74.0 5.4 %collective-permute-start.21 = (bf16[1392,256]{1,0:T(8,128)(2,1)S(1)}, bf16[1392,256]{1,0:T(8,128)(2,1)S(1)}, u32[]{:S(2)}, u32[]{:S(2)}) collective-permute-start(bf16[1392,256]{1,0:T(8,128)(2,1)S(1)} %collective-permute-done.15.zs_2_.zs_1_), channel_id=1, source_target_pairs={{0,1},{1,0},{2,3},{3,2},{4,5},{5,4},{6,7},{7,6},{8,9},{9,8},{10,11... | collective-permute-start | bytes 2138120 | tf_op jit(solution)/shard_map/ppermute | solution.py:736
  75.6 3.8 %collective-permute-start.22 = (f32[24,256]{1,0:T(8,128)S(1)}, f32[24,256]{1,0:T(8,128)S(1)}, u32[]{:S(2)}, u32[]{:S(2)}) collective-permute-start(f32[24,256]{1,0:T(8,128)S(1)} %shard_map.315.stats_0_), channel_id=1, source_target_pairs={{0,2},{1,3},{2,0},{3,1},{4,6},{5,7},{6,4},{7,5},{8,10},{9,11},{10,... | collective-permute-start | bytes 73736 | tf_op jit(solution)/shard_map/ppermute | solution.py:736
  81.6 12.7 %collective-permute-start.24 = (bf16[512,256]{1,0:T(8,128)(2,1)S(1)}, bf16[512,256]{1,0:T(8,128)(2,1)S(1)}, u32[]{:S(2)}, u32[]{:S(2)}) collective-permute-start(bf16[512,256]{1,0:T(8,128)(2,1)S(1)} %get-tuple-element.195), channel_id=1, source_target_pairs={{0,1},{1,0},{2,3},{3,2},{4,5},{5,4},{6,7},{7,6},{8,9},{9,8},{10,11... | collective-permute-start | bytes 786440 | tf_op jit(solution)/shard_map/ppermute | solution.py:736
  81.7 12.6 %collective-permute-start.25 = (bf16[512,256]{1,0:T(8,128)(2,1)S(1)}, bf16[512,256]{1,0:T(8,128)(2,1)S(1)}, u32[]{:S(2)}, u32[]{:S(2)}) collective-permute-start(bf16[512,256]{1,0:T(8,128)(2,1)S(1)} %get-tuple-element.196), channel_id=1, source_target_pairs={{0,2},{1,3},{2,0},{3,1},{4,6},{5,7},{6,4},{7,5},{8,10},{9,11},{10,... | collective-permute-start | bytes 786440 | tf_op jit(solution)/shard_map/ppermute | solution.py:736
  82.3 5.5 %collective-permute-start.28 = (f32[8,512]{1,0:T(8,128)S(1)}, f32[8,512]{1,0:T(8,128)S(1)}, u32[]{:S(2)}, u32[]{:S(2)}) collective-permute-start(f32[8,512]{1,0:T(8,128)S(1)} %get-tuple-element.197), channel_id=1, source_target_pairs={{0,24},{4,28},{8,16},{12,20},{16,8},{20,12},{24,0},{28,4},{1,25},{... | collective-permute-start | bytes 49160 | tf_op jit(solution)/shard_map/ppermute | solution.py:739
  85.8 4.6 %collective-permute-start.27 = (f32[8,512]{1,0:T(8,128)S(1)}, f32[8,512]{1,0:T(8,128)S(1)}, u32[]{:S(2)}, u32[]{:S(2)}) collective-permute-start(f32[8,512]{1,0:T(8,128)S(1)} %get-tuple-element.197), channel_id=1, source_target_pairs={{0,16},{4,20},{8,24},{12,28},{16,0},{20,4},{24,8},{28,12},{1,17},{... | collective-permute-start | bytes 49160 | tf_op jit(solution)/shard_map/ppermute | solution.py:739
  85.8 4.6 %collective-permute-start.26 = (f32[8,512]{1,0:T(8,128)S(1)}, f32[8,512]{1,0:T(8,128)S(1)}, u32[]{:S(2)}, u32[]{:S(2)}) collective-permute-start(f32[8,512]{1,0:T(8,128)S(1)} %get-tuple-element.197), channel_id=1, source_target_pairs={{0,8},{4,12},{8,0},{12,4},{16,24},{20,28},{24,16},{28,20},{1,9},{5... | collective-permute-start | bytes 49160 | tf_op jit(solution)/shard_map/ppermute | solution.py:739
  96.6 10.7 %collective-permute-start.34 = (bf16[512,256]{1,0:T(8,128)(2,1)S(1)}, bf16[512,256]{1,0:T(8,128)(2,1)S(1)}, u32[]{:S(2)}, u32[]{:S(2)}) collective-permute-start(bf16[512,256]{1,0:T(8,128)(2,1)S(1)} %get-tuple-element.212), channel_id=1, source_target_pairs={{0,3},{1,2},{2,1},{3,0},{4,7},{5,6},{6,5},{7,4},{8,11},{9,10},{10,... | collective-permute-start | bytes 786440 | tf_op jit(solution)/shard_map/ppermute | solution.py:736
  96.7 5.6 %collective-permute-start.32 = (f32[8,512]{1,0:T(8,128)S(1)}, f32[8,512]{1,0:T(8,128)S(1)}, u32[]{:S(2)}, u32[]{:S(2)}) collective-permute-start(f32[8,512]{1,0:T(8,128)S(1)} %get-tuple-element.202), channel_id=1, source_target_pairs={{0,24},{4,28},{8,16},{12,20},{16,8},{20,12},{24,0},{28,4},{1,25},{... | collective-permute-start | bytes 49160 | tf_op jit(solution)/shard_map/ppermute | solution.py:739
  98.2 4.9 %collective-permute-start.31 = (f32[8,512]{1,0:T(8,128)S(1)}, f32[8,512]{1,0:T(8,128)S(1)}, u32[]{:S(2)}, u32[]{:S(2)}) collective-permute-start(f32[8,512]{1,0:T(8,128)S(1)} %get-tuple-element.202), channel_id=1, source_target_pairs={{0,16},{4,20},{8,24},{12,28},{16,0},{20,4},{24,8},{28,12},{1,17},{... | collective-permute-start | bytes 49160 | tf_op jit(solution)/shard_map/ppermute | solution.py:739
  98.9 4.7 %collective-permute-start.30 = (f32[8,512]{1,0:T(8,128)S(1)}, f32[8,512]{1,0:T(8,128)S(1)}, u32[]{:S(2)}, u32[]{:S(2)}) collective-permute-start(f32[8,512]{1,0:T(8,128)S(1)} %get-tuple-element.202), channel_id=1, source_target_pairs={{0,8},{4,12},{8,0},{12,4},{16,24},{20,28},{24,16},{28,20},{1,9},{5... | collective-permute-start | bytes 49160 | tf_op jit(solution)/shard_map/ppermute | solution.py:739
  109.0 12.7 %collective-permute-start.35 = (bf16[2,1392,256]{2,1,0:T(8,128)(2,1)S(1)}, bf16[2,1392,256]{2,1,0:T(8,128)(2,1)S(1)}, u32[]{:S(2)}, u32[]{:S(2)}) collective-permute-start(bf16[2,1392,256]{2,1,0:T(8,128)(2,1)S(1)} %get-tuple-element.219.send), channel_id=1, source_target_pairs={{0,1},{1,0},{2,3},{3,2},{4,5},{5,4},{6,7},{7,6},{8,9},{9,8},{10,11... | collective-permute-start | bytes 4276232 | tf_op jit(solution)/shard_map/ppermute | solution.py:736
  111.4 8.8 %collective-permute-start.37 = (bf16[2,4,32,512]{3,2,1,0:T(8,128)(2,1)S(1)}, bf16[2,4,32,512]{3,2,1,0:T(8,128)(2,1)S(1)}, u32[]{:S(2)}, u32[]{:S(2)}) collective-permute-start(bf16[2,4,32,512]{3,2,1,0:T(8,128)(2,1)S(1)} %get-tuple-element.227), channel_id=1, source_target_pairs={{0,4},{4,0},{8,12},{12,8},{16,20},{20,16},{24,28},{28,24},{1,5},{5... | collective-permute-start | bytes 786440 | tf_op jit(solution)/shard_map/ppermute | solution.py:739
  114.6 8.3 %collective-permute-start.40 = (f32[8,256]{1,0:T(8,128)S(1)}, f32[8,256]{1,0:T(8,128)S(1)}, u32[]{:S(2)}, u32[]{:S(2)}) collective-permute-start(f32[8,256]{1,0:T(8,128)S(1)} %get-tuple-element.230), channel_id=1, source_target_pairs={{0,1},{1,0},{2,3},{3,2},{4,5},{5,4},{6,7},{7,6},{8,9},{9,8},{10,11... | collective-permute-start | bytes 24584 | tf_op jit(solution)/shard_map/ppermute | solution.py:736
  114.9 8.0 %collective-permute-start.42 = (f32[8,256]{1,0:T(8,128)S(1)}, f32[8,256]{1,0:T(8,128)S(1)}, u32[]{:S(2)}, u32[]{:S(2)}) collective-permute-start(f32[8,256]{1,0:T(8,128)S(1)} %get-tuple-element.232), channel_id=1, source_target_pairs={{0,3},{1,2},{2,1},{3,0},{4,7},{5,6},{6,5},{7,4},{8,11},{9,10},{10,... | collective-permute-start | bytes 24584 | tf_op jit(solution)/shard_map/ppermute | solution.py:736
  117.8 5.2 %collective-permute-start.41 = (f32[8,256]{1,0:T(8,128)S(1)}, f32[8,256]{1,0:T(8,128)S(1)}, u32[]{:S(2)}, u32[]{:S(2)}) collective-permute-start(f32[8,256]{1,0:T(8,128)S(1)} %get-tuple-element.231), channel_id=1, source_target_pairs={{0,2},{1,3},{2,0},{3,1},{4,6},{5,7},{6,4},{7,5},{8,10},{9,11},{10,... | collective-permute-start | bytes 24584 | tf_op jit(solution)/shard_map/ppermute | solution.py:736
  120.1 7.9 %collective-permute-start.38 = (bf16[2,4,32,512]{3,2,1,0:T(8,128)(2,1)S(1)}, bf16[2,4,32,512]{3,2,1,0:T(8,128)(2,1)S(1)}, u32[]{:S(2)}, u32[]{:S(2)}) collective-permute-start(bf16[2,4,32,512]{3,2,1,0:T(8,128)(2,1)S(1)} %get-tuple-element.228), channel_id=1, source_target_pairs={{0,4},{4,0},{8,12},{12,8},{16,20},{20,16},{24,28},{28,24},{1,5},{5... | collective-permute-start | bytes 786440 | tf_op jit(solution)/shard_map/ppermute | solution.py:739
  121.8 18.4 %collective-permute-start.36 = (bf16[1392,256]{1,0:T(8,128)(2,1)S(1)}, bf16[1392,256]{1,0:T(8,128)(2,1)S(1)}, u32[]{:S(2)}, u32[]{:S(2)}) collective-permute-start(bf16[1392,256]{1,0:T(8,128)(2,1)S(1)} %fusion), channel_id=1, source_target_pairs={{0,2},{1,3},{2,0},{3,1},{4,6},{5,7},{6,4},{7,5},{8,10},{9,11},{10,... | collective-permute-start | bytes 2138120 | tf_op jit(solution)/shard_map/ppermute | solution.py:736
  122.9 6.7 %collective-permute-start.45 = (f32[8,256]{1,0:T(8,128)S(1)}, f32[8,256]{1,0:T(8,128)S(1)}, u32[]{:S(2)}, u32[]{:S(2)}) collective-permute-start(f32[8,256]{1,0:T(8,128)S(1)} %add_add_fusion.4), channel_id=1, source_target_pairs={{0,24},{4,28},{8,16},{12,20},{16,8},{20,12},{24,0},{28,4},{1,25},{... | collective-permute-start | bytes 24584 | tf_op jit(solution)/shard_map/ppermute | solution.py:739
  125.4 6.7 %collective-permute-start.44 = (f32[8,256]{1,0:T(8,128)S(1)}, f32[8,256]{1,0:T(8,128)S(1)}, u32[]{:S(2)}, u32[]{:S(2)}) collective-permute-start(f32[8,256]{1,0:T(8,128)S(1)} %add_add_fusion.4), channel_id=1, source_target_pairs={{0,16},{4,20},{8,24},{12,28},{16,0},{20,4},{24,8},{28,12},{1,17},{... | collective-permute-start | bytes 24584 | tf_op jit(solution)/shard_map/ppermute | solution.py:739
  126.3 5.8 %collective-permute-start.43 = (f32[8,256]{1,0:T(8,128)S(1)}, f32[8,256]{1,0:T(8,128)S(1)}, u32[]{:S(2)}, u32[]{:S(2)}) collective-permute-start(f32[8,256]{1,0:T(8,128)S(1)} %add_add_fusion.4), channel_id=1, source_target_pairs={{0,8},{4,12},{8,0},{12,4},{16,24},{20,28},{24,16},{28,20},{1,9},{5... | collective-permute-start | bytes 24584 | tf_op jit(solution)/shard_map/ppermute | solution.py:739
  128.1 12.2 %collective-permute-start.47 = (bf16[4,32,512]{2,1,0:T(8,128)(2,1)S(1)}, bf16[4,32,512]{2,1,0:T(8,128)(2,1)S(1)}, u32[]{:S(2)}, u32[]{:S(2)}) collective-permute-start(bf16[4,32,512]{2,1,0:T(8,128)(2,1)S(1)} %get-tuple-element.313), channel_id=1, source_target_pairs={{0,16},{4,20},{8,24},{12,28},{16,0},{20,4},{24,8},{28,12},{1,17},{... | collective-permute-start | bytes 393224 | tf_op jit(solution)/shard_map/ppermute | solution.py:739
  129.6 10.6 %collective-permute-start.48 = (bf16[4,32,512]{2,1,0:T(8,128)(2,1)S(1)}, bf16[4,32,512]{2,1,0:T(8,128)(2,1)S(1)}, u32[]{:S(2)}, u32[]{:S(2)}) collective-permute-start(bf16[4,32,512]{2,1,0:T(8,128)(2,1)S(1)} %get-tuple-element.314), channel_id=1, source_target_pairs={{0,24},{4,28},{8,16},{12,20},{16,8},{20,12},{24,0},{28,4},{1,25},{... | collective-permute-start | bytes 393224 | tf_op jit(solution)/shard_map/ppermute | solution.py:739
  132.1 8.2 %collective-permute-start.39 = (bf16[4,32,512]{2,1,0:T(8,128)(2,1)S(1)}, bf16[4,32,512]{2,1,0:T(8,128)(2,1)S(1)}, u32[]{:S(2)}, u32[]{:S(2)}) collective-permute-start(bf16[4,32,512]{2,1,0:T(8,128)(2,1)S(1)} %fusion.8), channel_id=1, source_target_pairs={{0,8},{4,12},{8,0},{12,4},{16,24},{20,28},{24,16},{28,20},{1,9},{5... | collective-permute-start | bytes 393224 | tf_op jit(solution)/shard_map/ppermute | solution.py:739
  144.9 5.6 %collective-permute-start.51 = (f32[8,256]{1,0:T(8,128)S(1)}, f32[8,256]{1,0:T(8,128)S(1)}, u32[]{:S(2)}, u32[]{:S(2)}) collective-permute-start(f32[8,256]{1,0:T(8,128)S(1)} %get-tuple-element.243), channel_id=1, source_target_pairs={{0,24},{4,28},{8,16},{12,20},{16,8},{20,12},{24,0},{28,4},{1,25},{... | collective-permute-start | bytes 24584 | tf_op jit(solution)/shard_map/ppermute | solution.py:739
  147.2 4.5 %collective-permute-start.50 = (f32[8,256]{1,0:T(8,128)S(1)}, f32[8,256]{1,0:T(8,128)S(1)}, u32[]{:S(2)}, u32[]{:S(2)}) collective-permute-start(f32[8,256]{1,0:T(8,128)S(1)} %get-tuple-element.243), channel_id=1, source_target_pairs={{0,16},{4,20},{8,24},{12,28},{16,0},{20,4},{24,8},{28,12},{1,17},{... | collective-permute-start | bytes 24584 | tf_op jit(solution)/shard_map/ppermute | solution.py:739
  149.4 7.5 %collective-permute-start.55 = (bf16[32,512]{1,0:T(8,128)(2,1)S(1)}, bf16[32,512]{1,0:T(8,128)(2,1)S(1)}, u32[]{:S(2)}, u32[]{:S(2)}) collective-permute-start(bf16[32,512]{1,0:T(8,128)(2,1)S(1)} %get-tuple-element.316), channel_id=1, source_target_pairs={{0,3},{1,2},{2,1},{3,0},{4,7},{5,6},{6,5},{7,4},{8,11},{9,10},{10,... | collective-permute-start | bytes 98312 | tf_op jit(solution)/shard_map/ppermute | solution.py:736
  149.5 7.5 %collective-permute-start.54 = (bf16[32,512]{1,0:T(8,128)(2,1)S(1)}, bf16[32,512]{1,0:T(8,128)(2,1)S(1)}, u32[]{:S(2)}, u32[]{:S(2)}) collective-permute-start(bf16[32,512]{1,0:T(8,128)(2,1)S(1)} %get-tuple-element.317), channel_id=1, source_target_pairs={{0,2},{1,3},{2,0},{3,1},{4,6},{5,7},{6,4},{7,5},{8,10},{9,11},{10,... | collective-permute-start | bytes 98312 | tf_op jit(solution)/shard_map/ppermute | solution.py:736
  150.5 6.4 %collective-permute-start.53 = (bf16[32,512]{1,0:T(8,128)(2,1)S(1)}, bf16[32,512]{1,0:T(8,128)(2,1)S(1)}, u32[]{:S(2)}, u32[]{:S(2)}) collective-permute-start(bf16[32,512]{1,0:T(8,128)(2,1)S(1)} %get-tuple-element.318), channel_id=1, source_target_pairs={{0,1},{1,0},{2,3},{3,2},{4,5},{5,4},{6,7},{7,6},{8,9},{9,8},{10,11... | collective-permute-start | bytes 98312 | tf_op jit(solution)/shard_map/ppermute | solution.py:736
  152.0 4.9 %collective-permute-start.52 = (f32[8,256]{1,0:T(8,128)S(1)}, f32[8,256]{1,0:T(8,128)S(1)}, u32[]{:S(2)}, u32[]{:S(2)}) collective-permute-start(f32[8,256]{1,0:T(8,128)S(1)} %add_add_fusion.2.sums6_0_), channel_id=1, source_target_pairs={{0,4},{4,0},{8,12},{12,8},{16,20},{20,16},{24,28},{28,24},{1,5},{5... | collective-permute-start | bytes 24584 | tf_op jit(solution)/shard_map/ppermute | solution.py:739
  159.3 15.0 %collective-permute-start.56 = (bf16[4,304,256]{2,1,0:T(8,128)(2,1)S(1)}, bf16[4,304,256]{2,1,0:T(8,128)(2,1)S(1)}, u32[]{:S(2)}, u32[]{:S(2)}) collective-permute-start(bf16[4,304,256]{2,1,0:T(8,128)(2,1)S(1)} %get-tuple-element.258), channel_id=1, source_target_pairs={{0,4},{4,0},{8,12},{12,8},{16,20},{20,16},{24,28},{28,24},{1,5},{5... | collective-permute-start | bytes 1867784 | tf_op jit(solution)/shard_map/ppermute | solution.py:739
  159.7 16.7 %collective-permute-start.63 = (bf16[1392,256]{1,0:T(8,128)(2,1)S(1)}, bf16[1392,256]{1,0:T(8,128)(2,1)S(1)}, u32[]{:S(2)}, u32[]{:S(2)}) collective-permute-start(bf16[1392,256]{1,0:T(8,128)(2,1)S(1)} %get-tuple-element.265.dz.d0), channel_id=1, source_target_pairs={{0,2},{1,3},{2,0},{3,1},{4,6},{5,7},{6,4},{7,5},{8,10},{9,11},{10,... | collective-permute-start | bytes 2138120 | tf_op jit(solution)/shard_map/ppermute | solution.py:736
  160.8 13.8 %collective-permute-start.59 = (bf16[4,32,512]{2,1,0:T(8,128)(2,1)S(1)}, bf16[4,32,512]{2,1,0:T(8,128)(2,1)S(1)}, u32[]{:S(2)}, u32[]{:S(2)}) collective-permute-start(bf16[4,32,512]{2,1,0:T(8,128)(2,1)S(1)} %pad_maximum_fusion.5.refs_0_), channel_id=1, source_target_pairs={{0,24},{4,28},{8,16},{12,20},{16,8},{20,12},{24,0},{28,4},{1,25},{... | collective-permute-start | bytes 393224 | tf_op jit(solution)/shard_map/ppermute | solution.py:739
  163.2 11.4 %collective-permute-start.58 = (bf16[4,32,512]{2,1,0:T(8,128)(2,1)S(1)}, bf16[4,32,512]{2,1,0:T(8,128)(2,1)S(1)}, u32[]{:S(2)}, u32[]{:S(2)}) collective-permute-start(bf16[4,32,512]{2,1,0:T(8,128)(2,1)S(1)} %pad_maximum_fusion.5.refs_0_), channel_id=1, source_target_pairs={{0,16},{4,20},{8,24},{12,28},{16,0},{20,4},{24,8},{28,12},{1,17},{... | collective-permute-start | bytes 393224 | tf_op jit(solution)/shard_map/ppermute | solution.py:739
  163.2 11.3 %collective-permute-start.57 = (bf16[4,32,512]{2,1,0:T(8,128)(2,1)S(1)}, bf16[4,32,512]{2,1,0:T(8,128)(2,1)S(1)}, u32[]{:S(2)}, u32[]{:S(2)}) collective-permute-start(bf16[4,32,512]{2,1,0:T(8,128)(2,1)S(1)} %pad_maximum_fusion.5.refs_0_), channel_id=1, source_target_pairs={{0,8},{4,12},{8,0},{12,4},{16,24},{20,28},{24,16},{28,20},{1,9},{5... | collective-permute-start | bytes 393224 | tf_op jit(solution)/shard_map/ppermute | solution.py:739
  176.4 5.1 %collective-permute-start.64 = (bf16[1392,256]{1,0:T(8,128)(2,1)S(1)}, bf16[1392,256]{1,0:T(8,128)(2,1)S(1)}, u32[]{:S(2)}, u32[]{:S(2)}) collective-permute-start(bf16[1392,256]{1,0:T(8,128)(2,1)S(1)} %get-tuple-element.265.dz.d0), channel_id=1, source_target_pairs={{0,1},{1,0},{2,3},{3,2},{4,5},{5,4},{6,7},{7,6},{8,9},{9,8},{10,11... | collective-permute-start | bytes 2138120 | tf_op jit(solution)/shard_map/ppermute | solution.py:736
  176.4 6.6 %collective-permute-start.65 = (bf16[1392,256]{1,0:T(8,128)(2,1)S(1)}, bf16[1392,256]{1,0:T(8,128)(2,1)S(1)}, u32[]{:S(2)}, u32[]{:S(2)}) collective-permute-start(bf16[1392,256]{1,0:T(8,128)(2,1)S(1)} %collective-permute-done.63.d2), channel_id=1, source_target_pairs={{0,1},{1,0},{2,3},{3,2},{4,5},{5,4},{6,7},{7,6},{8,9},{9,8},{10,11... | collective-permute-start | bytes 2138120 | tf_op jit(solution)/shard_map/ppermute | solution.py:736
  177.0 34.4 %collective-permute-start.73 = (bf16[4,4,32,512]{3,2,1,0:T(8,128)(2,1)S(1)}, bf16[4,4,32,512]{3,2,1,0:T(8,128)(2,1)S(1)}, u32[]{:S(2)}, u32[]{:S(2)}) collective-permute-start(bf16[4,4,32,512]{3,2,1,0:T(8,128)(2,1)S(1)} %pad_maximum_fusion), channel_id=1, source_target_pairs={{0,4},{4,0},{8,12},{12,8},{16,20},{20,16},{24,28},{28,24},{1,5},{5... | collective-permute-start | bytes 1572872 | tf_op jit(solution)/shard_map/ppermute | solution.py:739
  178.6 7.9 %collective-permute-start.60 = (bf16[304,256]{1,0:T(8,128)(2,1)S(1)}, bf16[304,256]{1,0:T(8,128)(2,1)S(1)}, u32[]{:S(2)}, u32[]{:S(2)}) collective-permute-start(bf16[304,256]{1,0:T(8,128)(2,1)S(1)} %get-tuple-element.261), channel_id=1, source_target_pairs={{0,8},{4,12},{8,0},{12,4},{16,24},{20,28},{24,16},{28,20},{1,9},{5... | collective-permute-start | bytes 466952 | tf_op jit(solution)/shard_map/ppermute | solution.py:739
  179.7 14.5 %collective-permute-start.61 = (bf16[304,256]{1,0:T(8,128)(2,1)S(1)}, bf16[304,256]{1,0:T(8,128)(2,1)S(1)}, u32[]{:S(2)}, u32[]{:S(2)}) collective-permute-start(bf16[304,256]{1,0:T(8,128)(2,1)S(1)} %get-tuple-element.262), channel_id=1, source_target_pairs={{0,16},{4,20},{8,24},{12,28},{16,0},{20,4},{24,8},{28,12},{1,17},{... | collective-permute-start | bytes 466952 | tf_op jit(solution)/shard_map/ppermute | solution.py:739
  181.5 12.8 %collective-permute-start.62 = (bf16[304,256]{1,0:T(8,128)(2,1)S(1)}, bf16[304,256]{1,0:T(8,128)(2,1)S(1)}, u32[]{:S(2)}, u32[]{:S(2)}) collective-permute-start(bf16[304,256]{1,0:T(8,128)(2,1)S(1)} %get-tuple-element.263), channel_id=1, source_target_pairs={{0,24},{4,28},{8,16},{12,20},{16,8},{20,12},{24,0},{28,4},{1,25},{... | collective-permute-start | bytes 466952 | tf_op jit(solution)/shard_map/ppermute | solution.py:739
  194.4 8.8 %collective-permute-start.71 = (bf16[304,256]{1,0:T(8,128)(2,1)S(1)}, bf16[304,256]{1,0:T(8,128)(2,1)S(1)}, u32[]{:S(2)}, u32[]{:S(2)}) collective-permute-start(bf16[304,256]{1,0:T(8,128)(2,1)S(1)} %shard_map.328.refs_0_), channel_id=1, source_target_pairs={{0,24},{4,28},{8,16},{12,20},{16,8},{20,12},{24,0},{28,4},{1,25},{... | collective-permute-start | bytes 466952 | tf_op jit(solution)/shard_map/ppermute | solution.py:739
  196.4 12.9 %collective-permute-start.69 = (bf16[304,256]{1,0:T(8,128)(2,1)S(1)}, bf16[304,256]{1,0:T(8,128)(2,1)S(1)}, u32[]{:S(2)}, u32[]{:S(2)}) collective-permute-start(bf16[304,256]{1,0:T(8,128)(2,1)S(1)} %shard_map.328.refs_0_), channel_id=1, source_target_pairs={{0,16},{4,20},{8,24},{12,28},{16,0},{20,4},{24,8},{28,12},{1,17},{... | collective-permute-start | bytes 466952 | tf_op jit(solution)/shard_map/ppermute | solution.py:739
  200.1 9.7 %collective-permute-start.67 = (bf16[304,256]{1,0:T(8,128)(2,1)S(1)}, bf16[304,256]{1,0:T(8,128)(2,1)S(1)}, u32[]{:S(2)}, u32[]{:S(2)}) collective-permute-start(bf16[304,256]{1,0:T(8,128)(2,1)S(1)} %shard_map.328.refs_0_), channel_id=1, source_target_pairs={{0,8},{4,12},{8,0},{12,4},{16,24},{20,28},{24,16},{28,20},{1,9},{5... | collective-permute-start | bytes 466952 | tf_op jit(solution)/shard_map/ppermute | solution.py:739
  200.1 13.4 %collective-permute-start.66 = (bf16[304,256]{1,0:T(8,128)(2,1)S(1)}, bf16[304,256]{1,0:T(8,128)(2,1)S(1)}, u32[]{:S(2)}, u32[]{:S(2)}) collective-permute-start(bf16[304,256]{1,0:T(8,128)(2,1)S(1)} %shard_map.328.refs_0_), channel_id=1, source_target_pairs={{0,4},{4,0},{8,12},{12,8},{16,20},{20,16},{24,28},{28,24},{1,5},{5... | collective-permute-start | bytes 466952 | tf_op jit(solution)/shard_map/ppermute | solution.py:739
  203.2 10.3 %collective-permute-start.72 = (bf16[304,256]{1,0:T(8,128)(2,1)S(1)}, bf16[304,256]{1,0:T(8,128)(2,1)S(1)}, u32[]{:S(2)}, u32[]{:S(2)}) collective-permute-start(bf16[304,256]{1,0:T(8,128)(2,1)S(1)} %collective-permute-done.71.refs_6_), channel_id=1, source_target_pairs={{0,4},{4,0},{8,12},{12,8},{16,20},{20,16},{24,28},{28,24},{1,5},{5... | collective-permute-start | bytes 466952 | tf_op jit(solution)/shard_map/ppermute | solution.py:739
  209.4 5.3 %collective-permute-start.70 = (bf16[304,256]{1,0:T(8,128)(2,1)S(1)}, bf16[304,256]{1,0:T(8,128)(2,1)S(1)}, u32[]{:S(2)}, u32[]{:S(2)}) collective-permute-start(bf16[304,256]{1,0:T(8,128)(2,1)S(1)} %collective-permute-done.69.refs_4_), channel_id=1, source_target_pairs={{0,4},{4,0},{8,12},{12,8},{16,20},{20,16},{24,28},{28,24},{1,5},{5... | collective-permute-start | bytes 466952 | tf_op jit(solution)/shard_map/ppermute | solution.py:739
  209.8 6.6 %collective-permute-start.68 = (bf16[304,256]{1,0:T(8,128)(2,1)S(1)}, bf16[304,256]{1,0:T(8,128)(2,1)S(1)}, u32[]{:S(2)}, u32[]{:S(2)}) collective-permute-start(bf16[304,256]{1,0:T(8,128)(2,1)S(1)} %collective-permute-done.67.refs_2_), channel_id=1, source_target_pairs={{0,4},{4,0},{8,12},{12,8},{16,20},{20,16},{24,28},{28,24},{1,5},{5... | collective-permute-start | bytes 466952 | tf_op jit(solution)/shard_map/ppermute | solution.py:739
  (29 other events, 177.5 us)

commit v6 on v5

--- a/solution.py
+++ b/solution.py
@@ -532,7 +532,7 @@
         to_slabs(slabs, i, rounded.astype(F32))
         return 0
 
-    lax.fori_loop(0, lay.rows // STEP, back, 0)
+    lax.fori_loop(0, lay.rows // STEP, back, 0, unroll=True)
     mean, inverse, _ = moments(sums1)
 
     def step(part, carry):
@@ -913,8 +913,8 @@
         ),
         (like((rows, chan), F32), tile3, *([like((rows, inner), BF16)] * shards)),
     )
-    weights_back[1:3], s3 = hold((weights_back[1:3], s3))
-    weights_back[1], weights_back[2] = swap(weights_back[1], 1), swap(weights_back[2], 2)
+    weights_back[1:4], s3 = hold((weights_back[1:4], s3))
+    weights_back[1:4] = [swap(weights_back[k], k) for k in (1, 2, 3)]
     s3 = allsum(s3)
     weights_back[1:3], s3 = hold((weights_back[1:3], s3))
     output, du3, s4 = run(
@@ -922,8 +922,6 @@
         (z3, s3, g3, b3, mask, maps, upstream),
         (like((rows, chan), BF16), like((rows, chan), F32), tile3),
     )
-    weights_back[3], s4 = hold((weights_back[3], s4))
-    weights_back[3] = swap(weights_back[3], 3)
     s4 = allsum(s4)
     output = run(
         functools.partial(move_kernel, lay),

time: 219 us -> 219 us (level)
  transfers between devices with their start and end apart: 74 -> 74, of which waited for: 35 -> 35; matrix products, arithmetic and copies ran while one was open for 0% -> 0% of each run, Pallas kernels for 11% -> 13%
where the time goes in v6:
time: 219 us
  waiting for transfers between devices  83.3 us (38%)
  starting transfers between devices  82.6 us (38%)
  Pallas kernels  45.2 us (21%)
  local copies, waits for them, and re-layouts  5.45 us (2%)
    ppermute x44, starting transfers between devices, pass_on(): return lax.ppermute(x, 'batch', [(i, i ^ k) for i in range(ranks)])  62.3 us
    ppermute x44, waiting for transfers between devices, pass_on(): return lax.ppermute(x, 'batch', [(i, i ^ k) for i in range(ranks)])  56.6 us
    pallas_call x24, Pallas kernels, run(): pl.pallas_call(kernel, out_shape=list(outs), in_specs=specs, out_specs=[p...  45.2 us
    ppermute x30, waiting for transfers between devices, swap(): return lax.ppermute(x, 'tensor', [(i, i ^ k) for i in range(shards)])  26.7 us
    ppermute x30, starting transfers between devices, swap(): return lax.ppermute(x, 'tensor', [(i, i ^ k) for i in range(shards)])  20.4 us
    unnamed x38, local copies, waits for them, and re-layouts  5.18 us
  transfers between devices with their start and end apart: 74, of which 35 were waited for; matrix products, arithmetic and copies ran while one was open for 0% of the time, Pallas kernels for 13%

profile of v6, /device:TPU:0, one launch (start us, length us, event | category | flops | bytes accessed | tf_op | source)
XLA Modules:
  0.0 218.7 jit_solution(8261235752655457863)
XLA Ops:
  3.6 2.6 %collective-permute-start.2 = (bf16[243,2,512]{2,1,0:T(2,128)(2,1)}, bf16[243,2,512]{2,1,0:T(2,128)(2,1)}, u32[]{:S(2)}, u32[]{:S(2)}) collective-permute-start(bf16[243,2,512]{2,1,0:T(2,128)(2,1)} %bitcast.7.refs_2_), channel_id=1, source_target_pairs={{0,2},{1,3},{2,0},{3,1},{4,6},{5,7},{6,4},{7,5},{8,10},{9,11},{10,... | collective-permute-start | bytes 1493000 | tf_op jit(solution)/shard_map/ppermute | solution.py:736
  13.8 4.8 %collective-permute-done.2.far_0_ = bf16[243,2,512]{2,1,0:T(2,128)(2,1)} collective-permute-done((bf16[243,2,512]{2,1,0:T(2,128)(2,1)}, bf16[243,2,512]{2,1,0:T(2,128)(2,1)}, u32[]{:S(2)}, u32[]{:S(2)}) %collective-permute-start.2) | collective-permute-done | bytes 497696 | tf_op jit(solution)/shard_map/ppermute | solution.py:736
  18.7 1.9 collective-permute-start
  20.7 1.6 shard_map.311
  22.3 15.4 %collective-permute-done.far_0_ = bf16[150,2,512]{2,1,0:T(2,128)(2,1)S(1)} collective-permute-done((bf16[150,2,512]{2,1,0:T(2,128)(2,1)S(1)}, bf16[150,2,512]{2,1,0:T(2,128)(2,1)S(1)}, u32[]{:S(2)}, u32[]{:S(2)}) %collective-permute-start) | collective-permute-done | bytes 307232 | tf_op jit(solution)/shard_map/ppermute | solution.py:736
  38.3 1.8 collective-permute-start.12
  40.2 1.6 shard_map.312
  43.0 3.9 %collective-permute-start.9 = (f32[8,256]{1,0:T(8,128)S(1)}, f32[8,256]{1,0:T(8,128)S(1)}, u32[]{:S(2)}, u32[]{:S(2)}) collective-permute-start(f32[8,256]{1,0:T(8,128)S(1)} %get-tuple-element.168), channel_id=1, source_target_pairs={{0,24},{4,28},{8,16},{12,20},{16,8},{20,12},{24,0},{28,4},{1,25},{... | collective-permute-start | bytes 24584 | tf_op jit(solution)/shard_map/ppermute | solution.py:739
  46.9 1.6 collective-permute-done.9
  48.5 2.9 %collective-permute-done.8 = f32[8,256]{1,0:T(8,128)S(1)} collective-permute-done((f32[8,256]{1,0:T(8,128)S(1)}, f32[8,256]{1,0:T(8,128)S(1)}, u32[]{:S(2)}, u32[]{:S(2)}) %collective-permute-start.8) | collective-permute-done | bytes 8224 | tf_op jit(solution)/shard_map/ppermute | solution.py:739
  52.1 1.7 collective-permute-start.10
  53.9 1.9 collective-permute-done.10.sums1_1_
  55.8 2.8 %shard_map.314 = (f32[1392,256]{1,0:T(8,128)S(1)}, f32[8,256]{1,0:T(8,128)S(1)}, bf16[1392,256]{1,0:T(8,128)(2,1)S(1)}, bf16[1392,256]{1,0:T(8,128)(2,1)S(1)}, f32[8,256]{1,0:T(8,128)S(1)}) custom-call(f32[1392,256]{1,0:T(8,128)S(1)} %get-tuple-element.167.z1, f32[8,256]{1,0:T(8,128)S(1)} %add_add_fusion.6.sums1_0_, ...), custom_call_target="tpu_custom_call" | custom-call | flops 1048576 | tf_op jit(solution)/shard_map/pallas_call | solution.py:685
  58.7 1.8 collective-permute-start.15
  60.4 3.6 %collective-permute-start.18 = (f32[8,256]{1,0:T(8,128)S(1)}, f32[8,256]{1,0:T(8,128)S(1)}, u32[]{:S(2)}, u32[]{:S(2)}) collective-permute-start(f32[8,256]{1,0:T(8,128)S(1)} %get-tuple-element.181), channel_id=1, source_target_pairs={{0,24},{4,28},{8,16},{12,20},{16,8},{20,12},{24,0},{28,4},{1,25},{... | collective-permute-start | bytes 24584 | tf_op jit(solution)/shard_map/ppermute | solution.py:739
  65.9 2.7 %collective-permute-done.17 = f32[8,256]{1,0:T(8,128)S(1)} collective-permute-done((f32[8,256]{1,0:T(8,128)S(1)}, f32[8,256]{1,0:T(8,128)S(1)}, u32[]{:S(2)}, u32[]{:S(2)}) %collective-permute-start.17) | collective-permute-done | bytes 8224 | tf_op jit(solution)/shard_map/ppermute | solution.py:739
  68.6 1.6 collective-permute-start.19
  70.2 2.1 collective-permute-done.19.sums_1_.sums2_1_
  74.0 1.6 collective-permute-start.23
  77.3 2.2 collective-permute-done.22.stats_2_.stats_1_
  79.4 2.1 shard_map.316
  82.3 3.5 %collective-permute-start.28 = (f32[8,512]{1,0:T(8,128)S(1)}, f32[8,512]{1,0:T(8,128)S(1)}, u32[]{:S(2)}, u32[]{:S(2)}) collective-permute-start(f32[8,512]{1,0:T(8,128)S(1)} %get-tuple-element.196), channel_id=1, source_target_pairs={{0,24},{4,28},{8,16},{12,20},{16,8},{20,12},{24,0},{28,4},{1,25},{... | collective-permute-start | bytes 49160 | tf_op jit(solution)/shard_map/ppermute | solution.py:739
  87.8 2.6 %collective-permute-done.27 = f32[8,512]{1,0:T(8,128)S(1)} collective-permute-done((f32[8,512]{1,0:T(8,128)S(1)}, f32[8,512]{1,0:T(8,128)S(1)}, u32[]{:S(2)}, u32[]{:S(2)}) %collective-permute-start.27) | collective-permute-done | bytes 16416 | tf_op jit(solution)/shard_map/ppermute | solution.py:739
  90.5 1.6 collective-permute-start.29
  92.0 2.2 %collective-permute-done.29.sums3_1_ = f32[8,512]{1,0:T(8,128)S(1)} collective-permute-done((f32[8,512]{1,0:T(8,128)S(1)}, f32[8,512]{1,0:T(8,128)S(1)}, u32[]{:S(2)}, u32[]{:S(2)}) %collective-permute-start.29) | collective-permute-done | bytes 16416 | tf_op jit(solution)/shard_map/ppermute | solution.py:739
  94.3 2.4 %shard_map.317 = (bf16[1392,512]{1,0:T(8,128)(2,1)S(1)}, f32[1392,512]{1,0:T(8,128)S(1)}, f32[8,512]{1,0:T(8,128)S(1)}) custom-call(f32[1392,512]{1,0:T(8,128)S(1)} %get-tuple-element.189.z3, f32[8,512]{1,0:T(8,128)S(1)} %add_add_fusion.1.sums3_0_, f32[8,512]{1,0:T(8,128)S(1)} %collective-permute-done.29.sums3_1_, f32[1,512]{1,0:T(1,128)S(1)} %bitcast.115, ...), custom_call_target="tpu_custom_call" | custom-call | flops 1048576 | tf_op jit(solution)/shard_map/pallas_call | solution.py:685
  96.6 1.5 collective-permute-start.32
  98.8 2.3 %collective-permute-start.30 = (f32[8,512]{1,0:T(8,128)S(1)}, f32[8,512]{1,0:T(8,128)S(1)}, u32[]{:S(2)}, u32[]{:S(2)}) collective-permute-start(f32[8,512]{1,0:T(8,128)S(1)} %get-tuple-element.200), channel_id=1, source_target_pairs={{0,8},{4,12},{8,0},{12,4},{16,24},{20,28},{24,16},{28,20},{1,9},{5... | collective-permute-start | bytes 49160 | tf_op jit(solution)/shard_map/ppermute | solution.py:739
  103.0 1.6 collective-permute-start.33
  104.6 2.1 shard_map.318
  106.8 1.6 shard_map.319
  108.4 2.4 %shard_map.321 = (bf16[2,4,32,512]{3,2,1,0:T(8,128)(2,1)S(1)}, bf16[2,4,32,512]{3,2,1,0:T(8,128)(2,1)S(1)}, bf16[2,4,32,512]{3,2,1,0:T(8,128)(2,1)S(1)}, bf16[2,4,32,512]{3,2,1,0:T(8,128)(2,1)S(1)}) custom-call(s32[2]{0:T(128)S(1)} %pad_add_fusion.ids, bf16[1392,256]{1,0:T(8,128)(2,1)S(1)} %get-tuple-element.219.acts_0_, ...), custom_call_target="tpu_custom_call" | custom-call | flops 1048576 | tf_op jit(solution)/shard_map/pallas_call | solution.py:685
  110.8 1.6 collective-permute-start.37
  112.3 1.7 shard_map.322
  115.7 1.9 shard_map.320
  119.6 1.5 collective-permute-start.38
  121.3 1.6 collective-permute-start.36
  122.8 2.5 %collective-permute-start.45 = (f32[8,256]{1,0:T(8,128)S(1)}, f32[8,256]{1,0:T(8,128)S(1)}, u32[]{:S(2)}, u32[]{:S(2)}) collective-permute-start(f32[8,256]{1,0:T(8,128)S(1)} %add_add_fusion.4), channel_id=1, source_target_pairs={{0,24},{4,28},{8,16},{12,20},{16,8},{20,12},{24,0},{28,4},{1,25},{... | collective-permute-start | bytes 24584 | tf_op jit(solution)/shard_map/ppermute | solution.py:739
  127.5 1.9 collective-permute-start.47
  129.4 2.4 %collective-permute-start.48 = (bf16[4,32,512]{2,1,0:T(8,128)(2,1)S(1)}, bf16[4,32,512]{2,1,0:T(8,128)(2,1)S(1)}, u32[]{:S(2)}, u32[]{:S(2)}) collective-permute-start(bf16[4,32,512]{2,1,0:T(8,128)(2,1)S(1)} %get-tuple-element.312), channel_id=1, source_target_pairs={{0,24},{4,28},{8,16},{12,20},{16,8},{20,12},{24,0},{28,4},{1,25},{... | collective-permute-start | bytes 393224 | tf_op jit(solution)/shard_map/ppermute | solution.py:739
  131.9 1.6 collective-permute-start.46
  133.4 2.1 collective-permute-done.46.sums5_1_
  135.6 4.1 %collective-permute-done.39 = bf16[4,32,512]{2,1,0:T(8,128)(2,1)S(1)} collective-permute-done((bf16[4,32,512]{2,1,0:T(8,128)(2,1)S(1)}, bf16[4,32,512]{2,1,0:T(8,128)(2,1)S(1)}, u32[]{:S(2)}, u32[]{:S(2)}) %collective-permute-start.39) | collective-permute-done | bytes 131104 | tf_op jit(solution)/shard_map/ppermute | solution.py:739
  139.8 4.8 %shard_map.323 = (f32[1392,256]{1,0:T(8,128)S(1)}, f32[8,256]{1,0:T(8,128)S(1)}, bf16[1392,256]{1,0:T(8,128)(2,1)S(1)}, f32[1,256]{1,0:T(1,128)}, f32[1,256]{1,0:T(1,128)}) custom-call(f32[1392,256]{1,0:T(8,128)S(1)} %get-tuple-element.216.own, bf16[2,1392,256]{2,1,0:T(8,128)(2,1)S(1)} %collective-permute-done.35.near, ...), custom_call_target="tpu_custom_call" | custom-call | flops 1048576 | tf_op jit(solution)/shard_map/pallas_call | solution.py:685
  144.6 2.4 %collective-permute-start.51 = (f32[8,256]{1,0:T(8,128)S(1)}, f32[8,256]{1,0:T(8,128)S(1)}, u32[]{:S(2)}, u32[]{:S(2)}) collective-permute-start(f32[8,256]{1,0:T(8,128)S(1)} %get-tuple-element.241), channel_id=1, source_target_pairs={{0,24},{4,28},{8,16},{12,20},{16,8},{20,12},{24,0},{28,4},{1,25},{... | collective-permute-start | bytes 24584 | tf_op jit(solution)/shard_map/ppermute | solution.py:739
  153.2 3.3 %shard_map.324.group = bf16[256,384]{1,0:T(8,128)(2,1)S(1)} custom-call(bf16[1392,256]{1,0:T(8,128)(2,1)S(1)} %get-tuple-element.242.act, bf16[1392,256]{1,0:T(8,128)(2,1)S(1)} %get-tuple-element.244.dz, s32[1392,128]{1,0:T(8,128)S(1)} %copy-done.1, f32[256,256]{1,0:T(8,128)S(1)} %copy-done.3, bf16[2304,384]{1,0:T(8,128)(2,1)S(1)} %copy-done.2), custom_call_target="tpu_custom_call" | custom-call | flops 1048576 | tf_op jit(solution)/shard_map/pallas_call | solution.py:685
  156.6 2.3 %shard_map.325 = (bf16[1392,256]{1,0:T(8,128)(2,1)S(1)}, f32[1,256]{1,0:T(1,128)}, f32[1,256]{1,0:T(1,128)}, bf16[4,304,256]{2,1,0:T(8,128)(2,1)S(1)}) custom-call(s32[2]{0:T(128)S(1)} %pad_add_fusion.ids, f32[1392,256]{1,0:T(8,128)S(1)} %get-tuple-element.236.du1, f32[1392,256]{1,0:T(8,128)S(1)} %get-tuple-element.167.z1, ...), custom_call_target="tpu_custom_call" | custom-call | flops 1048576 | tf_op jit(solution)/shard_map/pallas_call | solution.py:685
  160.8 2.4 %collective-permute-start.59 = (bf16[4,32,512]{2,1,0:T(8,128)(2,1)S(1)}, bf16[4,32,512]{2,1,0:T(8,128)(2,1)S(1)}, u32[]{:S(2)}, u32[]{:S(2)}) collective-permute-start(bf16[4,32,512]{2,1,0:T(8,128)(2,1)S(1)} %pad_maximum_fusion.5.refs_0_), channel_id=1, source_target_pairs={{0,24},{4,28},{8,16},{12,20},{16,8},{20,12},{24,0},{28,4},{1,25},{... | collective-permute-start | bytes 393224 | tf_op jit(solution)/shard_map/ppermute | solution.py:739
  163.3 1.9 collective-permute-start.57
  165.2 1.6 shard_map.326
  166.8 7.3 %collective-permute-done.56 = bf16[4,304,256]{2,1,0:T(8,128)(2,1)S(1)} collective-permute-done((bf16[4,304,256]{2,1,0:T(8,128)(2,1)S(1)}, bf16[4,304,256]{2,1,0:T(8,128)(2,1)S(1)}, u32[]{:S(2)}, u32[]{:S(2)}) %collective-permute-start.56) | collective-permute-done | bytes 622624 | tf_op jit(solution)/shard_map/ppermute | solution.py:739
  174.3 1.9 collective-permute-done.63.d2
  176.8 1.7 collective-permute-start.73
  179.5 1.9 collective-permute-start.61
  182.8 2.8 %shard_map.327 = (f32[150,2,512]{2,1,0:T(2,128)}, f32[294,2,512]{2,1,0:T(2,128)}, f32[243,2,512]{2,1,0:T(2,128)}) custom-call(f32[1392,512]{1,0:T(8,128)S(1)} %get-tuple-element.209.du3, bf16[1392,256]{1,0:T(8,128)(2,1)S(1)} %get-tuple-element.263.dz.d0, bf16[1392,256]{1,0:T(8,128)(2,1)S(1)} %collective-permute-done.64.d1, ...), custom_call_target="tpu_custom_call" | custom-call | flops 1048576 | tf_op jit(solution)/shard_map/pallas_call | solution.py:685
  186.4 7.6 %collective-permute-done.61.refs_2_ = bf16[304,256]{1,0:T(8,128)(2,1)S(1)} collective-permute-done((bf16[304,256]{1,0:T(8,128)(2,1)S(1)}, bf16[304,256]{1,0:T(8,128)(2,1)S(1)}, u32[]{:S(2)}, u32[]{:S(2)}) %collective-permute-start.61) | collective-permute-done | bytes 155680 | tf_op jit(solution)/shard_map/ppermute | solution.py:739
  194.2 2.1 collective-permute-start.71
  196.3 3.4 %collective-permute-start.69 = (bf16[304,256]{1,0:T(8,128)(2,1)S(1)}, bf16[304,256]{1,0:T(8,128)(2,1)S(1)}, u32[]{:S(2)}, u32[]{:S(2)}) collective-permute-start(bf16[304,256]{1,0:T(8,128)(2,1)S(1)} %shard_map.328.refs_0_), channel_id=1, source_target_pairs={{0,16},{4,20},{8,24},{12,28},{16,0},{20,4},{24,8},{28,12},{1,17},{... | collective-permute-start | bytes 466952 | tf_op jit(solution)/shard_map/ppermute | solution.py:739
  200.1 2.9 %collective-permute-done.71.refs_6_ = bf16[304,256]{1,0:T(8,128)(2,1)S(1)} collective-permute-done((bf16[304,256]{1,0:T(8,128)(2,1)S(1)}, bf16[304,256]{1,0:T(8,128)(2,1)S(1)}, u32[]{:S(2)}, u32[]{:S(2)}) %collective-permute-start.71) | collective-permute-done | bytes 155680 | tf_op jit(solution)/shard_map/ppermute | solution.py:739
  203.4 5.7 %collective-permute-done.69.refs_4_ = bf16[304,256]{1,0:T(8,128)(2,1)S(1)} collective-permute-done((bf16[304,256]{1,0:T(8,128)(2,1)S(1)}, bf16[304,256]{1,0:T(8,128)(2,1)S(1)}, u32[]{:S(2)}, u32[]{:S(2)}) %collective-permute-start.69) | collective-permute-done | bytes 155680 | tf_op jit(solution)/shard_map/ppermute | solution.py:739
  209.6 1.6 collective-permute-start.68
  211.2 2.0 shard_map.330
  214.4 1.7 collective-permute-done.68.refs_3_
  216.0 2.6 %shard_map.329 = (f32[2048,256]{1,0:T(8,128)}, f32[9,8,32,32]{3,2,1,0:T(8,128)}) custom-call(s32[2]{0:T(128)S(1)} %pad_add_fusion.ids, bf16[304,256]{1,0:T(8,128)(2,1)S(1)} %shard_map.328.refs_0_, bf16[304,256]{1,0:T(8,128)(2,1)S(1)} %collective-permute-done.66.refs_1_, bf16[304,256]{1,0:T(8,128)(2,1)S(1)} %collective-permute-done.67.refs_2_, ...), custom_call_target="tpu_custom_call" | custom-call | flops 1048576 | tf_op jit(solution)/shard_map/pallas_call | solution.py:685
  (167 shorter events, 44.6 us)
Async XLA Ops:
  3.0 9.3 %collective-permute-start.3 = (bf16[1392,512]{1,0:T(8,128)(2,1)S(1)}, bf16[1392,512]{1,0:T(8,128)(2,1)S(1)}, u32[]{:S(2)}, u32[]{:S(2)}) collective-permute-start(bf16[1392,512]{1,0:T(8,128)(2,1)S(1)} %shard_map.309.own.x.xs_0__0_), channel_id=1, source_target_pairs={{0,1},{1,0},{2,3},{3,2},{4,5},{5,4},{6,7},{7,6},{8,9},{9,8},{10,11... | collective-permute-start | bytes 4276232 | tf_op jit(solution)/shard_map/ppermute | solution.py:736
  3.6 15.1 %collective-permute-start.2 = (bf16[243,2,512]{2,1,0:T(2,128)(2,1)}, bf16[243,2,512]{2,1,0:T(2,128)(2,1)}, u32[]{:S(2)}, u32[]{:S(2)}) collective-permute-start(bf16[243,2,512]{2,1,0:T(2,128)(2,1)} %bitcast.7.refs_2_), channel_id=1, source_target_pairs={{0,2},{1,3},{2,0},{3,1},{4,6},{5,7},{6,4},{7,5},{8,10},{9,11},{10,... | collective-permute-start | bytes 1493000 | tf_op jit(solution)/shard_map/ppermute | solution.py:736
  6.1 31.6 %collective-permute-start.1 = (bf16[294,2,512]{2,1,0:T(2,128)(2,1)}, bf16[294,2,512]{2,1,0:T(2,128)(2,1)}, u32[]{:S(2)}, u32[]{:S(2)}) collective-permute-start(bf16[294,2,512]{2,1,0:T(2,128)(2,1)} %bitcast.5.refs_1_), channel_id=1, source_target_pairs={{0,2},{1,3},{2,0},{3,1},{4,6},{5,7},{6,4},{7,5},{8,10},{9,11},{10,... | collective-permute-start | bytes 1806344 | tf_op jit(solution)/shard_map/ppermute | solution.py:736
  18.7 19.1 %collective-permute-start = (bf16[150,2,512]{2,1,0:T(2,128)(2,1)S(1)}, bf16[150,2,512]{2,1,0:T(2,128)(2,1)S(1)}, u32[]{:S(2)}, u32[]{:S(2)}) collective-permute-start(bf16[150,2,512]{2,1,0:T(2,128)(2,1)S(1)} %bitcast.111), channel_id=1, source_target_pairs={{0,2},{1,3},{2,0},{3,1},{4,6},{5,7},{6,4},{7,5},{8,10},{9,11},{10,... | collective-permute-start | bytes 921608 | tf_op jit(solution)/shard_map/ppermute | solution.py:736
  37.8 4.0 %collective-permute-start.6 = (bf16[294,2,512]{2,1,0:T(2,128)(2,1)}, bf16[294,2,512]{2,1,0:T(2,128)(2,1)S(1)}, u32[]{:S(2)}, u32[]{:S(2)}) collective-permute-start(bf16[294,2,512]{2,1,0:T(2,128)(2,1)} %collective-permute-done.1.far_1_), channel_id=1, source_target_pairs={{0,1},{1,0},{2,3},{3,2},{4,5},{5,4},{6,7},{7,6},{8,9},{9,8},{10,11... | collective-permute-start | bytes 1806344 | tf_op jit(solution)/shard_map/ppermute | solution.py:736
  37.8 4.0 %collective-permute-start.5 = (bf16[150,2,512]{2,1,0:T(2,128)(2,1)S(1)}, bf16[150,2,512]{2,1,0:T(2,128)(2,1)S(1)}, u32[]{:S(2)}, u32[]{:S(2)}) collective-permute-start(bf16[150,2,512]{2,1,0:T(2,128)(2,1)S(1)} %collective-permute-done.far_0_), channel_id=1, source_target_pairs={{0,1},{1,0},{2,3},{3,2},{4,5},{5,4},{6,7},{7,6},{8,9},{9,8},{10,11... | collective-permute-start | bytes 921608 | tf_op jit(solution)/shard_map/ppermute | solution.py:736
  38.3 15.6 %collective-permute-start.11 = (bf16[512,256]{1,0:T(8,128)(2,1)S(1)}, bf16[512,256]{1,0:T(8,128)(2,1)S(1)}, u32[]{:S(2)}, u32[]{:S(2)}) collective-permute-start(bf16[512,256]{1,0:T(8,128)(2,1)S(1)} %get-tuple-element.174), channel_id=1, source_target_pairs={{0,1},{1,0},{2,3},{3,2},{4,5},{5,4},{6,7},{7,6},{8,9},{9,8},{10,11... | collective-permute-start | bytes 786440 | tf_op jit(solution)/shard_map/ppermute | solution.py:736
  38.3 15.6 %collective-permute-start.12 = (bf16[512,256]{1,0:T(8,128)(2,1)S(1)}, bf16[512,256]{1,0:T(8,128)(2,1)S(1)}, u32[]{:S(2)}, u32[]{:S(2)}) collective-permute-start(bf16[512,256]{1,0:T(8,128)(2,1)S(1)} %get-tuple-element.175), channel_id=1, source_target_pairs={{0,2},{1,3},{2,0},{3,1},{4,6},{5,7},{6,4},{7,5},{8,10},{9,11},{10,... | collective-permute-start | bytes 786440 | tf_op jit(solution)/shard_map/ppermute | solution.py:736
  40.0 13.9 %collective-permute-start.13 = (bf16[512,256]{1,0:T(8,128)(2,1)S(1)}, bf16[512,256]{1,0:T(8,128)(2,1)S(1)}, u32[]{:S(2)}, u32[]{:S(2)}) collective-permute-start(bf16[512,256]{1,0:T(8,128)(2,1)S(1)} %get-tuple-element.176), channel_id=1, source_target_pairs={{0,3},{1,2},{2,1},{3,0},{4,7},{5,6},{6,5},{7,4},{8,11},{9,10},{10,... | collective-permute-start | bytes 786440 | tf_op jit(solution)/shard_map/ppermute | solution.py:736
  43.0 5.5 %collective-permute-start.9 = (f32[8,256]{1,0:T(8,128)S(1)}, f32[8,256]{1,0:T(8,128)S(1)}, u32[]{:S(2)}, u32[]{:S(2)}) collective-permute-start(f32[8,256]{1,0:T(8,128)S(1)} %get-tuple-element.168), channel_id=1, source_target_pairs={{0,24},{4,28},{8,16},{12,20},{16,8},{20,12},{24,0},{28,4},{1,25},{... | collective-permute-start | bytes 24584 | tf_op jit(solution)/shard_map/ppermute | solution.py:739
  46.9 4.5 %collective-permute-start.8 = (f32[8,256]{1,0:T(8,128)S(1)}, f32[8,256]{1,0:T(8,128)S(1)}, u32[]{:S(2)}, u32[]{:S(2)}) collective-permute-start(f32[8,256]{1,0:T(8,128)S(1)} %get-tuple-element.168), channel_id=1, source_target_pairs={{0,16},{4,20},{8,24},{12,28},{16,0},{20,4},{24,8},{28,12},{1,17},{... | collective-permute-start | bytes 24584 | tf_op jit(solution)/shard_map/ppermute | solution.py:739
  58.7 15.3 %collective-permute-start.15 = (bf16[1392,256]{1,0:T(8,128)(2,1)S(1)}, bf16[1392,256]{1,0:T(8,128)(2,1)S(1)}, u32[]{:S(2)}, u32[]{:S(2)}) collective-permute-start(bf16[1392,256]{1,0:T(8,128)(2,1)S(1)} %get-tuple-element.180.zs_0_), channel_id=1, source_target_pairs={{0,2},{1,3},{2,0},{3,1},{4,6},{5,7},{6,4},{7,5},{8,10},{9,11},{10,... | collective-permute-start | bytes 2138120 | tf_op jit(solution)/shard_map/ppermute | solution.py:736
  60.4 5.4 %collective-permute-start.18 = (f32[8,256]{1,0:T(8,128)S(1)}, f32[8,256]{1,0:T(8,128)S(1)}, u32[]{:S(2)}, u32[]{:S(2)}) collective-permute-start(f32[8,256]{1,0:T(8,128)S(1)} %get-tuple-element.181), channel_id=1, source_target_pairs={{0,24},{4,28},{8,16},{12,20},{16,8},{20,12},{24,0},{28,4},{1,25},{... | collective-permute-start | bytes 24584 | tf_op jit(solution)/shard_map/ppermute | solution.py:739
  64.0 4.5 %collective-permute-start.17 = (f32[8,256]{1,0:T(8,128)S(1)}, f32[8,256]{1,0:T(8,128)S(1)}, u32[]{:S(2)}, u32[]{:S(2)}) collective-permute-start(f32[8,256]{1,0:T(8,128)S(1)} %get-tuple-element.181), channel_id=1, source_target_pairs={{0,16},{4,20},{8,24},{12,28},{16,0},{20,4},{24,8},{28,12},{1,17},{... | collective-permute-start | bytes 24584 | tf_op jit(solution)/shard_map/ppermute | solution.py:739
  64.0 4.5 %collective-permute-start.16 = (f32[8,256]{1,0:T(8,128)S(1)}, f32[8,256]{1,0:T(8,128)S(1)}, u32[]{:S(2)}, u32[]{:S(2)}) collective-permute-start(f32[8,256]{1,0:T(8,128)S(1)} %get-tuple-element.181), channel_id=1, source_target_pairs={{0,8},{4,12},{8,0},{12,4},{16,24},{20,28},{24,16},{28,20},{1,9},{5... | collective-permute-start | bytes 24584 | tf_op jit(solution)/shard_map/ppermute | solution.py:739
  72.4 7.0 %collective-permute-start.14 = (bf16[1392,256]{1,0:T(8,128)(2,1)S(1)}, bf16[1392,256]{1,0:T(8,128)(2,1)S(1)}, u32[]{:S(2)}, u32[]{:S(2)}) collective-permute-start(bf16[1392,256]{1,0:T(8,128)(2,1)S(1)} %get-tuple-element.180.zs_0_), channel_id=1, source_target_pairs={{0,1},{1,0},{2,3},{3,2},{4,5},{5,4},{6,7},{7,6},{8,9},{9,8},{10,11... | collective-permute-start | bytes 2138120 | tf_op jit(solution)/shard_map/ppermute | solution.py:736
  74.0 5.4 %collective-permute-start.21 = (bf16[1392,256]{1,0:T(8,128)(2,1)S(1)}, bf16[1392,256]{1,0:T(8,128)(2,1)S(1)}, u32[]{:S(2)}, u32[]{:S(2)}) collective-permute-start(bf16[1392,256]{1,0:T(8,128)(2,1)S(1)} %collective-permute-done.15.zs_2_.zs_1_), channel_id=1, source_target_pairs={{0,1},{1,0},{2,3},{3,2},{4,5},{5,4},{6,7},{7,6},{8,9},{9,8},{10,11... | collective-permute-start | bytes 2138120 | tf_op jit(solution)/shard_map/ppermute | solution.py:736
  75.6 3.8 %collective-permute-start.22 = (f32[24,256]{1,0:T(8,128)S(1)}, f32[24,256]{1,0:T(8,128)S(1)}, u32[]{:S(2)}, u32[]{:S(2)}) collective-permute-start(f32[24,256]{1,0:T(8,128)S(1)} %shard_map.315.stats_0_), channel_id=1, source_target_pairs={{0,2},{1,3},{2,0},{3,1},{4,6},{5,7},{6,4},{7,5},{8,10},{9,11},{10,... | collective-permute-start | bytes 73736 | tf_op jit(solution)/shard_map/ppermute | solution.py:736
  81.6 12.7 %collective-permute-start.24 = (bf16[512,256]{1,0:T(8,128)(2,1)S(1)}, bf16[512,256]{1,0:T(8,128)(2,1)S(1)}, u32[]{:S(2)}, u32[]{:S(2)}) collective-permute-start(bf16[512,256]{1,0:T(8,128)(2,1)S(1)} %get-tuple-element.194), channel_id=1, source_target_pairs={{0,1},{1,0},{2,3},{3,2},{4,5},{5,4},{6,7},{7,6},{8,9},{9,8},{10,11... | collective-permute-start | bytes 786440 | tf_op jit(solution)/shard_map/ppermute | solution.py:736
  81.7 12.6 %collective-permute-start.25 = (bf16[512,256]{1,0:T(8,128)(2,1)S(1)}, bf16[512,256]{1,0:T(8,128)(2,1)S(1)}, u32[]{:S(2)}, u32[]{:S(2)}) collective-permute-start(bf16[512,256]{1,0:T(8,128)(2,1)S(1)} %get-tuple-element.195), channel_id=1, source_target_pairs={{0,2},{1,3},{2,0},{3,1},{4,6},{5,7},{6,4},{7,5},{8,10},{9,11},{10,... | collective-permute-start | bytes 786440 | tf_op jit(solution)/shard_map/ppermute | solution.py:736
  82.3 5.5 %collective-permute-start.28 = (f32[8,512]{1,0:T(8,128)S(1)}, f32[8,512]{1,0:T(8,128)S(1)}, u32[]{:S(2)}, u32[]{:S(2)}) collective-permute-start(f32[8,512]{1,0:T(8,128)S(1)} %get-tuple-element.196), channel_id=1, source_target_pairs={{0,24},{4,28},{8,16},{12,20},{16,8},{20,12},{24,0},{28,4},{1,25},{... | collective-permute-start | bytes 49160 | tf_op jit(solution)/shard_map/ppermute | solution.py:739
  85.8 4.6 %collective-permute-start.27 = (f32[8,512]{1,0:T(8,128)S(1)}, f32[8,512]{1,0:T(8,128)S(1)}, u32[]{:S(2)}, u32[]{:S(2)}) collective-permute-start(f32[8,512]{1,0:T(8,128)S(1)} %get-tuple-element.196), channel_id=1, source_target_pairs={{0,16},{4,20},{8,24},{12,28},{16,0},{20,4},{24,8},{28,12},{1,17},{... | collective-permute-start | bytes 49160 | tf_op jit(solution)/shard_map/ppermute | solution.py:739
  85.8 4.6 %collective-permute-start.26 = (f32[8,512]{1,0:T(8,128)S(1)}, f32[8,512]{1,0:T(8,128)S(1)}, u32[]{:S(2)}, u32[]{:S(2)}) collective-permute-start(f32[8,512]{1,0:T(8,128)S(1)} %get-tuple-element.196), channel_id=1, source_target_pairs={{0,8},{4,12},{8,0},{12,4},{16,24},{20,28},{24,16},{28,20},{1,9},{5... | collective-permute-start | bytes 49160 | tf_op jit(solution)/shard_map/ppermute | solution.py:739
  92.0 14.7 %collective-permute-start.34 = (bf16[512,256]{1,0:T(8,128)(2,1)S(1)}, bf16[512,256]{1,0:T(8,128)(2,1)S(1)}, u32[]{:S(2)}, u32[]{:S(2)}) collective-permute-start(bf16[512,256]{1,0:T(8,128)(2,1)S(1)} %get-tuple-element.210), channel_id=1, source_target_pairs={{0,3},{1,2},{2,1},{3,0},{4,7},{5,6},{6,5},{7,4},{8,11},{9,10},{10,... | collective-permute-start | bytes 786440 | tf_op jit(solution)/shard_map/ppermute | solution.py:736
  96.6 5.7 %collective-permute-start.32 = (f32[8,512]{1,0:T(8,128)S(1)}, f32[8,512]{1,0:T(8,128)S(1)}, u32[]{:S(2)}, u32[]{:S(2)}) collective-permute-start(f32[8,512]{1,0:T(8,128)S(1)} %get-tuple-element.200), channel_id=1, source_target_pairs={{0,24},{4,28},{8,16},{12,20},{16,8},{20,12},{24,0},{28,4},{1,25},{... | collective-permute-start | bytes 49160 | tf_op jit(solution)/shard_map/ppermute | solution.py:739
  98.2 4.7 %collective-permute-start.31 = (f32[8,512]{1,0:T(8,128)S(1)}, f32[8,512]{1,0:T(8,128)S(1)}, u32[]{:S(2)}, u32[]{:S(2)}) collective-permute-start(f32[8,512]{1,0:T(8,128)S(1)} %get-tuple-element.200), channel_id=1, source_target_pairs={{0,16},{4,20},{8,24},{12,28},{16,0},{20,4},{24,8},{28,12},{1,17},{... | collective-permute-start | bytes 49160 | tf_op jit(solution)/shard_map/ppermute | solution.py:739
  98.8 4.2 %collective-permute-start.30 = (f32[8,512]{1,0:T(8,128)S(1)}, f32[8,512]{1,0:T(8,128)S(1)}, u32[]{:S(2)}, u32[]{:S(2)}) collective-permute-start(f32[8,512]{1,0:T(8,128)S(1)} %get-tuple-element.200), channel_id=1, source_target_pairs={{0,8},{4,12},{8,0},{12,4},{16,24},{20,28},{24,16},{28,20},{1,9},{5... | collective-permute-start | bytes 49160 | tf_op jit(solution)/shard_map/ppermute | solution.py:739
  108.4 12.7 %collective-permute-start.35 = (bf16[2,1392,256]{2,1,0:T(8,128)(2,1)S(1)}, bf16[2,1392,256]{2,1,0:T(8,128)(2,1)S(1)}, u32[]{:S(2)}, u32[]{:S(2)}) collective-permute-start(bf16[2,1392,256]{2,1,0:T(8,128)(2,1)S(1)} %get-tuple-element.217.send), channel_id=1, source_target_pairs={{0,1},{1,0},{2,3},{3,2},{4,5},{5,4},{6,7},{7,6},{8,9},{9,8},{10,11... | collective-permute-start | bytes 4276232 | tf_op jit(solution)/shard_map/ppermute | solution.py:736
  110.8 8.8 %collective-permute-start.37 = (bf16[2,4,32,512]{3,2,1,0:T(8,128)(2,1)S(1)}, bf16[2,4,32,512]{3,2,1,0:T(8,128)(2,1)S(1)}, u32[]{:S(2)}, u32[]{:S(2)}) collective-permute-start(bf16[2,4,32,512]{3,2,1,0:T(8,128)(2,1)S(1)} %get-tuple-element.225), channel_id=1, source_target_pairs={{0,4},{4,0},{8,12},{12,8},{16,20},{20,16},{24,28},{28,24},{1,5},{5... | collective-permute-start | bytes 786440 | tf_op jit(solution)/shard_map/ppermute | solution.py:739
  114.1 8.8 %collective-permute-start.40 = (f32[8,256]{1,0:T(8,128)S(1)}, f32[8,256]{1,0:T(8,128)S(1)}, u32[]{:S(2)}, u32[]{:S(2)}) collective-permute-start(f32[8,256]{1,0:T(8,128)S(1)} %get-tuple-element.228), channel_id=1, source_target_pairs={{0,1},{1,0},{2,3},{3,2},{4,5},{5,4},{6,7},{7,6},{8,9},{9,8},{10,11... | collective-permute-start | bytes 24584 | tf_op jit(solution)/shard_map/ppermute | solution.py:736
  114.4 8.5 %collective-permute-start.42 = (f32[8,256]{1,0:T(8,128)S(1)}, f32[8,256]{1,0:T(8,128)S(1)}, u32[]{:S(2)}, u32[]{:S(2)}) collective-permute-start(f32[8,256]{1,0:T(8,128)S(1)} %get-tuple-element.230), channel_id=1, source_target_pairs={{0,3},{1,2},{2,1},{3,0},{4,7},{5,6},{6,5},{7,4},{8,11},{9,10},{10,... | collective-permute-start | bytes 24584 | tf_op jit(solution)/shard_map/ppermute | solution.py:736
  117.7 5.2 %collective-permute-start.41 = (f32[8,256]{1,0:T(8,128)S(1)}, f32[8,256]{1,0:T(8,128)S(1)}, u32[]{:S(2)}, u32[]{:S(2)}) collective-permute-start(f32[8,256]{1,0:T(8,128)S(1)} %get-tuple-element.229), channel_id=1, source_target_pairs={{0,2},{1,3},{2,0},{3,1},{4,6},{5,7},{6,4},{7,5},{8,10},{9,11},{10,... | collective-permute-start | bytes 24584 | tf_op jit(solution)/shard_map/ppermute | solution.py:736
  119.6 7.9 %collective-permute-start.38 = (bf16[2,4,32,512]{3,2,1,0:T(8,128)(2,1)S(1)}, bf16[2,4,32,512]{3,2,1,0:T(8,128)(2,1)S(1)}, u32[]{:S(2)}, u32[]{:S(2)}) collective-permute-start(bf16[2,4,32,512]{3,2,1,0:T(8,128)(2,1)S(1)} %get-tuple-element.226), channel_id=1, source_target_pairs={{0,4},{4,0},{8,12},{12,8},{16,20},{20,16},{24,28},{28,24},{1,5},{5... | collective-permute-start | bytes 786440 | tf_op jit(solution)/shard_map/ppermute | solution.py:739
  121.3 18.4 %collective-permute-start.36 = (bf16[1392,256]{1,0:T(8,128)(2,1)S(1)}, bf16[1392,256]{1,0:T(8,128)(2,1)S(1)}, u32[]{:S(2)}, u32[]{:S(2)}) collective-permute-start(bf16[1392,256]{1,0:T(8,128)(2,1)S(1)} %fusion), channel_id=1, source_target_pairs={{0,2},{1,3},{2,0},{3,1},{4,6},{5,7},{6,4},{7,5},{8,10},{9,11},{10,... | collective-permute-start | bytes 2138120 | tf_op jit(solution)/shard_map/ppermute | solution.py:736
  122.8 6.5 %collective-permute-start.45 = (f32[8,256]{1,0:T(8,128)S(1)}, f32[8,256]{1,0:T(8,128)S(1)}, u32[]{:S(2)}, u32[]{:S(2)}) collective-permute-start(f32[8,256]{1,0:T(8,128)S(1)} %add_add_fusion.4), channel_id=1, source_target_pairs={{0,24},{4,28},{8,16},{12,20},{16,8},{20,12},{24,0},{28,4},{1,25},{... | collective-permute-start | bytes 24584 | tf_op jit(solution)/shard_map/ppermute | solution.py:739
  125.3 6.5 %collective-permute-start.44 = (f32[8,256]{1,0:T(8,128)S(1)}, f32[8,256]{1,0:T(8,128)S(1)}, u32[]{:S(2)}, u32[]{:S(2)}) collective-permute-start(f32[8,256]{1,0:T(8,128)S(1)} %add_add_fusion.4), channel_id=1, source_target_pairs={{0,16},{4,20},{8,24},{12,28},{16,0},{20,4},{24,8},{28,12},{1,17},{... | collective-permute-start | bytes 24584 | tf_op jit(solution)/shard_map/ppermute | solution.py:739
  126.2 5.6 %collective-permute-start.43 = (f32[8,256]{1,0:T(8,128)S(1)}, f32[8,256]{1,0:T(8,128)S(1)}, u32[]{:S(2)}, u32[]{:S(2)}) collective-permute-start(f32[8,256]{1,0:T(8,128)S(1)} %add_add_fusion.4), channel_id=1, source_target_pairs={{0,8},{4,12},{8,0},{12,4},{16,24},{20,28},{24,16},{28,20},{1,9},{5... | collective-permute-start | bytes 24584 | tf_op jit(solution)/shard_map/ppermute | solution.py:739
  127.5 12.2 %collective-permute-start.47 = (bf16[4,32,512]{2,1,0:T(8,128)(2,1)S(1)}, bf16[4,32,512]{2,1,0:T(8,128)(2,1)S(1)}, u32[]{:S(2)}, u32[]{:S(2)}) collective-permute-start(bf16[4,32,512]{2,1,0:T(8,128)(2,1)S(1)} %get-tuple-element.311), channel_id=1, source_target_pairs={{0,16},{4,20},{8,24},{12,28},{16,0},{20,4},{24,8},{28,12},{1,17},{... | collective-permute-start | bytes 393224 | tf_op jit(solution)/shard_map/ppermute | solution.py:739
  129.4 10.3 %collective-permute-start.48 = (bf16[4,32,512]{2,1,0:T(8,128)(2,1)S(1)}, bf16[4,32,512]{2,1,0:T(8,128)(2,1)S(1)}, u32[]{:S(2)}, u32[]{:S(2)}) collective-permute-start(bf16[4,32,512]{2,1,0:T(8,128)(2,1)S(1)} %get-tuple-element.312), channel_id=1, source_target_pairs={{0,24},{4,28},{8,16},{12,20},{16,8},{20,12},{24,0},{28,4},{1,25},{... | collective-permute-start | bytes 393224 | tf_op jit(solution)/shard_map/ppermute | solution.py:739
  131.8 7.9 %collective-permute-start.39 = (bf16[4,32,512]{2,1,0:T(8,128)(2,1)S(1)}, bf16[4,32,512]{2,1,0:T(8,128)(2,1)S(1)}, u32[]{:S(2)}, u32[]{:S(2)}) collective-permute-start(bf16[4,32,512]{2,1,0:T(8,128)(2,1)S(1)} %fusion.8), channel_id=1, source_target_pairs={{0,8},{4,12},{8,0},{12,4},{16,24},{20,28},{24,16},{28,20},{1,9},{5... | collective-permute-start | bytes 393224 | tf_op jit(solution)/shard_map/ppermute | solution.py:739
  144.6 6.0 %collective-permute-start.51 = (f32[8,256]{1,0:T(8,128)S(1)}, f32[8,256]{1,0:T(8,128)S(1)}, u32[]{:S(2)}, u32[]{:S(2)}) collective-permute-start(f32[8,256]{1,0:T(8,128)S(1)} %get-tuple-element.241), channel_id=1, source_target_pairs={{0,24},{4,28},{8,16},{12,20},{16,8},{20,12},{24,0},{28,4},{1,25},{... | collective-permute-start | bytes 24584 | tf_op jit(solution)/shard_map/ppermute | solution.py:739
  147.0 4.5 %collective-permute-start.50 = (f32[8,256]{1,0:T(8,128)S(1)}, f32[8,256]{1,0:T(8,128)S(1)}, u32[]{:S(2)}, u32[]{:S(2)}) collective-permute-start(f32[8,256]{1,0:T(8,128)S(1)} %get-tuple-element.241), channel_id=1, source_target_pairs={{0,16},{4,20},{8,24},{12,28},{16,0},{20,4},{24,8},{28,12},{1,17},{... | collective-permute-start | bytes 24584 | tf_op jit(solution)/shard_map/ppermute | solution.py:739
  149.0 7.5 %collective-permute-start.55 = (bf16[32,512]{1,0:T(8,128)(2,1)S(1)}, bf16[32,512]{1,0:T(8,128)(2,1)S(1)}, u32[]{:S(2)}, u32[]{:S(2)}) collective-permute-start(bf16[32,512]{1,0:T(8,128)(2,1)S(1)} %get-tuple-element.314), channel_id=1, source_target_pairs={{0,3},{1,2},{2,1},{3,0},{4,7},{5,6},{6,5},{7,4},{8,11},{9,10},{10,... | collective-permute-start | bytes 98312 | tf_op jit(solution)/shard_map/ppermute | solution.py:736
  149.1 7.4 %collective-permute-start.54 = (bf16[32,512]{1,0:T(8,128)(2,1)S(1)}, bf16[32,512]{1,0:T(8,128)(2,1)S(1)}, u32[]{:S(2)}, u32[]{:S(2)}) collective-permute-start(bf16[32,512]{1,0:T(8,128)(2,1)S(1)} %get-tuple-element.315), channel_id=1, source_target_pairs={{0,2},{1,3},{2,0},{3,1},{4,6},{5,7},{6,4},{7,5},{8,10},{9,11},{10,... | collective-permute-start | bytes 98312 | tf_op jit(solution)/shard_map/ppermute | solution.py:736
  150.6 5.9 %collective-permute-start.53 = (bf16[32,512]{1,0:T(8,128)(2,1)S(1)}, bf16[32,512]{1,0:T(8,128)(2,1)S(1)}, u32[]{:S(2)}, u32[]{:S(2)}) collective-permute-start(bf16[32,512]{1,0:T(8,128)(2,1)S(1)} %get-tuple-element.316), channel_id=1, source_target_pairs={{0,1},{1,0},{2,3},{3,2},{4,5},{5,4},{6,7},{7,6},{8,9},{9,8},{10,11... | collective-permute-start | bytes 98312 | tf_op jit(solution)/shard_map/ppermute | solution.py:736
  151.7 4.9 %collective-permute-start.52 = (f32[8,256]{1,0:T(8,128)S(1)}, f32[8,256]{1,0:T(8,128)S(1)}, u32[]{:S(2)}, u32[]{:S(2)}) collective-permute-start(f32[8,256]{1,0:T(8,128)S(1)} %add_add_fusion.2.sums6_0_), channel_id=1, source_target_pairs={{0,4},{4,0},{8,12},{12,8},{16,20},{20,16},{24,28},{28,24},{1,5},{5... | collective-permute-start | bytes 24584 | tf_op jit(solution)/shard_map/ppermute | solution.py:739
  158.9 15.2 %collective-permute-start.56 = (bf16[4,304,256]{2,1,0:T(8,128)(2,1)S(1)}, bf16[4,304,256]{2,1,0:T(8,128)(2,1)S(1)}, u32[]{:S(2)}, u32[]{:S(2)}) collective-permute-start(bf16[4,304,256]{2,1,0:T(8,128)(2,1)S(1)} %get-tuple-element.256), channel_id=1, source_target_pairs={{0,4},{4,0},{8,12},{12,8},{16,20},{20,16},{24,28},{28,24},{1,5},{5... | collective-permute-start | bytes 1867784 | tf_op jit(solution)/shard_map/ppermute | solution.py:739
  159.4 16.8 %collective-permute-start.63 = (bf16[1392,256]{1,0:T(8,128)(2,1)S(1)}, bf16[1392,256]{1,0:T(8,128)(2,1)S(1)}, u32[]{:S(2)}, u32[]{:S(2)}) collective-permute-start(bf16[1392,256]{1,0:T(8,128)(2,1)S(1)} %get-tuple-element.263.dz.d0), channel_id=1, source_target_pairs={{0,2},{1,3},{2,0},{3,1},{4,6},{5,7},{6,4},{7,5},{8,10},{9,11},{10,... | collective-permute-start | bytes 2138120 | tf_op jit(solution)/shard_map/ppermute | solution.py:736
  160.8 13.5 %collective-permute-start.59 = (bf16[4,32,512]{2,1,0:T(8,128)(2,1)S(1)}, bf16[4,32,512]{2,1,0:T(8,128)(2,1)S(1)}, u32[]{:S(2)}, u32[]{:S(2)}) collective-permute-start(bf16[4,32,512]{2,1,0:T(8,128)(2,1)S(1)} %pad_maximum_fusion.5.refs_0_), channel_id=1, source_target_pairs={{0,24},{4,28},{8,16},{12,20},{16,8},{20,12},{24,0},{28,4},{1,25},{... | collective-permute-start | bytes 393224 | tf_op jit(solution)/shard_map/ppermute | solution.py:739
  163.2 11.1 %collective-permute-start.58 = (bf16[4,32,512]{2,1,0:T(8,128)(2,1)S(1)}, bf16[4,32,512]{2,1,0:T(8,128)(2,1)S(1)}, u32[]{:S(2)}, u32[]{:S(2)}) collective-permute-start(bf16[4,32,512]{2,1,0:T(8,128)(2,1)S(1)} %pad_maximum_fusion.5.refs_0_), channel_id=1, source_target_pairs={{0,16},{4,20},{8,24},{12,28},{16,0},{20,4},{24,8},{28,12},{1,17},{... | collective-permute-start | bytes 393224 | tf_op jit(solution)/shard_map/ppermute | solution.py:739
  163.3 11.0 %collective-permute-start.57 = (bf16[4,32,512]{2,1,0:T(8,128)(2,1)S(1)}, bf16[4,32,512]{2,1,0:T(8,128)(2,1)S(1)}, u32[]{:S(2)}, u32[]{:S(2)}) collective-permute-start(bf16[4,32,512]{2,1,0:T(8,128)(2,1)S(1)} %pad_maximum_fusion.5.refs_0_), channel_id=1, source_target_pairs={{0,8},{4,12},{8,0},{12,4},{16,24},{20,28},{24,16},{28,20},{1,9},{5... | collective-permute-start | bytes 393224 | tf_op jit(solution)/shard_map/ppermute | solution.py:739
  176.2 5.2 %collective-permute-start.64 = (bf16[1392,256]{1,0:T(8,128)(2,1)S(1)}, bf16[1392,256]{1,0:T(8,128)(2,1)S(1)}, u32[]{:S(2)}, u32[]{:S(2)}) collective-permute-start(bf16[1392,256]{1,0:T(8,128)(2,1)S(1)} %get-tuple-element.263.dz.d0), channel_id=1, source_target_pairs={{0,1},{1,0},{2,3},{3,2},{4,5},{5,4},{6,7},{7,6},{8,9},{9,8},{10,11... | collective-permute-start | bytes 2138120 | tf_op jit(solution)/shard_map/ppermute | solution.py:736
  176.2 6.6 %collective-permute-start.65 = (bf16[1392,256]{1,0:T(8,128)(2,1)S(1)}, bf16[1392,256]{1,0:T(8,128)(2,1)S(1)}, u32[]{:S(2)}, u32[]{:S(2)}) collective-permute-start(bf16[1392,256]{1,0:T(8,128)(2,1)S(1)} %collective-permute-done.63.d2), channel_id=1, source_target_pairs={{0,1},{1,0},{2,3},{3,2},{4,5},{5,4},{6,7},{7,6},{8,9},{9,8},{10,11... | collective-permute-start | bytes 2138120 | tf_op jit(solution)/shard_map/ppermute | solution.py:736
  176.8 34.4 %collective-permute-start.73 = (bf16[4,4,32,512]{3,2,1,0:T(8,128)(2,1)S(1)}, bf16[4,4,32,512]{3,2,1,0:T(8,128)(2,1)S(1)}, u32[]{:S(2)}, u32[]{:S(2)}) collective-permute-start(bf16[4,4,32,512]{3,2,1,0:T(8,128)(2,1)S(1)} %pad_maximum_fusion), channel_id=1, source_target_pairs={{0,4},{4,0},{8,12},{12,8},{16,20},{20,16},{24,28},{28,24},{1,5},{5... | collective-permute-start | bytes 1572872 | tf_op jit(solution)/shard_map/ppermute | solution.py:739
  178.4 8.0 %collective-permute-start.60 = (bf16[304,256]{1,0:T(8,128)(2,1)S(1)}, bf16[304,256]{1,0:T(8,128)(2,1)S(1)}, u32[]{:S(2)}, u32[]{:S(2)}) collective-permute-start(bf16[304,256]{1,0:T(8,128)(2,1)S(1)} %get-tuple-element.259), channel_id=1, source_target_pairs={{0,8},{4,12},{8,0},{12,4},{16,24},{20,28},{24,16},{28,20},{1,9},{5... | collective-permute-start | bytes 466952 | tf_op jit(solution)/shard_map/ppermute | solution.py:739
  179.5 14.5 %collective-permute-start.61 = (bf16[304,256]{1,0:T(8,128)(2,1)S(1)}, bf16[304,256]{1,0:T(8,128)(2,1)S(1)}, u32[]{:S(2)}, u32[]{:S(2)}) collective-permute-start(bf16[304,256]{1,0:T(8,128)(2,1)S(1)} %get-tuple-element.260), channel_id=1, source_target_pairs={{0,16},{4,20},{8,24},{12,28},{16,0},{20,4},{24,8},{28,12},{1,17},{... | collective-permute-start | bytes 466952 | tf_op jit(solution)/shard_map/ppermute | solution.py:739
  181.4 12.6 %collective-permute-start.62 = (bf16[304,256]{1,0:T(8,128)(2,1)S(1)}, bf16[304,256]{1,0:T(8,128)(2,1)S(1)}, u32[]{:S(2)}, u32[]{:S(2)}) collective-permute-start(bf16[304,256]{1,0:T(8,128)(2,1)S(1)} %get-tuple-element.261), channel_id=1, source_target_pairs={{0,24},{4,28},{8,16},{12,20},{16,8},{20,12},{24,0},{28,4},{1,25},{... | collective-permute-start | bytes 466952 | tf_op jit(solution)/shard_map/ppermute | solution.py:739
  194.2 8.9 %collective-permute-start.71 = (bf16[304,256]{1,0:T(8,128)(2,1)S(1)}, bf16[304,256]{1,0:T(8,128)(2,1)S(1)}, u32[]{:S(2)}, u32[]{:S(2)}) collective-permute-start(bf16[304,256]{1,0:T(8,128)(2,1)S(1)} %shard_map.328.refs_0_), channel_id=1, source_target_pairs={{0,24},{4,28},{8,16},{12,20},{16,8},{20,12},{24,0},{28,4},{1,25},{... | collective-permute-start | bytes 466952 | tf_op jit(solution)/shard_map/ppermute | solution.py:739
  196.3 12.9 %collective-permute-start.69 = (bf16[304,256]{1,0:T(8,128)(2,1)S(1)}, bf16[304,256]{1,0:T(8,128)(2,1)S(1)}, u32[]{:S(2)}, u32[]{:S(2)}) collective-permute-start(bf16[304,256]{1,0:T(8,128)(2,1)S(1)} %shard_map.328.refs_0_), channel_id=1, source_target_pairs={{0,16},{4,20},{8,24},{12,28},{16,0},{20,4},{24,8},{28,12},{1,17},{... | collective-permute-start | bytes 466952 | tf_op jit(solution)/shard_map/ppermute | solution.py:739
  199.7 9.9 %collective-permute-start.67 = (bf16[304,256]{1,0:T(8,128)(2,1)S(1)}, bf16[304,256]{1,0:T(8,128)(2,1)S(1)}, u32[]{:S(2)}, u32[]{:S(2)}) collective-permute-start(bf16[304,256]{1,0:T(8,128)(2,1)S(1)} %shard_map.328.refs_0_), channel_id=1, source_target_pairs={{0,8},{4,12},{8,0},{12,4},{16,24},{20,28},{24,16},{28,20},{1,9},{5... | collective-permute-start | bytes 466952 | tf_op jit(solution)/shard_map/ppermute | solution.py:739
  199.7 13.5 %collective-permute-start.66 = (bf16[304,256]{1,0:T(8,128)(2,1)S(1)}, bf16[304,256]{1,0:T(8,128)(2,1)S(1)}, u32[]{:S(2)}, u32[]{:S(2)}) collective-permute-start(bf16[304,256]{1,0:T(8,128)(2,1)S(1)} %shard_map.328.refs_0_), channel_id=1, source_target_pairs={{0,4},{4,0},{8,12},{12,8},{16,20},{20,16},{24,28},{28,24},{1,5},{5... | collective-permute-start | bytes 466952 | tf_op jit(solution)/shard_map/ppermute | solution.py:739
  203.0 10.2 %collective-permute-start.72 = (bf16[304,256]{1,0:T(8,128)(2,1)S(1)}, bf16[304,256]{1,0:T(8,128)(2,1)S(1)}, u32[]{:S(2)}, u32[]{:S(2)}) collective-permute-start(bf16[304,256]{1,0:T(8,128)(2,1)S(1)} %collective-permute-done.71.refs_6_), channel_id=1, source_target_pairs={{0,4},{4,0},{8,12},{12,8},{16,20},{20,16},{24,28},{28,24},{1,5},{5... | collective-permute-start | bytes 466952 | tf_op jit(solution)/shard_map/ppermute | solution.py:739
  209.1 5.2 %collective-permute-start.70 = (bf16[304,256]{1,0:T(8,128)(2,1)S(1)}, bf16[304,256]{1,0:T(8,128)(2,1)S(1)}, u32[]{:S(2)}, u32[]{:S(2)}) collective-permute-start(bf16[304,256]{1,0:T(8,128)(2,1)S(1)} %collective-permute-done.69.refs_4_), channel_id=1, source_target_pairs={{0,4},{4,0},{8,12},{12,8},{16,20},{20,16},{24,28},{28,24},{1,5},{5... | collective-permute-start | bytes 466952 | tf_op jit(solution)/shard_map/ppermute | solution.py:739
  209.6 6.5 %collective-permute-start.68 = (bf16[304,256]{1,0:T(8,128)(2,1)S(1)}, bf16[304,256]{1,0:T(8,128)(2,1)S(1)}, u32[]{:S(2)}, u32[]{:S(2)}) collective-permute-start(bf16[304,256]{1,0:T(8,128)(2,1)S(1)} %collective-permute-done.67.refs_2_), channel_id=1, source_target_pairs={{0,4},{4,0},{8,12},{12,8},{16,20},{20,16},{24,28},{28,24},{1,5},{5... | collective-permute-start | bytes 466952 | tf_op jit(solution)/shard_map/ppermute | solution.py:739
  (29 other events, 177.7 us)
